TPU v7x, 512 devices: a whole 4x4x16 slice. The times are simulated.
512 devices in a mesh: rows: 128 (over x, z, core), rep: 4 (over y).
Axes of the slice: x: 4, y: 4, z: 16, core: 2. Of those that a mesh axis runs over, the one named last changes fastest.
Arguments:
- feats: bfloat16 [4, 32768, 512], P('rep', 'rows'), may hold values from -24 to 24
- grad_out: bfloat16 [4, 32768, 512], P('rep', 'rows'), may hold values from -6 to 6
- qkv_weight: bfloat16 [512, 1536], P('rows'), may hold values from -0.25 to 0.25
- proj_weight: bfloat16 [512, 512], P('rows'), may hold values from -0.25 to 0.25
- to_hilbert: int32 [4, 16384], P('rep', 'rows'), may hold values from 0 to 16383, as said below
- to_zorder: int32 [4, 16384], P('rep', 'rows'), may hold values from 0 to 16383, as said below
Outputs:
- grad_feats: bfloat16 [4, 32768, 512], P('rep', 'rows')
- qkv_grad: float32 [512, 1536], P('rows')
- proj_grad: float32 [512, 512], P('rows')
Inputs may be any that keep to these rules, and one draw needn't show every extreme that they name: to_hilbert[s] is a permutation of the blocks of scene s and to_zorder[s] its inverse; of the 128 Z-order blocks of one device, at most 2 have Hilbert positions on any one device, and exactly 2 for some pair of devices in every scene. `to_zorder`: the inverse of to_hilbert in every scene.
All inputs are finite; a program needn't handle non-finite values.
Results may differ from a plain program's by a relative error of at most 0.015.
The roundings to bfloat16 on the way count: a program that leaves them out, or rounds other values in their place, can miss the bound.
Values may be sent and summed in bfloat16 or wider, within the bound.
No kernel may reach another device: no remote copies, remote signals or barrier semaphores. Data moves between devices by JAX's collectives and lax.ppermute only.
A program may use at most 64 MiB of HBM per device.

v0:
```python
import jax
import jax.numpy as jnp
from jax import lax
from jax.sharding import PartitionSpec as P

HEADS = 8
CAP = 2


def from_partner(block, axis, apart):
    count = lax.axis_size(axis)
    route = []
    for low in range(count):
        high = low | 1 << apart
        if high != low and high < count:
            route += [(low, high), (high, low)]
    return lax.ppermute(block, axis, route)


def move_blocks(outgoing):
    return lax.all_to_all(outgoing, "rows", split_axis=0, concat_axis=0, tiled=True)


def rank_within(order_keys, owners):
    same_owner = owners[None, :] == owners[:, None]
    earlier = order_keys[None, :] < order_keys[:, None]
    return jnp.sum(jnp.logical_and(same_owner, earlier).astype(jnp.int32), axis=1)


def contract_rows(left, right):
    return lax.dot_general(
        left, right, (((0,), (0,)), ((), ())), preferred_element_type=jnp.float32
    )


def contract_cols(left, right):
    return lax.dot_general(
        left, right, (((1,), (1,)), ((), ())), preferred_element_type=jnp.float32
    )


def per_device(feats, grad_out, qkv_weight, proj_weight, to_hilbert, to_zorder):
    peer_count = lax.axis_size("rows")
    feature = feats[0]
    rows_dev, channels = feature.shape
    head_size = channels // HEADS
    scale = head_size ** (-0.5)
    blocks_dev = to_hilbert.shape[1]
    slot_count = peer_count * CAP
    w_qkv, w_proj = (
        lax.all_gather(qkv_weight, "rows", axis=0, tiled=True),
        lax.all_gather(proj_weight, "rows", axis=0, tiled=True),
    )
    forward_list = to_hilbert[0]
    inverse_list = to_zorder[0]
    local_ids = jnp.arange(blocks_dev, dtype=jnp.int32)
    slot_ids = jnp.arange(slot_count, dtype=jnp.int32)
    target_dev = forward_list // blocks_dev
    send_slot = target_dev * CAP + rank_within(local_ids, target_dev)
    send_table = (send_slot[None, :] == slot_ids[:, None]).astype(jnp.bfloat16)
    source_dev = inverse_list // blocks_dev
    recv_slot = source_dev * CAP + rank_within(inverse_list, source_dev)
    recv_table = (recv_slot[:, None] == slot_ids[None, :]).astype(jnp.bfloat16)
    zblocks = grad_out[0].reshape(blocks_dev, -1)
    outgoing = jnp.dot(send_table, zblocks, preferred_element_type=jnp.float32).astype(jnp.bfloat16)
    arrived = move_blocks(outgoing.reshape(peer_count, CAP, -1)).reshape(slot_count, -1)
    grad_hil = jnp.dot(recv_table, arrived, preferred_element_type=jnp.float32).astype(jnp.bfloat16)
    grad_hil = grad_hil.reshape(rows_dev, channels)
    qkv = jnp.dot(feature, w_qkv, preferred_element_type=jnp.float32).astype(jnp.bfloat16)
    query = qkv[:, :channels]
    keyval = qkv[:, channels:]
    grad_attn = contract_cols(grad_hil, w_proj).astype(jnp.bfloat16)
    other_kv = from_partner(keyval, "rows", 0)
    keys_all = jnp.concatenate([keyval[:, :channels], other_kv[:, :channels]], axis=0)
    values_all = jnp.concatenate([keyval[:, channels:], other_kv[:, channels:]], axis=0)
    attn_parts, dq_parts, dk_parts, dv_parts = ([], [], [], [])
    for head_index in range(HEADS):
        lo_col = head_index * head_size
        q_head = query[:, lo_col : lo_col + head_size]
        k_head = keys_all[:, lo_col : lo_col + head_size]
        v_head = values_all[:, lo_col : lo_col + head_size]
        g_head = grad_attn[:, lo_col : lo_col + head_size]
        score = contract_cols(q_head, k_head) * scale
        row_max = jnp.max(score, axis=1, keepdims=True)
        raised = jnp.exp(score - row_max)
        row_sum = jnp.sum(raised, axis=1, keepdims=True)
        probs = raised / row_sum
        probs_b = probs.astype(jnp.bfloat16)
        attn_parts.append(
            jnp.dot(probs_b, v_head, preferred_element_type=jnp.float32).astype(jnp.bfloat16)
        )
        dprob = contract_cols(g_head, v_head)
        delta = jnp.sum(probs * dprob, axis=1, keepdims=True)
        dscore = (probs * (dprob - delta) * scale).astype(jnp.bfloat16)
        dq_parts.append(jnp.dot(dscore, k_head, preferred_element_type=jnp.float32))
        dk_parts.append(contract_rows(dscore, q_head))
        dv_parts.append(contract_rows(probs_b, g_head))
    grad_q = jnp.concatenate(dq_parts, axis=1)
    grad_k = jnp.concatenate(dk_parts, axis=1)
    grad_v = jnp.concatenate(dv_parts, axis=1)
    other_k, other_v = (
        from_partner(grad_k[rows_dev:].astype(jnp.bfloat16), "rows", 0).astype(jnp.float32),
        from_partner(grad_v[rows_dev:].astype(jnp.bfloat16), "rows", 0).astype(jnp.float32),
    )
    grad_k = grad_k[:rows_dev] + other_k
    grad_v = grad_v[:rows_dev] + other_v
    grad_qkv = jnp.concatenate([grad_q, grad_k, grad_v], axis=1).astype(jnp.bfloat16)
    attn = jnp.concatenate(attn_parts, axis=1)
    grad_hfeat = contract_cols(grad_qkv, w_qkv).astype(jnp.bfloat16)
    hblocks = grad_hfeat.reshape(blocks_dev, -1)
    going_back = contract_rows(recv_table, hblocks).astype(jnp.bfloat16)
    returned = move_blocks(going_back.reshape(peer_count, CAP, -1)).reshape(slot_count, -1)
    grad_z = contract_rows(send_table, returned).astype(jnp.bfloat16).reshape(rows_dev, channels)
    share = channels // peer_count
    term = jnp.concatenate(
        [contract_rows(feature, grad_qkv), contract_rows(attn, grad_hil)], axis=1
    )
    total = lax.psum(term, ("rows", "rep"))
    owned = lax.dynamic_slice_in_dim(total, lax.axis_index("rows") * share, share, 0)
    return (grad_z[None], owned[:, : 3 * channels], owned[:, 3 * channels :])


def solution(mesh):
    placed = (
        P("rep", "rows", None),
        P("rep", "rows", None),
        P("rows", None),
        P("rows", None),
        P("rep", "rows"),
        P("rep", "rows"),
    )
    return jax.shard_map(
        per_device,
        mesh=mesh,
        in_specs=placed,
        out_specs=(P("rep", "rows", None), P("rows", None), P("rows", None)),
        check_vma=False,
    )
```

profile of v0, /device:TPU:6, one launch (start us, length us, event | category | flops | bytes accessed | tf_op | source)
XLA Modules:
  0.0 720.7 jit_solution(14029525855574183305)
XLA Ops:
  7.2 0.7 all-gather.4.cloned.1.call-update
  7.9 1.0 reshape_squeeze.3
  9.0 0.7 and_select_fusion.2
  9.6 0.7 fusion.202
  10.5 0.7 fusion.113
  11.5 1.0 reshape.119
  12.5 19.9 %all-to-all-start = ((bf16[128,2,1024]{2,1,0:T(2,128)(2,1)}), bf16[128,2,1024]{2,1,0:T(2,128)(2,1)S(1)}, u32[]{:S(2)}, u32[]{:S(2)}) async-start(bf16[128,2,1024]{2,1,0:T(2,128)(2,1)} %reshape.119), calls=%async_computation | async-start | bytes 1048576 | tf_op jit(solution)/shard_map/all_to_all | solution.py:21
  32.4 100.1 %all-gather.1 = bf16[128,4,512]{2,1,0:T(4,128)(2,1)S(1)} all-gather(bf16[1,4,512]{2,1,0:T(4,128)(2,1)S(1)} %bitcast.64), channel_id=1, replica_groups=mesh['rows'=128,'rep'=4] {'rows'}, dimensions={0}, use_global_device_ids=true | all-gather | bytes 528384 | tf_op jit(solution)/shard_map/all_gather | solution.py:52
  132.9 1.0 reshape.120
  133.9 23.0 %all-gather.4.cloned.1.call-done = bf16[128,4,1536]{2,1,0:T(4,128)(2,1)} async-done(((bf16[1,4,1536]{2,1,0:T(4,128)(2,1)}), bf16[128,4,1536]{2,1,0:T(4,128)(2,1)}) %all-gather.4.cloned.1.call-update) | async-done | bytes 1572880 | tf_op jit(solution)/shard_map/all_gather | solution.py:51
  156.9 2.7 reshape.126
  159.7 0.6 convolution_convert_fusion
  160.2 0.9 slice.187
  161.1 2.3 collective-permute-start
  163.5 1.0 convolution_convert_fusion.6
  164.4 1.0 reshape.121
  165.9 1.1 fusion.160
  168.6 0.4 fusion.162
  169.4 0.4 fusion.164
  170.1 0.4 fusion.166
  171.4 0.4 fusion.168
  172.0 0.4 multiply_reduce_fusion.6
  172.7 0.4 fusion.6
  174.5 0.4 multiply_reduce_fusion.4
  175.2 0.4 fusion.4
  175.8 0.3 multiply_reduce_fusion.3
  177.0 0.4 multiply_reduce_fusion.2
  177.7 0.4 fusion.2
  179.2 0.4 multiply_reduce_fusion
  180.5 2.1 collective-permute-start.2
  182.7 1.3 fusion.169
  188.7 2.4 collective-permute-start.1
  191.5 0.6 collective-permute-done.1
  192.3 1.3 convolution_convert_fusion.4
  193.6 0.6 convolution_bitcast_fusion
  194.2 1.7 reshape.122
  195.9 2.2 convolution_convert_fusion.1
  198.1 2.1 reshape.123
  200.2 13.1 %all-to-all-start.1 = ((bf16[128,2,1024]{2,1,0:T(2,128)(2,1)}), bf16[128,2,1024]{2,1,0:T(2,128)(2,1)}, u32[]{:S(2)}, u32[]{:S(2)}) async-start(bf16[128,2,1024]{2,1,0:T(2,128)(2,1)} %reshape.123), calls=%async_computation.1 | async-start | bytes 1048576 | tf_op jit(solution)/shard_map/all_to_all | solution.py:21
  213.3 3.6 pad_maximum_fusion
  216.9 28.1 %all-to-all-done.1 = bf16[128,2,1024]{2,1,0:T(2,128)(2,1)} async-done(((bf16[128,2,1024]{2,1,0:T(2,128)(2,1)}), bf16[128,2,1024]{2,1,0:T(2,128)(2,1)}, u32[]{:S(2)}, u32[]{:S(2)}) %all-to-all-start.1) | async-done | bytes 524320 | tf_op jit(solution)/shard_map/all_to_all | solution.py:21
  245.0 1.2 reshape.124
  246.5 0.8 broadcast_in_dim_reshape.3
  247.3 462.5 %all-reduce.2.cloned.1.call-done = f32[512,2048]{0,1:T(8,128)} async-done(((f32[512,2048]{0,1:T(8,128)}), f32[512,2048]{0,1:T(8,128)}) %all-reduce.2.cloned.1.call-update) | async-done | bytes 4194320 | tf_op jit(solution)/shard_map/psum | solution.py:118
  709.8 1.4 constant_dynamic-slice_fusion
  711.2 0.9 copy.13
  712.1 1.1 dynamic-slice.1
  713.1 0.7 copy.14
  (82 shorter events, 15.7 us)
Async XLA Ops:
  7.2 152.5 %copy-start = (bf16[1,256,512]{2,1,0:T(8,128)(2,1)S(1)}, bf16[1,256,512]{2,1,0:T(8,128)(2,1)}, u32[]{:S(2)}) copy-start(bf16[1,256,512]{2,1,0:T(8,128)(2,1)} %param.6) | copy-start | bytes 786436
  7.2 25.2 %copy-start.2 = (bf16[4,512]{1,0:T(4,128)(2,1)S(1)}, bf16[4,512]{1,0:T(4,128)(2,1)}, u32[]{:S(2)}) copy-start(bf16[4,512]{1,0:T(4,128)(2,1)} %param.9) | copy-start | bytes 12292
  7.2 125.4 %copy-start.3 = (s32[1,128]{1,0:T(1,128)S(1)}, s32[1,128]{1,0:T(1,128)}, u32[]{:S(2)}) copy-start(s32[1,128]{1,0:T(1,128)} %param.11) | copy-start | bytes 1540
  7.2 149.7 %all-gather.4.cloned.1.call-start = ((), (), s32[]{:S(2)}) async-start(), calls=%async_computation.3 | async-start | bytes 1585152 | tf_op jit(solution)/shard_map/all_gather | solution.py:51
  12.5 120.4 %all-to-all-start = ((bf16[128,2,1024]{2,1,0:T(2,128)(2,1)}), bf16[128,2,1024]{2,1,0:T(2,128)(2,1)S(1)}, u32[]{:S(2)}, u32[]{:S(2)}) async-start(bf16[128,2,1024]{2,1,0:T(2,128)(2,1)} %reshape.119), calls=%async_computation | async-start | bytes 1048576 | tf_op jit(solution)/shard_map/all_to_all | solution.py:21
  159.7 3.8 copy-start.1
  161.1 4.8 collective-permute-start
  180.5 11.7 %collective-permute-start.2 = (bf16[256,512]{0,1:T(8,128)(2,1)S(1)}, bf16[256,512]{0,1:T(8,128)(2,1)S(1)}, u32[]{:S(2)}, u32[]{:S(2)}) collective-permute-start(bf16[256,512]{0,1:T(8,128)(2,1)S(1)} %slice.454), channel_id=1, source_target_pairs={{0,4},{4,0},{8,12},{12,8},{16,20},{20,16},{24,28},{28,24},{32,36},... | collective-permute-start | bytes 786440 | tf_op jit(solution)/shard_map/ppermute | solution.py:17
  188.7 3.4 collective-permute-start.1
  200.2 44.9 %all-to-all-start.1 = ((bf16[128,2,1024]{2,1,0:T(2,128)(2,1)}), bf16[128,2,1024]{2,1,0:T(2,128)(2,1)}, u32[]{:S(2)}, u32[]{:S(2)}) async-start(bf16[128,2,1024]{2,1,0:T(2,128)(2,1)} %reshape.123), calls=%async_computation.1 | async-start | bytes 1048576 | tf_op jit(solution)/shard_map/all_to_all | solution.py:21
  213.3 496.5 %all-reduce.2.cloned.1.call-start = ((), (), s32[]{:S(2)}) async-start(), calls=%async_computation.2 | async-start | bytes 8388608 | tf_op jit(solution)/shard_map/psum | solution.py:118
Sparse Core Ops, SparseCore 0:
  11.1 145.7 all-gather.3
  219.5 490.2 all-reduce.1
where the time goes:
time: 722 us; the launch traced here: 721 us
  waiting for transfers between devices  515 us (71%)
  blocking collectives  100 us (14%)
  starting transfers between devices  40 us (6%)
  matrix products  22.5 us (3%)
  local copies, waits for them, and re-layouts  18.9 us (3%)
  between operations  14.4 us (2%)
  other arithmetic  9.94 us (1%)
    psum x1, waiting for transfers between devices, per_device(): total = lax.psum(term, ('rows', 'rep'))  462 us
    all_gather x1, blocking collectives, per_device(): lax.all_gather(proj_weight, 'rows', axis=0, tiled=True)  100 us
    all_to_all x2, starting transfers between devices, move_blocks(): lax.all_to_all(outgoing, 'rows', split_axis=0, concat_axis=0, tiled=True)  33 us
    all_to_all x2, waiting for transfers between devices, move_blocks(): lax.all_to_all(outgoing, 'rows', split_axis=0, concat_axis=0, tiled=True)  28.1 us
    all_gather x1, waiting for transfers between devices, per_device(): lax.all_gather(qkv_weight, 'rows', axis=0, tiled=True)  23 us
  transfers between devices with their start and end apart: 7, of which 4 were waited for; matrix products, arithmetic and copies ran while one was open for 3% of the time, Pallas kernels for 0%

commit v1 on v0

v1 whole, which is shorter than its diff:
```python
import jax
import jax.numpy as jnp
from jax import lax
from jax.sharding import Mesh
from jax.sharding import PartitionSpec as P

HEADS = 8
CAP = 2
BLK = 2
Z_SIZE = 16
CORES = 2
ROWS = ("x", "z", "core")
NEAR = ("x", "core", "rep")


def mm(left, right, dims, out=jnp.float32):
    res = lax.dot_general(left, right, (dims, ((), ())), preferred_element_type=jnp.float32)
    return res.astype(out)


NN = ((1,), (0,))
NT = ((1,), (1,))
TN = ((0,), (0,))


def swap(block, axis, parts):
    return lax.all_to_all(block, axis, split_axis=0, concat_axis=0, tiled=True)


def rank_within(order_keys, owners):
    same_owner = owners[None, :] == owners[:, None]
    earlier = order_keys[None, :] < order_keys[:, None]
    return jnp.sum(jnp.logical_and(same_owner, earlier).astype(jnp.int32), axis=1)


def slot_tables(owners, ranks, count):
    base = owners * (2 * CAP * BLK) + ranks * BLK
    rows = (base[:, None] + jnp.arange(BLK, dtype=jnp.int32)[None, :]).reshape(-1)
    slots = jnp.arange(count * 2 * CAP * BLK, dtype=jnp.int32)
    return [
        (slots[:, None] == (rows + half * CAP * BLK)[None, :]).astype(jnp.bfloat16)
        for half in range(2)
    ]


def per_device(feats, grad_out, qkv_weight, proj_weight, to_hilbert, to_zorder):
    bf = jnp.bfloat16
    nx, nz, nc, nr = (lax.axis_size(a) for a in ("x", "z", "core", "rep"))
    peers = nx * nz * nc
    core = lax.axis_index("core")
    rep = lax.axis_index("rep")
    feature = feats[0]
    rows_dev, channels = feature.shape
    own = channels // nc
    head_size = channels // HEADS
    heads_own = HEADS // nc
    scale = head_size ** (-0.5)
    share = qkv_weight.shape[0]
    per = share // nr
    wide = 4 * channels
    blocks_dev = to_hilbert.shape[1]

    both = jnp.concatenate([qkv_weight, proj_weight], axis=1)
    mine = lax.dynamic_slice_in_dim(both, rep * per, per, 0)
    mine = jnp.broadcast_to(mine.reshape(1, per * wide // 256, 256), (nz, per * wide // 256, 256))
    plane = swap(mine, "z", nz).reshape(nz * per, wide)
    views = []
    for c in range(nc):
        cols = [plane[:, part * channels + c * own : part * channels + (c + 1) * own] for part in range(3)]
        views.append(jnp.concatenate(cols + [plane[:, 3 * channels :]], axis=1))
    width = 3 * own + channels
    views = jnp.stack(views, axis=0)
    views = jnp.broadcast_to(views[None, :, None], (nx, nc, nr, nz * per, width))
    weights = swap(views.reshape(nx * nc * nr, nz * per, width), NEAR, None).reshape(channels, width)

    ids = jnp.arange(blocks_dev, dtype=jnp.int32)
    target = to_hilbert[0] // blocks_dev
    send = slot_tables(target, rank_within(ids, target), peers)
    source = to_zorder[0] // blocks_dev
    recv = slot_tables(source, rank_within(to_zorder[0], source), peers)
    half = channels // 2
    grad_z_in = grad_out[0]
    chunk = 2 * CAP * BLK
    outgoing = (mm(send[0], grad_z_in[:, :half], NN) + mm(send[1], grad_z_in[:, half:], NN)).astype(bf)
    arrived = swap(outgoing.reshape(peers, chunk, half), ROWS, None).reshape(peers * chunk, half)
    grad_hil = jnp.concatenate([mm(recv[h], arrived, TN, bf) for h in range(2)], axis=1)

    nat = jnp.arange(channels, dtype=jnp.int32)
    place = nat % per
    r_of = nat // per % nr
    c_of = nat // share % nc
    z_of = nat // (share * nc) % nz
    x_of = nat // (share * nc * nz)
    pos = (((x_of * nc + c_of) * nr + r_of) * nz + z_of) * per + place
    perm = (pos[:, None] == nat[None, :]).astype(bf)
    pos_own = lax.dynamic_slice_in_dim(pos, core * own, own, 0)
    perm_own = (pos_own[:, None] == nat[None, :]).astype(bf)

    pair = [(0, 1), (1, 0)]
    other_feat = lax.ppermute(feature, "core", pair)
    xf = mm(jnp.concatenate([feature, other_feat], axis=0), perm, NN, bf)
    w_qkv = weights[:, : 3 * own]
    w_proj = mm(perm_own, weights[:, 3 * own :], NN, bf)
    qkv = mm(xf, w_qkv, NN, bf)
    other_grad = lax.ppermute(grad_hil, "core", pair)
    grad_pair = jnp.concatenate([grad_hil, other_grad], axis=0)
    grad_attn = mm(grad_pair, w_proj, NT, bf)

    attn_parts, dq_parts, dk_parts, dv_parts = ([], [], [], [])
    for head_index in range(heads_own):
        lo = head_index * head_size
        q_head = qkv[:, lo : lo + head_size]
        k_head = qkv[:, own + lo : own + lo + head_size]
        v_head = qkv[:, 2 * own + lo : 2 * own + lo + head_size]
        g_head = grad_attn[:, lo : lo + head_size]
        score = mm(q_head, k_head, NT) * scale
        row_max = jnp.max(score, axis=1, keepdims=True)
        raised = jnp.exp(score - row_max)
        row_sum = jnp.sum(raised, axis=1, keepdims=True)
        probs = raised / row_sum
        probs_b = probs.astype(bf)
        attn_parts.append(mm(probs_b, v_head, NN, bf))
        dprob = mm(g_head, v_head, NT)
        delta = jnp.sum(probs * dprob, axis=1, keepdims=True)
        dscore = (probs * (dprob - delta) * scale).astype(bf)
        dq_parts.append(mm(dscore, k_head, NN, bf))
        dk_parts.append(mm(dscore, q_head, TN, bf))
        dv_parts.append(mm(probs_b, g_head, TN, bf))
    grad_qkv = jnp.concatenate(dq_parts + dk_parts + dv_parts, axis=1)
    attn = jnp.concatenate(attn_parts, axis=1)

    partial = mm(grad_qkv, w_qkv, NT)
    from_other = lax.ppermute(partial[rows_dev:].astype(bf), "core", pair)
    grad_hfeat = (partial[:rows_dev] + from_other.astype(jnp.float32)).astype(bf)
    going = (mm(recv[0], grad_hfeat[:, :half], NN) + mm(recv[1], grad_hfeat[:, half:], NN)).astype(bf)
    returned = swap(going.reshape(peers, chunk, half), ROWS, None).reshape(peers * chunk, half)
    grad_perm = jnp.concatenate([mm(send[h], returned, TN, bf) for h in range(2)], axis=1)
    grad_z = mm(grad_perm, perm, NT, bf)

    qkv_term = mm(xf, grad_qkv, TN, bf)
    attn_perm = mm(attn, perm_own, NN, bf)
    proj_term = mm(attn_perm, grad_pair, TN, bf)
    term = jnp.concatenate([qkv_term, proj_term], axis=1)
    near = swap(term.reshape(nx * nc * nr, nz * per, width), NEAR, None)
    near = near.reshape(nx, nc, nr, nz * per, width).astype(jnp.float32)
    near_qkv = jnp.sum(near[..., : 3 * own], axis=(0, 2))
    near_proj = jnp.sum(near[..., 3 * own :], axis=(0, 1, 2))
    pieces = []
    for part in range(3):
        for c in range(nc):
            pieces.append(near_qkv[c, :, part * own : (part + 1) * own])
    rows = jnp.concatenate(pieces + [near_proj], axis=1).astype(bf)
    line = per * wide // 256
    far = swap(rows.reshape(nz, line, 256), "z", nz)
    summed = jnp.sum(far.astype(jnp.float32), axis=0)
    last = swap(jnp.broadcast_to(summed[None], (nr, line, 256)), "rep", nr)
    owned = last.reshape(share, wide)
    return (grad_z[None], owned[:, : 3 * channels], owned[:, 3 * channels :])


def solution(mesh):
    rows, reps = mesh.devices.shape
    fine = Mesh(
        mesh.devices.reshape(rows // (Z_SIZE * CORES), Z_SIZE, CORES, reps),
        ("x", "z", "core", "rep"),
    )
    placed = (
        P("rep", ROWS, None),
        P("rep", ROWS, None),
        P(ROWS, None),
        P(ROWS, None),
        P("rep", ROWS),
        P("rep", ROWS),
    )
    return jax.shard_map(
        per_device,
        mesh=fine,
        in_specs=placed,
        out_specs=(P("rep", ROWS, None), P(ROWS, None), P(ROWS, None)),
        check_vma=False,
    )
```

time: 722 us -> 217 us (0.30)
  waiting for transfers between devices: 515 us -> 113 us
  blocking collectives: 100 us -> 0 us
  starting transfers between devices: 40 us -> 59.7 us
  between operations: 14.4 us -> 1.21 us
  local copies, waits for them, and re-layouts: 18.9 us -> 6.77 us
    psum x1 -> x0, waiting for transfers between devices: 462 us -> none  [per_device(): total = lax.psum(term, ('rows', 'rep'))]
    all_gather x1 -> x0, blocking collectives: 100 us -> none  [per_device(): lax.all_gather(proj_weight, 'rows', axis=0, tiled=True)]
    all_to_all x2 -> x7, waiting for transfers between devices: 28.1 us -> 111 us  [swap(): return lax.all_to_all(block, axis, split_axis=0, concat_axis=0, tiled=True)]
    all_gather x1 -> x0, waiting for transfers between devices: 23 us -> none  [per_device(): lax.all_gather(qkv_weight, 'rows', axis=0, tiled=True)]
    all_to_all x2 -> x7, starting transfers between devices: 33 us -> 53.6 us  [swap(): return lax.all_to_all(block, axis, split_axis=0, concat_axis=0, tiled=True)]
    reshape x6 -> x0, local copies, waits for them, and re-layouts: 8.12 us -> none  [the longest x1 2.08 us: per_device(): going_back.reshape(peer_count, CAP, -1)]
    dot_general x57 -> x39, matrix products: 22.5 us -> 27.7 us  [mm(): lax.dot_general(left, right, (dims, ((), ())), preferred_element_type=jnp...]
  transfers between devices with their start and end apart: 7 -> 10, of which waited for: 4 -> 8; matrix products, arithmetic and copies ran while one was open for 3% -> 8% of each run, Pallas kernels for 0% -> 0%
where the time goes in v1:
time: 217 us; the launch traced here: 214 us
  waiting for transfers between devices  113 us (52%)
  starting transfers between devices  59.7 us (28%)
  matrix products  27.7 us (13%)
  local copies, waits for them, and re-layouts  6.77 us (3%)
  other arithmetic  6.35 us (3%)
    all_to_all x7, waiting for transfers between devices, swap(): return lax.all_to_all(block, axis, split_axis=0, concat_axis=0, tiled=True)  111 us
    all_to_all x7, starting transfers between devices, swap(): return lax.all_to_all(block, axis, split_axis=0, concat_axis=0, tiled=True)  53.6 us
    dot_general x39, matrix products, mm(): lax.dot_general(left, right, (dims, ((), ())), preferred_element_type=jnp...  27.7 us
  transfers between devices with their start and end apart: 10, of which 8 were waited for; matrix products, arithmetic and copies ran while one was open for 8% of the time, Pallas kernels for 0%

profile of v1, /device:TPU:6, one launch (start us, length us, event | category | flops | bytes accessed | tf_op | source)
XLA Modules:
  0.0 214.3 jit_solution(16904024079732657732)
XLA Ops:
  0.6 0.8 fusion.121
  1.4 0.6 broadcast_in_dim.11
  2.0 15.2 %all-to-all-start = ((bf16[16,8,256]{2,1,0:T(8,128)(2,1)}), bf16[16,8,256]{2,1,0:T(8,128)(2,1)S(1)}, u32[]{:S(2)}, u32[]{:S(2)}) async-start(bf16[16,8,256]{2,1,0:T(8,128)(2,1)} %broadcast_in_dim.11), calls=%async_computation | async-start | bytes 131072 | tf_op jit(solution)/shard_map/all_to_all | solution.py:27
  17.3 1.9 collective-permute-start
  19.2 0.7 and_select_fusion.1
  19.9 0.7 fusion.140
  21.0 1.2 fusion.18
  22.2 7.8 %all-to-all-done = bf16[16,8,256]{2,1,0:T(8,128)(2,1)S(1)} async-done(((bf16[16,8,256]{2,1,0:T(8,128)(2,1)}), bf16[16,8,256]{2,1,0:T(8,128)(2,1)S(1)}, u32[]{:S(2)}, u32[]{:S(2)}) %all-to-all-start) | async-done | bytes 65568 | tf_op jit(solution)/shard_map/all_to_all | solution.py:27
  30.1 1.2 broadcast_in_dim.12
  31.2 7.7 %all-to-all-start.1 = ((bf16[32,16,1280]{2,1,0:T(8,128)(2,1)}), bf16[32,16,1280]{2,1,0:T(8,128)(2,1)S(1)}, u32[]{:S(2)}, u32[]{:S(2)}) async-start(bf16[32,16,1280]{2,1,0:T(8,128)(2,1)} %bitcast.7), calls=%async_computation.1 | async-start | bytes 2621440 | tf_op jit(solution)/shard_map/all_to_all | solution.py:27
  39.2 1.1 fusion.3
  40.7 0.6 convolution_convert_fusion.3
  41.3 15.9 %all-to-all-done.1 = bf16[32,16,1280]{2,1,0:T(8,128)(2,1)S(1)} async-done(((bf16[32,16,1280]{2,1,0:T(8,128)(2,1)}), bf16[32,16,1280]{2,1,0:T(8,128)(2,1)S(1)}, u32[]{:S(2)}, u32[]{:S(2)}) %all-to-all-start.1) | async-done | bytes 1310752 | tf_op jit(solution)/shard_map/all_to_all | solution.py:27
  57.1 9.5 %all-to-all-start.2 = ((bf16[128,8,256]{2,1,0:T(8,128)(2,1)}), bf16[128,8,256]{2,1,0:T(8,128)(2,1)}, u32[]{:S(2)}, u32[]{:S(2)}) async-start(bf16[128,8,256]{2,1,0:T(8,128)(2,1)} %fusion.3), calls=%async_computation.2 | async-start | bytes 1048576 | tf_op jit(solution)/shard_map/all_to_all | solution.py:27
  66.6 0.6 convolution_convert_fusion.1
  69.2 0.9 convolution_convert_fusion.13
  70.2 1.0 convolution_convert_fusion.14
  71.1 1.3 fusion.156
  72.4 25.9 %all-to-all-done.2 = bf16[128,8,256]{2,1,0:T(8,128)(2,1)} async-done(((bf16[128,8,256]{2,1,0:T(8,128)(2,1)}), bf16[128,8,256]{2,1,0:T(8,128)(2,1)}, u32[]{:S(2)}, u32[]{:S(2)}) %all-to-all-start.2) | async-done | bytes 524320 | tf_op jit(solution)/shard_map/all_to_all | solution.py:27
  98.4 1.6 convolution_convert_fusion.11
  99.9 1.5 convolution_convert_fusion.10
  101.4 2.1 collective-permute-start.1
  103.7 1.8 convolution_convert_fusion.15
  105.6 2.4 %convolution_convert_fusion.5 = bf16[512,256]{0,1:T(8,128)(2,1)} fusion(bf16[512,1280]{1,0:T(8,128)(2,1)} %bitcast.85, s32[256]{0:T(256)S(1)} %dynamic_slice.7, bf16[256,512]{0,1:T(8,128)(2,1)} %collective-permute-done.1, bf16[256,256]{0,1:T(8,128)(2,1)S(1)} %convolution_convert_fusion.10, bf16[256,256]{0,1:T(8,128)(2,1)S(1)} %convolution_convert_fusion.11), kind=kOutput, calls=%fused_computation.17 | convolution fusion | flops 270401536 | bytes 1311744 | tf_op jit(solution)/shard_map/dot_general | solution.py:17
  107.9 1.3 multiply_reduce_fusion
  110.0 0.8 copy-done.1
  116.0 0.9 copy-done.6
  116.9 0.6 convolution_convert_fusion
  117.8 1.8 convolution_convert_fusion.2
  119.5 1.2 pad_maximum_fusion
  120.7 6.9 %all-to-all-start.4 = ((bf16[32,16,1280]{2,1,0:T(8,128)(2,1)}), bf16[32,16,1280]{2,1,0:T(8,128)(2,1)S(1)}, u32[]{:S(2)}, u32[]{:S(2)}) async-start(bf16[32,16,1280]{2,1,0:T(8,128)(2,1)} %bitcast.15), calls=%async_computation.4 | async-start | bytes 2621440 | tf_op jit(solution)/shard_map/all_to_all | solution.py:27
  127.6 0.6 fusion.27
  128.3 2.1 collective-permute-start.2
  130.3 1.4 collective-permute-done.2
  131.8 13.9 %all-to-all-done.4 = bf16[32,16,1280]{2,1,0:T(8,128)(2,1)S(1)} async-done(((bf16[32,16,1280]{2,1,0:T(8,128)(2,1)}), bf16[32,16,1280]{2,1,0:T(8,128)(2,1)S(1)}, u32[]{:S(2)}, u32[]{:S(2)}) %all-to-all-start.4) | async-done | bytes 1310752 | tf_op jit(solution)/shard_map/all_to_all | solution.py:27
  146.3 0.6 copy.14
  146.9 3.5 %all-to-all-start.5 = ((bf16[16,8,256]{2,1,0:T(8,128)(2,1)}), bf16[16,8,256]{2,1,0:T(8,128)(2,1)S(1)}, u32[]{:S(2)}, u32[]{:S(2)}) async-start(bf16[16,8,256]{2,1,0:T(8,128)(2,1)} %bitcast.27), calls=%async_computation.5 | async-start | bytes 131072 | tf_op jit(solution)/shard_map/all_to_all | solution.py:27
  150.7 12.5 %all-to-all-done.5 = bf16[16,8,256]{2,1,0:T(8,128)(2,1)S(1)} async-done(((bf16[16,8,256]{2,1,0:T(8,128)(2,1)}), bf16[16,8,256]{2,1,0:T(8,128)(2,1)S(1)}, u32[]{:S(2)}, u32[]{:S(2)}) %all-to-all-start.5) | async-done | bytes 65568 | tf_op jit(solution)/shard_map/all_to_all | solution.py:27
  163.3 0.6 broadcast_in_dim.14
  163.9 3.3 %all-to-all-start.6 = ((f32[4,8,256]{2,1,0:T(8,128)}), f32[4,8,256]{2,1,0:T(8,128)S(1)}, u32[]{:S(2)}, u32[]{:S(2)}) async-start(f32[4,8,256]{2,1,0:T(8,128)} %broadcast_in_dim.14), calls=%async_computation.6 | async-start | bytes 65536 | tf_op jit(solution)/shard_map/all_to_all | solution.py:27
  167.2 1.1 fusion.2
  168.3 4.3 %all-to-all-done.6 = f32[4,8,256]{2,1,0:T(8,128)S(1)} async-done(((f32[4,8,256]{2,1,0:T(8,128)}), f32[4,8,256]{2,1,0:T(8,128)S(1)}, u32[]{:S(2)}, u32[]{:S(2)}) %all-to-all-start.6) | async-done | bytes 32800 | tf_op jit(solution)/shard_map/all_to_all | solution.py:27
  172.6 7.6 %all-to-all-start.3 = ((bf16[128,8,256]{2,1,0:T(8,128)(2,1)}), bf16[128,8,256]{2,1,0:T(8,128)(2,1)S(1)}, u32[]{:S(2)}, u32[]{:S(2)}) async-start(bf16[128,8,256]{2,1,0:T(8,128)(2,1)} %fusion.2), calls=%async_computation.3 | async-start | bytes 1048576 | tf_op jit(solution)/shard_map/all_to_all | solution.py:27
  180.2 0.6 slice.213
  180.8 0.6 slice.212
  181.4 30.9 %all-to-all-done.3 = bf16[128,8,256]{2,1,0:T(8,128)(2,1)S(1)} async-done(((bf16[128,8,256]{2,1,0:T(8,128)(2,1)}), bf16[128,8,256]{2,1,0:T(8,128)(2,1)S(1)}, u32[]{:S(2)}, u32[]{:S(2)}) %all-to-all-start.3) | async-done | bytes 524320 | tf_op jit(solution)/shard_map/all_to_all | solution.py:27
  212.3 0.4 convolution_convert_fusion.8
  213.2 1.2 fusion.4
  (97 shorter events, 10.6 us)
Async XLA Ops:
  2.0 27.9 %all-to-all-start = ((bf16[16,8,256]{2,1,0:T(8,128)(2,1)}), bf16[16,8,256]{2,1,0:T(8,128)(2,1)S(1)}, u32[]{:S(2)}, u32[]{:S(2)}) async-start(bf16[16,8,256]{2,1,0:T(8,128)(2,1)} %broadcast_in_dim.11), calls=%async_computation | async-start | bytes 131072 | tf_op jit(solution)/shard_map/all_to_all | solution.py:27
  17.3 23.4 %collective-permute-start = (bf16[256,512]{1,0:T(8,128)(2,1)}, bf16[256,512]{1,0:T(8,128)(2,1)S(1)}, u32[]{:S(2)}, u32[]{:S(2)}) collective-permute-start(bf16[256,512]{1,0:T(8,128)(2,1)} %bitcast.98), channel_id=1, source_target_pairs={{0,4},{4,0},{1,5},{5,1},{2,6},{6,2},{3,7},{7,3},{8,12},{12,8},{9,1... | collective-permute-start | bytes 786440 | tf_op jit(solution)/shard_map/ppermute | solution.py:100
  31.2 7.8 %copy-start.9 = (s32[1,128]{1,0:T(1,128)S(1)}, s32[1,128]{1,0:T(1,128)}, u32[]{:S(2)}) copy-start(s32[1,128]{1,0:T(1,128)} %param.11) | copy-start | bytes 1540
  31.2 8.0 %copy-start.8 = (bf16[1,256,512]{2,1,0:T(8,128)(2,1)S(1)}, bf16[1,256,512]{2,1,0:T(8,128)(2,1)}, u32[]{:S(2)}) copy-start(bf16[1,256,512]{2,1,0:T(8,128)(2,1)} %param.7) | copy-start | bytes 786436
  31.2 25.9 %all-to-all-start.1 = ((bf16[32,16,1280]{2,1,0:T(8,128)(2,1)}), bf16[32,16,1280]{2,1,0:T(8,128)(2,1)S(1)}, u32[]{:S(2)}, u32[]{:S(2)}) async-start(bf16[32,16,1280]{2,1,0:T(8,128)(2,1)} %bitcast.7), calls=%async_computation.1 | async-start | bytes 2621440 | tf_op jit(solution)/shard_map/all_to_all | solution.py:27
  39.0 1.7 copy-start.10
  41.2 25.4 %copy-start.11 = (bf16[512,512]{1,0:T(8,128)(2,1)}, bf16[512,512]{1,0:T(8,128)(2,1)S(1)}, u32[]{:S(2)}) copy-start(bf16[512,512]{1,0:T(8,128)(2,1)S(1)} %convolution_convert_fusion.3) | copy-start | bytes 1572868
  57.1 10.1 %copy-start.4 = (bf16[32,16,1280]{2,1,0:T(8,128)(2,1)}, bf16[32,16,1280]{2,1,0:T(8,128)(2,1)S(1)}, u32[]{:S(2)}) copy-start(bf16[32,16,1280]{2,1,0:T(8,128)(2,1)S(1)} %all-to-all-done.1) | copy-start | bytes 3932164
  57.1 41.2 %all-to-all-start.2 = ((bf16[128,8,256]{2,1,0:T(8,128)(2,1)}), bf16[128,8,256]{2,1,0:T(8,128)(2,1)}, u32[]{:S(2)}, u32[]{:S(2)}) async-start(bf16[128,8,256]{2,1,0:T(8,128)(2,1)} %fusion.3), calls=%async_computation.2 | async-start | bytes 1048576 | tf_op jit(solution)/shard_map/all_to_all | solution.py:27
  67.2 3.9 %copy-start.2 = (bf16[512,768]{1,0:T(8,128)(2,1)}, bf16[512,768]{1,0:T(8,128)(2,1)S(1)}, u32[]{:S(2)}) copy-start(bf16[512,768]{1,0:T(8,128)(2,1)S(1)} %convolution_convert_fusion.1) | copy-start | bytes 2359300
  98.4 5.2 %copy-start = (f32[512,512]{0,1:T(8,128)S(1)}, f32[512,512]{0,1:T(8,128)}, u32[]{:S(2)}) copy-start(f32[512,512]{0,1:T(8,128)} %get-tuple-element.9) | copy-start | bytes 3145732
  101.4 4.2 %collective-permute-start.1 = (bf16[256,512]{0,1:T(8,128)(2,1)S(1)}, bf16[256,512]{0,1:T(8,128)(2,1)}, u32[]{:S(2)}, u32[]{:S(2)}) collective-permute-start(bf16[256,512]{0,1:T(8,128)(2,1)S(1)} %pad_maximum_fusion.2), channel_id=1, source_target_pairs={{0,4},{4,0},{1,5},{5,1},{2,6},{6,2},{3,7},{7,3},{8,12},{12,8},{9,1... | collective-permute-start | bytes 786440 | tf_op jit(solution)/shard_map/ppermute | solution.py:105
  107.9 1.4 copy-start.3
  107.9 1.4 copy-start.13
  109.6 1.2 copy-start.1
  115.7 1.2 copy-start.12
  116.0 0.9 copy-start.6
  116.9 0.8 copy-start.14
  116.9 0.9 copy-start.15
  116.9 0.9 copy-start.16
  120.7 6.9 %copy-start.5 = (bf16[32,16,1280]{2,1,0:T(8,128)(2,1)S(1)}, bf16[32,16,1280]{2,1,0:T(8,128)(2,1)}, u32[]{:S(2)}) copy-start(bf16[32,16,1280]{2,1,0:T(8,128)(2,1)} %copy-done.4) | copy-start | bytes 3932164
  120.7 6.9 %copy-start.7 = (bf16[512,768]{0,1:T(8,128)(2,1)S(1)}, bf16[512,768]{0,1:T(8,128)(2,1)}, u32[]{:S(2)}) copy-start(bf16[512,768]{0,1:T(8,128)(2,1)} %copy-done.6) | copy-start | bytes 2359300
  120.7 25.0 %all-to-all-start.4 = ((bf16[32,16,1280]{2,1,0:T(8,128)(2,1)}), bf16[32,16,1280]{2,1,0:T(8,128)(2,1)S(1)}, u32[]{:S(2)}, u32[]{:S(2)}) async-start(bf16[32,16,1280]{2,1,0:T(8,128)(2,1)} %bitcast.15), calls=%async_computation.4 | async-start | bytes 2621440 | tf_op jit(solution)/shard_map/all_to_all | solution.py:27
  128.3 3.4 %collective-permute-start.2 = (bf16[256,512]{1,0:T(8,128)(2,1)S(1)}, bf16[256,512]{1,0:T(8,128)(2,1)S(1)}, u32[]{:S(2)}, u32[]{:S(2)}) collective-permute-start(bf16[256,512]{1,0:T(8,128)(2,1)S(1)} %slice.317), channel_id=1, source_target_pairs={{0,4},{4,0},{1,5},{5,1},{2,6},{6,2},{3,7},{7,3},{8,12},{12,8},{9,1... | collective-permute-start | bytes 786440 | tf_op jit(solution)/shard_map/ppermute | solution.py:133
  146.9 16.4 %all-to-all-start.5 = ((bf16[16,8,256]{2,1,0:T(8,128)(2,1)}), bf16[16,8,256]{2,1,0:T(8,128)(2,1)S(1)}, u32[]{:S(2)}, u32[]{:S(2)}) async-start(bf16[16,8,256]{2,1,0:T(8,128)(2,1)} %bitcast.27), calls=%async_computation.5 | async-start | bytes 131072 | tf_op jit(solution)/shard_map/all_to_all | solution.py:27
  163.9 8.7 %all-to-all-start.6 = ((f32[4,8,256]{2,1,0:T(8,128)}), f32[4,8,256]{2,1,0:T(8,128)S(1)}, u32[]{:S(2)}, u32[]{:S(2)}) async-start(f32[4,8,256]{2,1,0:T(8,128)} %broadcast_in_dim.14), calls=%async_computation.6 | async-start | bytes 65536 | tf_op jit(solution)/shard_map/all_to_all | solution.py:27
  172.6 39.7 %all-to-all-start.3 = ((bf16[128,8,256]{2,1,0:T(8,128)(2,1)}), bf16[128,8,256]{2,1,0:T(8,128)(2,1)S(1)}, u32[]{:S(2)}, u32[]{:S(2)}) async-start(bf16[128,8,256]{2,1,0:T(8,128)(2,1)} %fusion.2), calls=%async_computation.3 | async-start | bytes 1048576 | tf_op jit(solution)/shard_map/all_to_all | solution.py:27

commit v2 on v1

v2 whole, which is shorter than its diff:
```python
import jax
import jax.numpy as jnp
from jax import lax
from jax.experimental import pallas as pl
from jax.experimental.pallas import tpu as pltpu
from jax.sharding import Mesh
from jax.sharding import PartitionSpec as P

HEADS = 8
CAP = 2
BLK = 2
Z_HIGH = 4
Z_LOW = 4
CORES = 2
ROWS = ("x", "zh", "zl", "core")
INTERPRET = False
NN = ((1,), (0,))
NT = ((1,), (1,))
TN = ((0,), (0,))


def mm(left, right, dims, out=jnp.float32):
    res = lax.dot_general(left, right, (dims, ((), ())), preferred_element_type=jnp.float32)
    return res.astype(out)


def rank_within(order_keys, owners):
    same_owner = owners[None, :] == owners[:, None]
    earlier = order_keys[None, :] < order_keys[:, None]
    return jnp.sum(jnp.logical_and(same_owner, earlier).astype(jnp.int32), axis=1)


def slot_tables(owners, ranks, count):
    base = owners * (2 * CAP * BLK) + ranks * BLK
    rows = (base[:, None] + jnp.arange(BLK, dtype=jnp.int32)[None, :]).reshape(-1)
    slots = jnp.arange(count * 2 * CAP * BLK, dtype=jnp.int32)
    return [
        (slots[:, None] == (rows + half * CAP * BLK)[None, :]).astype(jnp.bfloat16)
        for half in range(2)
    ]


def swap(block, axis):
    return lax.all_to_all(block, axis, split_axis=0, concat_axis=0, tiled=True)


def shift(block, axis, step):
    count = lax.axis_size(axis)
    return lax.ppermute(block, axis, [(here, (here + step) % count) for here in range(count)])


def attend(qkv, grad_attn, own, head_size):
    bf = jnp.bfloat16
    rows = qkv.shape[0]
    scale = head_size ** (-0.5)
    query, key, value = qkv[:, :own], qkv[:, own : 2 * own], qkv[:, 2 * own :]
    key_t, value_t = key.T, value.T
    two = 2 * head_size
    first = lax.broadcasted_iota(jnp.int32, (rows, two), 1) < head_size
    attn_t, dq_t, dk, dv = [], [], [], []
    for pair in range(own // two):
        cols = slice(pair * two, (pair + 1) * two)
        q_pair, k_pair, v_pair, g_pair = query[:, cols], key[:, cols], value[:, cols], grad_attn[:, cols]
        zero = jnp.zeros_like(k_pair)
        dk_pair, dv_pair = [], []
        for member in range(2):
            k_head = jnp.where(first, k_pair, zero) if member == 0 else jnp.where(first, zero, k_pair)
            v_head = jnp.where(first, v_pair, zero) if member == 0 else jnp.where(first, zero, v_pair)
            score = mm(k_head, q_pair, NT)
            raised = jnp.exp((score - jnp.max(score, axis=0, keepdims=True)) * scale)
            probs = raised * (1.0 / jnp.sum(raised, axis=0, keepdims=True))
            probs_b = probs.astype(bf)
            dprob = mm(v_head, g_pair, NT)
            delta = jnp.sum(probs * dprob, axis=0, keepdims=True)
            dscore = (probs * (dprob - delta) * scale).astype(bf)
            lo = pair * two + member * head_size
            attn_t.append(mm(value_t[lo : lo + head_size], probs_b, NN, bf))
            dq_t.append(mm(key_t[lo : lo + head_size], dscore, NN, bf))
            dk_pair.append(mm(dscore, q_pair, NN))
            dv_pair.append(mm(probs_b, g_pair, NN))
        dk.append(jnp.where(first, dk_pair[0], dk_pair[1]).astype(bf))
        dv.append(jnp.where(first, dv_pair[0], dv_pair[1]).astype(bf))
    grad_q = jnp.concatenate(dq_t, axis=0).T
    return jnp.concatenate(attn_t, axis=0), jnp.concatenate([grad_q] + dk + dv, axis=1)


def patch_body(
    core_ref, x_ref, mine_ref, recv_ref, gown_ref, goth_ref, own_perm_ref,
    pown_ref, poth_ref, keep_ref, send_ref, w_ref, tq_ref, tp_ref,
):
    bf = jnp.bfloat16
    core = core_ref[0]
    channels = x_ref.shape[1]
    own = channels // CORES
    rows = gown_ref.shape[0]
    part = own // CORES
    w_ref[core] = mine_ref[...]
    w_ref[1 - core] = recv_ref[...]
    w_qkv = jnp.concatenate([w_ref[c, :, : 3 * own] for c in range(CORES)], axis=0)
    lo = pl.multiple_of(core * part, part)
    w_proj = jnp.concatenate([w_ref[c, pl.ds(lo, part), 3 * own :] for c in range(CORES)], axis=0)
    own_perm = own_perm_ref[...]
    w_proj = mm(own_perm, w_proj, NN, bf)
    x = x_ref[...]
    grad_pair = jnp.concatenate([gown_ref[...], goth_ref[...]], axis=0)
    qkv = mm(x, w_qkv, NN, bf)
    grad_attn = mm(grad_pair, w_proj, NT, bf)
    attn_t, grad_qkv = attend(qkv, grad_attn, own, channels // HEADS)
    tq_ref[...] = mm(x, grad_qkv, TN, bf).reshape(CORES, own, 3 * own)
    proj_term = mm(attn_t, grad_pair, NN, bf)
    tp_ref[...] = mm(own_perm, proj_term, TN, bf).reshape(CORES, part, channels)
    for out_ref, side in ((keep_ref, core), (send_ref, 1 - core)):
        out_ref[:, : 3 * own] = tq_ref[side]
        out_ref[:part, 3 * own :] = tp_ref[side, :, :own]
        out_ref[part:, 3 * own :] = tp_ref[side, :, own:]
    partial = mm(grad_qkv, w_qkv, NT)
    pown_ref[...] = partial[:rows]
    poth_ref[...] = partial[rows:].astype(bf)


def patch_step(core, x, mine, recv, gown, goth, own_perm):
    bf = jnp.bfloat16
    rows, channels = gown.shape
    own = channels // CORES
    vmem = pl.BlockSpec(memory_space=pltpu.VMEM)
    return pl.pallas_call(
        patch_body,
        out_shape=[
            jax.ShapeDtypeStruct((rows, channels), jnp.float32),
            jax.ShapeDtypeStruct((rows, channels), bf),
            jax.ShapeDtypeStruct((own, 4 * own), bf),
            jax.ShapeDtypeStruct((own, 4 * own), bf),
        ],
        in_specs=[pl.BlockSpec(memory_space=pltpu.SMEM)] + [vmem] * 6,
        out_specs=[vmem] * 4,
        scratch_shapes=[
            pltpu.VMEM((CORES, own, 3 * own + channels), bf),
            pltpu.VMEM((CORES, own, 3 * own), bf),
            pltpu.VMEM((CORES, own // CORES, channels), bf),
        ],
        compiler_params=pltpu.CompilerParams(vmem_limit_bytes=48 << 20),
        interpret=INTERPRET,
    )(core.reshape(1), x, mine, recv, gown, goth, own_perm)


def per_device(feats, grad_out, qkv_weight, proj_weight, to_hilbert, to_zorder):
    bf = jnp.bfloat16
    f32 = jnp.float32
    nx, zh, zl, nc, nr = (lax.axis_size(a) for a in ("x", "zh", "zl", "core", "rep"))
    nz = zh * zl
    peers = nx * nz * nc
    x_here, zh_here, zl_here, core = (lax.axis_index(a) for a in ROWS)
    feature = feats[0]
    rows_dev, channels = feature.shape
    own = channels // nc
    part = own // nc
    half = channels // 2
    share = qkv_weight.shape[0]
    blocks_dev = to_hilbert.shape[1]
    chunk = 2 * CAP * BLK
    pair = [(0, 1), (1, 0)]

    ids = jnp.arange(blocks_dev, dtype=jnp.int32)
    target = to_hilbert[0] // blocks_dev
    send = slot_tables(target, rank_within(ids, target), peers)
    source = to_zorder[0] // blocks_dev
    recv = slot_tables(source, rank_within(to_zorder[0], source), peers)
    grad_z_in = grad_out[0]
    outgoing = (mm(send[0], grad_z_in[:, :half], NN) + mm(send[1], grad_z_in[:, half:], NN)).astype(bf)

    halves = []
    for c in range(nc):
        cols = [qkv_weight[:, p * channels + c * own : p * channels + (c + 1) * own] for p in range(3)]
        halves.append(jnp.concatenate(cols + [proj_weight[:, c * own : (c + 1) * own]], axis=1))
    piece = jnp.concatenate(halves, axis=0)
    other_feat = lax.ppermute(feature, "core", pair)
    gathered = piece
    for axis in ("zh", "zl", "x"):
        gathered = jnp.concatenate([gathered] + [shift(gathered, axis, k) for k in range(1, lax.axis_size(axis))], axis=0)

    def group_index(x, z):
        low = (zl_here - z) % zl
        high = (zh_here - z // zl) % zh
        return (((x_here - x) % nx) * zl + low) * zh + high

    a = jnp.arange(own, dtype=jnp.int32)
    i_of, z_of, x_of = a % share, a // share % nz, a // (share * nz)
    slot = jnp.arange(2 * own, dtype=jnp.int32)
    picked = []
    for h in range(2):
        place = (group_index(x_of, z_of) * 2 + h) * share + i_of
        picked.append(mm((place[:, None] == slot[None, :]).astype(bf), gathered, NN, bf))
    proj_rows = [p[:, 3 * own :] for p in picked]
    qkv_mine = jnp.where(core == 0, picked[0][:, : 3 * own], picked[1][:, : 3 * own])
    qkv_theirs = jnp.where(core == 0, picked[1][:, : 3 * own], picked[0][:, : 3 * own])
    mine = jnp.concatenate([qkv_mine] + proj_rows, axis=1)
    theirs = lax.ppermute(jnp.concatenate([qkv_theirs] + proj_rows, axis=1), "core", pair)

    def order(count):
        nat = jnp.arange(count, dtype=jnp.int32)
        i, c, z, x = nat % share, nat // share % nc, nat // (share * nc) % nz, nat // (share * nc * nz)
        pos = c * (count // nc) + (x * nz + z) * share + i
        return (pos[:, None] == nat[None, :]).astype(bf)

    perm = order(channels)
    own_perm = order(own)
    x_pair = mm(jnp.concatenate([feature, other_feat], axis=0), perm, NN, bf)
    arrived = swap(outgoing.reshape(peers, chunk, half), ROWS).reshape(peers * chunk, half)
    grad_hil = jnp.concatenate([mm(recv[h], arrived, TN, bf) for h in range(2)], axis=1)
    other_grad = lax.ppermute(grad_hil, "core", pair)
    p_own, p_other, keep, away = patch_step(core, x_pair, mine, theirs, grad_hil, other_grad, own_perm)

    from_other = lax.ppermute(p_other, "core", pair)
    grad_hfeat = (p_own + from_other.astype(f32)).astype(bf)
    going = (mm(recv[0], grad_hfeat[:, :half], NN) + mm(recv[1], grad_hfeat[:, half:], NN)).astype(bf)
    returned = swap(going.reshape(peers, chunk, half), ROWS).reshape(peers * chunk, half)

    got = lax.ppermute(away, "core", pair)
    proj_all = jnp.concatenate([keep[:, 3 * own :], got[:, 3 * own :]], axis=0)
    plane = own // nx

    def toward(step):
        x_to = (x_here + step) % nx
        first = x_to * plane
        base = (x_to // (nx // nc) + core) % nc * own + x_to % (nx // nc) * plane
        pieces = [lax.dynamic_slice_in_dim(m[:, : 3 * own], first, plane, 0) for m in (keep, got)]
        pieces += [lax.dynamic_slice_in_dim(proj_all, base + k * part, plane, 0) for k in range(2)]
        return jnp.concatenate(pieces, axis=1)

    total = toward(0).astype(f32)
    arrivals = [shift(toward(step), "x", step) for step in range(1, nx)]
    total = (total + sum(t.astype(f32) for t in arrivals)).astype(bf)
    rows_left = total.shape[0] // zh

    def toward_zh(step):
        return lax.dynamic_slice_in_dim(total, (zh_here + step) % zh * rows_left, rows_left, 0)

    arrivals = [shift(toward_zh(step), "zh", step) for step in range(1, zh)]
    total = (toward_zh(0).astype(f32) + sum(t.astype(f32) for t in arrivals)).astype(bf)
    total, returned = lax.optimization_barrier((total, returned))
    wide = 4 * channels
    last = jnp.broadcast_to(total.reshape(zl, 1, share, wide), (zl, nr, share, wide))
    last = swap(last.reshape(zl * nr, share, wide), ("zl", "rep"))
    last = jnp.sum(last.astype(f32), axis=0)
    grad_perm = jnp.concatenate([mm(send[h], returned, TN, bf) for h in range(2)], axis=1)
    grad_z = mm(grad_perm, perm, NT, bf)
    lower = jnp.where(core == 0, last[:, : 3 * own], last[:, 3 * own : 6 * own])
    upper = jnp.where(core == 0, last[:, 3 * own : 6 * own], last[:, : 3 * own])
    cols = []
    for p in range(3):
        cols += [lower[:, p * own : (p + 1) * own], upper[:, p * own : (p + 1) * own]]
    return (grad_z[None], jnp.concatenate(cols, axis=1), last[:, 6 * own :])


def solution(mesh):
    rows, reps = mesh.devices.shape
    fine = Mesh(
        mesh.devices.reshape(rows // (Z_HIGH * Z_LOW * CORES), Z_HIGH, Z_LOW, CORES, reps),
        ROWS + ("rep",),
    )
    placed = (
        P("rep", ROWS, None),
        P("rep", ROWS, None),
        P(ROWS, None),
        P(ROWS, None),
        P("rep", ROWS),
        P("rep", ROWS),
    )
    return jax.shard_map(
        per_device,
        mesh=fine,
        in_specs=placed,
        out_specs=(P("rep", ROWS, None), P(ROWS, None), P(ROWS, None)),
        check_vma=False,
    )
```

time: 217 us -> 201 us (0.926)
  starting transfers between devices: 59.7 us -> 117 us
  waiting for transfers between devices: 113 us -> 56.1 us
  matrix products: 27.7 us -> 9.29 us
  Pallas kernels: 0 us -> 6.77 us
  other arithmetic: 6.35 us -> 3.46 us
  local copies, waits for them, and re-layouts: 6.77 us -> 4.51 us
    all_to_all x7 -> x3, waiting for transfers between devices: 111 us -> 8.82 us  [swap(): return lax.all_to_all(block, axis, split_axis=0, concat_axis=0, tiled=True)]
    ppermute x1 -> x18, starting transfers between devices: 2.07 us -> 81.5 us  [the longest x15 75.2 us: shift(): lax.ppermute(block, axis, [(here, (here + step) % count) for here in rang...]
    ppermute x1 -> x18, waiting for transfers between devices: 1.36 us -> 47.3 us  [the longest x15 47.3 us: shift(): lax.ppermute(block, axis, [(here, (here + step) % count) for here in rang...]
    all_to_all x7 -> x3, starting transfers between devices: 53.6 us -> 30.7 us  [swap(): return lax.all_to_all(block, axis, split_axis=0, concat_axis=0, tiled=True)]
    dot_general x39 -> x12, matrix products: 27.7 us -> 9.29 us  [mm(): lax.dot_general(left, right, (dims, ((), ())), preferred_element_type=jnp...]
    pallas_call x0 -> x1, Pallas kernels: none -> 6.77 us  [patch_step(): pl.pallas_call(patch_body, out_shape=[jax.ShapeDtypeStruct((rows, channel...]
  transfers between devices with their start and end apart: 10 -> 23, of which waited for: 8 -> 11; matrix products, arithmetic and copies ran while one was open for 8% -> 7% of each run, Pallas kernels for 0% -> 0%
where the time goes in v2:
time: 201 us; the launch traced here: 199 us
  starting transfers between devices  117 us (58%)
  waiting for transfers between devices  56.1 us (28%)
  matrix products  9.29 us (5%)
  Pallas kernels  6.77 us (3%)
  local copies, waits for them, and re-layouts  4.51 us (2%)
  other arithmetic  3.46 us (2%)
    ppermute x15, starting transfers between devices, shift(): lax.ppermute(block, axis, [(here, (here + step) % count) for here in rang...  75.2 us
    ppermute x15, waiting for transfers between devices, shift(): lax.ppermute(block, axis, [(here, (here + step) % count) for here in rang...  47.3 us
    all_to_all x3, starting transfers between devices, swap(): return lax.all_to_all(block, axis, split_axis=0, concat_axis=0, tiled=True)  30.7 us
    dot_general x12, matrix products, mm(): lax.dot_general(left, right, (dims, ((), ())), preferred_element_type=jnp...  9.29 us
    all_to_all x3, waiting for transfers between devices, swap(): return lax.all_to_all(block, axis, split_axis=0, concat_axis=0, tiled=True)  8.82 us
    pallas_call x1, Pallas kernels, patch_step(): pl.pallas_call(patch_body, out_shape=[jax.ShapeDtypeStruct((rows, channel...  6.77 us
  transfers between devices with their start and end apart: 23, of which 11 were waited for; matrix products, arithmetic and copies ran while one was open for 7% of the time, Pallas kernels for 0%

profile of v2, /device:TPU:6, one launch (start us, length us, event | category | flops | bytes accessed | tf_op | source)
XLA Modules:
  0.0 198.6 jit_solution(3236456603395720020)
XLA Ops:
  0.6 0.8 fusion.78
  1.5 0.7 fusion.79
  2.2 9.1 %collective-permute-start.1 = (bf16[8,1024]{1,0:T(8,128)(2,1)S(1)}, bf16[8,1024]{1,0:T(8,128)(2,1)S(1)}, u32[]{:S(2)}, u32[]{:S(2)}) collective-permute-start(bf16[8,1024]{1,0:T(8,128)(2,1)S(1)} %maximum_maximum_fusion), channel_id=1, source_target_pairs={{0,32},{32,64},{64,96},{96,0},{1,33},{33,65},{65,97},{97,1},{2,34}... | collective-permute-start | bytes 49160 | tf_op jit(solution)/shard_map/ppermute | solution.py:49
  11.3 10.9 %collective-permute-start.2 = (bf16[8,1024]{1,0:T(8,128)(2,1)S(1)}, bf16[8,1024]{1,0:T(8,128)(2,1)S(1)}, u32[]{:S(2)}, u32[]{:S(2)}) collective-permute-start(bf16[8,1024]{1,0:T(8,128)(2,1)S(1)} %maximum_maximum_fusion), channel_id=1, source_target_pairs={{0,64},{32,96},{64,0},{96,32},{1,65},{33,97},{65,1},{97,33},{2,66}... | collective-permute-start | bytes 49160 | tf_op jit(solution)/shard_map/ppermute | solution.py:49
  22.2 5.5 %collective-permute-start.3 = (bf16[8,1024]{1,0:T(8,128)(2,1)S(1)}, bf16[8,1024]{1,0:T(8,128)(2,1)S(1)}, u32[]{:S(2)}, u32[]{:S(2)}) collective-permute-start(bf16[8,1024]{1,0:T(8,128)(2,1)S(1)} %maximum_maximum_fusion), channel_id=1, source_target_pairs={{0,96},{32,0},{64,32},{96,64},{1,97},{33,1},{65,33},{97,65},{2,98}... | collective-permute-start | bytes 49160 | tf_op jit(solution)/shard_map/ppermute | solution.py:49
  27.7 0.7 and_select_fusion.5
  28.4 0.7 fusion.74
  29.5 1.2 fusion.6
  30.7 1.1 fusion.3
  31.9 9.8 %all-to-all-start = ((bf16[128,8,256]{2,1,0:T(8,128)(2,1)}), bf16[128,8,256]{2,1,0:T(8,128)(2,1)S(1)}, u32[]{:S(2)}, u32[]{:S(2)}) async-start(bf16[128,8,256]{2,1,0:T(8,128)(2,1)} %fusion.3), calls=%async_computation | async-start | bytes 1048576 | tf_op jit(solution)/shard_map/all_to_all | solution.py:44
  41.7 2.1 %collective-permute-start = (bf16[256,512]{1,0:T(8,128)(2,1)S(1)}, bf16[256,512]{1,0:T(8,128)(2,1)}, u32[]{:S(2)}, u32[]{:S(2)}) collective-permute-start(bf16[256,512]{1,0:T(8,128)(2,1)S(1)} %bitcast.39), channel_id=1, source_target_pairs={{0,4},{4,0},{1,5},{5,1},{2,6},{6,2},{3,7},{7,3},{8,12},{12,8},{9,1... | collective-permute-start | bytes 786440 | tf_op jit(solution)/shard_map/ppermute | solution.py:176
  44.3 3.4 %collective-permute-start.4 = (bf16[32,1024]{1,0:T(8,128)(2,1)S(1)}, bf16[32,1024]{1,0:T(8,128)(2,1)S(1)}, u32[]{:S(2)}, u32[]{:S(2)}) collective-permute-start(bf16[32,1024]{1,0:T(8,128)(2,1)S(1)} %concatenate.58), channel_id=1, source_target_pairs={{0,8},{8,16},{16,24},{24,0},{1,9},{9,17},{17,25},{25,1},{2,10},{10... | collective-permute-start | bytes 196616 | tf_op jit(solution)/shard_map/ppermute | solution.py:49
  47.7 4.3 %collective-permute-start.5 = (bf16[32,1024]{1,0:T(8,128)(2,1)S(1)}, bf16[32,1024]{1,0:T(8,128)(2,1)S(1)}, u32[]{:S(2)}, u32[]{:S(2)}) collective-permute-start(bf16[32,1024]{1,0:T(8,128)(2,1)S(1)} %concatenate.58), channel_id=1, source_target_pairs={{0,16},{8,24},{16,0},{24,8},{1,17},{9,25},{17,1},{25,9},{2,18},{10... | collective-permute-start | bytes 196616 | tf_op jit(solution)/shard_map/ppermute | solution.py:49
  52.0 3.4 %collective-permute-start.6 = (bf16[32,1024]{1,0:T(8,128)(2,1)S(1)}, bf16[32,1024]{1,0:T(8,128)(2,1)S(1)}, u32[]{:S(2)}, u32[]{:S(2)}) collective-permute-start(bf16[32,1024]{1,0:T(8,128)(2,1)S(1)} %concatenate.58), channel_id=1, source_target_pairs={{0,24},{8,0},{16,8},{24,16},{1,25},{9,1},{17,9},{25,17},{2,26},{10... | collective-permute-start | bytes 196616 | tf_op jit(solution)/shard_map/ppermute | solution.py:49
  55.4 13.0 %collective-permute-done.4 = bf16[32,1024]{1,0:T(8,128)(2,1)S(1)} collective-permute-done((bf16[32,1024]{1,0:T(8,128)(2,1)S(1)}, bf16[32,1024]{1,0:T(8,128)(2,1)S(1)}, u32[]{:S(2)}, u32[]{:S(2)}) %collective-permute-start.4) | collective-permute-done | bytes 65568 | tf_op jit(solution)/shard_map/ppermute | solution.py:49
  68.4 2.8 %collective-permute-done.5 = bf16[32,1024]{1,0:T(8,128)(2,1)S(1)} collective-permute-done((bf16[32,1024]{1,0:T(8,128)(2,1)S(1)}, bf16[32,1024]{1,0:T(8,128)(2,1)S(1)}, u32[]{:S(2)}, u32[]{:S(2)}) %collective-permute-start.5) | collective-permute-done | bytes 65568 | tf_op jit(solution)/shard_map/ppermute | solution.py:49
  71.3 1.9 collective-permute-start.7
  73.2 4.6 %collective-permute-start.8 = (bf16[128,1024]{1,0:T(8,128)(2,1)S(1)}, bf16[128,1024]{1,0:T(8,128)(2,1)S(1)}, u32[]{:S(2)}, u32[]{:S(2)}) collective-permute-start(bf16[128,1024]{1,0:T(8,128)(2,1)S(1)} %concatenate.59), channel_id=1, source_target_pairs={{0,256},{128,384},{256,0},{384,128},{1,257},{129,385},{257,1},{385... | collective-permute-start | bytes 786440 | tf_op jit(solution)/shard_map/ppermute | solution.py:49
  77.8 1.9 collective-permute-start.9
  79.9 2.5 %collective-permute-done.7 = bf16[128,1024]{1,0:T(8,128)(2,1)S(1)} collective-permute-done((bf16[128,1024]{1,0:T(8,128)(2,1)S(1)}, bf16[128,1024]{1,0:T(8,128)(2,1)S(1)}, u32[]{:S(2)}, u32[]{:S(2)}) %collective-permute-start.7) | collective-permute-done | bytes 262176 | tf_op jit(solution)/shard_map/ppermute | solution.py:49
  82.4 2.7 %collective-permute-done.8 = bf16[128,1024]{1,0:T(8,128)(2,1)S(1)} collective-permute-done((bf16[128,1024]{1,0:T(8,128)(2,1)S(1)}, bf16[128,1024]{1,0:T(8,128)(2,1)S(1)}, u32[]{:S(2)}, u32[]{:S(2)}) %collective-permute-start.8) | collective-permute-done | bytes 262176 | tf_op jit(solution)/shard_map/ppermute | solution.py:49
  85.1 4.0 %collective-permute-done.9 = bf16[128,1024]{1,0:T(8,128)(2,1)S(1)} collective-permute-done((bf16[128,1024]{1,0:T(8,128)(2,1)S(1)}, bf16[128,1024]{1,0:T(8,128)(2,1)S(1)}, u32[]{:S(2)}, u32[]{:S(2)}) %collective-permute-start.9) | collective-permute-done | bytes 262176 | tf_op jit(solution)/shard_map/ppermute | solution.py:49
  90.7 1.9 collective-permute-start.10
  93.7 2.6 %collective-permute-start.11 = (bf16[256,512]{1,0:T(8,128)(2,1)S(1)}, bf16[256,512]{1,0:T(8,128)(2,1)S(1)}, u32[]{:S(2)}, u32[]{:S(2)}) collective-permute-start(bf16[256,512]{1,0:T(8,128)(2,1)S(1)} %pad_maximum_fusion.4.gown_ref), channel_id=1, source_target_pairs={{0,4},{4,0},{1,5},{5,1},{2,6},{6,2},{3,7},{7,3},{8,12},{12,8},{9,1... | collective-permute-start | bytes 786440 | tf_op jit(solution)/shard_map/ppermute | solution.py:210
  96.3 1.5 convolution_convert_fusion.2.x_ref
  97.8 6.8 %shard_map.85 = (f32[256,512]{1,0:T(8,128)S(1)}, bf16[256,512]{1,0:T(8,128)(2,1)S(1)}, bf16[256,1024]{1,0:T(8,128)(2,1)S(1)}, bf16[256,1024]{1,0:T(8,128)(2,1)S(1)}) custom-call(s32[1]{0:T(128)} %bitcast.2.core_ref, bf16[512,512]{1,0:T(8,128)(2,1)S(1)} %convolution_convert_fusion.2.x_ref, bf16[256,1280]{1,0:T(8,128)(2,1)S(1)} %get-tuple-element.37.mine_ref, ...), custom_call_target="tpu_custom_call" | custom-call | tf_op jit(solution)/shard_map/pallas_call | solution.py:126
  104.6 1.9 collective-permute-start.19
  106.9 2.4 %collective-permute-start.12 = (bf16[256,1024]{1,0:T(8,128)(2,1)S(1)}, bf16[256,1024]{1,0:T(8,128)(2,1)S(1)}, u32[]{:S(2)}, u32[]{:S(2)}) collective-permute-start(bf16[256,1024]{1,0:T(8,128)(2,1)S(1)} %get-tuple-element.10), channel_id=1, source_target_pairs={{0,4},{4,0},{1,5},{5,1},{2,6},{6,2},{3,7},{7,3},{8,12},{12,8},{9,1... | collective-permute-start | bytes 1572872 | tf_op jit(solution)/shard_map/ppermute | solution.py:218
  109.8 1.1 fusion.2
  110.9 16.3 %all-to-all-start.1 = ((bf16[128,8,256]{2,1,0:T(8,128)(2,1)}), bf16[128,8,256]{2,1,0:T(8,128)(2,1)S(1)}, u32[]{:S(2)}, u32[]{:S(2)}) async-start(bf16[128,8,256]{2,1,0:T(8,128)(2,1)} %fusion.2), calls=%async_computation.1 | async-start | bytes 1048576 | tf_op jit(solution)/shard_map/all_to_all | solution.py:44
  127.3 0.5 fusion.34
  127.8 2.3 %collective-permute-start.13 = (bf16[64,2048]{1,0:T(8,128)(2,1)S(1)}, bf16[64,2048]{1,0:T(8,128)(2,1)S(1)}, u32[]{:S(2)}, u32[]{:S(2)}) collective-permute-start(bf16[64,2048]{1,0:T(8,128)(2,1)S(1)} %pad_maximum_fusion.5), channel_id=1, source_target_pairs={{0,128},{128,256},{256,384},{384,0},{1,129},{129,257},{257,385},{3... | collective-permute-start | bytes 786440 | tf_op jit(solution)/shard_map/ppermute | solution.py:49
  130.1 4.3 %collective-permute-start.14 = (bf16[64,2048]{1,0:T(8,128)(2,1)S(1)}, bf16[64,2048]{1,0:T(8,128)(2,1)S(1)}, u32[]{:S(2)}, u32[]{:S(2)}) collective-permute-start(bf16[64,2048]{1,0:T(8,128)(2,1)S(1)} %pad_maximum_fusion.6), channel_id=1, source_target_pairs={{0,256},{128,384},{256,0},{384,128},{1,257},{129,385},{257,1},{385... | collective-permute-start | bytes 786440 | tf_op jit(solution)/shard_map/ppermute | solution.py:49
  134.6 1.9 collective-permute-start.15
  136.5 4.1 %collective-permute-done.13 = bf16[64,2048]{1,0:T(8,128)(2,1)S(1)} collective-permute-done((bf16[64,2048]{1,0:T(8,128)(2,1)S(1)}, bf16[64,2048]{1,0:T(8,128)(2,1)S(1)}, u32[]{:S(2)}, u32[]{:S(2)}) %collective-permute-start.13) | collective-permute-done | bytes 262176 | tf_op jit(solution)/shard_map/ppermute | solution.py:49
  140.7 3.7 %collective-permute-done.14 = bf16[64,2048]{1,0:T(8,128)(2,1)S(1)} collective-permute-done((bf16[64,2048]{1,0:T(8,128)(2,1)S(1)}, bf16[64,2048]{1,0:T(8,128)(2,1)S(1)}, u32[]{:S(2)}, u32[]{:S(2)}) %collective-permute-start.14) | collective-permute-done | bytes 262176 | tf_op jit(solution)/shard_map/ppermute | solution.py:49
  144.4 6.3 %collective-permute-done.15 = bf16[64,2048]{1,0:T(8,128)(2,1)S(1)} collective-permute-done((bf16[64,2048]{1,0:T(8,128)(2,1)S(1)}, bf16[64,2048]{1,0:T(8,128)(2,1)S(1)}, u32[]{:S(2)}, u32[]{:S(2)}) %collective-permute-start.15) | collective-permute-done | bytes 262176 | tf_op jit(solution)/shard_map/ppermute | solution.py:49
  150.9 7.1 %collective-permute-start.16 = (bf16[16,2048]{1,0:T(8,128)(2,1)S(1)}, bf16[16,2048]{1,0:T(8,128)(2,1)S(1)}, u32[]{:S(2)}, u32[]{:S(2)}) collective-permute-start(bf16[16,2048]{1,0:T(8,128)(2,1)S(1)} %get-tuple-element.25), channel_id=1, source_target_pairs={{0,32},{32,64},{64,96},{96,0},{1,33},{33,65},{65,97},{97,1},{2,34}... | collective-permute-start | bytes 196616 | tf_op jit(solution)/shard_map/ppermute | solution.py:49
  158.0 7.4 %collective-permute-start.17 = (bf16[16,2048]{1,0:T(8,128)(2,1)S(1)}, bf16[16,2048]{1,0:T(8,128)(2,1)S(1)}, u32[]{:S(2)}, u32[]{:S(2)}) collective-permute-start(bf16[16,2048]{1,0:T(8,128)(2,1)S(1)} %get-tuple-element.27), channel_id=1, source_target_pairs={{0,64},{32,96},{64,0},{96,32},{1,65},{33,97},{65,1},{97,33},{2,66}... | collective-permute-start | bytes 196616 | tf_op jit(solution)/shard_map/ppermute | solution.py:49
  165.4 7.3 %collective-permute-start.18 = (bf16[16,2048]{1,0:T(8,128)(2,1)S(1)}, bf16[16,2048]{1,0:T(8,128)(2,1)S(1)}, u32[]{:S(2)}, u32[]{:S(2)}) collective-permute-start(bf16[16,2048]{1,0:T(8,128)(2,1)S(1)} %get-tuple-element.26), channel_id=1, source_target_pairs={{0,96},{32,0},{64,32},{96,64},{1,97},{33,1},{65,33},{97,65},{2,98}... | collective-permute-start | bytes 196616 | tf_op jit(solution)/shard_map/ppermute | solution.py:49
  172.7 3.8 %collective-permute-done.17 = bf16[16,2048]{1,0:T(8,128)(2,1)S(1)} collective-permute-done((bf16[16,2048]{1,0:T(8,128)(2,1)S(1)}, bf16[16,2048]{1,0:T(8,128)(2,1)S(1)}, u32[]{:S(2)}, u32[]{:S(2)}) %collective-permute-start.17) | collective-permute-done | bytes 65568 | tf_op jit(solution)/shard_map/ppermute | solution.py:49
  176.5 4.2 %collective-permute-done.18 = bf16[16,2048]{1,0:T(8,128)(2,1)S(1)} collective-permute-done((bf16[16,2048]{1,0:T(8,128)(2,1)S(1)}, bf16[16,2048]{1,0:T(8,128)(2,1)S(1)}, u32[]{:S(2)}, u32[]{:S(2)}) %collective-permute-start.18) | collective-permute-done | bytes 65568 | tf_op jit(solution)/shard_map/ppermute | solution.py:49
  180.8 0.8 broadcast_in_dim.8
  181.6 4.6 %all-to-all-start.2 = ((bf16[16,4,2048]{2,1,0:T(4,128)(2,1)}), bf16[16,4,2048]{2,1,0:T(4,128)(2,1)S(1)}, u32[]{:S(2)}, u32[]{:S(2)}) async-start(bf16[16,4,2048]{2,1,0:T(4,128)(2,1)} %bitcast.12), calls=%async_computation.2 | async-start | bytes 524288 | tf_op jit(solution)/shard_map/all_to_all | solution.py:44
  187.1 1.2 fusion.4
  188.3 8.8 %all-to-all-done.2 = bf16[16,4,2048]{2,1,0:T(4,128)(2,1)S(1)} async-done(((bf16[16,4,2048]{2,1,0:T(4,128)(2,1)}), bf16[16,4,2048]{2,1,0:T(4,128)(2,1)S(1)}, u32[]{:S(2)}, u32[]{:S(2)}) %all-to-all-start.2) | async-done | bytes 262176 | tf_op jit(solution)/shard_map/all_to_all | solution.py:44
  197.3 0.6 slice.144
  198.0 0.6 copy-done.2
  (73 shorter events, 5.7 us)
Async XLA Ops:
  0.6 30.1 %copy-start = (bf16[1,256,512]{2,1,0:T(8,128)(2,1)S(1)}, bf16[1,256,512]{2,1,0:T(8,128)(2,1)}, u32[]{:S(2)}) copy-start(bf16[1,256,512]{2,1,0:T(8,128)(2,1)} %param.7) | copy-start | bytes 786436
  2.2 42.1 %collective-permute-start.1 = (bf16[8,1024]{1,0:T(8,128)(2,1)S(1)}, bf16[8,1024]{1,0:T(8,128)(2,1)S(1)}, u32[]{:S(2)}, u32[]{:S(2)}) collective-permute-start(bf16[8,1024]{1,0:T(8,128)(2,1)S(1)} %maximum_maximum_fusion), channel_id=1, source_target_pairs={{0,32},{32,64},{64,96},{96,0},{1,33},{33,65},{65,97},{97,1},{2,34}... | collective-permute-start | bytes 49160 | tf_op jit(solution)/shard_map/ppermute | solution.py:49
  11.3 33.0 %collective-permute-start.2 = (bf16[8,1024]{1,0:T(8,128)(2,1)S(1)}, bf16[8,1024]{1,0:T(8,128)(2,1)S(1)}, u32[]{:S(2)}, u32[]{:S(2)}) collective-permute-start(bf16[8,1024]{1,0:T(8,128)(2,1)S(1)} %maximum_maximum_fusion), channel_id=1, source_target_pairs={{0,64},{32,96},{64,0},{96,32},{1,65},{33,97},{65,1},{97,33},{2,66}... | collective-permute-start | bytes 49160 | tf_op jit(solution)/shard_map/ppermute | solution.py:49
  22.2 22.1 %collective-permute-start.3 = (bf16[8,1024]{1,0:T(8,128)(2,1)S(1)}, bf16[8,1024]{1,0:T(8,128)(2,1)S(1)}, u32[]{:S(2)}, u32[]{:S(2)}) collective-permute-start(bf16[8,1024]{1,0:T(8,128)(2,1)S(1)} %maximum_maximum_fusion), channel_id=1, source_target_pairs={{0,96},{32,0},{64,32},{96,64},{1,97},{33,1},{65,33},{97,65},{2,98}... | collective-permute-start | bytes 49160 | tf_op jit(solution)/shard_map/ppermute | solution.py:49
  30.7 11.0 %copy-start.3 = (bf16[1,256,512]{2,1,0:T(8,128)(2,1)S(1)}, bf16[1,256,512]{2,1,0:T(8,128)(2,1)}, u32[]{:S(2)}) copy-start(bf16[1,256,512]{2,1,0:T(8,128)(2,1)} %param.6) | copy-start | bytes 786436
  30.7 13.1 %copy-start.1 = (s32[1,128]{1,0:T(1,128)S(1)}, s32[1,128]{1,0:T(1,128)}, u32[]{:S(2)}) copy-start(s32[1,128]{1,0:T(1,128)} %param.11) | copy-start | bytes 1540
  31.9 60.8 %all-to-all-start = ((bf16[128,8,256]{2,1,0:T(8,128)(2,1)}), bf16[128,8,256]{2,1,0:T(8,128)(2,1)S(1)}, u32[]{:S(2)}, u32[]{:S(2)}) async-start(bf16[128,8,256]{2,1,0:T(8,128)(2,1)} %fusion.3), calls=%async_computation | async-start | bytes 1048576 | tf_op jit(solution)/shard_map/all_to_all | solution.py:44
  41.7 54.6 %collective-permute-start = (bf16[256,512]{1,0:T(8,128)(2,1)S(1)}, bf16[256,512]{1,0:T(8,128)(2,1)}, u32[]{:S(2)}, u32[]{:S(2)}) collective-permute-start(bf16[256,512]{1,0:T(8,128)(2,1)S(1)} %bitcast.39), channel_id=1, source_target_pairs={{0,4},{4,0},{1,5},{5,1},{2,6},{6,2},{3,7},{7,3},{8,12},{12,8},{9,1... | collective-permute-start | bytes 786440 | tf_op jit(solution)/shard_map/ppermute | solution.py:176
  44.3 24.1 %collective-permute-start.4 = (bf16[32,1024]{1,0:T(8,128)(2,1)S(1)}, bf16[32,1024]{1,0:T(8,128)(2,1)S(1)}, u32[]{:S(2)}, u32[]{:S(2)}) collective-permute-start(bf16[32,1024]{1,0:T(8,128)(2,1)S(1)} %concatenate.58), channel_id=1, source_target_pairs={{0,8},{8,16},{16,24},{24,0},{1,9},{9,17},{17,25},{25,1},{2,10},{10... | collective-permute-start | bytes 196616 | tf_op jit(solution)/shard_map/ppermute | solution.py:49
  47.7 23.5 %collective-permute-start.5 = (bf16[32,1024]{1,0:T(8,128)(2,1)S(1)}, bf16[32,1024]{1,0:T(8,128)(2,1)S(1)}, u32[]{:S(2)}, u32[]{:S(2)}) collective-permute-start(bf16[32,1024]{1,0:T(8,128)(2,1)S(1)} %concatenate.58), channel_id=1, source_target_pairs={{0,16},{8,24},{16,0},{24,8},{1,17},{9,25},{17,1},{25,9},{2,18},{10... | collective-permute-start | bytes 196616 | tf_op jit(solution)/shard_map/ppermute | solution.py:49
  52.0 19.2 %collective-permute-start.6 = (bf16[32,1024]{1,0:T(8,128)(2,1)S(1)}, bf16[32,1024]{1,0:T(8,128)(2,1)S(1)}, u32[]{:S(2)}, u32[]{:S(2)}) collective-permute-start(bf16[32,1024]{1,0:T(8,128)(2,1)S(1)} %concatenate.58), channel_id=1, source_target_pairs={{0,24},{8,0},{16,8},{24,16},{1,25},{9,1},{17,9},{25,17},{2,26},{10... | collective-permute-start | bytes 196616 | tf_op jit(solution)/shard_map/ppermute | solution.py:49
  71.3 11.1 %collective-permute-start.7 = (bf16[128,1024]{1,0:T(8,128)(2,1)S(1)}, bf16[128,1024]{1,0:T(8,128)(2,1)S(1)}, u32[]{:S(2)}, u32[]{:S(2)}) collective-permute-start(bf16[128,1024]{1,0:T(8,128)(2,1)S(1)} %concatenate.59), channel_id=1, source_target_pairs={{0,128},{128,256},{256,384},{384,0},{1,129},{129,257},{257,385},{3... | collective-permute-start | bytes 786440 | tf_op jit(solution)/shard_map/ppermute | solution.py:49
  73.2 11.9 %collective-permute-start.8 = (bf16[128,1024]{1,0:T(8,128)(2,1)S(1)}, bf16[128,1024]{1,0:T(8,128)(2,1)S(1)}, u32[]{:S(2)}, u32[]{:S(2)}) collective-permute-start(bf16[128,1024]{1,0:T(8,128)(2,1)S(1)} %concatenate.59), channel_id=1, source_target_pairs={{0,256},{128,384},{256,0},{384,128},{1,257},{129,385},{257,1},{385... | collective-permute-start | bytes 786440 | tf_op jit(solution)/shard_map/ppermute | solution.py:49
  77.8 11.3 %collective-permute-start.9 = (bf16[128,1024]{1,0:T(8,128)(2,1)S(1)}, bf16[128,1024]{1,0:T(8,128)(2,1)S(1)}, u32[]{:S(2)}, u32[]{:S(2)}) collective-permute-start(bf16[128,1024]{1,0:T(8,128)(2,1)S(1)} %concatenate.59), channel_id=1, source_target_pairs={{0,384},{128,0},{256,128},{384,256},{1,385},{129,1},{257,129},{385... | collective-permute-start | bytes 786440 | tf_op jit(solution)/shard_map/ppermute | solution.py:49
  90.7 7.1 %collective-permute-start.10 = (bf16[256,1280]{1,0:T(8,128)(2,1)S(1)}, bf16[256,1280]{1,0:T(8,128)(2,1)S(1)}, u32[]{:S(2)}, u32[]{:S(2)}) collective-permute-start(bf16[256,1280]{1,0:T(8,128)(2,1)S(1)} %get-tuple-element.36), channel_id=1, source_target_pairs={{0,4},{4,0},{1,5},{5,1},{2,6},{6,2},{3,7},{7,3},{8,12},{12,8},{9,1... | collective-permute-start | bytes 1966088 | tf_op jit(solution)/shard_map/ppermute | solution.py:197
  93.7 4.1 %collective-permute-start.11 = (bf16[256,512]{1,0:T(8,128)(2,1)S(1)}, bf16[256,512]{1,0:T(8,128)(2,1)S(1)}, u32[]{:S(2)}, u32[]{:S(2)}) collective-permute-start(bf16[256,512]{1,0:T(8,128)(2,1)S(1)} %pad_maximum_fusion.4.gown_ref), channel_id=1, source_target_pairs={{0,4},{4,0},{1,5},{5,1},{2,6},{6,2},{3,7},{7,3},{8,12},{12,8},{9,1... | collective-permute-start | bytes 786440 | tf_op jit(solution)/shard_map/ppermute | solution.py:210
  104.6 4.7 %collective-permute-start.19 = (bf16[256,512]{1,0:T(8,128)(2,1)S(1)}, bf16[256,512]{1,0:T(8,128)(2,1)S(1)}, u32[]{:S(2)}, u32[]{:S(2)}) collective-permute-start(bf16[256,512]{1,0:T(8,128)(2,1)S(1)} %get-tuple-element.12), channel_id=1, source_target_pairs={{0,4},{4,0},{1,5},{5,1},{2,6},{6,2},{3,7},{7,3},{8,12},{12,8},{9,1... | collective-permute-start | bytes 786440 | tf_op jit(solution)/shard_map/ppermute | solution.py:213
  106.9 20.3 %collective-permute-start.12 = (bf16[256,1024]{1,0:T(8,128)(2,1)S(1)}, bf16[256,1024]{1,0:T(8,128)(2,1)S(1)}, u32[]{:S(2)}, u32[]{:S(2)}) collective-permute-start(bf16[256,1024]{1,0:T(8,128)(2,1)S(1)} %get-tuple-element.10), channel_id=1, source_target_pairs={{0,4},{4,0},{1,5},{5,1},{2,6},{6,2},{3,7},{7,3},{8,12},{12,8},{9,1... | collective-permute-start | bytes 1572872 | tf_op jit(solution)/shard_map/ppermute | solution.py:218
  110.9 69.9 %all-to-all-start.1 = ((bf16[128,8,256]{2,1,0:T(8,128)(2,1)}), bf16[128,8,256]{2,1,0:T(8,128)(2,1)S(1)}, u32[]{:S(2)}, u32[]{:S(2)}) async-start(bf16[128,8,256]{2,1,0:T(8,128)(2,1)} %fusion.2), calls=%async_computation.1 | async-start | bytes 1048576 | tf_op jit(solution)/shard_map/all_to_all | solution.py:44
  127.8 12.8 %collective-permute-start.13 = (bf16[64,2048]{1,0:T(8,128)(2,1)S(1)}, bf16[64,2048]{1,0:T(8,128)(2,1)S(1)}, u32[]{:S(2)}, u32[]{:S(2)}) collective-permute-start(bf16[64,2048]{1,0:T(8,128)(2,1)S(1)} %pad_maximum_fusion.5), channel_id=1, source_target_pairs={{0,128},{128,256},{256,384},{384,0},{1,129},{129,257},{257,385},{3... | collective-permute-start | bytes 786440 | tf_op jit(solution)/shard_map/ppermute | solution.py:49
  130.1 14.2 %collective-permute-start.14 = (bf16[64,2048]{1,0:T(8,128)(2,1)S(1)}, bf16[64,2048]{1,0:T(8,128)(2,1)S(1)}, u32[]{:S(2)}, u32[]{:S(2)}) collective-permute-start(bf16[64,2048]{1,0:T(8,128)(2,1)S(1)} %pad_maximum_fusion.6), channel_id=1, source_target_pairs={{0,256},{128,384},{256,0},{384,128},{1,257},{129,385},{257,1},{385... | collective-permute-start | bytes 786440 | tf_op jit(solution)/shard_map/ppermute | solution.py:49
  134.6 16.1 %collective-permute-start.15 = (bf16[64,2048]{1,0:T(8,128)(2,1)S(1)}, bf16[64,2048]{1,0:T(8,128)(2,1)S(1)}, u32[]{:S(2)}, u32[]{:S(2)}) collective-permute-start(bf16[64,2048]{1,0:T(8,128)(2,1)S(1)} %pad_maximum_fusion.7), channel_id=1, source_target_pairs={{0,384},{128,0},{256,128},{384,256},{1,385},{129,1},{257,129},{385... | collective-permute-start | bytes 786440 | tf_op jit(solution)/shard_map/ppermute | solution.py:49
  150.9 21.9 %collective-permute-start.16 = (bf16[16,2048]{1,0:T(8,128)(2,1)S(1)}, bf16[16,2048]{1,0:T(8,128)(2,1)S(1)}, u32[]{:S(2)}, u32[]{:S(2)}) collective-permute-start(bf16[16,2048]{1,0:T(8,128)(2,1)S(1)} %get-tuple-element.25), channel_id=1, source_target_pairs={{0,32},{32,64},{64,96},{96,0},{1,33},{33,65},{65,97},{97,1},{2,34}... | collective-permute-start | bytes 196616 | tf_op jit(solution)/shard_map/ppermute | solution.py:49
  158.0 18.5 %collective-permute-start.17 = (bf16[16,2048]{1,0:T(8,128)(2,1)S(1)}, bf16[16,2048]{1,0:T(8,128)(2,1)S(1)}, u32[]{:S(2)}, u32[]{:S(2)}) collective-permute-start(bf16[16,2048]{1,0:T(8,128)(2,1)S(1)} %get-tuple-element.27), channel_id=1, source_target_pairs={{0,64},{32,96},{64,0},{96,32},{1,65},{33,97},{65,1},{97,33},{2,66}... | collective-permute-start | bytes 196616 | tf_op jit(solution)/shard_map/ppermute | solution.py:49
  165.4 15.4 %collective-permute-start.18 = (bf16[16,2048]{1,0:T(8,128)(2,1)S(1)}, bf16[16,2048]{1,0:T(8,128)(2,1)S(1)}, u32[]{:S(2)}, u32[]{:S(2)}) collective-permute-start(bf16[16,2048]{1,0:T(8,128)(2,1)S(1)} %get-tuple-element.26), channel_id=1, source_target_pairs={{0,96},{32,0},{64,32},{96,64},{1,97},{33,1},{65,33},{97,65},{2,98}... | collective-permute-start | bytes 196616 | tf_op jit(solution)/shard_map/ppermute | solution.py:49
  181.6 15.4 %all-to-all-start.2 = ((bf16[16,4,2048]{2,1,0:T(4,128)(2,1)}), bf16[16,4,2048]{2,1,0:T(4,128)(2,1)S(1)}, u32[]{:S(2)}, u32[]{:S(2)}) async-start(bf16[16,4,2048]{2,1,0:T(4,128)(2,1)} %bitcast.12), calls=%async_computation.2 | async-start | bytes 524288 | tf_op jit(solution)/shard_map/all_to_all | solution.py:44
  197.9 0.6 copy-start.2

commit v3 on v2

v3 whole, which is shorter than its diff:
```python
import jax
import jax.numpy as jnp
from jax import lax
from jax.experimental import pallas as pl
from jax.experimental.pallas import tpu as pltpu
from jax.sharding import Mesh
from jax.sharding import PartitionSpec as P

HEADS = 8
CAP = 2
BLK = 2
Z_HIGH = 4
Z_LOW = 4
CORES = 2
ROWS = ("x", "zh", "zl", "core")
INTERPRET = False
NN = ((1,), (0,))
NT = ((1,), (1,))
TN = ((0,), (0,))


def mm(left, right, dims, out=jnp.float32):
    res = lax.dot_general(left, right, (dims, ((), ())), preferred_element_type=jnp.float32)
    return res.astype(out)


def rank_within(order_keys, owners):
    same_owner = owners[None, :] == owners[:, None]
    earlier = order_keys[None, :] < order_keys[:, None]
    return jnp.sum(jnp.logical_and(same_owner, earlier).astype(jnp.int32), axis=1)


def slot_tables(owners, ranks, count):
    base = owners * (2 * CAP * BLK) + ranks * BLK
    rows = (base[:, None] + jnp.arange(BLK, dtype=jnp.int32)[None, :]).reshape(-1)
    slots = jnp.arange(count * 2 * CAP * BLK, dtype=jnp.int32)
    return [
        (slots[:, None] == (rows + half * CAP * BLK)[None, :]).astype(jnp.bfloat16)
        for half in range(2)
    ]


def swap(block, axis):
    return lax.all_to_all(block, axis, split_axis=0, concat_axis=0, tiled=True)


def across_x(block):
    count = lax.axis_size("x")
    return lax.ppermute(block, "x", [(here, (here + count // 2) % count) for here in range(count)])


def attend(qkv, grad_attn, own, head_size):
    bf = jnp.bfloat16
    rows = qkv.shape[0]
    scale = head_size ** (-0.5)
    query, key, value = qkv[:, :own], qkv[:, own : 2 * own], qkv[:, 2 * own :]
    key_t, value_t = key.T, value.T
    two = 2 * head_size
    first = lax.broadcasted_iota(jnp.int32, (rows, two), 1) < head_size
    attn_t, dq_t, dk, dv = [], [], [], []
    for pair in range(own // two):
        cols = slice(pair * two, (pair + 1) * two)
        q_pair, k_pair, v_pair, g_pair = query[:, cols], key[:, cols], value[:, cols], grad_attn[:, cols]
        zero = jnp.zeros_like(k_pair)
        dk_pair, dv_pair = [], []
        for member in range(2):
            k_head = jnp.where(first, k_pair, zero) if member == 0 else jnp.where(first, zero, k_pair)
            v_head = jnp.where(first, v_pair, zero) if member == 0 else jnp.where(first, zero, v_pair)
            score = mm(k_head, q_pair, NT)
            raised = jnp.exp((score - jnp.max(score, axis=0, keepdims=True)) * scale)
            probs = raised * (1.0 / jnp.sum(raised, axis=0, keepdims=True))
            probs_b = probs.astype(bf)
            dprob = mm(v_head, g_pair, NT)
            delta = jnp.sum(probs * dprob, axis=0, keepdims=True)
            dscore = (probs * (dprob - delta) * scale).astype(bf)
            lo = pair * two + member * head_size
            attn_t.append(mm(value_t[lo : lo + head_size], probs_b, NN, bf))
            dq_t.append(mm(key_t[lo : lo + head_size], dscore, NN, bf))
            dk_pair.append(mm(dscore, q_pair, NN))
            dv_pair.append(mm(probs_b, g_pair, NN))
        dk.append(jnp.where(first, dk_pair[0], dk_pair[1]).astype(bf))
        dv.append(jnp.where(first, dv_pair[0], dv_pair[1]).astype(bf))
    grad_q = jnp.concatenate(dq_t, axis=0).T
    return jnp.concatenate(attn_t, axis=0), jnp.concatenate([grad_q] + dk + dv, axis=1)


def patch_body(
    core_ref, xown_ref, xoth_ref, w_ref, gown_ref, goth_ref, pown_ref, poth_ref, term_ref
):
    bf = jnp.bfloat16
    core = core_ref[0]
    rows, channels = gown_ref.shape
    own = channels // CORES
    first = pl.multiple_of(core * own, own)
    second = pl.multiple_of((1 - core) * own, own)
    w_qkv = jnp.concatenate([w_ref[p] for p in range(3)], axis=1)
    w_proj = jnp.concatenate([w_ref[3, pl.ds(first, own), :], w_ref[3, pl.ds(second, own), :]], axis=1)
    x = jnp.concatenate([xown_ref[...], xoth_ref[...]], axis=0)
    grad_pair = jnp.concatenate([gown_ref[...], goth_ref[...]], axis=0)
    qkv = mm(x, w_qkv, NN, bf)
    grad_attn = mm(grad_pair, w_proj, NT, bf)
    attn_t, grad_qkv = attend(qkv, grad_attn, own, channels // HEADS)
    qkv_term = mm(x, grad_qkv, TN, bf)
    for p in range(3):
        term_ref[p] = qkv_term[:, p * own : (p + 1) * own]
    proj_term = mm(attn_t, grad_pair, NN, bf)
    term_ref[3, pl.ds(first, own), :] = proj_term[:, :own]
    term_ref[3, pl.ds(second, own), :] = proj_term[:, own:]
    partial = mm(grad_qkv, w_qkv, NT)
    pown_ref[...] = partial[:rows]
    poth_ref[...] = partial[rows:].astype(bf)


def patch_step(core, xown, xoth, weights, gown, goth):
    bf = jnp.bfloat16
    rows, channels = gown.shape
    vmem = pl.BlockSpec(memory_space=pltpu.VMEM)
    return pl.pallas_call(
        patch_body,
        out_shape=[
            jax.ShapeDtypeStruct((rows, channels), jnp.float32),
            jax.ShapeDtypeStruct((rows, channels), bf),
            jax.ShapeDtypeStruct(weights.shape, bf),
        ],
        in_specs=[pl.BlockSpec(memory_space=pltpu.SMEM)] + [vmem] * 5,
        out_specs=[vmem] * 3,
        compiler_params=pltpu.CompilerParams(vmem_limit_bytes=48 << 20),
        interpret=INTERPRET,
    )(core.reshape(1), xown, xoth, weights, gown, goth)


def per_device(feats, grad_out, qkv_weight, proj_weight, to_hilbert, to_zorder):
    bf = jnp.bfloat16
    f32 = jnp.float32
    nx, zh, zl, nc, nr = (lax.axis_size(a) for a in ROWS + ("rep",))
    peers = nx * zh * zl * nc
    x_here, core, rep = (lax.axis_index(a) for a in ("x", "core", "rep"))
    feature = feats[0]
    rows_dev, channels = feature.shape
    own = channels // nc
    half = channels // 2
    lanes = own // 2
    share = qkv_weight.shape[0]
    blocks_dev = to_hilbert.shape[1]
    chunk = 2 * CAP * BLK
    pair = [(0, 1), (1, 0)]
    side = x_here // (nx // nc)

    partner_proj = across_x(proj_weight[:, own:])
    other_feat = lax.ppermute(feature, "core", pair)

    ids = jnp.arange(blocks_dev, dtype=jnp.int32)
    target = to_hilbert[0] // blocks_dev
    send = slot_tables(target, rank_within(ids, target), peers)
    source = to_zorder[0] // blocks_dev
    recv = slot_tables(source, rank_within(to_zorder[0], source), peers)
    grad_z_in = grad_out[0]
    outgoing = (mm(send[0], grad_z_in[:, :half], NN) + mm(send[1], grad_z_in[:, half:], NN)).astype(bf)

    parts = lax.dynamic_slice_in_dim(jnp.concatenate([qkv_weight, proj_weight], axis=1), rep * channels, channels, 1)
    riding = []
    for c in range(nc):
        piece = parts[:, c * own : (c + 1) * own]
        proj = jnp.where(side == c, proj_weight[:, :own], partner_proj)
        piece = jnp.where(rep == nr - 1, proj, piece)
        riding.append(jnp.concatenate([piece[:, :lanes], piece[:, lanes:]], axis=0))
    riding = jnp.broadcast_to(jnp.stack(riding)[None], (peers // nc, nc, 2 * share, lanes))
    both = jnp.concatenate([outgoing.reshape(peers, chunk, half), riding.reshape(peers, 2 * share, lanes)], axis=2)
    both = swap(both, ROWS)
    arrived = both[:, :, :half].reshape(peers * chunk, half)
    rode = both[:, :, half:].reshape(2 * channels, lanes)

    nat = jnp.arange(channels, dtype=jnp.int32)
    wide = jnp.arange(2 * channels, dtype=jnp.int32)
    pick = [
        ((nat // share * (2 * share) + h * share + nat % share)[:, None] == wide[None, :]).astype(bf)
        for h in range(2)
    ]
    part = jnp.concatenate([mm(pick[h], rode, NN, bf) for h in range(2)], axis=1)
    weights = swap(jnp.broadcast_to(part[None], (nr, channels, own)), "rep")

    grad_hil = jnp.concatenate([mm(recv[h], arrived, TN, bf) for h in range(2)], axis=1)
    other_grad = lax.ppermute(grad_hil, "core", pair)
    p_own, p_other, term = patch_step(core, feature, other_feat, weights, grad_hil, other_grad)

    near = jnp.sum(swap(term, "rep").astype(f32), axis=0).astype(bf)
    riding = (mm(pick[0], near[:, :lanes], TN) + mm(pick[1], near[:, lanes:], TN)).astype(bf)

    from_other = lax.ppermute(p_other, "core", pair)
    grad_hfeat = (p_own + from_other.astype(f32)).astype(bf)
    going = (mm(recv[0], grad_hfeat[:, :half], NN) + mm(recv[1], grad_hfeat[:, half:], NN)).astype(bf)
    both = jnp.concatenate([going.reshape(peers, chunk, half), riding.reshape(peers, 2 * share, lanes)], axis=2)
    both = swap(both, ROWS)
    returned = both[:, :, :half].reshape(peers * chunk, half)
    rode = both[:, :, half:].reshape(peers // nc, nc, 2 * share, lanes)
    summed = jnp.sum(rode.astype(f32), axis=0)
    last = swap(jnp.broadcast_to(summed[None], (nx * nr, nc, 2 * share, lanes)), ("x", "rep"))
    last = last.reshape(nx, nr, nc, 2, share, lanes)
    mine = lax.dynamic_index_in_dim(last, x_here, 0, keepdims=False)
    partner = lax.dynamic_index_in_dim(last, (x_here + nx // 2) % nx, 0, keepdims=False)
    cols = [mine[p, c, h] for p in range(3) for c in range(nc) for h in range(2)]
    proj = [lax.dynamic_index_in_dim(m[3], side, 0, keepdims=False) for m in (mine, partner)]
    proj_cols = [m[h] for m in proj for h in range(2)]

    grad_z = jnp.concatenate([mm(send[h], returned, TN, bf) for h in range(2)], axis=1)
    return (grad_z[None], jnp.concatenate(cols, axis=1), jnp.concatenate(proj_cols, axis=1))


def solution(mesh):
    rows, reps = mesh.devices.shape
    fine = Mesh(
        mesh.devices.reshape(rows // (Z_HIGH * Z_LOW * CORES), Z_HIGH, Z_LOW, CORES, reps),
        ROWS + ("rep",),
    )
    placed = (
        P("rep", ROWS, None),
        P("rep", ROWS, None),
        P(ROWS, None),
        P(ROWS, None),
        P("rep", ROWS),
        P("rep", ROWS),
    )
    return jax.shard_map(
        per_device,
        mesh=fine,
        in_specs=placed,
        out_specs=(P("rep", ROWS, None), P(ROWS, None), P(ROWS, None)),
        check_vma=False,
    )
```

time: 201 us -> 193 us (0.960)
  starting transfers between devices: 117 us -> 53.6 us
  waiting for transfers between devices: 56.1 us -> 114 us
  matrix products: 9.29 us -> 6.94 us
    all_to_all x3 -> x5, waiting for transfers between devices: 8.82 us -> 112 us  [swap(): return lax.all_to_all(block, axis, split_axis=0, concat_axis=0, tiled=True)]
    ppermute x17 -> x1, starting transfers between devices: 79.6 us -> 3.3 us  [across_x(): lax.ppermute(block, 'x', [(here, (here + count // 2) % count) for here in...]
    ppermute x17 -> x1, waiting for transfers between devices: 47.3 us -> 0.01 us  [across_x(): lax.ppermute(block, 'x', [(here, (here + count // 2) % count) for here in...]
    all_to_all x3 -> x5, starting transfers between devices: 30.7 us -> 44.4 us  [swap(): return lax.all_to_all(block, axis, split_axis=0, concat_axis=0, tiled=True)]
    dot_general x12, matrix products: 9.29 us -> 6.94 us  [mm(): lax.dot_general(left, right, (dims, ((), ())), preferred_element_type=jnp...]
  transfers between devices with their start and end apart: 23 -> 9, of which waited for: 11 -> 6; matrix products, arithmetic and copies ran while one was open for 7% -> 5% of each run, Pallas kernels for 0% -> 0%
where the time goes in v3:
time: 193 us; the launch traced here: 192 us
  waiting for transfers between devices  114 us (59%)
  starting transfers between devices  53.6 us (28%)
  Pallas kernels  7.29 us (4%)
  matrix products  6.94 us (4%)
  other arithmetic  5.01 us (3%)
  local copies, waits for them, and re-layouts  4.27 us (2%)
    all_to_all x5, waiting for transfers between devices, swap(): return lax.all_to_all(block, axis, split_axis=0, concat_axis=0, tiled=True)  112 us
    all_to_all x5, starting transfers between devices, swap(): return lax.all_to_all(block, axis, split_axis=0, concat_axis=0, tiled=True)  44.4 us
    pallas_call x1, Pallas kernels, patch_step(): pl.pallas_call(patch_body, out_shape=[jax.ShapeDtypeStruct((rows, channel...  7.29 us
    dot_general x12, matrix products, mm(): lax.dot_general(left, right, (dims, ((), ())), preferred_element_type=jnp...  6.94 us
  transfers between devices with their start and end apart: 9, of which 6 were waited for; matrix products, arithmetic and copies ran while one was open for 5% of the time, Pallas kernels for 0%

profile of v3, /device:TPU:6, one launch (start us, length us, event | category | flops | bytes accessed | tf_op | source)
XLA Modules:
  0.0 191.8 jit_solution(2890476637901220230)
XLA Ops:
  0.6 0.7 slice.118
  1.4 3.3 %collective-permute-start.1 = (bf16[4,256]{1,0:T(4,128)(2,1)S(1)}, bf16[4,256]{1,0:T(4,128)(2,1)S(1)}, u32[]{:S(2)}, u32[]{:S(2)}) collective-permute-start(bf16[4,256]{1,0:T(4,128)(2,1)S(1)} %slice.118), channel_id=1, source_target_pairs={{0,256},{128,384},{256,0},{384,128},{1,257},{129,385},{257,1},{385... | collective-permute-start | bytes 6152 | tf_op jit(solution)/shard_map/ppermute | solution.py:49
  4.7 0.7 and_select_fusion.1
  5.4 0.7 fusion.44
  6.0 0.2 convert_reduce_fusion.2
  6.2 0.1 iota_add_fusion.1
  6.3 0.1 add.190
  6.5 1.2 fusion.18
  7.7 0.3 fusion.7
  8.1 0.3 copy-done.2
  8.6 1.0 pad_maximum_fusion
  9.6 19.9 %all-to-all-start = ((bf16[128,8,384]{2,1,0:T(8,128)(2,1)}), bf16[128,8,384]{2,1,0:T(8,128)(2,1)S(1)}, u32[]{:S(2)}, u32[]{:S(2)}) async-start(bf16[128,8,384]{2,1,0:T(8,128)(2,1)} %pad_maximum_fusion), calls=%async_computation | async-start | bytes 1572864 | tf_op jit(solution)/shard_map/all_to_all | solution.py:44
  29.5 2.1 %collective-permute-start = (bf16[256,512]{1,0:T(8,128)(2,1)S(1)}, bf16[256,512]{1,0:T(8,128)(2,1)S(1)}, u32[]{:S(2)}, u32[]{:S(2)}) collective-permute-start(bf16[256,512]{1,0:T(8,128)(2,1)S(1)} %bitcast.103), channel_id=1, source_target_pairs={{0,4},{4,0},{1,5},{5,1},{2,6},{6,2},{3,7},{7,3},{8,12},{12,8},{9,1... | collective-permute-start | bytes 786440 | tf_op jit(solution)/shard_map/ppermute | solution.py:150
  31.6 0.2 convert_reduce_fusion.1
  31.8 0.1 iota_add_fusion
  31.9 0.1 add.195
  32.0 40.5 %all-to-all-done = bf16[128,8,384]{2,1,0:T(8,128)(2,1)S(1)} async-done(((bf16[128,8,384]{2,1,0:T(8,128)(2,1)}), bf16[128,8,384]{2,1,0:T(8,128)(2,1)S(1)}, u32[]{:S(2)}, u32[]{:S(2)}) %all-to-all-start) | async-done | bytes 786464 | tf_op jit(solution)/shard_map/all_to_all | solution.py:44
  72.5 0.6 fusion.11
  73.2 0.6 fusion.12
  73.8 0.1 copy.17
  74.0 1.0 broadcast_in_dim.9
  75.0 4.5 %all-to-all-start.1 = ((bf16[4,512,256]{2,1,0:T(8,128)(2,1)}), bf16[4,512,256]{2,1,0:T(8,128)(2,1)S(1)}, u32[]{:S(2)}, u32[]{:S(2)}) async-start(bf16[4,512,256]{2,1,0:T(8,128)(2,1)} %broadcast_in_dim.9), calls=%async_computation.1 | async-start | bytes 2097152 | tf_op jit(solution)/shard_map/all_to_all | solution.py:44
  79.5 0.5 convolution_convert_fusion.3
  80.0 0.5 convolution_convert_fusion.2
  80.5 1.9 %collective-permute-start.2 = (bf16[256,512]{1,0:T(8,128)(2,1)S(1)}, bf16[256,512]{1,0:T(8,128)(2,1)S(1)}, u32[]{:S(2)}, u32[]{:S(2)}) collective-permute-start(bf16[256,512]{1,0:T(8,128)(2,1)S(1)} %pad_maximum_fusion.3.gown_ref), channel_id=1, source_target_pairs={{0,4},{4,0},{1,5},{5,1},{2,6},{6,2},{3,7},{7,3},{8,12},{12,8},{9,1... | collective-permute-start | bytes 786440 | tf_op jit(solution)/shard_map/ppermute | solution.py:183
  82.5 1.5 collective-permute-done.2.goth_ref
  84.0 9.4 %all-to-all-done.1.w_ref = bf16[4,512,256]{2,1,0:T(8,128)(2,1)S(1)} async-done(((bf16[4,512,256]{2,1,0:T(8,128)(2,1)}), bf16[4,512,256]{2,1,0:T(8,128)(2,1)S(1)}, u32[]{:S(2)}, u32[]{:S(2)}) %all-to-all-start.1) | async-done | bytes 1048608 | tf_op jit(solution)/shard_map/all_to_all | solution.py:44
  93.4 7.3 %shard_map.85 = (f32[256,512]{1,0:T(8,128)S(1)}, bf16[256,512]{1,0:T(8,128)(2,1)S(1)}, bf16[4,512,256]{2,1,0:T(8,128)(2,1)}) custom-call(s32[1]{0:T(128)} %bitcast.4.core_ref, bf16[256,512]{1,0:T(8,128)(2,1)S(1)} %bitcast.104, bf16[256,512]{1,0:T(8,128)(2,1)S(1)} %collective-permute-done.xoth_ref, bf16[4,512,256]{2,1,0:T(8,128)(2,1)S(1)} %all-to-all-done.1.w_ref, ...), custom_call_target="tpu_custom_call" | custom-call | tf_op jit(solution)/shard_map/pallas_call | solution.py:118
  100.7 1.9 collective-permute-start.3
  102.6 3.7 %all-to-all-start.2 = ((bf16[4,512,256]{2,1,0:T(8,128)(2,1)}), bf16[4,512,256]{2,1,0:T(8,128)(2,1)S(1)}, u32[]{:S(2)}, u32[]{:S(2)}) async-start(bf16[4,512,256]{2,1,0:T(8,128)(2,1)} %get-tuple-element.8), calls=%async_computation.2 | async-start | bytes 2097152 | tf_op jit(solution)/shard_map/all_to_all | solution.py:44
  106.3 0.1 add_convert_fusion
  106.4 0.3 fusion.13
  106.7 0.3 fusion.6
  107.0 15.1 %all-to-all-done.2 = bf16[4,512,256]{2,1,0:T(8,128)(2,1)S(1)} async-done(((bf16[4,512,256]{2,1,0:T(8,128)(2,1)}), bf16[4,512,256]{2,1,0:T(8,128)(2,1)S(1)}, u32[]{:S(2)}, u32[]{:S(2)}) %all-to-all-start.2) | async-done | bytes 1048608 | tf_op jit(solution)/shard_map/all_to_all | solution.py:44
  122.1 0.3 reduce_sum.41
  122.4 0.8 fusion
  123.2 0.8 fusion.10
  124.0 1.0 pad_maximum_fusion.1
  125.0 9.6 %all-to-all-start.3 = ((bf16[128,8,384]{2,1,0:T(8,128)(2,1)}), bf16[128,8,384]{2,1,0:T(8,128)(2,1)S(1)}, u32[]{:S(2)}, u32[]{:S(2)}) async-start(bf16[128,8,384]{2,1,0:T(8,128)(2,1)} %pad_maximum_fusion.1), calls=%async_computation.3 | async-start | bytes 1572864 | tf_op jit(solution)/shard_map/all_to_all | solution.py:44
  134.7 43.0 %all-to-all-done.3 = bf16[128,8,384]{2,1,0:T(8,128)(2,1)S(1)} async-done(((bf16[128,8,384]{2,1,0:T(8,128)(2,1)}), bf16[128,8,384]{2,1,0:T(8,128)(2,1)S(1)}, u32[]{:S(2)}, u32[]{:S(2)}) %all-to-all-start.3) | async-done | bytes 786464 | tf_op jit(solution)/shard_map/all_to_all | solution.py:44
  177.7 0.1 convert_reduce_fusion
  177.8 0.7 broadcast_in_dim.11
  178.4 6.7 %all-to-all-start.4 = ((f32[16,2,8,128]{3,2,1,0:T(8,128)}), f32[16,2,8,128]{3,2,1,0:T(8,128)S(1)}, u32[]{:S(2)}, u32[]{:S(2)}) async-start(f32[16,2,8,128]{3,2,1,0:T(8,128)} %broadcast_in_dim.11), calls=%async_computation.4 | async-start | bytes 262144 | tf_op jit(solution)/shard_map/all_to_all | solution.py:44
  185.2 0.4 convolution_convert_fusion.1
  185.6 0.4 convolution_convert_fusion
  186.1 0.8 copy.20
  186.9 4.1 %all-to-all-done.4 = f32[16,2,8,128]{3,2,1,0:T(8,128)S(1)} async-done(((f32[16,2,8,128]{3,2,1,0:T(8,128)}), f32[16,2,8,128]{3,2,1,0:T(8,128)S(1)}, u32[]{:S(2)}, u32[]{:S(2)}) %all-to-all-start.4) | async-done | bytes 131104 | tf_op jit(solution)/shard_map/all_to_all | solution.py:44
  191.2 0.6 pad_maximum_fusion.4
  (44 shorter events, 0.4 us)
Async XLA Ops:
  0.6 7.1 %copy-start.1 = (bf16[1,256,512]{2,1,0:T(8,128)(2,1)S(1)}, bf16[1,256,512]{2,1,0:T(8,128)(2,1)}, u32[]{:S(2)}) copy-start(bf16[1,256,512]{2,1,0:T(8,128)(2,1)} %param.7) | copy-start | bytes 786436
  1.4 7.1 %collective-permute-start.1 = (bf16[4,256]{1,0:T(4,128)(2,1)S(1)}, bf16[4,256]{1,0:T(4,128)(2,1)S(1)}, u32[]{:S(2)}, u32[]{:S(2)}) collective-permute-start(bf16[4,256]{1,0:T(4,128)(2,1)S(1)} %slice.118), channel_id=1, source_target_pairs={{0,256},{128,384},{256,0},{384,128},{1,257},{129,385},{257,1},{385... | collective-permute-start | bytes 6152 | tf_op jit(solution)/shard_map/ppermute | solution.py:49
  7.7 0.7 copy-start.2
  7.7 0.7 copy-start.3
  9.6 19.9 %copy-start = (bf16[1,256,512]{2,1,0:T(8,128)(2,1)S(1)}, bf16[1,256,512]{2,1,0:T(8,128)(2,1)}, u32[]{:S(2)}) copy-start(bf16[1,256,512]{2,1,0:T(8,128)(2,1)} %param.6) | copy-start | bytes 786436
  9.6 22.0 %copy-start.4 = (s32[1,128]{1,0:T(1,128)S(1)}, s32[1,128]{1,0:T(1,128)}, u32[]{:S(2)}) copy-start(s32[1,128]{1,0:T(1,128)} %param.11) | copy-start | bytes 1540
  9.6 62.9 %all-to-all-start = ((bf16[128,8,384]{2,1,0:T(8,128)(2,1)}), bf16[128,8,384]{2,1,0:T(8,128)(2,1)S(1)}, u32[]{:S(2)}, u32[]{:S(2)}) async-start(bf16[128,8,384]{2,1,0:T(8,128)(2,1)} %pad_maximum_fusion), calls=%async_computation | async-start | bytes 1572864 | tf_op jit(solution)/shard_map/all_to_all | solution.py:44
  29.5 53.0 %collective-permute-start = (bf16[256,512]{1,0:T(8,128)(2,1)S(1)}, bf16[256,512]{1,0:T(8,128)(2,1)S(1)}, u32[]{:S(2)}, u32[]{:S(2)}) collective-permute-start(bf16[256,512]{1,0:T(8,128)(2,1)S(1)} %bitcast.103), channel_id=1, source_target_pairs={{0,4},{4,0},{1,5},{5,1},{2,6},{6,2},{3,7},{7,3},{8,12},{12,8},{9,1... | collective-permute-start | bytes 786440 | tf_op jit(solution)/shard_map/ppermute | solution.py:150
  75.0 18.4 %all-to-all-start.1 = ((bf16[4,512,256]{2,1,0:T(8,128)(2,1)}), bf16[4,512,256]{2,1,0:T(8,128)(2,1)S(1)}, u32[]{:S(2)}, u32[]{:S(2)}) async-start(bf16[4,512,256]{2,1,0:T(8,128)(2,1)} %broadcast_in_dim.9), calls=%async_computation.1 | async-start | bytes 2097152 | tf_op jit(solution)/shard_map/all_to_all | solution.py:44
  80.5 3.4 %collective-permute-start.2 = (bf16[256,512]{1,0:T(8,128)(2,1)S(1)}, bf16[256,512]{1,0:T(8,128)(2,1)S(1)}, u32[]{:S(2)}, u32[]{:S(2)}) collective-permute-start(bf16[256,512]{1,0:T(8,128)(2,1)S(1)} %pad_maximum_fusion.3.gown_ref), channel_id=1, source_target_pairs={{0,4},{4,0},{1,5},{5,1},{2,6},{6,2},{3,7},{7,3},{8,12},{12,8},{9,1... | collective-permute-start | bytes 786440 | tf_op jit(solution)/shard_map/ppermute | solution.py:183
  100.7 5.6 %collective-permute-start.3 = (bf16[256,512]{1,0:T(8,128)(2,1)S(1)}, bf16[256,512]{1,0:T(8,128)(2,1)S(1)}, u32[]{:S(2)}, u32[]{:S(2)}) collective-permute-start(bf16[256,512]{1,0:T(8,128)(2,1)S(1)} %get-tuple-element.7), channel_id=1, source_target_pairs={{0,4},{4,0},{1,5},{5,1},{2,6},{6,2},{3,7},{7,3},{8,12},{12,8},{9,1... | collective-permute-start | bytes 786440 | tf_op jit(solution)/shard_map/ppermute | solution.py:189
  102.6 19.5 %all-to-all-start.2 = ((bf16[4,512,256]{2,1,0:T(8,128)(2,1)}), bf16[4,512,256]{2,1,0:T(8,128)(2,1)S(1)}, u32[]{:S(2)}, u32[]{:S(2)}) async-start(bf16[4,512,256]{2,1,0:T(8,128)(2,1)} %get-tuple-element.8), calls=%async_computation.2 | async-start | bytes 2097152 | tf_op jit(solution)/shard_map/all_to_all | solution.py:44
  125.0 52.7 %all-to-all-start.3 = ((bf16[128,8,384]{2,1,0:T(8,128)(2,1)}), bf16[128,8,384]{2,1,0:T(8,128)(2,1)S(1)}, u32[]{:S(2)}, u32[]{:S(2)}) async-start(bf16[128,8,384]{2,1,0:T(8,128)(2,1)} %pad_maximum_fusion.1), calls=%async_computation.3 | async-start | bytes 1572864 | tf_op jit(solution)/shard_map/all_to_all | solution.py:44
  178.4 12.6 %all-to-all-start.4 = ((f32[16,2,8,128]{3,2,1,0:T(8,128)}), f32[16,2,8,128]{3,2,1,0:T(8,128)S(1)}, u32[]{:S(2)}, u32[]{:S(2)}) async-start(f32[16,2,8,128]{3,2,1,0:T(8,128)} %broadcast_in_dim.11), calls=%async_computation.4 | async-start | bytes 262144 | tf_op jit(solution)/shard_map/all_to_all | solution.py:44
  191.2 0.6 copy-start.5

commit v4 on v2

--- a/solution.py
+++ b/solution.py
@@ -47,6 +47,11 @@
 def shift(block, axis, step):
     count = lax.axis_size(axis)
     return lax.ppermute(block, axis, [(here, (here + step) % count) for here in range(count)])
+
+
+def flip(block, axis, bit):
+    count = lax.axis_size(axis)
+    return lax.ppermute(block, axis, [(here, here ^ bit) for here in range(count)])
 
 
 def attend(qkv, grad_attn, own, head_size):
@@ -85,22 +90,25 @@
 
 
 def patch_body(
-    core_ref, x_ref, mine_ref, recv_ref, gown_ref, goth_ref, own_perm_ref,
+    place_ref, x_ref, w0_ref, w1_ref, w2_ref, w3_ref, gown_ref, goth_ref, own_perm_ref,
     pown_ref, poth_ref, keep_ref, send_ref, w_ref, tq_ref, tp_ref,
 ):
     bf = jnp.bfloat16
-    core = core_ref[0]
+    core, rep = place_ref[0], place_ref[1]
     channels = x_ref.shape[1]
     own = channels // CORES
     rows = gown_ref.shape[0]
     part = own // CORES
-    w_ref[core] = mine_ref[...]
-    w_ref[1 - core] = recv_ref[...]
-    w_qkv = jnp.concatenate([w_ref[c, :, : 3 * own] for c in range(CORES)], axis=0)
-    lo = pl.multiple_of(core * part, part)
-    w_proj = jnp.concatenate([w_ref[c, pl.ds(lo, part), 3 * own :] for c in range(CORES)], axis=0)
+    for k, ref in enumerate((w0_ref, w1_ref, w2_ref, w3_ref)):
+        slot = lax.rem(rep + 4 - k, 4)
+        w_ref[slot, core] = ref[:own]
+        w_ref[slot, 1 - core] = ref[own:]
+    w_qkv = jnp.concatenate([w_ref[p].reshape(channels, own) for p in range(3)], axis=1)
+    cols = [
+        jnp.concatenate([w_ref[3, c, h * part : (h + 1) * part] for c in range(CORES)], axis=0) for h in range(2)
+    ]
     own_perm = own_perm_ref[...]
-    w_proj = mm(own_perm, w_proj, NN, bf)
+    w_proj = mm(own_perm, jnp.concatenate(cols, axis=1), NN, bf)
     x = x_ref[...]
     grad_pair = jnp.concatenate([gown_ref[...], goth_ref[...]], axis=0)
     qkv = mm(x, w_qkv, NN, bf)
@@ -118,7 +126,7 @@
     poth_ref[...] = partial[rows:].astype(bf)
 
 
-def patch_step(core, x, mine, recv, gown, goth, own_perm):
+def patch_step(place, x, weights, gown, goth, own_perm):
     bf = jnp.bfloat16
     rows, channels = gown.shape
     own = channels // CORES
@@ -131,25 +139,25 @@
             jax.ShapeDtypeStruct((own, 4 * own), bf),
             jax.ShapeDtypeStruct((own, 4 * own), bf),
         ],
-        in_specs=[pl.BlockSpec(memory_space=pltpu.SMEM)] + [vmem] * 6,
+        in_specs=[pl.BlockSpec(memory_space=pltpu.SMEM)] + [vmem] * 8,
         out_specs=[vmem] * 4,
         scratch_shapes=[
-            pltpu.VMEM((CORES, own, 3 * own + channels), bf),
+            pltpu.VMEM((4, CORES, own, own), bf),
             pltpu.VMEM((CORES, own, 3 * own), bf),
             pltpu.VMEM((CORES, own // CORES, channels), bf),
         ],
         compiler_params=pltpu.CompilerParams(vmem_limit_bytes=48 << 20),
         interpret=INTERPRET,
-    )(core.reshape(1), x, mine, recv, gown, goth, own_perm)
+    )(place, x, *weights, gown, goth, own_perm)
 
 
 def per_device(feats, grad_out, qkv_weight, proj_weight, to_hilbert, to_zorder):
     bf = jnp.bfloat16
     f32 = jnp.float32
-    nx, zh, zl, nc, nr = (lax.axis_size(a) for a in ("x", "zh", "zl", "core", "rep"))
+    nx, zh, zl, nc, nr = (lax.axis_size(a) for a in ROWS + ("rep",))
     nz = zh * zl
     peers = nx * nz * nc
-    x_here, zh_here, zl_here, core = (lax.axis_index(a) for a in ROWS)
+    x_here, core, rep = (lax.axis_index(a) for a in ("x", "core", "rep"))
     feature = feats[0]
     rows_dev, channels = feature.shape
     own = channels // nc
@@ -159,6 +167,11 @@
     blocks_dev = to_hilbert.shape[1]
     chunk = 2 * CAP * BLK
     pair = [(0, 1), (1, 0)]
+    bits = [1 << b for b in range(nx.bit_length() - 1)]
+
+    mine = lax.dynamic_slice_in_dim(jnp.concatenate([qkv_weight, proj_weight], axis=1), rep * channels, channels, 1)
+    mine = jnp.concatenate([mine[:, :own], mine[:, own:]], axis=0)
+    plane = swap(jnp.broadcast_to(mine[None], (nz, 2 * share, own)), ("zh", "zl")).reshape(nz * 2 * share, own)
 
     ids = jnp.arange(blocks_dev, dtype=jnp.int32)
     target = to_hilbert[0] // blocks_dev
@@ -167,34 +180,34 @@
     recv = slot_tables(source, rank_within(to_zorder[0], source), peers)
     grad_z_in = grad_out[0]
     outgoing = (mm(send[0], grad_z_in[:, :half], NN) + mm(send[1], grad_z_in[:, half:], NN)).astype(bf)
-
-    halves = []
-    for c in range(nc):
-        cols = [qkv_weight[:, p * channels + c * own : p * channels + (c + 1) * own] for p in range(3)]
-        halves.append(jnp.concatenate(cols + [proj_weight[:, c * own : (c + 1) * own]], axis=1))
-    piece = jnp.concatenate(halves, axis=0)
-    other_feat = lax.ppermute(feature, "core", pair)
-    gathered = piece
-    for axis in ("zh", "zl", "x"):
-        gathered = jnp.concatenate([gathered] + [shift(gathered, axis, k) for k in range(1, lax.axis_size(axis))], axis=0)
-
-    def group_index(x, z):
-        low = (zl_here - z) % zl
-        high = (zh_here - z // zl) % zh
-        return (((x_here - x) % nx) * zl + low) * zh + high
+    outgoing, plane = lax.optimization_barrier((outgoing, plane))
+    arrived = swap(outgoing.reshape(peers, chunk, half), ROWS).reshape(peers * chunk, half)
+
+    gathered = plane
+    for bit in bits[::-1]:
+        gathered = jnp.concatenate([gathered, flip(gathered, "x", bit)], axis=0)
+
+    def x_index(x):
+        apart = x ^ x_here
+        index = jnp.zeros_like(apart)
+        for bit in bits:
+            index = index * 2 + (apart // bit) % 2
+        return index
 
     a = jnp.arange(own, dtype=jnp.int32)
-    i_of, z_of, x_of = a % share, a // share % nz, a // (share * nz)
+    i_of, z_of, top = a % share, a // share % nz, a // (share * nz)
     slot = jnp.arange(2 * own, dtype=jnp.int32)
     picked = []
-    for h in range(2):
-        place = (group_index(x_of, z_of) * 2 + h) * share + i_of
+    for c in range(nc):
+        side = nx // nc
+        for_qkv = (x_index(top) * nz + z_of) * 2 + c
+        for_proj = (x_index(c * side + top % side) * nz + z_of) * 2 + top // side
+        place = jnp.where(rep == 3, for_proj, for_qkv) * share + i_of
         picked.append(mm((place[:, None] == slot[None, :]).astype(bf), gathered, NN, bf))
-    proj_rows = [p[:, 3 * own :] for p in picked]
-    qkv_mine = jnp.where(core == 0, picked[0][:, : 3 * own], picked[1][:, : 3 * own])
-    qkv_theirs = jnp.where(core == 0, picked[1][:, : 3 * own], picked[0][:, : 3 * own])
-    mine = jnp.concatenate([qkv_mine] + proj_rows, axis=1)
-    theirs = lax.ppermute(jnp.concatenate([qkv_theirs] + proj_rows, axis=1), "core", pair)
+    kept = jnp.where(core == 0, picked[0], picked[1])
+    theirs = lax.ppermute(jnp.where(core == 0, picked[1], picked[0]), "core", pair)
+    parts = jnp.concatenate([kept, theirs], axis=0)
+    weights = [parts] + [shift(parts, "rep", k) for k in range(1, nr)]
 
     def order(count):
         nat = jnp.arange(count, dtype=jnp.int32)
@@ -204,11 +217,12 @@
 
     perm = order(channels)
     own_perm = order(own)
+    other_feat = lax.ppermute(feature, "core", pair)
     x_pair = mm(jnp.concatenate([feature, other_feat], axis=0), perm, NN, bf)
-    arrived = swap(outgoing.reshape(peers, chunk, half), ROWS).reshape(peers * chunk, half)
     grad_hil = jnp.concatenate([mm(recv[h], arrived, TN, bf) for h in range(2)], axis=1)
     other_grad = lax.ppermute(grad_hil, "core", pair)
-    p_own, p_other, keep, away = patch_step(core, x_pair, mine, theirs, grad_hil, other_grad, own_perm)
+    place = jnp.stack([core, rep])
+    p_own, p_other, keep, away = patch_step(place, x_pair, weights, grad_hil, other_grad, own_perm)
 
     from_other = lax.ppermute(p_other, "core", pair)
     grad_hfeat = (p_own + from_other.astype(f32)).astype(bf)
@@ -216,32 +230,30 @@
     returned = swap(going.reshape(peers, chunk, half), ROWS).reshape(peers * chunk, half)
 
     got = lax.ppermute(away, "core", pair)
-    proj_all = jnp.concatenate([keep[:, 3 * own :], got[:, 3 * own :]], axis=0)
-    plane = own // nx
-
-    def toward(step):
-        x_to = (x_here + step) % nx
-        first = x_to * plane
-        base = (x_to // (nx // nc) + core) % nc * own + x_to % (nx // nc) * plane
-        pieces = [lax.dynamic_slice_in_dim(m[:, : 3 * own], first, plane, 0) for m in (keep, got)]
-        pieces += [lax.dynamic_slice_in_dim(proj_all, base + k * part, plane, 0) for k in range(2)]
-        return jnp.concatenate(pieces, axis=1)
-
-    total = toward(0).astype(f32)
-    arrivals = [shift(toward(step), "x", step) for step in range(1, nx)]
-    total = (total + sum(t.astype(f32) for t in arrivals)).astype(bf)
-    rows_left = total.shape[0] // zh
-
-    def toward_zh(step):
-        return lax.dynamic_slice_in_dim(total, (zh_here + step) % zh * rows_left, rows_left, 0)
-
-    arrivals = [shift(toward_zh(step), "zh", step) for step in range(1, zh)]
-    total = (toward_zh(0).astype(f32) + sum(t.astype(f32) for t in arrivals)).astype(bf)
+    proj = [jnp.concatenate([m[:part, 3 * own :], m[part:, 3 * own :]], axis=1) for m in (keep, got)]
+    proj = jnp.concatenate([jnp.where(core == 0, proj[0], proj[1]), jnp.where(core == 0, proj[1], proj[0])], axis=0)
+    total = jnp.concatenate([keep[:, : 3 * own], got[:, : 3 * own], proj], axis=1)
+
+    def halve(value, axis, here, bit, first, second):
+        mine_set = here // bit % 2 == 1
+        stay = jnp.where(mine_set, second, first)
+        come = flip(jnp.where(mine_set, first, second), axis, bit)
+        return (stay.astype(f32) + come.astype(f32)).astype(bf)
+
+    for bit in bits:
+        count = nx // bit
+        blocks = total.reshape(count // 2, 2, nz * share, total.shape[1])
+        flat = (count // 2 * nz * share, total.shape[1])
+        total = halve(total, "x", x_here, bit, blocks[:, 0].reshape(flat), blocks[:, 1].reshape(flat))
+    for bit in (1, 2):
+        wide = total.shape[1] // 2
+        total = halve(total, "rep", rep, bit, total[:, :wide], total[:, wide:])
     total, returned = lax.optimization_barrier((total, returned))
-    wide = 4 * channels
-    last = jnp.broadcast_to(total.reshape(zl, 1, share, wide), (zl, nr, share, wide))
-    last = swap(last.reshape(zl * nr, share, wide), ("zl", "rep"))
-    last = jnp.sum(last.astype(f32), axis=0)
+    wide = total.shape[1]
+    far = swap(total.reshape(nz, share, wide), ("zh", "zl"))
+    summed = jnp.sum(far.astype(f32), axis=0)
+    last = swap(jnp.broadcast_to(summed[None], (nr, share, wide)), "rep")
+    last = jnp.concatenate([last[r] for r in (0, 2, 1, 3)], axis=1)
     grad_perm = jnp.concatenate([mm(send[h], returned, TN, bf) for h in range(2)], axis=1)
     grad_z = mm(grad_perm, perm, NT, bf)
     lower = jnp.where(core == 0, last[:, : 3 * own], last[:, 3 * own : 6 * own])

time: 201 us -> 179 us (0.89); the launches traced: 199 us -> 179 us
  starting transfers between devices: 117 us -> 96.7 us
    ppermute x15 -> x3, starting transfers between devices: 75.2 us -> 11.7 us  [shift(): lax.ppermute(block, axis, [(here, (here + step) % count) for here in rang...]
    ppermute x15 -> x3, waiting for transfers between devices: 47.3 us -> 3.68 us  [shift(): lax.ppermute(block, axis, [(here, (here + step) % count) for here in rang...]
    ppermute x1 -> x7, waiting for transfers between devices: 0.01 us -> 27.8 us  [the longest x6 26.6 us: flip(): lax.ppermute(block, axis, [(here, here ^ bit) for here in range(count)])]
    all_to_all x3 -> x5, starting transfers between devices: 30.7 us -> 55.1 us  [swap(): return lax.all_to_all(block, axis, split_axis=0, concat_axis=0, tiled=True)]
    ppermute x1 -> x7, starting transfers between devices: 1.92 us -> 21.6 us  [the longest x6 19.7 us: flip(): lax.ppermute(block, axis, [(here, here ^ bit) for here in range(count)])]
    all_to_all x3 -> x5, waiting for transfers between devices: 8.82 us -> 26.5 us  [swap(): return lax.all_to_all(block, axis, split_axis=0, concat_axis=0, tiled=True)]
    slice x9 -> x5, local copies, waits for them, and re-layouts: 2.26 us -> 0.12 us  [the longest x2 0.07 us: per_device(): total = jnp.concatenate([keep[:, :3 * own], got[:, :3 * own], proj], axis=1)]
  transfers between devices with their start and end apart: 23 -> 19, of which waited for: 11 -> 13; matrix products, arithmetic and copies ran while one was open for 7% -> 6% of each run, Pallas kernels for 0% -> 0%
where the time goes in v4:
time: 179 us
  starting transfers between devices  96.7 us (54%)
  waiting for transfers between devices  58.1 us (32%)
  matrix products  7.94 us (4%)
  Pallas kernels  7.28 us (4%)
  other arithmetic  3.7 us (2%)
  local copies, waits for them, and re-layouts  3.6 us (2%)
    all_to_all x5, starting transfers between devices, swap(): return lax.all_to_all(block, axis, split_axis=0, concat_axis=0, tiled=True)  55.1 us
    ppermute x6, waiting for transfers between devices, flip(): lax.ppermute(block, axis, [(here, here ^ bit) for here in range(count)])  26.6 us
    all_to_all x5, waiting for transfers between devices, swap(): return lax.all_to_all(block, axis, split_axis=0, concat_axis=0, tiled=True)  26.5 us
    ppermute x6, starting transfers between devices, flip(): lax.ppermute(block, axis, [(here, here ^ bit) for here in range(count)])  19.7 us
    ppermute x3, starting transfers between devices, shift(): lax.ppermute(block, axis, [(here, (here + step) % count) for here in rang...  11.7 us
    dot_general x12, matrix products, mm(): lax.dot_general(left, right, (dims, ((), ())), preferred_element_type=jnp...  7.94 us
    pallas_call x1, Pallas kernels, patch_step(): pl.pallas_call(patch_body, out_shape=[jax.ShapeDtypeStruct((rows, channel...  7.28 us
    ppermute x3, waiting for transfers between devices, shift(): lax.ppermute(block, axis, [(here, (here + step) % count) for here in rang...  3.68 us
  transfers between devices with their start and end apart: 19, of which 13 were waited for; matrix products, arithmetic and copies ran while one was open for 6% of the time, Pallas kernels for 0%

profile of v4, /device:TPU:6, one launch (start us, length us, event | category | flops | bytes accessed | tf_op | source)
XLA Modules:
  0.0 178.6 jit_solution(12246665073280298730)
XLA Ops:
  0.7 0.7 fusion.38
  1.4 0.6 broadcast_in_dim.6
  2.1 15.2 %all-to-all-start = ((bf16[16,8,256]{2,1,0:T(8,128)(2,1)}), bf16[16,8,256]{2,1,0:T(8,128)(2,1)S(1)}, u32[]{:S(2)}, u32[]{:S(2)}) async-start(bf16[16,8,256]{2,1,0:T(8,128)(2,1)} %broadcast_in_dim.6), calls=%async_computation | async-start | bytes 131072 | tf_op jit(solution)/shard_map/all_to_all | solution.py:44
  17.3 1.9 %collective-permute-start = (bf16[256,512]{1,0:T(8,128)(2,1)}, bf16[256,512]{1,0:T(8,128)(2,1)S(1)}, u32[]{:S(2)}, u32[]{:S(2)}) collective-permute-start(bf16[256,512]{1,0:T(8,128)(2,1)} %bitcast.65), channel_id=1, source_target_pairs={{0,4},{4,0},{1,5},{5,1},{2,6},{6,2},{3,7},{7,3},{8,12},{12,8},{9,1... | collective-permute-start | bytes 786440 | tf_op jit(solution)/shard_map/ppermute | solution.py:220
  19.2 0.7 and_select_fusion.5
  19.9 0.7 fusion.70
  21.0 1.2 fusion.6
  22.4 1.1 fusion
  23.5 6.5 %all-to-all-done = bf16[16,8,256]{2,1,0:T(8,128)(2,1)S(1)} async-done(((bf16[16,8,256]{2,1,0:T(8,128)(2,1)}), bf16[16,8,256]{2,1,0:T(8,128)(2,1)S(1)}, u32[]{:S(2)}, u32[]{:S(2)}) %all-to-all-start) | async-done | bytes 65568 | tf_op jit(solution)/shard_map/all_to_all | solution.py:44
  30.0 10.4 %all-to-all-start.1 = ((bf16[128,8,256]{2,1,0:T(8,128)(2,1)}), bf16[128,8,256]{2,1,0:T(8,128)(2,1)S(1)}, u32[]{:S(2)}, u32[]{:S(2)}) async-start(bf16[128,8,256]{2,1,0:T(8,128)(2,1)} %bitcast.9), calls=%async_computation.1 | async-start | bytes 1048576 | tf_op jit(solution)/shard_map/all_to_all | solution.py:44
  40.8 2.9 %collective-permute-start.1 = (bf16[128,256]{1,0:T(8,128)(2,1)S(1)}, bf16[128,256]{1,0:T(8,128)(2,1)S(1)}, u32[]{:S(2)}, u32[]{:S(2)}) collective-permute-start(bf16[128,256]{1,0:T(8,128)(2,1)S(1)} %bitcast.56), channel_id=1, source_target_pairs={{0,256},{128,384},{256,0},{384,128},{1,257},{129,385},{257,1},{385... | collective-permute-start | bytes 196616 | tf_op jit(solution)/shard_map/ppermute | solution.py:54
  43.7 5.0 %collective-permute-done.1 = bf16[128,256]{1,0:T(8,128)(2,1)S(1)} collective-permute-done((bf16[128,256]{1,0:T(8,128)(2,1)S(1)}, bf16[128,256]{1,0:T(8,128)(2,1)S(1)}, u32[]{:S(2)}, u32[]{:S(2)}) %collective-permute-start.1) | collective-permute-done | bytes 65568 | tf_op jit(solution)/shard_map/ppermute | solution.py:54
  48.8 2.4 %collective-permute-start.2 = (bf16[256,256]{1,0:T(8,128)(2,1)S(1)}, bf16[256,256]{1,0:T(8,128)(2,1)S(1)}, u32[]{:S(2)}, u32[]{:S(2)}) collective-permute-start(bf16[256,256]{1,0:T(8,128)(2,1)S(1)} %pad_maximum_fusion.2), channel_id=1, source_target_pairs={{0,128},{128,0},{256,384},{384,256},{1,129},{129,1},{257,385},{385... | collective-permute-start | bytes 393224 | tf_op jit(solution)/shard_map/ppermute | solution.py:54
  51.2 5.0 %collective-permute-done.2 = bf16[256,256]{1,0:T(8,128)(2,1)S(1)} collective-permute-done((bf16[256,256]{1,0:T(8,128)(2,1)S(1)}, bf16[256,256]{1,0:T(8,128)(2,1)S(1)}, u32[]{:S(2)}, u32[]{:S(2)}) %collective-permute-start.2) | collective-permute-done | bytes 131104 | tf_op jit(solution)/shard_map/ppermute | solution.py:54
  56.8 1.9 %collective-permute-start.3 = (bf16[256,256]{1,0:T(8,128)(2,1)S(1)}, bf16[256,256]{1,0:T(8,128)(2,1)S(1)}, u32[]{:S(2)}, u32[]{:S(2)}) collective-permute-start(bf16[256,256]{1,0:T(8,128)(2,1)S(1)} %get-tuple-element.28), channel_id=1, source_target_pairs={{0,4},{4,0},{1,5},{5,1},{2,6},{6,2},{3,7},{7,3},{8,12},{12,8},{9,1... | collective-permute-start | bytes 393224 | tf_op jit(solution)/shard_map/ppermute | solution.py:208
  58.7 1.3 collective-permute-done.3
  60.0 3.6 %collective-permute-start.4 = (bf16[512,256]{1,0:T(8,128)(2,1)S(1)}, bf16[512,256]{1,0:T(8,128)(2,1)S(1)}, u32[]{:S(2)}, u32[]{:S(2)}) collective-permute-start(bf16[512,256]{1,0:T(8,128)(2,1)S(1)} %pad_maximum_fusion.w0_ref), channel_id=1, source_target_pairs={{0,1},{1,2},{2,3},{3,0},{4,5},{5,6},{6,7},{7,4},{8,9},{9,10},{10,1... | collective-permute-start | bytes 786440 | tf_op jit(solution)/shard_map/ppermute | solution.py:49
  63.7 4.8 %collective-permute-start.5 = (bf16[512,256]{1,0:T(8,128)(2,1)S(1)}, bf16[512,256]{1,0:T(8,128)(2,1)S(1)}, u32[]{:S(2)}, u32[]{:S(2)}) collective-permute-start(bf16[512,256]{1,0:T(8,128)(2,1)S(1)} %pad_maximum_fusion.w0_ref), channel_id=1, source_target_pairs={{0,2},{1,3},{2,0},{3,1},{4,6},{5,7},{6,4},{7,5},{8,10},{9,11},{10,... | collective-permute-start | bytes 786440 | tf_op jit(solution)/shard_map/ppermute | solution.py:49
  68.5 3.3 %collective-permute-start.6 = (bf16[512,256]{1,0:T(8,128)(2,1)S(1)}, bf16[512,256]{1,0:T(8,128)(2,1)S(1)}, u32[]{:S(2)}, u32[]{:S(2)}) collective-permute-start(bf16[512,256]{1,0:T(8,128)(2,1)S(1)} %pad_maximum_fusion.w0_ref), channel_id=1, source_target_pairs={{0,3},{1,0},{2,1},{3,2},{4,7},{5,4},{6,5},{7,6},{8,11},{9,8},{10,9... | collective-permute-start | bytes 786440 | tf_op jit(solution)/shard_map/ppermute | solution.py:49
  71.8 0.7 all-to-all-done.1
  72.5 0.5 convolution_convert_fusion.5
  73.0 0.5 convolution_convert_fusion.4
  73.5 1.9 %collective-permute-start.7 = (bf16[256,512]{1,0:T(8,128)(2,1)S(1)}, bf16[256,512]{1,0:T(8,128)(2,1)S(1)}, u32[]{:S(2)}, u32[]{:S(2)}) collective-permute-start(bf16[256,512]{1,0:T(8,128)(2,1)S(1)} %pad_maximum_fusion.1.gown_ref), channel_id=1, source_target_pairs={{0,4},{4,0},{1,5},{5,1},{2,6},{6,2},{3,7},{7,3},{8,12},{12,8},{9,1... | collective-permute-start | bytes 786440 | tf_op jit(solution)/shard_map/ppermute | solution.py:223
  75.6 0.6 convolution_convert_fusion.x_ref
  76.1 2.4 %collective-permute-done.5.w2_ref = bf16[512,256]{1,0:T(8,128)(2,1)S(1)} collective-permute-done((bf16[512,256]{1,0:T(8,128)(2,1)S(1)}, bf16[512,256]{1,0:T(8,128)(2,1)S(1)}, u32[]{:S(2)}, u32[]{:S(2)}) %collective-permute-start.5) | collective-permute-done | bytes 262176 | tf_op jit(solution)/shard_map/ppermute | solution.py:49
  78.5 1.3 collective-permute-done.6.w3_ref
  79.8 7.3 %shard_map.85 = (f32[256,512]{1,0:T(8,128)S(1)}, bf16[256,512]{1,0:T(8,128)(2,1)S(1)}, bf16[256,1024]{1,0:T(8,128)(2,1)S(1)}, bf16[256,1024]{1,0:T(8,128)(2,1)S(1)}) custom-call(s32[2]{0:T(128)S(1)} %pad_add_fusion.place_ref, bf16[512,512]{1,0:T(8,128)(2,1)S(1)} %convolution_convert_fusion.x_ref, bf16[512,256]{1,0:T(8,128)(2,1)S(1)} %pad_maximum_fusion.w0_ref, ...), custom_call_target="tpu_custom_call" | custom-call | tf_op jit(solution)/shard_map/pallas_call | solution.py:134
  87.1 2.1 %collective-permute-start.8 = (bf16[256,1024]{1,0:T(8,128)(2,1)S(1)}, bf16[256,1024]{1,0:T(8,128)(2,1)S(1)}, u32[]{:S(2)}, u32[]{:S(2)}) collective-permute-start(bf16[256,1024]{1,0:T(8,128)(2,1)S(1)} %get-tuple-element.14), channel_id=1, source_target_pairs={{0,4},{4,0},{1,5},{5,1},{2,6},{6,2},{3,7},{7,3},{8,12},{12,8},{9,1... | collective-permute-start | bytes 1572872 | tf_op jit(solution)/shard_map/ppermute | solution.py:232
  89.3 2.4 %collective-permute-start.13 = (bf16[256,512]{1,0:T(8,128)(2,1)S(1)}, bf16[256,512]{1,0:T(8,128)(2,1)S(1)}, u32[]{:S(2)}, u32[]{:S(2)}) collective-permute-start(bf16[256,512]{1,0:T(8,128)(2,1)S(1)} %get-tuple-element.16), channel_id=1, source_target_pairs={{0,4},{4,0},{1,5},{5,1},{2,6},{6,2},{3,7},{7,3},{8,12},{12,8},{9,1... | collective-permute-start | bytes 786440 | tf_op jit(solution)/shard_map/ppermute | solution.py:227
  92.1 2.4 %collective-permute-start.9 = (bf16[128,2048]{1,0:T(8,128)(2,1)S(1)}, bf16[128,2048]{1,0:T(8,128)(2,1)S(1)}, u32[]{:S(2)}, u32[]{:S(2)}) collective-permute-start(bf16[128,2048]{1,0:T(8,128)(2,1)S(1)} %bitcast.59), channel_id=1, source_target_pairs={{0,128},{128,0},{256,384},{384,256},{1,129},{129,1},{257,385},{385... | collective-permute-start | bytes 1572872 | tf_op jit(solution)/shard_map/ppermute | solution.py:54
  94.9 1.1 fusion.2
  96.0 16.9 %all-to-all-start.2 = ((bf16[128,8,256]{2,1,0:T(8,128)(2,1)}), bf16[128,8,256]{2,1,0:T(8,128)(2,1)S(1)}, u32[]{:S(2)}, u32[]{:S(2)}) async-start(bf16[128,8,256]{2,1,0:T(8,128)(2,1)} %fusion.2), calls=%async_computation.2 | async-start | bytes 1048576 | tf_op jit(solution)/shard_map/all_to_all | solution.py:44
  113.2 2.9 %collective-permute-start.10 = (bf16[64,2048]{1,0:T(8,128)(2,1)S(1)}, bf16[64,2048]{1,0:T(8,128)(2,1)S(1)}, u32[]{:S(2)}, u32[]{:S(2)}) collective-permute-start(bf16[64,2048]{1,0:T(8,128)(2,1)S(1)} %select_bitcast_fusion), channel_id=1, source_target_pairs={{0,256},{128,384},{256,0},{384,128},{1,257},{129,385},{257,1},{385... | collective-permute-start | bytes 786440 | tf_op jit(solution)/shard_map/ppermute | solution.py:54
  116.1 10.6 %collective-permute-done.10 = bf16[64,2048]{1,0:T(8,128)(2,1)S(1)} collective-permute-done((bf16[64,2048]{1,0:T(8,128)(2,1)S(1)}, bf16[64,2048]{1,0:T(8,128)(2,1)S(1)}, u32[]{:S(2)}, u32[]{:S(2)}) %collective-permute-start.10) | collective-permute-done | bytes 262176 | tf_op jit(solution)/shard_map/ppermute | solution.py:54
  126.9 4.4 %collective-permute-start.11 = (bf16[64,1024]{1,0:T(8,128)(2,1)S(1)}, bf16[64,1024]{1,0:T(8,128)(2,1)S(1)}, u32[]{:S(2)}, u32[]{:S(2)}) collective-permute-start(bf16[64,1024]{1,0:T(8,128)(2,1)S(1)} %broadcast_select_fusion.6), channel_id=1, source_target_pairs={{0,1},{1,0},{2,3},{3,2},{4,5},{5,4},{6,7},{7,6},{8,9},{9,8},{10,11... | collective-permute-start | bytes 393224 | tf_op jit(solution)/shard_map/ppermute | solution.py:54
  131.3 2.9 %collective-permute-done.11 = bf16[64,1024]{1,0:T(8,128)(2,1)S(1)} collective-permute-done((bf16[64,1024]{1,0:T(8,128)(2,1)S(1)}, bf16[64,1024]{1,0:T(8,128)(2,1)S(1)}, u32[]{:S(2)}, u32[]{:S(2)}) %collective-permute-start.11) | collective-permute-done | bytes 131104 | tf_op jit(solution)/shard_map/ppermute | solution.py:54
  134.3 4.6 %collective-permute-start.12 = (bf16[64,512]{1,0:T(8,128)(2,1)S(1)}, bf16[64,512]{1,0:T(8,128)(2,1)S(1)}, u32[]{:S(2)}, u32[]{:S(2)}) collective-permute-start(bf16[64,512]{1,0:T(8,128)(2,1)S(1)} %broadcast_select_fusion.7), channel_id=1, source_target_pairs={{0,2},{1,3},{2,0},{3,1},{4,6},{5,7},{6,4},{7,5},{8,10},{9,11},{10,... | collective-permute-start | bytes 196616 | tf_op jit(solution)/shard_map/ppermute | solution.py:54
  138.9 3.1 %collective-permute-done.12 = bf16[64,512]{1,0:T(8,128)(2,1)S(1)} collective-permute-done((bf16[64,512]{1,0:T(8,128)(2,1)S(1)}, bf16[64,512]{1,0:T(8,128)(2,1)S(1)}, u32[]{:S(2)}, u32[]{:S(2)}) %collective-permute-start.12) | collective-permute-done | bytes 65568 | tf_op jit(solution)/shard_map/ppermute | solution.py:54
  142.0 3.1 %all-to-all-done.2 = bf16[128,8,256]{2,1,0:T(8,128)(2,1)S(1)} async-done(((bf16[128,8,256]{2,1,0:T(8,128)(2,1)}), bf16[128,8,256]{2,1,0:T(8,128)(2,1)S(1)}, u32[]{:S(2)}, u32[]{:S(2)}) %all-to-all-start.2) | async-done | bytes 524320 | tf_op jit(solution)/shard_map/all_to_all | solution.py:44
  145.1 0.6 reshape.502
  145.7 8.7 %all-to-all-start.3 = ((bf16[16,4,512]{2,1,0:T(4,128)(2,1)}), bf16[16,4,512]{2,1,0:T(4,128)(2,1)S(1)}, u32[]{:S(2)}, u32[]{:S(2)}) async-start(bf16[16,4,512]{2,1,0:T(4,128)(2,1)} %reshape.502), calls=%async_computation.3 | async-start | bytes 131072 | tf_op jit(solution)/shard_map/all_to_all | solution.py:44
  155.3 12.0 %all-to-all-done.3 = bf16[16,4,512]{2,1,0:T(4,128)(2,1)S(1)} async-done(((bf16[16,4,512]{2,1,0:T(4,128)(2,1)}), bf16[16,4,512]{2,1,0:T(4,128)(2,1)S(1)}, u32[]{:S(2)}, u32[]{:S(2)}) %all-to-all-start.3) | async-done | bytes 65568 | tf_op jit(solution)/shard_map/all_to_all | solution.py:44
  167.3 0.6 broadcast_in_dim.8
  167.9 3.9 %all-to-all-start.4 = ((f32[4,4,512]{2,1,0:T(4,128)}), f32[4,4,512]{2,1,0:T(4,128)S(1)}, u32[]{:S(2)}, u32[]{:S(2)}) async-start(f32[4,4,512]{2,1,0:T(4,128)} %broadcast_in_dim.8), calls=%async_computation.4 | async-start | bytes 65536 | tf_op jit(solution)/shard_map/all_to_all | solution.py:44
  171.8 1.2 fusion.3
  173.0 4.3 %all-to-all-done.4 = f32[4,4,512]{2,1,0:T(4,128)S(1)} async-done(((f32[4,4,512]{2,1,0:T(4,128)}), f32[4,4,512]{2,1,0:T(4,128)S(1)}, u32[]{:S(2)}, u32[]{:S(2)}) %all-to-all-start.4) | async-done | bytes 32800 | tf_op jit(solution)/shard_map/all_to_all | solution.py:44
  177.3 0.6 slice_bitcast_fusion
  178.0 0.6 copy-done.4
  (68 shorter events, 3.8 us)
Async XLA Ops:
  0.6 21.6 %copy-start.1 = (s32[1,128]{1,0:T(1,128)S(1)}, s32[1,128]{1,0:T(1,128)}, u32[]{:S(2)}) copy-start(s32[1,128]{1,0:T(1,128)} %param.11) | copy-start | bytes 1540
  0.6 21.8 %copy-start = (bf16[1,256,512]{2,1,0:T(8,128)(2,1)S(1)}, bf16[1,256,512]{2,1,0:T(8,128)(2,1)}, u32[]{:S(2)}) copy-start(bf16[1,256,512]{2,1,0:T(8,128)(2,1)} %param.7) | copy-start | bytes 786436
  2.1 27.9 %all-to-all-start = ((bf16[16,8,256]{2,1,0:T(8,128)(2,1)}), bf16[16,8,256]{2,1,0:T(8,128)(2,1)S(1)}, u32[]{:S(2)}, u32[]{:S(2)}) async-start(bf16[16,8,256]{2,1,0:T(8,128)(2,1)} %broadcast_in_dim.6), calls=%async_computation | async-start | bytes 131072 | tf_op jit(solution)/shard_map/all_to_all | solution.py:44
  17.3 58.3 %collective-permute-start = (bf16[256,512]{1,0:T(8,128)(2,1)}, bf16[256,512]{1,0:T(8,128)(2,1)S(1)}, u32[]{:S(2)}, u32[]{:S(2)}) collective-permute-start(bf16[256,512]{1,0:T(8,128)(2,1)} %bitcast.65), channel_id=1, source_target_pairs={{0,4},{4,0},{1,5},{5,1},{2,6},{6,2},{3,7},{7,3},{8,12},{12,8},{9,1... | collective-permute-start | bytes 786440 | tf_op jit(solution)/shard_map/ppermute | solution.py:220
  30.0 42.5 %all-to-all-start.1 = ((bf16[128,8,256]{2,1,0:T(8,128)(2,1)}), bf16[128,8,256]{2,1,0:T(8,128)(2,1)S(1)}, u32[]{:S(2)}, u32[]{:S(2)}) async-start(bf16[128,8,256]{2,1,0:T(8,128)(2,1)} %bitcast.9), calls=%async_computation.1 | async-start | bytes 1048576 | tf_op jit(solution)/shard_map/all_to_all | solution.py:44
  40.8 8.0 %collective-permute-start.1 = (bf16[128,256]{1,0:T(8,128)(2,1)S(1)}, bf16[128,256]{1,0:T(8,128)(2,1)S(1)}, u32[]{:S(2)}, u32[]{:S(2)}) collective-permute-start(bf16[128,256]{1,0:T(8,128)(2,1)S(1)} %bitcast.56), channel_id=1, source_target_pairs={{0,256},{128,384},{256,0},{384,128},{1,257},{129,385},{257,1},{385... | collective-permute-start | bytes 196616 | tf_op jit(solution)/shard_map/ppermute | solution.py:54
  48.8 7.4 %collective-permute-start.2 = (bf16[256,256]{1,0:T(8,128)(2,1)S(1)}, bf16[256,256]{1,0:T(8,128)(2,1)S(1)}, u32[]{:S(2)}, u32[]{:S(2)}) collective-permute-start(bf16[256,256]{1,0:T(8,128)(2,1)S(1)} %pad_maximum_fusion.2), channel_id=1, source_target_pairs={{0,128},{128,0},{256,384},{384,256},{1,129},{129,1},{257,385},{385... | collective-permute-start | bytes 393224 | tf_op jit(solution)/shard_map/ppermute | solution.py:54
  56.8 3.2 %collective-permute-start.3 = (bf16[256,256]{1,0:T(8,128)(2,1)S(1)}, bf16[256,256]{1,0:T(8,128)(2,1)S(1)}, u32[]{:S(2)}, u32[]{:S(2)}) collective-permute-start(bf16[256,256]{1,0:T(8,128)(2,1)S(1)} %get-tuple-element.28), channel_id=1, source_target_pairs={{0,4},{4,0},{1,5},{5,1},{2,6},{6,2},{3,7},{7,3},{8,12},{12,8},{9,1... | collective-permute-start | bytes 393224 | tf_op jit(solution)/shard_map/ppermute | solution.py:208
  58.7 16.8 %copy-start.2 = (s32[512]{0:T(512)}, s32[512]{0:T(512)S(1)}, u32[]{:S(2)}) copy-start(s32[512]{0:T(512)S(1)} %fusion.42) | copy-start | bytes 6148
  60.0 15.5 %copy-start.5 = (bf16[1,256,512]{2,1,0:T(8,128)(2,1)S(1)}, bf16[1,256,512]{2,1,0:T(8,128)(2,1)}, u32[]{:S(2)}) copy-start(bf16[1,256,512]{2,1,0:T(8,128)(2,1)} %param.6) | copy-start | bytes 786436
  60.0 16.1 %collective-permute-start.4 = (bf16[512,256]{1,0:T(8,128)(2,1)S(1)}, bf16[512,256]{1,0:T(8,128)(2,1)S(1)}, u32[]{:S(2)}, u32[]{:S(2)}) collective-permute-start(bf16[512,256]{1,0:T(8,128)(2,1)S(1)} %pad_maximum_fusion.w0_ref), channel_id=1, source_target_pairs={{0,1},{1,2},{2,3},{3,0},{4,5},{5,6},{6,7},{7,4},{8,9},{9,10},{10,1... | collective-permute-start | bytes 786440 | tf_op jit(solution)/shard_map/ppermute | solution.py:49
  63.7 14.8 %collective-permute-start.5 = (bf16[512,256]{1,0:T(8,128)(2,1)S(1)}, bf16[512,256]{1,0:T(8,128)(2,1)S(1)}, u32[]{:S(2)}, u32[]{:S(2)}) collective-permute-start(bf16[512,256]{1,0:T(8,128)(2,1)S(1)} %pad_maximum_fusion.w0_ref), channel_id=1, source_target_pairs={{0,2},{1,3},{2,0},{3,1},{4,6},{5,7},{6,4},{7,5},{8,10},{9,11},{10,... | collective-permute-start | bytes 786440 | tf_op jit(solution)/shard_map/ppermute | solution.py:49
  68.5 11.3 %collective-permute-start.6 = (bf16[512,256]{1,0:T(8,128)(2,1)S(1)}, bf16[512,256]{1,0:T(8,128)(2,1)S(1)}, u32[]{:S(2)}, u32[]{:S(2)}) collective-permute-start(bf16[512,256]{1,0:T(8,128)(2,1)S(1)} %pad_maximum_fusion.w0_ref), channel_id=1, source_target_pairs={{0,3},{1,0},{2,1},{3,2},{4,7},{5,4},{6,5},{7,6},{8,11},{9,8},{10,9... | collective-permute-start | bytes 786440 | tf_op jit(solution)/shard_map/ppermute | solution.py:49
  73.5 6.3 %collective-permute-start.7 = (bf16[256,512]{1,0:T(8,128)(2,1)S(1)}, bf16[256,512]{1,0:T(8,128)(2,1)S(1)}, u32[]{:S(2)}, u32[]{:S(2)}) collective-permute-start(bf16[256,512]{1,0:T(8,128)(2,1)S(1)} %pad_maximum_fusion.1.gown_ref), channel_id=1, source_target_pairs={{0,4},{4,0},{1,5},{5,1},{2,6},{6,2},{3,7},{7,3},{8,12},{12,8},{9,1... | collective-permute-start | bytes 786440 | tf_op jit(solution)/shard_map/ppermute | solution.py:223
  87.1 4.6 %collective-permute-start.8 = (bf16[256,1024]{1,0:T(8,128)(2,1)S(1)}, bf16[256,1024]{1,0:T(8,128)(2,1)S(1)}, u32[]{:S(2)}, u32[]{:S(2)}) collective-permute-start(bf16[256,1024]{1,0:T(8,128)(2,1)S(1)} %get-tuple-element.14), channel_id=1, source_target_pairs={{0,4},{4,0},{1,5},{5,1},{2,6},{6,2},{3,7},{7,3},{8,12},{12,8},{9,1... | collective-permute-start | bytes 1572872 | tf_op jit(solution)/shard_map/ppermute | solution.py:232
  89.3 5.2 %collective-permute-start.13 = (bf16[256,512]{1,0:T(8,128)(2,1)S(1)}, bf16[256,512]{1,0:T(8,128)(2,1)S(1)}, u32[]{:S(2)}, u32[]{:S(2)}) collective-permute-start(bf16[256,512]{1,0:T(8,128)(2,1)S(1)} %get-tuple-element.16), channel_id=1, source_target_pairs={{0,4},{4,0},{1,5},{5,1},{2,6},{6,2},{3,7},{7,3},{8,12},{12,8},{9,1... | collective-permute-start | bytes 786440 | tf_op jit(solution)/shard_map/ppermute | solution.py:227
  92.1 20.9 %collective-permute-start.9 = (bf16[128,2048]{1,0:T(8,128)(2,1)S(1)}, bf16[128,2048]{1,0:T(8,128)(2,1)S(1)}, u32[]{:S(2)}, u32[]{:S(2)}) collective-permute-start(bf16[128,2048]{1,0:T(8,128)(2,1)S(1)} %bitcast.59), channel_id=1, source_target_pairs={{0,128},{128,0},{256,384},{384,256},{1,129},{129,1},{257,385},{385... | collective-permute-start | bytes 1572872 | tf_op jit(solution)/shard_map/ppermute | solution.py:54
  96.0 49.0 %all-to-all-start.2 = ((bf16[128,8,256]{2,1,0:T(8,128)(2,1)}), bf16[128,8,256]{2,1,0:T(8,128)(2,1)S(1)}, u32[]{:S(2)}, u32[]{:S(2)}) async-start(bf16[128,8,256]{2,1,0:T(8,128)(2,1)} %fusion.2), calls=%async_computation.2 | async-start | bytes 1048576 | tf_op jit(solution)/shard_map/all_to_all | solution.py:44
  113.2 13.6 %collective-permute-start.10 = (bf16[64,2048]{1,0:T(8,128)(2,1)S(1)}, bf16[64,2048]{1,0:T(8,128)(2,1)S(1)}, u32[]{:S(2)}, u32[]{:S(2)}) collective-permute-start(bf16[64,2048]{1,0:T(8,128)(2,1)S(1)} %select_bitcast_fusion), channel_id=1, source_target_pairs={{0,256},{128,384},{256,0},{384,128},{1,257},{129,385},{257,1},{385... | collective-permute-start | bytes 786440 | tf_op jit(solution)/shard_map/ppermute | solution.py:54
  126.9 7.4 %collective-permute-start.11 = (bf16[64,1024]{1,0:T(8,128)(2,1)S(1)}, bf16[64,1024]{1,0:T(8,128)(2,1)S(1)}, u32[]{:S(2)}, u32[]{:S(2)}) collective-permute-start(bf16[64,1024]{1,0:T(8,128)(2,1)S(1)} %broadcast_select_fusion.6), channel_id=1, source_target_pairs={{0,1},{1,0},{2,3},{3,2},{4,5},{5,4},{6,7},{7,6},{8,9},{9,8},{10,11... | collective-permute-start | bytes 393224 | tf_op jit(solution)/shard_map/ppermute | solution.py:54
  134.3 7.7 %collective-permute-start.12 = (bf16[64,512]{1,0:T(8,128)(2,1)S(1)}, bf16[64,512]{1,0:T(8,128)(2,1)S(1)}, u32[]{:S(2)}, u32[]{:S(2)}) collective-permute-start(bf16[64,512]{1,0:T(8,128)(2,1)S(1)} %broadcast_select_fusion.7), channel_id=1, source_target_pairs={{0,2},{1,3},{2,0},{3,1},{4,6},{5,7},{6,4},{7,5},{8,10},{9,11},{10,... | collective-permute-start | bytes 196616 | tf_op jit(solution)/shard_map/ppermute | solution.py:54
  145.7 21.6 %all-to-all-start.3 = ((bf16[16,4,512]{2,1,0:T(4,128)(2,1)}), bf16[16,4,512]{2,1,0:T(4,128)(2,1)S(1)}, u32[]{:S(2)}, u32[]{:S(2)}) async-start(bf16[16,4,512]{2,1,0:T(4,128)(2,1)} %reshape.502), calls=%async_computation.3 | async-start | bytes 131072 | tf_op jit(solution)/shard_map/all_to_all | solution.py:44
  154.4 17.4 %copy-start.3 = (s32[512]{0:T(512)S(1)}, s32[512]{0:T(512)}, u32[]{:S(2)}) copy-start(s32[512]{0:T(512)} %copy-done.2) | copy-start | bytes 6148
  167.9 9.4 %all-to-all-start.4 = ((f32[4,4,512]{2,1,0:T(4,128)}), f32[4,4,512]{2,1,0:T(4,128)S(1)}, u32[]{:S(2)}, u32[]{:S(2)}) async-start(f32[4,4,512]{2,1,0:T(4,128)} %broadcast_in_dim.8), calls=%async_computation.4 | async-start | bytes 65536 | tf_op jit(solution)/shard_map/all_to_all | solution.py:44
  178.0 0.6 copy-start.4

commit v5 on v4

--- a/solution.py
+++ b/solution.py
@@ -91,7 +91,7 @@
 
 def patch_body(
     place_ref, x_ref, w0_ref, w1_ref, w2_ref, w3_ref, gown_ref, goth_ref, own_perm_ref,
-    pown_ref, poth_ref, keep_ref, send_ref, w_ref, tq_ref, tp_ref,
+    pown_ref, poth_ref, term_ref, w_ref,
 ):
     bf = jnp.bfloat16
     core, rep = place_ref[0], place_ref[1]
@@ -114,19 +114,24 @@
     qkv = mm(x, w_qkv, NN, bf)
     grad_attn = mm(grad_pair, w_proj, NT, bf)
     attn_t, grad_qkv = attend(qkv, grad_attn, own, channels // HEADS)
-    tq_ref[...] = mm(x, grad_qkv, TN, bf).reshape(CORES, own, 3 * own)
-    proj_term = mm(attn_t, grad_pair, NN, bf)
-    tp_ref[...] = mm(own_perm, proj_term, TN, bf).reshape(CORES, part, channels)
-    for out_ref, side in ((keep_ref, core), (send_ref, 1 - core)):
-        out_ref[:, : 3 * own] = tq_ref[side]
-        out_ref[:part, 3 * own :] = tp_ref[side, :, :own]
-        out_ref[part:, 3 * own :] = tp_ref[side, :, own:]
+    qkv_term = mm(x, grad_qkv, TN, bf)
+    proj_term = mm(own_perm, mm(attn_t, grad_pair, NN, bf), TN, bf)
+    nx = term_ref.shape[0]
+    tall = own // nx
+    for c in range(CORES):
+        for there in range(nx):
+            lo = c * own + there * tall
+            for p in range(3):
+                term_ref[there, c, p] = qkv_term[lo : lo + tall, p * own : (p + 1) * own]
+            lo = c * part + there % (nx // CORES) * tall
+            block = proj_term[lo : lo + tall]
+            term_ref[there, c, 3] = jnp.where(core == there // (nx // CORES), block[:, :own], block[:, own:])
     partial = mm(grad_qkv, w_qkv, NT)
     pown_ref[...] = partial[:rows]
     poth_ref[...] = partial[rows:].astype(bf)
 
 
-def patch_step(place, x, weights, gown, goth, own_perm):
+def patch_step(place, x, weights, gown, goth, own_perm, nx):
     bf = jnp.bfloat16
     rows, channels = gown.shape
     own = channels // CORES
@@ -136,15 +141,12 @@
         out_shape=[
             jax.ShapeDtypeStruct((rows, channels), jnp.float32),
             jax.ShapeDtypeStruct((rows, channels), bf),
-            jax.ShapeDtypeStruct((own, 4 * own), bf),
-            jax.ShapeDtypeStruct((own, 4 * own), bf),
+            jax.ShapeDtypeStruct((nx, CORES, 4, own // nx, own), bf),
         ],
         in_specs=[pl.BlockSpec(memory_space=pltpu.SMEM)] + [vmem] * 8,
-        out_specs=[vmem] * 4,
+        out_specs=[vmem] * 3,
         scratch_shapes=[
             pltpu.VMEM((4, CORES, own, own), bf),
-            pltpu.VMEM((CORES, own, 3 * own), bf),
-            pltpu.VMEM((CORES, own // CORES, channels), bf),
         ],
         compiler_params=pltpu.CompilerParams(vmem_limit_bytes=48 << 20),
         interpret=INTERPRET,
@@ -222,46 +224,40 @@
     grad_hil = jnp.concatenate([mm(recv[h], arrived, TN, bf) for h in range(2)], axis=1)
     other_grad = lax.ppermute(grad_hil, "core", pair)
     place = jnp.stack([core, rep])
-    p_own, p_other, keep, away = patch_step(place, x_pair, weights, grad_hil, other_grad, own_perm)
+    p_own, p_other, term = patch_step(place, x_pair, weights, grad_hil, other_grad, own_perm, nx)
+
+    near = swap(term.reshape(nx * nc * nr, own // nx, own), ("x", "core", "rep"))
+    near = jnp.sum(near.reshape(nx, nc, nr, nz, share, own).astype(f32), axis=(0, 2)).astype(bf)
+    total = jnp.swapaxes(near, 0, 1).reshape(nz, nc * share, own)
 
     from_other = lax.ppermute(p_other, "core", pair)
     grad_hfeat = (p_own + from_other.astype(f32)).astype(bf)
     going = (mm(recv[0], grad_hfeat[:, :half], NN) + mm(recv[1], grad_hfeat[:, half:], NN)).astype(bf)
-    returned = swap(going.reshape(peers, chunk, half), ROWS).reshape(peers * chunk, half)
-
-    got = lax.ppermute(away, "core", pair)
-    proj = [jnp.concatenate([m[:part, 3 * own :], m[part:, 3 * own :]], axis=1) for m in (keep, got)]
-    proj = jnp.concatenate([jnp.where(core == 0, proj[0], proj[1]), jnp.where(core == 0, proj[1], proj[0])], axis=0)
-    total = jnp.concatenate([keep[:, : 3 * own], got[:, : 3 * own], proj], axis=1)
-
-    def halve(value, axis, here, bit, first, second):
-        mine_set = here // bit % 2 == 1
-        stay = jnp.where(mine_set, second, first)
-        come = flip(jnp.where(mine_set, first, second), axis, bit)
-        return (stay.astype(f32) + come.astype(f32)).astype(bf)
-
-    for bit in bits:
-        count = nx // bit
-        blocks = total.reshape(count // 2, 2, nz * share, total.shape[1])
-        flat = (count // 2 * nz * share, total.shape[1])
-        total = halve(total, "x", x_here, bit, blocks[:, 0].reshape(flat), blocks[:, 1].reshape(flat))
-    for bit in (1, 2):
-        wide = total.shape[1] // 2
-        total = halve(total, "rep", rep, bit, total[:, :wide], total[:, wide:])
-    total, returned = lax.optimization_barrier((total, returned))
-    wide = total.shape[1]
-    far = swap(total.reshape(nz, share, wide), ("zh", "zl"))
-    summed = jnp.sum(far.astype(f32), axis=0)
-    last = swap(jnp.broadcast_to(summed[None], (nr, share, wide)), "rep")
-    last = jnp.concatenate([last[r] for r in (0, 2, 1, 3)], axis=1)
+    total, going = lax.optimization_barrier((total, going))
+    returned = swap(going.reshape(peers, chunk, half), ROWS)
+
+    for axis, here in (("zl", lax.axis_index("zl")), ("zh", lax.axis_index("zh"))):
+        size = lax.axis_size(axis)
+        bit = 1
+        while bit < size:
+            blocks = total.reshape(total.shape[0] // 2, 2, nc * share, own)
+            odd = here // bit % 2 == 1
+            stay = jnp.where(odd, blocks[:, 1], blocks[:, 0])
+            come = flip(jnp.where(odd, blocks[:, 0], blocks[:, 1]), axis, bit)
+            total = stay.astype(f32) + come.astype(f32)
+            total = total if total.shape[0] == 1 else total.astype(bf)
+            bit *= 2
+    total, returned = lax.optimization_barrier((total[0], returned))
+    returned = returned.reshape(peers * chunk, half)
+    last = swap(jnp.broadcast_to(total[None], (nx * nr, nc * share, own)), ("x", "rep"))
+    last = last.reshape(nx, nr, nc, share, own)
+    here = lax.dynamic_index_in_dim(last, x_here, 0, keepdims=False)
+    partner = lax.dynamic_index_in_dim(last, (x_here + nx // 2) % nx, 0, keepdims=False)
+    cols = [here[p, c] for p in range(3) for c in range(nc)]
+    proj_cols = [lax.dynamic_index_in_dim(m[3], x_here // (nx // nc), 0, keepdims=False) for m in (here, partner)]
     grad_perm = jnp.concatenate([mm(send[h], returned, TN, bf) for h in range(2)], axis=1)
     grad_z = mm(grad_perm, perm, NT, bf)
-    lower = jnp.where(core == 0, last[:, : 3 * own], last[:, 3 * own : 6 * own])
-    upper = jnp.where(core == 0, last[:, 3 * own : 6 * own], last[:, : 3 * own])
-    cols = []
-    for p in range(3):
-        cols += [lower[:, p * own : (p + 1) * own], upper[:, p * own : (p + 1) * own]]
-    return (grad_z[None], jnp.concatenate(cols, axis=1), last[:, 6 * own :])
+    return (grad_z[None], jnp.concatenate(cols, axis=1), jnp.concatenate(proj_cols, axis=1))
 
 
 def solution(mesh):

time: 179 us -> 199 us (1.11)
  waiting for transfers between devices: 58.1 us -> 69.6 us
  starting transfers between devices: 96.7 us -> 105 us
    ppermute x6, waiting for transfers between devices: 26.6 us -> 38.4 us  [flip(): lax.ppermute(block, axis, [(here, here ^ bit) for here in range(count)])]
    ppermute x6, starting transfers between devices: 19.7 us -> 30.9 us  [flip(): lax.ppermute(block, axis, [(here, here ^ bit) for here in range(count)])]
    ppermute x1 -> x0, starting transfers between devices: 2.1 us -> none  [per_device(): got = lax.ppermute(away, 'core', pair)]
  transfers between devices with their start and end apart: 19 -> 18, of which waited for: 13 -> 13; matrix products, arithmetic and copies ran while one was open for 6% -> 4% of each run, Pallas kernels for 0% -> 0%
where the time goes in v5:
time: 199 us; the launch traced here: 197 us
  starting transfers between devices  105 us (53%)
  waiting for transfers between devices  69.6 us (35%)
  Pallas kernels  7.86 us (4%)
  matrix products  7.07 us (4%)
  other arithmetic  3.43 us (2%)
  local copies, waits for them, and re-layouts  3.37 us (2%)
    all_to_all x5, starting transfers between devices, swap(): return lax.all_to_all(block, axis, split_axis=0, concat_axis=0, tiled=True)  54.4 us
    ppermute x6, waiting for transfers between devices, flip(): lax.ppermute(block, axis, [(here, here ^ bit) for here in range(count)])  38.4 us
    ppermute x6, starting transfers between devices, flip(): lax.ppermute(block, axis, [(here, here ^ bit) for here in range(count)])  30.9 us
    all_to_all x5, waiting for transfers between devices, swap(): return lax.all_to_all(block, axis, split_axis=0, concat_axis=0, tiled=True)  25.8 us
    ppermute x3, starting transfers between devices, shift(): lax.ppermute(block, axis, [(here, (here + step) % count) for here in rang...  11.5 us
    pallas_call x1, Pallas kernels, patch_step(): pl.pallas_call(patch_body, out_shape=[jax.ShapeDtypeStruct((rows, channel...  7.86 us
    dot_general x12, matrix products, mm(): lax.dot_general(left, right, (dims, ((), ())), preferred_element_type=jnp...  7.07 us
    ppermute x3, waiting for transfers between devices, shift(): lax.ppermute(block, axis, [(here, (here + step) % count) for here in rang...  4.1 us
  transfers between devices with their start and end apart: 18, of which 13 were waited for; matrix products, arithmetic and copies ran while one was open for 4% of the time, Pallas kernels for 0%

profile of v5, /device:TPU:6, one launch (start us, length us, event | category | flops | bytes accessed | tf_op | source)
XLA Modules:
  0.0 197.2 jit_solution(3486442408626071441)
XLA Ops:
  0.7 0.7 copy-done.1
  1.4 0.6 broadcast_in_dim.6
  2.0 15.2 %all-to-all-start = ((bf16[16,8,256]{2,1,0:T(8,128)(2,1)}), bf16[16,8,256]{2,1,0:T(8,128)(2,1)S(1)}, u32[]{:S(2)}, u32[]{:S(2)}) async-start(bf16[16,8,256]{2,1,0:T(8,128)(2,1)} %broadcast_in_dim.6), calls=%async_computation | async-start | bytes 131072 | tf_op jit(solution)/shard_map/all_to_all | solution.py:44
  17.2 1.9 collective-permute-start
  19.2 0.7 and_select_fusion.5
  19.8 0.7 fusion.80
  21.3 0.6 copy-done.2
  22.1 1.1 fusion
  23.3 6.7 %all-to-all-done = bf16[16,8,256]{2,1,0:T(8,128)(2,1)S(1)} async-done(((bf16[16,8,256]{2,1,0:T(8,128)(2,1)}), bf16[16,8,256]{2,1,0:T(8,128)(2,1)S(1)}, u32[]{:S(2)}, u32[]{:S(2)}) %all-to-all-start) | async-done | bytes 65568 | tf_op jit(solution)/shard_map/all_to_all | solution.py:44
  30.0 10.1 %all-to-all-start.1 = ((bf16[128,8,256]{2,1,0:T(8,128)(2,1)}), bf16[128,8,256]{2,1,0:T(8,128)(2,1)S(1)}, u32[]{:S(2)}, u32[]{:S(2)}) async-start(bf16[128,8,256]{2,1,0:T(8,128)(2,1)} %bitcast.9), calls=%async_computation.1 | async-start | bytes 1048576 | tf_op jit(solution)/shard_map/all_to_all | solution.py:44
  40.5 2.9 %collective-permute-start.1 = (bf16[128,256]{1,0:T(8,128)(2,1)S(1)}, bf16[128,256]{1,0:T(8,128)(2,1)S(1)}, u32[]{:S(2)}, u32[]{:S(2)}) collective-permute-start(bf16[128,256]{1,0:T(8,128)(2,1)S(1)} %bitcast.145), channel_id=1, source_target_pairs={{0,256},{128,384},{256,0},{384,128},{1,257},{129,385},{257,1},{385... | collective-permute-start | bytes 196616 | tf_op jit(solution)/shard_map/ppermute | solution.py:54
  43.5 5.0 %collective-permute-done.1 = bf16[128,256]{1,0:T(8,128)(2,1)S(1)} collective-permute-done((bf16[128,256]{1,0:T(8,128)(2,1)S(1)}, bf16[128,256]{1,0:T(8,128)(2,1)S(1)}, u32[]{:S(2)}, u32[]{:S(2)}) %collective-permute-start.1) | collective-permute-done | bytes 65568 | tf_op jit(solution)/shard_map/ppermute | solution.py:54
  48.5 2.4 %collective-permute-start.2 = (bf16[256,256]{1,0:T(8,128)(2,1)S(1)}, bf16[256,256]{1,0:T(8,128)(2,1)S(1)}, u32[]{:S(2)}, u32[]{:S(2)}) collective-permute-start(bf16[256,256]{1,0:T(8,128)(2,1)S(1)} %pad_maximum_fusion.2), channel_id=1, source_target_pairs={{0,128},{128,0},{256,384},{384,256},{1,129},{129,1},{257,385},{385... | collective-permute-start | bytes 393224 | tf_op jit(solution)/shard_map/ppermute | solution.py:54
  51.0 5.0 %collective-permute-done.2 = bf16[256,256]{1,0:T(8,128)(2,1)S(1)} collective-permute-done((bf16[256,256]{1,0:T(8,128)(2,1)S(1)}, bf16[256,256]{1,0:T(8,128)(2,1)S(1)}, u32[]{:S(2)}, u32[]{:S(2)}) %collective-permute-start.2) | collective-permute-done | bytes 131104 | tf_op jit(solution)/shard_map/ppermute | solution.py:54
  56.5 1.9 collective-permute-start.3
  58.4 1.3 collective-permute-done.3
  59.8 3.5 %collective-permute-start.4 = (bf16[512,256]{1,0:T(8,128)(2,1)S(1)}, bf16[512,256]{1,0:T(8,128)(2,1)S(1)}, u32[]{:S(2)}, u32[]{:S(2)}) collective-permute-start(bf16[512,256]{1,0:T(8,128)(2,1)S(1)} %pad_maximum_fusion.w0_ref), channel_id=1, source_target_pairs={{0,1},{1,2},{2,3},{3,0},{4,5},{5,6},{6,7},{7,4},{8,9},{9,10},{10,1... | collective-permute-start | bytes 786440 | tf_op jit(solution)/shard_map/ppermute | solution.py:49
  63.2 5.5 %collective-permute-start.5 = (bf16[512,256]{1,0:T(8,128)(2,1)S(1)}, bf16[512,256]{1,0:T(8,128)(2,1)S(1)}, u32[]{:S(2)}, u32[]{:S(2)}) collective-permute-start(bf16[512,256]{1,0:T(8,128)(2,1)S(1)} %pad_maximum_fusion.w0_ref), channel_id=1, source_target_pairs={{0,2},{1,3},{2,0},{3,1},{4,6},{5,7},{6,4},{7,5},{8,10},{9,11},{10,... | collective-permute-start | bytes 786440 | tf_op jit(solution)/shard_map/ppermute | solution.py:49
  68.7 2.6 %collective-permute-start.6 = (bf16[512,256]{1,0:T(8,128)(2,1)S(1)}, bf16[512,256]{1,0:T(8,128)(2,1)S(1)}, u32[]{:S(2)}, u32[]{:S(2)}) collective-permute-start(bf16[512,256]{1,0:T(8,128)(2,1)S(1)} %pad_maximum_fusion.w0_ref), channel_id=1, source_target_pairs={{0,3},{1,0},{2,1},{3,2},{4,7},{5,4},{6,5},{7,6},{8,11},{9,8},{10,9... | collective-permute-start | bytes 786440 | tf_op jit(solution)/shard_map/ppermute | solution.py:49
  71.3 0.9 all-to-all-done.1
  72.2 0.5 convolution_convert_fusion.5
  72.7 0.5 convolution_convert_fusion.4
  73.3 2.1 %collective-permute-start.7 = (bf16[256,512]{1,0:T(8,128)(2,1)S(1)}, bf16[256,512]{1,0:T(8,128)(2,1)S(1)}, u32[]{:S(2)}, u32[]{:S(2)}) collective-permute-start(bf16[256,512]{1,0:T(8,128)(2,1)S(1)} %pad_maximum_fusion.1.gown_ref), channel_id=1, source_target_pairs={{0,4},{4,0},{1,5},{5,1},{2,6},{6,2},{3,7},{7,3},{8,12},{12,8},{9,1... | collective-permute-start | bytes 786440 | tf_op jit(solution)/shard_map/ppermute | solution.py:225
  75.4 0.6 convolution_convert_fusion.x_ref
  76.0 2.8 %collective-permute-done.5.w2_ref = bf16[512,256]{1,0:T(8,128)(2,1)S(1)} collective-permute-done((bf16[512,256]{1,0:T(8,128)(2,1)S(1)}, bf16[512,256]{1,0:T(8,128)(2,1)S(1)}, u32[]{:S(2)}, u32[]{:S(2)}) %collective-permute-start.5) | collective-permute-done | bytes 262176 | tf_op jit(solution)/shard_map/ppermute | solution.py:49
  78.8 1.3 collective-permute-done.6.w3_ref
  80.1 7.9 %shard_map.85 = (f32[256,512]{1,0:T(8,128)S(1)}, bf16[256,512]{1,0:T(8,128)(2,1)S(1)}, bf16[4,2,4,64,256]{4,3,2,1,0:T(8,128)(2,1)}) custom-call(s32[2]{0:T(128)S(1)} %pad_add_fusion.place_ref, bf16[512,512]{1,0:T(8,128)(2,1)S(1)} %convolution_convert_fusion.x_ref, bf16[512,256]{1,0:T(8,128)(2,1)S(1)} %pad_maximum_fusion.w0_ref, ...), custom_call_target="tpu_custom_call" | custom-call | tf_op jit(solution)/shard_map/pallas_call | solution.py:139
  88.0 1.9 collective-permute-start.8
  89.9 7.1 %all-to-all-start.2 = ((bf16[32,64,256]{2,1,0:T(8,128)(2,1)}), bf16[32,64,256]{2,1,0:T(8,128)(2,1)S(1)}, u32[]{:S(2)}, u32[]{:S(2)}) async-start(bf16[32,64,256]{2,1,0:T(8,128)(2,1)} %bitcast.11), calls=%async_computation.2 | async-start | bytes 2097152 | tf_op jit(solution)/shard_map/all_to_all | solution.py:44
  97.4 1.1 fusion.1
  98.5 13.5 %all-to-all-done.2 = bf16[32,64,256]{2,1,0:T(8,128)(2,1)S(1)} async-done(((bf16[32,64,256]{2,1,0:T(8,128)(2,1)}), bf16[32,64,256]{2,1,0:T(8,128)(2,1)S(1)}, u32[]{:S(2)}, u32[]{:S(2)}) %all-to-all-start.2) | async-done | bytes 1048608 | tf_op jit(solution)/shard_map/all_to_all | solution.py:44
  112.3 0.5 reduce_sum.32
  112.8 16.9 %all-to-all-start.3 = ((bf16[128,8,256]{2,1,0:T(8,128)(2,1)}), bf16[128,8,256]{2,1,0:T(8,128)(2,1)S(1)}, u32[]{:S(2)}, u32[]{:S(2)}) async-start(bf16[128,8,256]{2,1,0:T(8,128)(2,1)} %bitcast.36), calls=%async_computation.3 | async-start | bytes 1048576 | tf_op jit(solution)/shard_map/all_to_all | solution.py:44
  129.8 3.4 %collective-permute-start.9 = (bf16[8,8,256]{2,1,0:T(8,128)(2,1)S(1)}, bf16[8,8,256]{2,1,0:T(8,128)(2,1)S(1)}, u32[]{:S(2)}, u32[]{:S(2)}) collective-permute-start(bf16[8,8,256]{2,1,0:T(8,128)(2,1)S(1)} %fusion.34), channel_id=1, source_target_pairs={{0,8},{8,0},{16,24},{24,16},{1,9},{9,1},{17,25},{25,17},{2,10},{10... | collective-permute-start | bytes 98312 | tf_op jit(solution)/shard_map/ppermute | solution.py:54
  133.2 20.4 %collective-permute-done.9 = bf16[8,8,256]{2,1,0:T(8,128)(2,1)S(1)} collective-permute-done((bf16[8,8,256]{2,1,0:T(8,128)(2,1)S(1)}, bf16[8,8,256]{2,1,0:T(8,128)(2,1)S(1)}, u32[]{:S(2)}, u32[]{:S(2)}) %collective-permute-start.9) | collective-permute-done | bytes 32800 | tf_op jit(solution)/shard_map/ppermute | solution.py:54
  153.7 3.1 %collective-permute-start.10 = (bf16[4,8,256]{2,1,0:T(8,128)(2,1)S(1)}, bf16[4,8,256]{2,1,0:T(8,128)(2,1)S(1)}, u32[]{:S(2)}, u32[]{:S(2)}) collective-permute-start(bf16[4,8,256]{2,1,0:T(8,128)(2,1)S(1)} %fusion.37), channel_id=1, source_target_pairs={{0,16},{8,24},{16,0},{24,8},{1,17},{9,25},{17,1},{25,9},{2,18},{10... | collective-permute-start | bytes 49160 | tf_op jit(solution)/shard_map/ppermute | solution.py:54
  156.8 3.4 %collective-permute-done.10 = bf16[4,8,256]{2,1,0:T(8,128)(2,1)S(1)} collective-permute-done((bf16[4,8,256]{2,1,0:T(8,128)(2,1)S(1)}, bf16[4,8,256]{2,1,0:T(8,128)(2,1)S(1)}, u32[]{:S(2)}, u32[]{:S(2)}) %collective-permute-start.10) | collective-permute-done | bytes 16416 | tf_op jit(solution)/shard_map/ppermute | solution.py:54
  160.3 6.5 %collective-permute-start.11 = (bf16[2,8,256]{2,1,0:T(8,128)(2,1)S(1)}, bf16[2,8,256]{2,1,0:T(8,128)(2,1)S(1)}, u32[]{:S(2)}, u32[]{:S(2)}) collective-permute-start(bf16[2,8,256]{2,1,0:T(8,128)(2,1)S(1)} %fusion.40), channel_id=1, source_target_pairs={{0,32},{32,0},{64,96},{96,64},{1,33},{33,1},{65,97},{97,65},{2,34}... | collective-permute-start | bytes 24584 | tf_op jit(solution)/shard_map/ppermute | solution.py:54
  166.8 2.9 %collective-permute-done.11 = bf16[2,8,256]{2,1,0:T(8,128)(2,1)S(1)} collective-permute-done((bf16[2,8,256]{2,1,0:T(8,128)(2,1)S(1)}, bf16[2,8,256]{2,1,0:T(8,128)(2,1)S(1)}, u32[]{:S(2)}, u32[]{:S(2)}) %collective-permute-start.11) | collective-permute-done | bytes 8224 | tf_op jit(solution)/shard_map/ppermute | solution.py:54
  169.7 12.5 %collective-permute-start.12 = (bf16[1,8,256]{2,1,0:T(8,128)(2,1)S(1)}, bf16[1,8,256]{2,1,0:T(8,128)(2,1)S(1)}, u32[]{:S(2)}, u32[]{:S(2)}) collective-permute-start(bf16[1,8,256]{2,1,0:T(8,128)(2,1)S(1)} %select_bitcast_fusion), channel_id=1, source_target_pairs={{0,64},{32,96},{64,0},{96,32},{1,65},{33,97},{65,1},{97,33},{2,66}... | collective-permute-start | bytes 12296 | tf_op jit(solution)/shard_map/ppermute | solution.py:54
  182.2 1.7 collective-permute-done.12
  183.9 0.4 convolution_convert_fusion.3
  184.4 0.4 convolution_convert_fusion.2
  184.8 0.7 broadcast_in_dim.8
  185.5 5.1 %all-to-all-start.4 = ((f32[16,8,256]{2,1,0:T(8,128)}), f32[16,8,256]{2,1,0:T(8,128)S(1)}, u32[]{:S(2)}, u32[]{:S(2)}) async-start(f32[16,8,256]{2,1,0:T(8,128)} %broadcast_in_dim.8), calls=%async_computation.4 | async-start | bytes 262144 | tf_op jit(solution)/shard_map/all_to_all | solution.py:44
  190.6 1.2 fusion.2
  191.7 4.7 %all-to-all-done.4 = f32[16,8,256]{2,1,0:T(8,128)S(1)} async-done(((f32[16,8,256]{2,1,0:T(8,128)}), f32[16,8,256]{2,1,0:T(8,128)S(1)}, u32[]{:S(2)}, u32[]{:S(2)}) %all-to-all-start.4) | async-done | bytes 131104 | tf_op jit(solution)/shard_map/all_to_all | solution.py:44
  196.6 0.6 pad_maximum_fusion.3
  (62 shorter events, 2.9 us)
Async XLA Ops:
  0.6 0.7 copy-start.1
  0.6 20.3 %copy-start = (bf16[1,256,512]{2,1,0:T(8,128)(2,1)S(1)}, bf16[1,256,512]{2,1,0:T(8,128)(2,1)}, u32[]{:S(2)}) copy-start(bf16[1,256,512]{2,1,0:T(8,128)(2,1)} %param.7) | copy-start | bytes 786436
  2.0 27.9 %all-to-all-start = ((bf16[16,8,256]{2,1,0:T(8,128)(2,1)}), bf16[16,8,256]{2,1,0:T(8,128)(2,1)S(1)}, u32[]{:S(2)}, u32[]{:S(2)}) async-start(bf16[16,8,256]{2,1,0:T(8,128)(2,1)} %broadcast_in_dim.6), calls=%async_computation | async-start | bytes 131072 | tf_op jit(solution)/shard_map/all_to_all | solution.py:44
  17.2 58.2 %collective-permute-start = (bf16[256,512]{1,0:T(8,128)(2,1)}, bf16[256,512]{1,0:T(8,128)(2,1)S(1)}, u32[]{:S(2)}, u32[]{:S(2)}) collective-permute-start(bf16[256,512]{1,0:T(8,128)(2,1)} %bitcast.157), channel_id=1, source_target_pairs={{0,4},{4,0},{1,5},{5,1},{2,6},{6,2},{3,7},{7,3},{8,12},{12,8},{9,1... | collective-permute-start | bytes 786440 | tf_op jit(solution)/shard_map/ppermute | solution.py:222
  21.3 0.7 copy-start.2
  30.0 42.3 %all-to-all-start.1 = ((bf16[128,8,256]{2,1,0:T(8,128)(2,1)}), bf16[128,8,256]{2,1,0:T(8,128)(2,1)S(1)}, u32[]{:S(2)}, u32[]{:S(2)}) async-start(bf16[128,8,256]{2,1,0:T(8,128)(2,1)} %bitcast.9), calls=%async_computation.1 | async-start | bytes 1048576 | tf_op jit(solution)/shard_map/all_to_all | solution.py:44
  40.5 8.0 %collective-permute-start.1 = (bf16[128,256]{1,0:T(8,128)(2,1)S(1)}, bf16[128,256]{1,0:T(8,128)(2,1)S(1)}, u32[]{:S(2)}, u32[]{:S(2)}) collective-permute-start(bf16[128,256]{1,0:T(8,128)(2,1)S(1)} %bitcast.145), channel_id=1, source_target_pairs={{0,256},{128,384},{256,0},{384,128},{1,257},{129,385},{257,1},{385... | collective-permute-start | bytes 196616 | tf_op jit(solution)/shard_map/ppermute | solution.py:54
  48.5 7.4 %collective-permute-start.2 = (bf16[256,256]{1,0:T(8,128)(2,1)S(1)}, bf16[256,256]{1,0:T(8,128)(2,1)S(1)}, u32[]{:S(2)}, u32[]{:S(2)}) collective-permute-start(bf16[256,256]{1,0:T(8,128)(2,1)S(1)} %pad_maximum_fusion.2), channel_id=1, source_target_pairs={{0,128},{128,0},{256,384},{384,256},{1,129},{129,1},{257,385},{385... | collective-permute-start | bytes 393224 | tf_op jit(solution)/shard_map/ppermute | solution.py:54
  56.5 3.2 %collective-permute-start.3 = (bf16[256,256]{1,0:T(8,128)(2,1)S(1)}, bf16[256,256]{1,0:T(8,128)(2,1)S(1)}, u32[]{:S(2)}, u32[]{:S(2)}) collective-permute-start(bf16[256,256]{1,0:T(8,128)(2,1)S(1)} %get-tuple-element.22), channel_id=1, source_target_pairs={{0,4},{4,0},{1,5},{5,1},{2,6},{6,2},{3,7},{7,3},{8,12},{12,8},{9,1... | collective-permute-start | bytes 393224 | tf_op jit(solution)/shard_map/ppermute | solution.py:210
  59.8 16.2 %collective-permute-start.4 = (bf16[512,256]{1,0:T(8,128)(2,1)S(1)}, bf16[512,256]{1,0:T(8,128)(2,1)S(1)}, u32[]{:S(2)}, u32[]{:S(2)}) collective-permute-start(bf16[512,256]{1,0:T(8,128)(2,1)S(1)} %pad_maximum_fusion.w0_ref), channel_id=1, source_target_pairs={{0,1},{1,2},{2,3},{3,0},{4,5},{5,6},{6,7},{7,4},{8,9},{9,10},{10,1... | collective-permute-start | bytes 786440 | tf_op jit(solution)/shard_map/ppermute | solution.py:49
  63.2 15.5 %collective-permute-start.5 = (bf16[512,256]{1,0:T(8,128)(2,1)S(1)}, bf16[512,256]{1,0:T(8,128)(2,1)S(1)}, u32[]{:S(2)}, u32[]{:S(2)}) collective-permute-start(bf16[512,256]{1,0:T(8,128)(2,1)S(1)} %pad_maximum_fusion.w0_ref), channel_id=1, source_target_pairs={{0,2},{1,3},{2,0},{3,1},{4,6},{5,7},{6,4},{7,5},{8,10},{9,11},{10,... | collective-permute-start | bytes 786440 | tf_op jit(solution)/shard_map/ppermute | solution.py:49
  68.7 11.4 %collective-permute-start.6 = (bf16[512,256]{1,0:T(8,128)(2,1)S(1)}, bf16[512,256]{1,0:T(8,128)(2,1)S(1)}, u32[]{:S(2)}, u32[]{:S(2)}) collective-permute-start(bf16[512,256]{1,0:T(8,128)(2,1)S(1)} %pad_maximum_fusion.w0_ref), channel_id=1, source_target_pairs={{0,3},{1,0},{2,1},{3,2},{4,7},{5,4},{6,5},{7,6},{8,11},{9,8},{10,9... | collective-permute-start | bytes 786440 | tf_op jit(solution)/shard_map/ppermute | solution.py:49
  73.2 2.2 %copy-start.4 = (bf16[1,256,512]{2,1,0:T(8,128)(2,1)S(1)}, bf16[1,256,512]{2,1,0:T(8,128)(2,1)}, u32[]{:S(2)}) copy-start(bf16[1,256,512]{2,1,0:T(8,128)(2,1)} %param.6) | copy-start | bytes 786436
  73.3 6.8 %collective-permute-start.7 = (bf16[256,512]{1,0:T(8,128)(2,1)S(1)}, bf16[256,512]{1,0:T(8,128)(2,1)S(1)}, u32[]{:S(2)}, u32[]{:S(2)}) collective-permute-start(bf16[256,512]{1,0:T(8,128)(2,1)S(1)} %pad_maximum_fusion.1.gown_ref), channel_id=1, source_target_pairs={{0,4},{4,0},{1,5},{5,1},{2,6},{6,2},{3,7},{7,3},{8,12},{12,8},{9,1... | collective-permute-start | bytes 786440 | tf_op jit(solution)/shard_map/ppermute | solution.py:225
  88.0 9.0 %collective-permute-start.8 = (bf16[256,512]{1,0:T(8,128)(2,1)S(1)}, bf16[256,512]{1,0:T(8,128)(2,1)S(1)}, u32[]{:S(2)}, u32[]{:S(2)}) collective-permute-start(bf16[256,512]{1,0:T(8,128)(2,1)S(1)} %get-tuple-element.16), channel_id=1, source_target_pairs={{0,4},{4,0},{1,5},{5,1},{2,6},{6,2},{3,7},{7,3},{8,12},{12,8},{9,1... | collective-permute-start | bytes 786440 | tf_op jit(solution)/shard_map/ppermute | solution.py:233
  89.9 22.2 %all-to-all-start.2 = ((bf16[32,64,256]{2,1,0:T(8,128)(2,1)}), bf16[32,64,256]{2,1,0:T(8,128)(2,1)S(1)}, u32[]{:S(2)}, u32[]{:S(2)}) async-start(bf16[32,64,256]{2,1,0:T(8,128)(2,1)} %bitcast.11), calls=%async_computation.2 | async-start | bytes 2097152 | tf_op jit(solution)/shard_map/all_to_all | solution.py:44
  112.8 71.1 %all-to-all-start.3 = ((bf16[128,8,256]{2,1,0:T(8,128)(2,1)}), bf16[128,8,256]{2,1,0:T(8,128)(2,1)S(1)}, u32[]{:S(2)}, u32[]{:S(2)}) async-start(bf16[128,8,256]{2,1,0:T(8,128)(2,1)} %bitcast.36), calls=%async_computation.3 | async-start | bytes 1048576 | tf_op jit(solution)/shard_map/all_to_all | solution.py:44
  129.8 23.8 %collective-permute-start.9 = (bf16[8,8,256]{2,1,0:T(8,128)(2,1)S(1)}, bf16[8,8,256]{2,1,0:T(8,128)(2,1)S(1)}, u32[]{:S(2)}, u32[]{:S(2)}) collective-permute-start(bf16[8,8,256]{2,1,0:T(8,128)(2,1)S(1)} %fusion.34), channel_id=1, source_target_pairs={{0,8},{8,0},{16,24},{24,16},{1,9},{9,1},{17,25},{25,17},{2,10},{10... | collective-permute-start | bytes 98312 | tf_op jit(solution)/shard_map/ppermute | solution.py:54
  153.7 6.5 %collective-permute-start.10 = (bf16[4,8,256]{2,1,0:T(8,128)(2,1)S(1)}, bf16[4,8,256]{2,1,0:T(8,128)(2,1)S(1)}, u32[]{:S(2)}, u32[]{:S(2)}) collective-permute-start(bf16[4,8,256]{2,1,0:T(8,128)(2,1)S(1)} %fusion.37), channel_id=1, source_target_pairs={{0,16},{8,24},{16,0},{24,8},{1,17},{9,25},{17,1},{25,9},{2,18},{10... | collective-permute-start | bytes 49160 | tf_op jit(solution)/shard_map/ppermute | solution.py:54
  160.3 9.5 %collective-permute-start.11 = (bf16[2,8,256]{2,1,0:T(8,128)(2,1)S(1)}, bf16[2,8,256]{2,1,0:T(8,128)(2,1)S(1)}, u32[]{:S(2)}, u32[]{:S(2)}) collective-permute-start(bf16[2,8,256]{2,1,0:T(8,128)(2,1)S(1)} %fusion.40), channel_id=1, source_target_pairs={{0,32},{32,0},{64,96},{96,64},{1,33},{33,1},{65,97},{97,65},{2,34}... | collective-permute-start | bytes 24584 | tf_op jit(solution)/shard_map/ppermute | solution.py:54
  169.7 14.2 %collective-permute-start.12 = (bf16[1,8,256]{2,1,0:T(8,128)(2,1)S(1)}, bf16[1,8,256]{2,1,0:T(8,128)(2,1)S(1)}, u32[]{:S(2)}, u32[]{:S(2)}) collective-permute-start(bf16[1,8,256]{2,1,0:T(8,128)(2,1)S(1)} %select_bitcast_fusion), channel_id=1, source_target_pairs={{0,64},{32,96},{64,0},{96,32},{1,65},{33,97},{65,1},{97,33},{2,66}... | collective-permute-start | bytes 12296 | tf_op jit(solution)/shard_map/ppermute | solution.py:54
  185.5 11.0 %all-to-all-start.4 = ((f32[16,8,256]{2,1,0:T(8,128)}), f32[16,8,256]{2,1,0:T(8,128)S(1)}, u32[]{:S(2)}, u32[]{:S(2)}) async-start(f32[16,8,256]{2,1,0:T(8,128)} %broadcast_in_dim.8), calls=%async_computation.4 | async-start | bytes 262144 | tf_op jit(solution)/shard_map/all_to_all | solution.py:44
  196.6 0.6 copy-start.3

commit v6 on v4

--- a/solution.py
+++ b/solution.py
@@ -240,20 +240,18 @@
         come = flip(jnp.where(mine_set, first, second), axis, bit)
         return (stay.astype(f32) + come.astype(f32)).astype(bf)
 
+    wide = total.shape[1] // 2
+    total = halve(total, "rep", rep, 1, total[:, :wide], total[:, wide:])
     for bit in bits:
         count = nx // bit
         blocks = total.reshape(count // 2, 2, nz * share, total.shape[1])
         flat = (count // 2 * nz * share, total.shape[1])
         total = halve(total, "x", x_here, bit, blocks[:, 0].reshape(flat), blocks[:, 1].reshape(flat))
-    for bit in (1, 2):
-        wide = total.shape[1] // 2
-        total = halve(total, "rep", rep, bit, total[:, :wide], total[:, wide:])
     total, returned = lax.optimization_barrier((total, returned))
-    wide = total.shape[1]
     far = swap(total.reshape(nz, share, wide), ("zh", "zl"))
     summed = jnp.sum(far.astype(f32), axis=0)
     last = swap(jnp.broadcast_to(summed[None], (nr, share, wide)), "rep")
-    last = jnp.concatenate([last[r] for r in (0, 2, 1, 3)], axis=1)
+    last = jnp.concatenate([last[0] + last[2], last[1] + last[3]], axis=1)
     grad_perm = jnp.concatenate([mm(send[h], returned, TN, bf) for h in range(2)], axis=1)
     grad_z = mm(grad_perm, perm, NT, bf)
     lower = jnp.where(core == 0, last[:, : 3 * own], last[:, 3 * own : 6 * own])

time: 179 us -> 179 us (level); the launches traced: 179 us -> 177 us
  starting transfers between devices: 96.7 us -> 85.1 us
  waiting for transfers between devices: 58.1 us -> 68 us
    all_to_all x5, waiting for transfers between devices: 26.5 us -> 35.8 us  [swap(): return lax.all_to_all(block, axis, split_axis=0, concat_axis=0, tiled=True)]
    all_to_all x5, starting transfers between devices: 55.1 us -> 48.7 us  [swap(): return lax.all_to_all(block, axis, split_axis=0, concat_axis=0, tiled=True)]
    ppermute x6 -> x5, starting transfers between devices: 19.7 us -> 14.6 us  [flip(): lax.ppermute(block, axis, [(here, here ^ bit) for here in range(count)])]
    ppermute x6 -> x5, waiting for transfers between devices: 26.6 us -> 25.7 us  [flip(): lax.ppermute(block, axis, [(here, here ^ bit) for here in range(count)])]
  transfers between devices with their start and end apart: 19 -> 18, of which waited for: 13 -> 13; matrix products, arithmetic and copies ran while one was open for 6% -> 6% of each run, Pallas kernels for 0% -> 0%
where the time goes in v6:
time: 179 us; the launch traced here: 177 us
  starting transfers between devices  85.1 us (48%)
  waiting for transfers between devices  68 us (38%)
  Pallas kernels  7.3 us (4%)
  matrix products  7.07 us (4%)
  local copies, waits for them, and re-layouts  4.99 us (3%)
  other arithmetic  2.93 us (2%)
    all_to_all x5, starting transfers between devices, swap(): return lax.all_to_all(block, axis, split_axis=0, concat_axis=0, tiled=True)  48.7 us
    all_to_all x5, waiting for transfers between devices, swap(): return lax.all_to_all(block, axis, split_axis=0, concat_axis=0, tiled=True)  35.8 us
    ppermute x5, waiting for transfers between devices, flip(): lax.ppermute(block, axis, [(here, here ^ bit) for here in range(count)])  25.7 us
    ppermute x5, starting transfers between devices, flip(): lax.ppermute(block, axis, [(here, here ^ bit) for here in range(count)])  14.6 us
    ppermute x3, starting transfers between devices, shift(): lax.ppermute(block, axis, [(here, (here + step) % count) for here in rang...  11.6 us
    pallas_call x1, Pallas kernels, patch_step(): pl.pallas_call(patch_body, out_shape=[jax.ShapeDtypeStruct((rows, channel...  7.3 us
    dot_general x12, matrix products, mm(): lax.dot_general(left, right, (dims, ((), ())), preferred_element_type=jnp...  7.07 us
    ppermute x3, waiting for transfers between devices, shift(): lax.ppermute(block, axis, [(here, (here + step) % count) for here in rang...  4.1 us
  transfers between devices with their start and end apart: 18, of which 13 were waited for; matrix products, arithmetic and copies ran while one was open for 6% of the time, Pallas kernels for 0%

profile of v6, /device:TPU:6, one launch (start us, length us, event | category | flops | bytes accessed | tf_op | source)
XLA Modules:
  0.0 176.6 jit_solution(13950674087403671717)
XLA Ops:
  0.7 0.7 copy-done.1
  1.4 0.6 broadcast_in_dim.6
  2.0 15.2 %all-to-all-start = ((bf16[16,8,256]{2,1,0:T(8,128)(2,1)}), bf16[16,8,256]{2,1,0:T(8,128)(2,1)S(1)}, u32[]{:S(2)}, u32[]{:S(2)}) async-start(bf16[16,8,256]{2,1,0:T(8,128)(2,1)} %broadcast_in_dim.6), calls=%async_computation | async-start | bytes 131072 | tf_op jit(solution)/shard_map/all_to_all | solution.py:44
  17.2 1.9 %collective-permute-start = (bf16[256,512]{1,0:T(8,128)(2,1)}, bf16[256,512]{1,0:T(8,128)(2,1)S(1)}, u32[]{:S(2)}, u32[]{:S(2)}) collective-permute-start(bf16[256,512]{1,0:T(8,128)(2,1)} %bitcast.61), channel_id=1, source_target_pairs={{0,4},{4,0},{1,5},{5,1},{2,6},{6,2},{3,7},{7,3},{8,12},{12,8},{9,1... | collective-permute-start | bytes 786440 | tf_op jit(solution)/shard_map/ppermute | solution.py:220
  19.2 0.7 and_select_fusion.5
  19.8 0.7 fusion.72
  21.3 0.6 copy-done.2
  22.1 1.1 fusion
  23.3 6.7 %all-to-all-done = bf16[16,8,256]{2,1,0:T(8,128)(2,1)S(1)} async-done(((bf16[16,8,256]{2,1,0:T(8,128)(2,1)}), bf16[16,8,256]{2,1,0:T(8,128)(2,1)S(1)}, u32[]{:S(2)}, u32[]{:S(2)}) %all-to-all-start) | async-done | bytes 65568 | tf_op jit(solution)/shard_map/all_to_all | solution.py:44
  30.0 10.1 %all-to-all-start.1 = ((bf16[128,8,256]{2,1,0:T(8,128)(2,1)}), bf16[128,8,256]{2,1,0:T(8,128)(2,1)S(1)}, u32[]{:S(2)}, u32[]{:S(2)}) async-start(bf16[128,8,256]{2,1,0:T(8,128)(2,1)} %bitcast.9), calls=%async_computation.1 | async-start | bytes 1048576 | tf_op jit(solution)/shard_map/all_to_all | solution.py:44
  40.5 2.9 %collective-permute-start.1 = (bf16[128,256]{1,0:T(8,128)(2,1)S(1)}, bf16[128,256]{1,0:T(8,128)(2,1)S(1)}, u32[]{:S(2)}, u32[]{:S(2)}) collective-permute-start(bf16[128,256]{1,0:T(8,128)(2,1)S(1)} %bitcast.52), channel_id=1, source_target_pairs={{0,256},{128,384},{256,0},{384,128},{1,257},{129,385},{257,1},{385... | collective-permute-start | bytes 196616 | tf_op jit(solution)/shard_map/ppermute | solution.py:54
  43.5 5.0 %collective-permute-done.1 = bf16[128,256]{1,0:T(8,128)(2,1)S(1)} collective-permute-done((bf16[128,256]{1,0:T(8,128)(2,1)S(1)}, bf16[128,256]{1,0:T(8,128)(2,1)S(1)}, u32[]{:S(2)}, u32[]{:S(2)}) %collective-permute-start.1) | collective-permute-done | bytes 65568 | tf_op jit(solution)/shard_map/ppermute | solution.py:54
  48.5 2.4 %collective-permute-start.2 = (bf16[256,256]{1,0:T(8,128)(2,1)S(1)}, bf16[256,256]{1,0:T(8,128)(2,1)S(1)}, u32[]{:S(2)}, u32[]{:S(2)}) collective-permute-start(bf16[256,256]{1,0:T(8,128)(2,1)S(1)} %pad_maximum_fusion.5), channel_id=1, source_target_pairs={{0,128},{128,0},{256,384},{384,256},{1,129},{129,1},{257,385},{385... | collective-permute-start | bytes 393224 | tf_op jit(solution)/shard_map/ppermute | solution.py:54
  51.0 5.0 %collective-permute-done.2 = bf16[256,256]{1,0:T(8,128)(2,1)S(1)} collective-permute-done((bf16[256,256]{1,0:T(8,128)(2,1)S(1)}, bf16[256,256]{1,0:T(8,128)(2,1)S(1)}, u32[]{:S(2)}, u32[]{:S(2)}) %collective-permute-start.2) | collective-permute-done | bytes 131104 | tf_op jit(solution)/shard_map/ppermute | solution.py:54
  56.5 1.9 %collective-permute-start.3 = (bf16[256,256]{1,0:T(8,128)(2,1)S(1)}, bf16[256,256]{1,0:T(8,128)(2,1)S(1)}, u32[]{:S(2)}, u32[]{:S(2)}) collective-permute-start(bf16[256,256]{1,0:T(8,128)(2,1)S(1)} %get-tuple-element.28), channel_id=1, source_target_pairs={{0,4},{4,0},{1,5},{5,1},{2,6},{6,2},{3,7},{7,3},{8,12},{12,8},{9,1... | collective-permute-start | bytes 393224 | tf_op jit(solution)/shard_map/ppermute | solution.py:208
  58.5 1.3 collective-permute-done.3
  59.8 3.5 %collective-permute-start.4 = (bf16[512,256]{1,0:T(8,128)(2,1)S(1)}, bf16[512,256]{1,0:T(8,128)(2,1)S(1)}, u32[]{:S(2)}, u32[]{:S(2)}) collective-permute-start(bf16[512,256]{1,0:T(8,128)(2,1)S(1)} %pad_maximum_fusion.3.w0_ref), channel_id=1, source_target_pairs={{0,1},{1,2},{2,3},{3,0},{4,5},{5,6},{6,7},{7,4},{8,9},{9,10},{10,1... | collective-permute-start | bytes 786440 | tf_op jit(solution)/shard_map/ppermute | solution.py:49
  63.3 5.5 %collective-permute-start.5 = (bf16[512,256]{1,0:T(8,128)(2,1)S(1)}, bf16[512,256]{1,0:T(8,128)(2,1)S(1)}, u32[]{:S(2)}, u32[]{:S(2)}) collective-permute-start(bf16[512,256]{1,0:T(8,128)(2,1)S(1)} %pad_maximum_fusion.3.w0_ref), channel_id=1, source_target_pairs={{0,2},{1,3},{2,0},{3,1},{4,6},{5,7},{6,4},{7,5},{8,10},{9,11},{10,... | collective-permute-start | bytes 786440 | tf_op jit(solution)/shard_map/ppermute | solution.py:49
  68.8 2.6 %collective-permute-start.6 = (bf16[512,256]{1,0:T(8,128)(2,1)S(1)}, bf16[512,256]{1,0:T(8,128)(2,1)S(1)}, u32[]{:S(2)}, u32[]{:S(2)}) collective-permute-start(bf16[512,256]{1,0:T(8,128)(2,1)S(1)} %pad_maximum_fusion.3.w0_ref), channel_id=1, source_target_pairs={{0,3},{1,0},{2,1},{3,2},{4,7},{5,4},{6,5},{7,6},{8,11},{9,8},{10,9... | collective-permute-start | bytes 786440 | tf_op jit(solution)/shard_map/ppermute | solution.py:49
  71.3 0.9 all-to-all-done.1
  72.2 0.5 convolution_convert_fusion.5
  72.7 0.5 convolution_convert_fusion.4
  73.3 2.1 %collective-permute-start.7 = (bf16[256,512]{1,0:T(8,128)(2,1)S(1)}, bf16[256,512]{1,0:T(8,128)(2,1)S(1)}, u32[]{:S(2)}, u32[]{:S(2)}) collective-permute-start(bf16[256,512]{1,0:T(8,128)(2,1)S(1)} %pad_maximum_fusion.4.gown_ref), channel_id=1, source_target_pairs={{0,4},{4,0},{1,5},{5,1},{2,6},{6,2},{3,7},{7,3},{8,12},{12,8},{9,1... | collective-permute-start | bytes 786440 | tf_op jit(solution)/shard_map/ppermute | solution.py:223
  75.4 0.6 convolution_convert_fusion.x_ref
  76.0 2.8 %collective-permute-done.5.w2_ref = bf16[512,256]{1,0:T(8,128)(2,1)S(1)} collective-permute-done((bf16[512,256]{1,0:T(8,128)(2,1)S(1)}, bf16[512,256]{1,0:T(8,128)(2,1)S(1)}, u32[]{:S(2)}, u32[]{:S(2)}) %collective-permute-start.5) | collective-permute-done | bytes 262176 | tf_op jit(solution)/shard_map/ppermute | solution.py:49
  78.8 1.3 collective-permute-done.6.w3_ref
  80.1 7.3 %shard_map.85 = (f32[256,512]{1,0:T(8,128)S(1)}, bf16[256,512]{1,0:T(8,128)(2,1)S(1)}, bf16[256,1024]{1,0:T(8,128)(2,1)S(1)}, bf16[256,1024]{1,0:T(8,128)(2,1)S(1)}) custom-call(s32[2]{0:T(128)S(1)} %pad_add_fusion.place_ref, bf16[512,512]{1,0:T(8,128)(2,1)S(1)} %convolution_convert_fusion.x_ref, bf16[512,256]{1,0:T(8,128)(2,1)S(1)} %pad_maximum_fusion.3.w0_ref, ...), custom_call_target="tpu_custom_call" | custom-call | tf_op jit(solution)/shard_map/pallas_call | solution.py:134
  87.4 1.9 %collective-permute-start.12 = (bf16[256,512]{1,0:T(8,128)(2,1)S(1)}, bf16[256,512]{1,0:T(8,128)(2,1)S(1)}, u32[]{:S(2)}, u32[]{:S(2)}) collective-permute-start(bf16[256,512]{1,0:T(8,128)(2,1)S(1)} %get-tuple-element.16), channel_id=1, source_target_pairs={{0,4},{4,0},{1,5},{5,1},{2,6},{6,2},{3,7},{7,3},{8,12},{12,8},{9,1... | collective-permute-start | bytes 786440 | tf_op jit(solution)/shard_map/ppermute | solution.py:227
  89.4 2.4 %collective-permute-start.8 = (bf16[256,1024]{1,0:T(8,128)(2,1)S(1)}, bf16[256,1024]{1,0:T(8,128)(2,1)S(1)}, u32[]{:S(2)}, u32[]{:S(2)}) collective-permute-start(bf16[256,1024]{1,0:T(8,128)(2,1)S(1)} %get-tuple-element.13), channel_id=1, source_target_pairs={{0,4},{4,0},{1,5},{5,1},{2,6},{6,2},{3,7},{7,3},{8,12},{12,8},{9,1... | collective-permute-start | bytes 1572872 | tf_op jit(solution)/shard_map/ppermute | solution.py:232
  92.3 1.1 collective-permute-done.8
  93.6 3.7 %collective-permute-start.9 = (bf16[256,1024]{1,0:T(8,128)(2,1)S(1)}, bf16[256,1024]{1,0:T(8,128)(2,1)S(1)}, u32[]{:S(2)}, u32[]{:S(2)}) collective-permute-start(bf16[256,1024]{1,0:T(8,128)(2,1)S(1)} %broadcast_select_fusion), channel_id=1, source_target_pairs={{0,1},{1,0},{2,3},{3,2},{4,5},{5,4},{6,7},{7,6},{8,9},{9,8},{10,11... | collective-permute-start | bytes 1572872 | tf_op jit(solution)/shard_map/ppermute | solution.py:54
  97.3 1.1 fusion.2
  98.5 16.3 %all-to-all-start.2 = ((bf16[128,8,256]{2,1,0:T(8,128)(2,1)}), bf16[128,8,256]{2,1,0:T(8,128)(2,1)S(1)}, u32[]{:S(2)}, u32[]{:S(2)}) async-start(bf16[128,8,256]{2,1,0:T(8,128)(2,1)} %fusion.2), calls=%async_computation.2 | async-start | bytes 1048576 | tf_op jit(solution)/shard_map/all_to_all | solution.py:44
  115.1 2.5 %collective-permute-start.10 = (bf16[128,1024]{1,0:T(8,128)(2,1)S(1)}, bf16[128,1024]{1,0:T(8,128)(2,1)S(1)}, u32[]{:S(2)}, u32[]{:S(2)}) collective-permute-start(bf16[128,1024]{1,0:T(8,128)(2,1)S(1)} %bitcast.59), channel_id=1, source_target_pairs={{0,128},{128,0},{256,384},{384,256},{1,129},{129,1},{257,385},{385... | collective-permute-start | bytes 786440 | tf_op jit(solution)/shard_map/ppermute | solution.py:54
  117.7 9.4 %collective-permute-done.10 = bf16[128,1024]{1,0:T(8,128)(2,1)S(1)} collective-permute-done((bf16[128,1024]{1,0:T(8,128)(2,1)S(1)}, bf16[128,1024]{1,0:T(8,128)(2,1)S(1)}, u32[]{:S(2)}, u32[]{:S(2)}) %collective-permute-start.10) | collective-permute-done | bytes 262176 | tf_op jit(solution)/shard_map/ppermute | solution.py:54
  127.2 3.0 %collective-permute-start.11 = (bf16[64,1024]{1,0:T(8,128)(2,1)S(1)}, bf16[64,1024]{1,0:T(8,128)(2,1)S(1)}, u32[]{:S(2)}, u32[]{:S(2)}) collective-permute-start(bf16[64,1024]{1,0:T(8,128)(2,1)S(1)} %select_bitcast_fusion), channel_id=1, source_target_pairs={{0,256},{128,384},{256,0},{384,128},{1,257},{129,385},{257,1},{385... | collective-permute-start | bytes 393224 | tf_op jit(solution)/shard_map/ppermute | solution.py:54
  130.2 6.3 %collective-permute-done.11 = bf16[64,1024]{1,0:T(8,128)(2,1)S(1)} collective-permute-done((bf16[64,1024]{1,0:T(8,128)(2,1)S(1)}, bf16[64,1024]{1,0:T(8,128)(2,1)S(1)}, u32[]{:S(2)}, u32[]{:S(2)}) %collective-permute-start.11) | collective-permute-done | bytes 131104 | tf_op jit(solution)/shard_map/ppermute | solution.py:54
  136.5 10.4 %all-to-all-done.2 = bf16[128,8,256]{2,1,0:T(8,128)(2,1)S(1)} async-done(((bf16[128,8,256]{2,1,0:T(8,128)(2,1)}), bf16[128,8,256]{2,1,0:T(8,128)(2,1)S(1)}, u32[]{:S(2)}, u32[]{:S(2)}) %all-to-all-start.2) | async-done | bytes 524320 | tf_op jit(solution)/shard_map/all_to_all | solution.py:44
  146.9 0.7 reshape.504
  147.6 3.5 %all-to-all-start.3 = ((bf16[16,4,1024]{2,1,0:T(4,128)(2,1)}), bf16[16,4,1024]{2,1,0:T(4,128)(2,1)S(1)}, u32[]{:S(2)}, u32[]{:S(2)}) async-start(bf16[16,4,1024]{2,1,0:T(4,128)(2,1)} %reshape.504), calls=%async_computation.3 | async-start | bytes 262144 | tf_op jit(solution)/shard_map/all_to_all | solution.py:44
  151.1 0.4 convolution_convert_fusion.3
  152.0 13.4 %all-to-all-done.3 = bf16[16,4,1024]{2,1,0:T(4,128)(2,1)S(1)} async-done(((bf16[16,4,1024]{2,1,0:T(4,128)(2,1)}), bf16[16,4,1024]{2,1,0:T(4,128)(2,1)S(1)}, u32[]{:S(2)}, u32[]{:S(2)}) %all-to-all-start.3) | async-done | bytes 131104 | tf_op jit(solution)/shard_map/all_to_all | solution.py:44
  165.5 0.6 broadcast_in_dim.8
  166.1 3.6 %all-to-all-start.4 = ((f32[4,4,1024]{2,1,0:T(4,128)}), f32[4,4,1024]{2,1,0:T(4,128)S(1)}, u32[]{:S(2)}, u32[]{:S(2)}) async-start(f32[4,4,1024]{2,1,0:T(4,128)} %broadcast_in_dim.8), calls=%async_computation.4 | async-start | bytes 131072 | tf_op jit(solution)/shard_map/all_to_all | solution.py:44
  169.7 1.2 fusion.3
  170.9 4.4 %all-to-all-done.4 = f32[4,4,1024]{2,1,0:T(4,128)S(1)} async-done(((f32[4,4,1024]{2,1,0:T(4,128)}), f32[4,4,1024]{2,1,0:T(4,128)S(1)}, u32[]{:S(2)}, u32[]{:S(2)}) %all-to-all-start.4) | async-done | bytes 65568 | tf_op jit(solution)/shard_map/all_to_all | solution.py:44
  175.3 0.6 slice.152
  176.0 0.6 copy-done.3
  (62 shorter events, 3.7 us)
Async XLA Ops:
  0.6 0.7 copy-start.1
  0.6 20.3 %copy-start = (bf16[1,256,512]{2,1,0:T(8,128)(2,1)S(1)}, bf16[1,256,512]{2,1,0:T(8,128)(2,1)}, u32[]{:S(2)}) copy-start(bf16[1,256,512]{2,1,0:T(8,128)(2,1)} %param.7) | copy-start | bytes 786436
  2.0 27.9 %all-to-all-start = ((bf16[16,8,256]{2,1,0:T(8,128)(2,1)}), bf16[16,8,256]{2,1,0:T(8,128)(2,1)S(1)}, u32[]{:S(2)}, u32[]{:S(2)}) async-start(bf16[16,8,256]{2,1,0:T(8,128)(2,1)} %broadcast_in_dim.6), calls=%async_computation | async-start | bytes 131072 | tf_op jit(solution)/shard_map/all_to_all | solution.py:44
  17.2 58.2 %collective-permute-start = (bf16[256,512]{1,0:T(8,128)(2,1)}, bf16[256,512]{1,0:T(8,128)(2,1)S(1)}, u32[]{:S(2)}, u32[]{:S(2)}) collective-permute-start(bf16[256,512]{1,0:T(8,128)(2,1)} %bitcast.61), channel_id=1, source_target_pairs={{0,4},{4,0},{1,5},{5,1},{2,6},{6,2},{3,7},{7,3},{8,12},{12,8},{9,1... | collective-permute-start | bytes 786440 | tf_op jit(solution)/shard_map/ppermute | solution.py:220
  21.3 0.7 copy-start.2
  30.0 42.3 %all-to-all-start.1 = ((bf16[128,8,256]{2,1,0:T(8,128)(2,1)}), bf16[128,8,256]{2,1,0:T(8,128)(2,1)S(1)}, u32[]{:S(2)}, u32[]{:S(2)}) async-start(bf16[128,8,256]{2,1,0:T(8,128)(2,1)} %bitcast.9), calls=%async_computation.1 | async-start | bytes 1048576 | tf_op jit(solution)/shard_map/all_to_all | solution.py:44
  40.5 8.0 %collective-permute-start.1 = (bf16[128,256]{1,0:T(8,128)(2,1)S(1)}, bf16[128,256]{1,0:T(8,128)(2,1)S(1)}, u32[]{:S(2)}, u32[]{:S(2)}) collective-permute-start(bf16[128,256]{1,0:T(8,128)(2,1)S(1)} %bitcast.52), channel_id=1, source_target_pairs={{0,256},{128,384},{256,0},{384,128},{1,257},{129,385},{257,1},{385... | collective-permute-start | bytes 196616 | tf_op jit(solution)/shard_map/ppermute | solution.py:54
  48.5 7.4 %collective-permute-start.2 = (bf16[256,256]{1,0:T(8,128)(2,1)S(1)}, bf16[256,256]{1,0:T(8,128)(2,1)S(1)}, u32[]{:S(2)}, u32[]{:S(2)}) collective-permute-start(bf16[256,256]{1,0:T(8,128)(2,1)S(1)} %pad_maximum_fusion.5), channel_id=1, source_target_pairs={{0,128},{128,0},{256,384},{384,256},{1,129},{129,1},{257,385},{385... | collective-permute-start | bytes 393224 | tf_op jit(solution)/shard_map/ppermute | solution.py:54
  56.5 3.2 %collective-permute-start.3 = (bf16[256,256]{1,0:T(8,128)(2,1)S(1)}, bf16[256,256]{1,0:T(8,128)(2,1)S(1)}, u32[]{:S(2)}, u32[]{:S(2)}) collective-permute-start(bf16[256,256]{1,0:T(8,128)(2,1)S(1)} %get-tuple-element.28), channel_id=1, source_target_pairs={{0,4},{4,0},{1,5},{5,1},{2,6},{6,2},{3,7},{7,3},{8,12},{12,8},{9,1... | collective-permute-start | bytes 393224 | tf_op jit(solution)/shard_map/ppermute | solution.py:208
  59.8 16.2 %collective-permute-start.4 = (bf16[512,256]{1,0:T(8,128)(2,1)S(1)}, bf16[512,256]{1,0:T(8,128)(2,1)S(1)}, u32[]{:S(2)}, u32[]{:S(2)}) collective-permute-start(bf16[512,256]{1,0:T(8,128)(2,1)S(1)} %pad_maximum_fusion.3.w0_ref), channel_id=1, source_target_pairs={{0,1},{1,2},{2,3},{3,0},{4,5},{5,6},{6,7},{7,4},{8,9},{9,10},{10,1... | collective-permute-start | bytes 786440 | tf_op jit(solution)/shard_map/ppermute | solution.py:49
  63.3 15.5 %collective-permute-start.5 = (bf16[512,256]{1,0:T(8,128)(2,1)S(1)}, bf16[512,256]{1,0:T(8,128)(2,1)S(1)}, u32[]{:S(2)}, u32[]{:S(2)}) collective-permute-start(bf16[512,256]{1,0:T(8,128)(2,1)S(1)} %pad_maximum_fusion.3.w0_ref), channel_id=1, source_target_pairs={{0,2},{1,3},{2,0},{3,1},{4,6},{5,7},{6,4},{7,5},{8,10},{9,11},{10,... | collective-permute-start | bytes 786440 | tf_op jit(solution)/shard_map/ppermute | solution.py:49
  68.8 11.4 %collective-permute-start.6 = (bf16[512,256]{1,0:T(8,128)(2,1)S(1)}, bf16[512,256]{1,0:T(8,128)(2,1)S(1)}, u32[]{:S(2)}, u32[]{:S(2)}) collective-permute-start(bf16[512,256]{1,0:T(8,128)(2,1)S(1)} %pad_maximum_fusion.3.w0_ref), channel_id=1, source_target_pairs={{0,3},{1,0},{2,1},{3,2},{4,7},{5,4},{6,5},{7,6},{8,11},{9,8},{10,9... | collective-permute-start | bytes 786440 | tf_op jit(solution)/shard_map/ppermute | solution.py:49
  73.3 2.2 %copy-start.4 = (bf16[1,256,512]{2,1,0:T(8,128)(2,1)S(1)}, bf16[1,256,512]{2,1,0:T(8,128)(2,1)}, u32[]{:S(2)}) copy-start(bf16[1,256,512]{2,1,0:T(8,128)(2,1)} %param.6) | copy-start | bytes 786436
  73.3 6.8 %collective-permute-start.7 = (bf16[256,512]{1,0:T(8,128)(2,1)S(1)}, bf16[256,512]{1,0:T(8,128)(2,1)S(1)}, u32[]{:S(2)}, u32[]{:S(2)}) collective-permute-start(bf16[256,512]{1,0:T(8,128)(2,1)S(1)} %pad_maximum_fusion.4.gown_ref), channel_id=1, source_target_pairs={{0,4},{4,0},{1,5},{5,1},{2,6},{6,2},{3,7},{7,3},{8,12},{12,8},{9,1... | collective-permute-start | bytes 786440 | tf_op jit(solution)/shard_map/ppermute | solution.py:223
  87.4 4.4 %collective-permute-start.12 = (bf16[256,512]{1,0:T(8,128)(2,1)S(1)}, bf16[256,512]{1,0:T(8,128)(2,1)S(1)}, u32[]{:S(2)}, u32[]{:S(2)}) collective-permute-start(bf16[256,512]{1,0:T(8,128)(2,1)S(1)} %get-tuple-element.16), channel_id=1, source_target_pairs={{0,4},{4,0},{1,5},{5,1},{2,6},{6,2},{3,7},{7,3},{8,12},{12,8},{9,1... | collective-permute-start | bytes 786440 | tf_op jit(solution)/shard_map/ppermute | solution.py:227
  89.4 4.0 %collective-permute-start.8 = (bf16[256,1024]{1,0:T(8,128)(2,1)S(1)}, bf16[256,1024]{1,0:T(8,128)(2,1)S(1)}, u32[]{:S(2)}, u32[]{:S(2)}) collective-permute-start(bf16[256,1024]{1,0:T(8,128)(2,1)S(1)} %get-tuple-element.13), channel_id=1, source_target_pairs={{0,4},{4,0},{1,5},{5,1},{2,6},{6,2},{3,7},{7,3},{8,12},{12,8},{9,1... | collective-permute-start | bytes 1572872 | tf_op jit(solution)/shard_map/ppermute | solution.py:232
  93.6 21.2 %collective-permute-start.9 = (bf16[256,1024]{1,0:T(8,128)(2,1)S(1)}, bf16[256,1024]{1,0:T(8,128)(2,1)S(1)}, u32[]{:S(2)}, u32[]{:S(2)}) collective-permute-start(bf16[256,1024]{1,0:T(8,128)(2,1)S(1)} %broadcast_select_fusion), channel_id=1, source_target_pairs={{0,1},{1,0},{2,3},{3,2},{4,5},{5,4},{6,7},{7,6},{8,9},{9,8},{10,11... | collective-permute-start | bytes 1572872 | tf_op jit(solution)/shard_map/ppermute | solution.py:54
  98.5 48.4 %all-to-all-start.2 = ((bf16[128,8,256]{2,1,0:T(8,128)(2,1)}), bf16[128,8,256]{2,1,0:T(8,128)(2,1)S(1)}, u32[]{:S(2)}, u32[]{:S(2)}) async-start(bf16[128,8,256]{2,1,0:T(8,128)(2,1)} %fusion.2), calls=%async_computation.2 | async-start | bytes 1048576 | tf_op jit(solution)/shard_map/all_to_all | solution.py:44
  115.1 12.0 %collective-permute-start.10 = (bf16[128,1024]{1,0:T(8,128)(2,1)S(1)}, bf16[128,1024]{1,0:T(8,128)(2,1)S(1)}, u32[]{:S(2)}, u32[]{:S(2)}) collective-permute-start(bf16[128,1024]{1,0:T(8,128)(2,1)S(1)} %bitcast.59), channel_id=1, source_target_pairs={{0,128},{128,0},{256,384},{384,256},{1,129},{129,1},{257,385},{385... | collective-permute-start | bytes 786440 | tf_op jit(solution)/shard_map/ppermute | solution.py:54
  127.2 9.3 %collective-permute-start.11 = (bf16[64,1024]{1,0:T(8,128)(2,1)S(1)}, bf16[64,1024]{1,0:T(8,128)(2,1)S(1)}, u32[]{:S(2)}, u32[]{:S(2)}) collective-permute-start(bf16[64,1024]{1,0:T(8,128)(2,1)S(1)} %select_bitcast_fusion), channel_id=1, source_target_pairs={{0,256},{128,384},{256,0},{384,128},{1,257},{129,385},{257,1},{385... | collective-permute-start | bytes 393224 | tf_op jit(solution)/shard_map/ppermute | solution.py:54
  147.6 17.8 %all-to-all-start.3 = ((bf16[16,4,1024]{2,1,0:T(4,128)(2,1)}), bf16[16,4,1024]{2,1,0:T(4,128)(2,1)S(1)}, u32[]{:S(2)}, u32[]{:S(2)}) async-start(bf16[16,4,1024]{2,1,0:T(4,128)(2,1)} %reshape.504), calls=%async_computation.3 | async-start | bytes 262144 | tf_op jit(solution)/shard_map/all_to_all | solution.py:44
  166.1 9.2 %all-to-all-start.4 = ((f32[4,4,1024]{2,1,0:T(4,128)}), f32[4,4,1024]{2,1,0:T(4,128)S(1)}, u32[]{:S(2)}, u32[]{:S(2)}) async-start(f32[4,4,1024]{2,1,0:T(4,128)} %broadcast_in_dim.8), calls=%async_computation.4 | async-start | bytes 131072 | tf_op jit(solution)/shard_map/all_to_all | solution.py:44
  176.0 0.6 copy-start.3

commit v7 on v6

--- a/solution.py
+++ b/solution.py
@@ -240,18 +240,28 @@
         come = flip(jnp.where(mine_set, first, second), axis, bit)
         return (stay.astype(f32) + come.astype(f32)).astype(bf)
 
+    def over_x(value, bit):
+        count = nx // bit
+        blocks = value.reshape(count // 2, 2, nz * share, value.shape[1])
+        flat = (count // 2 * nz * share, value.shape[1])
+        return halve(value, "x", x_here, bit, blocks[:, 0].reshape(flat), blocks[:, 1].reshape(flat))
+
+    def over_rep(value):
+        wide = value.shape[1] // 2
+        return halve(value, "rep", rep, 1, value[:, :wide], value[:, wide:])
+
     wide = total.shape[1] // 2
-    total = halve(total, "rep", rep, 1, total[:, :wide], total[:, wide:])
-    for bit in bits:
-        count = nx // bit
-        blocks = total.reshape(count // 2, 2, nz * share, total.shape[1])
-        flat = (count // 2 * nz * share, total.shape[1])
-        total = halve(total, "x", x_here, bit, blocks[:, 0].reshape(flat), blocks[:, 1].reshape(flat))
+    left, right = total[:, :wide], total[:, wide:]
+    left = over_x(over_rep(left), 1)
+    right = over_rep(over_x(right, 1))
+    for bit in bits[1:]:
+        left, right = over_x(left, bit), over_x(right, bit)
+    total = jnp.concatenate([left, right], axis=1)
     total, returned = lax.optimization_barrier((total, returned))
     far = swap(total.reshape(nz, share, wide), ("zh", "zl"))
     summed = jnp.sum(far.astype(f32), axis=0)
     last = swap(jnp.broadcast_to(summed[None], (nr, share, wide)), "rep")
-    last = jnp.concatenate([last[0] + last[2], last[1] + last[3]], axis=1)
+    last = jnp.concatenate([last[k, :, s] + last[k + 2, :, s] for s in (slice(None, wide // 2), slice(wide // 2, None)) for k in range(2)], axis=1)
     grad_perm = jnp.concatenate([mm(send[h], returned, TN, bf) for h in range(2)], axis=1)
     grad_z = mm(grad_perm, perm, NT, bf)
     lower = jnp.where(core == 0, last[:, : 3 * own], last[:, 3 * own : 6 * own])

time: 179 us -> 181 us (1.011)
  waiting for transfers between devices: 68 us -> 51.7 us
  starting transfers between devices: 85.1 us -> 101 us
  matrix products: 7.07 us -> 9.14 us
    all_to_all x5, waiting for transfers between devices: 35.8 us -> 22.4 us  [swap(): return lax.all_to_all(block, axis, split_axis=0, concat_axis=0, tiled=True)]
    all_to_all x5, starting transfers between devices: 48.7 us -> 56.7 us  [swap(): return lax.all_to_all(block, axis, split_axis=0, concat_axis=0, tiled=True)]
    ppermute x5 -> x8, starting transfers between devices: 14.6 us -> 22.3 us  [flip(): lax.ppermute(block, axis, [(here, here ^ bit) for here in range(count)])]
    dot_general x12, matrix products: 7.07 us -> 9.14 us  [mm(): lax.dot_general(left, right, (dims, ((), ())), preferred_element_type=jnp...]
    ppermute x5 -> x8, waiting for transfers between devices: 25.7 us -> 24 us  [flip(): lax.ppermute(block, axis, [(here, here ^ bit) for here in range(count)])]
  transfers between devices with their start and end apart: 18 -> 21, of which waited for: 13 -> 15; matrix products, arithmetic and copies ran while one was open for 6% -> 7% of each run, Pallas kernels for 0% -> 0%
where the time goes in v7:
time: 181 us; the launch traced here: 179 us
  starting transfers between devices  101 us (56%)
  waiting for transfers between devices  51.7 us (29%)
  matrix products  9.14 us (5%)
  Pallas kernels  7.29 us (4%)
  local copies, waits for them, and re-layouts  5.04 us (3%)
  other arithmetic  3.58 us (2%)
    all_to_all x5, starting transfers between devices, swap(): return lax.all_to_all(block, axis, split_axis=0, concat_axis=0, tiled=True)  56.7 us
    ppermute x8, waiting for transfers between devices, flip(): lax.ppermute(block, axis, [(here, here ^ bit) for here in range(count)])  24 us
    all_to_all x5, waiting for transfers between devices, swap(): return lax.all_to_all(block, axis, split_axis=0, concat_axis=0, tiled=True)  22.4 us
    ppermute x8, starting transfers between devices, flip(): lax.ppermute(block, axis, [(here, here ^ bit) for here in range(count)])  22.3 us
    ppermute x3, starting transfers between devices, shift(): lax.ppermute(block, axis, [(here, (here + step) % count) for here in rang...  11.5 us
    dot_general x12, matrix products, mm(): lax.dot_general(left, right, (dims, ((), ())), preferred_element_type=jnp...  9.14 us
    pallas_call x1, Pallas kernels, patch_step(): pl.pallas_call(patch_body, out_shape=[jax.ShapeDtypeStruct((rows, channel...  7.29 us
    ppermute x3, waiting for transfers between devices, shift(): lax.ppermute(block, axis, [(here, (here + step) % count) for here in rang...  4.09 us
  transfers between devices with their start and end apart: 21, of which 15 were waited for; matrix products, arithmetic and copies ran while one was open for 7% of the time, Pallas kernels for 0%

profile of v7, /device:TPU:6, one launch (start us, length us, event | category | flops | bytes accessed | tf_op | source)
XLA Modules:
  0.0 179.0 jit_solution(17386864715632082836)
XLA Ops:
  0.7 0.7 copy-done.3
  1.4 0.6 broadcast_in_dim.6
  2.0 15.2 %all-to-all-start = ((bf16[16,8,256]{2,1,0:T(8,128)(2,1)}), bf16[16,8,256]{2,1,0:T(8,128)(2,1)S(1)}, u32[]{:S(2)}, u32[]{:S(2)}) async-start(bf16[16,8,256]{2,1,0:T(8,128)(2,1)} %broadcast_in_dim.6), calls=%async_computation | async-start | bytes 131072 | tf_op jit(solution)/shard_map/all_to_all | solution.py:44
  17.2 1.9 %collective-permute-start = (bf16[256,512]{1,0:T(8,128)(2,1)}, bf16[256,512]{1,0:T(8,128)(2,1)S(1)}, u32[]{:S(2)}, u32[]{:S(2)}) collective-permute-start(bf16[256,512]{1,0:T(8,128)(2,1)} %bitcast.78), channel_id=1, source_target_pairs={{0,4},{4,0},{1,5},{5,1},{2,6},{6,2},{3,7},{7,3},{8,12},{12,8},{9,1... | collective-permute-start | bytes 786440 | tf_op jit(solution)/shard_map/ppermute | solution.py:220
  19.2 0.7 and_select_fusion.5
  19.8 0.7 fusion.76
  21.3 0.6 copy-done.4
  22.1 1.1 fusion
  23.3 6.7 %all-to-all-done = bf16[16,8,256]{2,1,0:T(8,128)(2,1)S(1)} async-done(((bf16[16,8,256]{2,1,0:T(8,128)(2,1)}), bf16[16,8,256]{2,1,0:T(8,128)(2,1)S(1)}, u32[]{:S(2)}, u32[]{:S(2)}) %all-to-all-start) | async-done | bytes 65568 | tf_op jit(solution)/shard_map/all_to_all | solution.py:44
  30.0 10.1 %all-to-all-start.1 = ((bf16[128,8,256]{2,1,0:T(8,128)(2,1)}), bf16[128,8,256]{2,1,0:T(8,128)(2,1)S(1)}, u32[]{:S(2)}, u32[]{:S(2)}) async-start(bf16[128,8,256]{2,1,0:T(8,128)(2,1)} %bitcast.9), calls=%async_computation.1 | async-start | bytes 1048576 | tf_op jit(solution)/shard_map/all_to_all | solution.py:44
  40.5 2.9 %collective-permute-start.1 = (bf16[128,256]{1,0:T(8,128)(2,1)S(1)}, bf16[128,256]{1,0:T(8,128)(2,1)S(1)}, u32[]{:S(2)}, u32[]{:S(2)}) collective-permute-start(bf16[128,256]{1,0:T(8,128)(2,1)S(1)} %bitcast.70), channel_id=1, source_target_pairs={{0,256},{128,384},{256,0},{384,128},{1,257},{129,385},{257,1},{385... | collective-permute-start | bytes 196616 | tf_op jit(solution)/shard_map/ppermute | solution.py:54
  43.4 5.0 %collective-permute-done.1 = bf16[128,256]{1,0:T(8,128)(2,1)S(1)} collective-permute-done((bf16[128,256]{1,0:T(8,128)(2,1)S(1)}, bf16[128,256]{1,0:T(8,128)(2,1)S(1)}, u32[]{:S(2)}, u32[]{:S(2)}) %collective-permute-start.1) | collective-permute-done | bytes 65568 | tf_op jit(solution)/shard_map/ppermute | solution.py:54
  48.5 2.4 %collective-permute-start.2 = (bf16[256,256]{1,0:T(8,128)(2,1)S(1)}, bf16[256,256]{1,0:T(8,128)(2,1)S(1)}, u32[]{:S(2)}, u32[]{:S(2)}) collective-permute-start(bf16[256,256]{1,0:T(8,128)(2,1)S(1)} %pad_maximum_fusion.5), channel_id=1, source_target_pairs={{0,128},{128,0},{256,384},{384,256},{1,129},{129,1},{257,385},{385... | collective-permute-start | bytes 393224 | tf_op jit(solution)/shard_map/ppermute | solution.py:54
  50.9 5.0 %collective-permute-done.2 = bf16[256,256]{1,0:T(8,128)(2,1)S(1)} collective-permute-done((bf16[256,256]{1,0:T(8,128)(2,1)S(1)}, bf16[256,256]{1,0:T(8,128)(2,1)S(1)}, u32[]{:S(2)}, u32[]{:S(2)}) %collective-permute-start.2) | collective-permute-done | bytes 131104 | tf_op jit(solution)/shard_map/ppermute | solution.py:54
  56.5 1.9 %collective-permute-start.3 = (bf16[256,256]{1,0:T(8,128)(2,1)S(1)}, bf16[256,256]{1,0:T(8,128)(2,1)S(1)}, u32[]{:S(2)}, u32[]{:S(2)}) collective-permute-start(bf16[256,256]{1,0:T(8,128)(2,1)S(1)} %get-tuple-element.30), channel_id=1, source_target_pairs={{0,4},{4,0},{1,5},{5,1},{2,6},{6,2},{3,7},{7,3},{8,12},{12,8},{9,1... | collective-permute-start | bytes 393224 | tf_op jit(solution)/shard_map/ppermute | solution.py:208
  58.4 1.3 collective-permute-done.3
  59.7 3.5 %collective-permute-start.4 = (bf16[512,256]{1,0:T(8,128)(2,1)S(1)}, bf16[512,256]{1,0:T(8,128)(2,1)S(1)}, u32[]{:S(2)}, u32[]{:S(2)}) collective-permute-start(bf16[512,256]{1,0:T(8,128)(2,1)S(1)} %pad_maximum_fusion.3.w0_ref), channel_id=1, source_target_pairs={{0,1},{1,2},{2,3},{3,0},{4,5},{5,6},{6,7},{7,4},{8,9},{9,10},{10,1... | collective-permute-start | bytes 786440 | tf_op jit(solution)/shard_map/ppermute | solution.py:49
  63.2 5.5 %collective-permute-start.5 = (bf16[512,256]{1,0:T(8,128)(2,1)S(1)}, bf16[512,256]{1,0:T(8,128)(2,1)S(1)}, u32[]{:S(2)}, u32[]{:S(2)}) collective-permute-start(bf16[512,256]{1,0:T(8,128)(2,1)S(1)} %pad_maximum_fusion.3.w0_ref), channel_id=1, source_target_pairs={{0,2},{1,3},{2,0},{3,1},{4,6},{5,7},{6,4},{7,5},{8,10},{9,11},{10,... | collective-permute-start | bytes 786440 | tf_op jit(solution)/shard_map/ppermute | solution.py:49
  68.7 2.6 %collective-permute-start.6 = (bf16[512,256]{1,0:T(8,128)(2,1)S(1)}, bf16[512,256]{1,0:T(8,128)(2,1)S(1)}, u32[]{:S(2)}, u32[]{:S(2)}) collective-permute-start(bf16[512,256]{1,0:T(8,128)(2,1)S(1)} %pad_maximum_fusion.3.w0_ref), channel_id=1, source_target_pairs={{0,3},{1,0},{2,1},{3,2},{4,7},{5,4},{6,5},{7,6},{8,11},{9,8},{10,9... | collective-permute-start | bytes 786440 | tf_op jit(solution)/shard_map/ppermute | solution.py:49
  71.3 0.9 all-to-all-done.1
  73.3 2.1 %collective-permute-start.7 = (bf16[256,512]{1,0:T(8,128)(2,1)S(1)}, bf16[256,512]{1,0:T(8,128)(2,1)S(1)}, u32[]{:S(2)}, u32[]{:S(2)}) collective-permute-start(bf16[256,512]{1,0:T(8,128)(2,1)S(1)} %pad_maximum_fusion.4.gown_ref), channel_id=1, source_target_pairs={{0,4},{4,0},{1,5},{5,1},{2,6},{6,2},{3,7},{7,3},{8,12},{12,8},{9,1... | collective-permute-start | bytes 786440 | tf_op jit(solution)/shard_map/ppermute | solution.py:223
  76.0 2.7 %collective-permute-done.5.w2_ref = bf16[512,256]{1,0:T(8,128)(2,1)S(1)} collective-permute-done((bf16[512,256]{1,0:T(8,128)(2,1)S(1)}, bf16[512,256]{1,0:T(8,128)(2,1)S(1)}, u32[]{:S(2)}, u32[]{:S(2)}) %collective-permute-start.5) | collective-permute-done | bytes 262176 | tf_op jit(solution)/shard_map/ppermute | solution.py:49
  78.7 1.3 collective-permute-done.6.w3_ref
  80.1 7.3 %shard_map.85 = (f32[256,512]{1,0:T(8,128)S(1)}, bf16[256,512]{1,0:T(8,128)(2,1)S(1)}, bf16[256,1024]{1,0:T(8,128)(2,1)S(1)}, bf16[256,1024]{1,0:T(8,128)(2,1)S(1)}) custom-call(s32[2]{0:T(128)S(1)} %pad_add_fusion.place_ref, bf16[512,512]{1,0:T(8,128)(2,1)S(1)} %convolution_convert_fusion.x_ref, bf16[512,256]{1,0:T(8,128)(2,1)S(1)} %pad_maximum_fusion.3.w0_ref, ...), custom_call_target="tpu_custom_call" | custom-call | tf_op jit(solution)/shard_map/pallas_call | solution.py:134
  87.4 2.1 %collective-permute-start.15 = (bf16[256,512]{1,0:T(8,128)(2,1)S(1)}, bf16[256,512]{1,0:T(8,128)(2,1)S(1)}, u32[]{:S(2)}, u32[]{:S(2)}) collective-permute-start(bf16[256,512]{1,0:T(8,128)(2,1)S(1)} %get-tuple-element.16), channel_id=1, source_target_pairs={{0,4},{4,0},{1,5},{5,1},{2,6},{6,2},{3,7},{7,3},{8,12},{12,8},{9,1... | collective-permute-start | bytes 786440 | tf_op jit(solution)/shard_map/ppermute | solution.py:227
  89.5 2.4 %collective-permute-start.8 = (bf16[256,1024]{1,0:T(8,128)(2,1)S(1)}, bf16[256,1024]{1,0:T(8,128)(2,1)S(1)}, u32[]{:S(2)}, u32[]{:S(2)}) collective-permute-start(bf16[256,1024]{1,0:T(8,128)(2,1)S(1)} %get-tuple-element.14), channel_id=1, source_target_pairs={{0,4},{4,0},{1,5},{5,1},{2,6},{6,2},{3,7},{7,3},{8,12},{12,8},{9,1... | collective-permute-start | bytes 1572872 | tf_op jit(solution)/shard_map/ppermute | solution.py:232
  92.0 0.7 fusion.80
  93.1 1.1 fusion.2
  94.2 16.8 %all-to-all-start.2 = ((bf16[128,8,256]{2,1,0:T(8,128)(2,1)}), bf16[128,8,256]{2,1,0:T(8,128)(2,1)}, u32[]{:S(2)}, u32[]{:S(2)}) async-start(bf16[128,8,256]{2,1,0:T(8,128)(2,1)} %fusion.2), calls=%async_computation.2 | async-start | bytes 1048576 | tf_op jit(solution)/shard_map/all_to_all | solution.py:44
  111.1 3.9 %collective-permute-start.9 = (bf16[256,512]{1,0:T(8,128)(2,1)S(1)}, bf16[256,512]{1,0:T(8,128)(2,1)S(1)}, u32[]{:S(2)}, u32[]{:S(2)}) collective-permute-start(bf16[256,512]{1,0:T(8,128)(2,1)S(1)} %broadcast_select_fusion.2), channel_id=1, source_target_pairs={{0,1},{1,0},{2,3},{3,2},{4,5},{5,4},{6,7},{7,6},{8,9},{9,8},{10,11... | collective-permute-start | bytes 786440 | tf_op jit(solution)/shard_map/ppermute | solution.py:54
  115.2 2.5 %collective-permute-start.12 = (bf16[128,1024]{1,0:T(8,128)(2,1)S(1)}, bf16[128,1024]{1,0:T(8,128)(2,1)S(1)}, u32[]{:S(2)}, u32[]{:S(2)}) collective-permute-start(bf16[128,1024]{1,0:T(8,128)(2,1)S(1)} %bitcast.75), channel_id=1, source_target_pairs={{0,128},{128,0},{256,384},{384,256},{1,129},{129,1},{257,385},{385... | collective-permute-start | bytes 786440 | tf_op jit(solution)/shard_map/ppermute | solution.py:54
  117.8 3.8 %collective-permute-done.9 = bf16[256,512]{1,0:T(8,128)(2,1)S(1)} collective-permute-done((bf16[256,512]{1,0:T(8,128)(2,1)S(1)}, bf16[256,512]{1,0:T(8,128)(2,1)S(1)}, u32[]{:S(2)}, u32[]{:S(2)}) %collective-permute-start.9) | collective-permute-done | bytes 262176 | tf_op jit(solution)/shard_map/ppermute | solution.py:54
  121.7 2.5 %collective-permute-start.10 = (bf16[128,512]{1,0:T(8,128)(2,1)S(1)}, bf16[128,512]{1,0:T(8,128)(2,1)S(1)}, u32[]{:S(2)}, u32[]{:S(2)}) collective-permute-start(bf16[128,512]{1,0:T(8,128)(2,1)S(1)} %bitcast.76), channel_id=1, source_target_pairs={{0,128},{128,0},{256,384},{384,256},{1,129},{129,1},{257,385},{385... | collective-permute-start | bytes 393224 | tf_op jit(solution)/shard_map/ppermute | solution.py:54
  124.3 3.7 %collective-permute-done.12 = bf16[128,1024]{1,0:T(8,128)(2,1)S(1)} collective-permute-done((bf16[128,1024]{1,0:T(8,128)(2,1)S(1)}, bf16[128,1024]{1,0:T(8,128)(2,1)S(1)}, u32[]{:S(2)}, u32[]{:S(2)}) %collective-permute-start.12) | collective-permute-done | bytes 262176 | tf_op jit(solution)/shard_map/ppermute | solution.py:54
  128.1 1.9 %collective-permute-start.13 = (bf16[128,512]{1,0:T(8,128)(2,1)S(1)}, bf16[128,512]{1,0:T(8,128)(2,1)S(1)}, u32[]{:S(2)}, u32[]{:S(2)}) collective-permute-start(bf16[128,512]{1,0:T(8,128)(2,1)S(1)} %broadcast_select_fusion.5), channel_id=1, source_target_pairs={{0,1},{1,0},{2,3},{3,2},{4,5},{5,4},{6,7},{7,6},{8,9},{9,8},{10,11... | collective-permute-start | bytes 393224 | tf_op jit(solution)/shard_map/ppermute | solution.py:54
  130.0 0.6 collective-permute-done.10
  130.7 2.9 %collective-permute-start.11 = (bf16[64,512]{1,0:T(8,128)(2,1)S(1)}, bf16[64,512]{1,0:T(8,128)(2,1)S(1)}, u32[]{:S(2)}, u32[]{:S(2)}) collective-permute-start(bf16[64,512]{1,0:T(8,128)(2,1)S(1)} %select_bitcast_fusion.1), channel_id=1, source_target_pairs={{0,256},{128,384},{256,0},{384,128},{1,257},{129,385},{257,1},{385... | collective-permute-start | bytes 196616 | tf_op jit(solution)/shard_map/ppermute | solution.py:54
  133.6 1.3 collective-permute-done.13
  135.0 3.1 %collective-permute-start.14 = (bf16[64,512]{1,0:T(8,128)(2,1)S(1)}, bf16[64,512]{1,0:T(8,128)(2,1)S(1)}, u32[]{:S(2)}, u32[]{:S(2)}) collective-permute-start(bf16[64,512]{1,0:T(8,128)(2,1)S(1)} %select_bitcast_fusion), channel_id=1, source_target_pairs={{0,256},{128,384},{256,0},{384,128},{1,257},{129,385},{257,1},{385... | collective-permute-start | bytes 196616 | tf_op jit(solution)/shard_map/ppermute | solution.py:54
  138.5 4.2 %collective-permute-done.14 = bf16[64,512]{1,0:T(8,128)(2,1)S(1)} collective-permute-done((bf16[64,512]{1,0:T(8,128)(2,1)S(1)}, bf16[64,512]{1,0:T(8,128)(2,1)S(1)}, u32[]{:S(2)}, u32[]{:S(2)}) %collective-permute-start.14) | collective-permute-done | bytes 65568 | tf_op jit(solution)/shard_map/ppermute | solution.py:54
  142.8 0.7 reshape.526
  143.5 11.2 %all-to-all-start.3 = ((bf16[16,4,1024]{2,1,0:T(4,128)(2,1)}), bf16[16,4,1024]{2,1,0:T(4,128)(2,1)S(1)}, u32[]{:S(2)}, u32[]{:S(2)}) async-start(bf16[16,4,1024]{2,1,0:T(4,128)(2,1)} %reshape.526), calls=%async_computation.3 | async-start | bytes 262144 | tf_op jit(solution)/shard_map/all_to_all | solution.py:44
  154.7 1.5 convolution_convert_fusion.3
  156.2 1.5 convolution_convert_fusion.2
  157.7 10.3 %all-to-all-done.3 = bf16[16,4,1024]{2,1,0:T(4,128)(2,1)S(1)} async-done(((bf16[16,4,1024]{2,1,0:T(4,128)(2,1)}), bf16[16,4,1024]{2,1,0:T(4,128)(2,1)S(1)}, u32[]{:S(2)}, u32[]{:S(2)}) %all-to-all-start.3) | async-done | bytes 131104 | tf_op jit(solution)/shard_map/all_to_all | solution.py:44
  168.7 3.4 %all-to-all-start.4 = ((f32[4,4,1024]{2,1,0:T(4,128)}), f32[4,4,1024]{2,1,0:T(4,128)S(1)}, u32[]{:S(2)}, u32[]{:S(2)}) async-start(f32[4,4,1024]{2,1,0:T(4,128)} %broadcast_in_dim.8), calls=%async_computation.4 | async-start | bytes 131072 | tf_op jit(solution)/shard_map/all_to_all | solution.py:44
  172.2 1.2 fusion.3
  173.3 4.4 %all-to-all-done.4 = f32[4,4,1024]{2,1,0:T(4,128)S(1)} async-done(((f32[4,4,1024]{2,1,0:T(4,128)}), f32[4,4,1024]{2,1,0:T(4,128)S(1)}, u32[]{:S(2)}, u32[]{:S(2)}) %all-to-all-start.4) | async-done | bytes 65568 | tf_op jit(solution)/shard_map/all_to_all | solution.py:44
  (83 shorter events, 7.0 us)
Async XLA Ops:
  0.6 0.7 copy-start.3
  0.6 20.3 %copy-start.2 = (bf16[1,256,512]{2,1,0:T(8,128)(2,1)S(1)}, bf16[1,256,512]{2,1,0:T(8,128)(2,1)}, u32[]{:S(2)}) copy-start(bf16[1,256,512]{2,1,0:T(8,128)(2,1)} %param.7) | copy-start | bytes 786436
  2.0 27.9 %all-to-all-start = ((bf16[16,8,256]{2,1,0:T(8,128)(2,1)}), bf16[16,8,256]{2,1,0:T(8,128)(2,1)S(1)}, u32[]{:S(2)}, u32[]{:S(2)}) async-start(bf16[16,8,256]{2,1,0:T(8,128)(2,1)} %broadcast_in_dim.6), calls=%async_computation | async-start | bytes 131072 | tf_op jit(solution)/shard_map/all_to_all | solution.py:44
  17.2 58.2 %collective-permute-start = (bf16[256,512]{1,0:T(8,128)(2,1)}, bf16[256,512]{1,0:T(8,128)(2,1)S(1)}, u32[]{:S(2)}, u32[]{:S(2)}) collective-permute-start(bf16[256,512]{1,0:T(8,128)(2,1)} %bitcast.78), channel_id=1, source_target_pairs={{0,4},{4,0},{1,5},{5,1},{2,6},{6,2},{3,7},{7,3},{8,12},{12,8},{9,1... | collective-permute-start | bytes 786440 | tf_op jit(solution)/shard_map/ppermute | solution.py:220
  21.3 0.7 copy-start.4
  30.0 42.2 %all-to-all-start.1 = ((bf16[128,8,256]{2,1,0:T(8,128)(2,1)}), bf16[128,8,256]{2,1,0:T(8,128)(2,1)S(1)}, u32[]{:S(2)}, u32[]{:S(2)}) async-start(bf16[128,8,256]{2,1,0:T(8,128)(2,1)} %bitcast.9), calls=%async_computation.1 | async-start | bytes 1048576 | tf_op jit(solution)/shard_map/all_to_all | solution.py:44
  40.5 8.0 %collective-permute-start.1 = (bf16[128,256]{1,0:T(8,128)(2,1)S(1)}, bf16[128,256]{1,0:T(8,128)(2,1)S(1)}, u32[]{:S(2)}, u32[]{:S(2)}) collective-permute-start(bf16[128,256]{1,0:T(8,128)(2,1)S(1)} %bitcast.70), channel_id=1, source_target_pairs={{0,256},{128,384},{256,0},{384,128},{1,257},{129,385},{257,1},{385... | collective-permute-start | bytes 196616 | tf_op jit(solution)/shard_map/ppermute | solution.py:54
  48.5 7.4 %collective-permute-start.2 = (bf16[256,256]{1,0:T(8,128)(2,1)S(1)}, bf16[256,256]{1,0:T(8,128)(2,1)S(1)}, u32[]{:S(2)}, u32[]{:S(2)}) collective-permute-start(bf16[256,256]{1,0:T(8,128)(2,1)S(1)} %pad_maximum_fusion.5), channel_id=1, source_target_pairs={{0,128},{128,0},{256,384},{384,256},{1,129},{129,1},{257,385},{385... | collective-permute-start | bytes 393224 | tf_op jit(solution)/shard_map/ppermute | solution.py:54
  56.5 3.2 %collective-permute-start.3 = (bf16[256,256]{1,0:T(8,128)(2,1)S(1)}, bf16[256,256]{1,0:T(8,128)(2,1)S(1)}, u32[]{:S(2)}, u32[]{:S(2)}) collective-permute-start(bf16[256,256]{1,0:T(8,128)(2,1)S(1)} %get-tuple-element.30), channel_id=1, source_target_pairs={{0,4},{4,0},{1,5},{5,1},{2,6},{6,2},{3,7},{7,3},{8,12},{12,8},{9,1... | collective-permute-start | bytes 393224 | tf_op jit(solution)/shard_map/ppermute | solution.py:208
  58.4 17.0 %copy-start.5 = (s32[512]{0:T(512)}, s32[512]{0:T(512)S(1)}, u32[]{:S(2)}) copy-start(s32[512]{0:T(512)S(1)} %fusion.48) | copy-start | bytes 6148
  59.7 16.2 %collective-permute-start.4 = (bf16[512,256]{1,0:T(8,128)(2,1)S(1)}, bf16[512,256]{1,0:T(8,128)(2,1)S(1)}, u32[]{:S(2)}, u32[]{:S(2)}) collective-permute-start(bf16[512,256]{1,0:T(8,128)(2,1)S(1)} %pad_maximum_fusion.3.w0_ref), channel_id=1, source_target_pairs={{0,1},{1,2},{2,3},{3,0},{4,5},{5,6},{6,7},{7,4},{8,9},{9,10},{10,1... | collective-permute-start | bytes 786440 | tf_op jit(solution)/shard_map/ppermute | solution.py:49
  63.2 15.5 %collective-permute-start.5 = (bf16[512,256]{1,0:T(8,128)(2,1)S(1)}, bf16[512,256]{1,0:T(8,128)(2,1)S(1)}, u32[]{:S(2)}, u32[]{:S(2)}) collective-permute-start(bf16[512,256]{1,0:T(8,128)(2,1)S(1)} %pad_maximum_fusion.3.w0_ref), channel_id=1, source_target_pairs={{0,2},{1,3},{2,0},{3,1},{4,6},{5,7},{6,4},{7,5},{8,10},{9,11},{10,... | collective-permute-start | bytes 786440 | tf_op jit(solution)/shard_map/ppermute | solution.py:49
  68.7 11.4 %collective-permute-start.6 = (bf16[512,256]{1,0:T(8,128)(2,1)S(1)}, bf16[512,256]{1,0:T(8,128)(2,1)S(1)}, u32[]{:S(2)}, u32[]{:S(2)}) collective-permute-start(bf16[512,256]{1,0:T(8,128)(2,1)S(1)} %pad_maximum_fusion.3.w0_ref), channel_id=1, source_target_pairs={{0,3},{1,0},{2,1},{3,2},{4,7},{5,4},{6,5},{7,6},{8,11},{9,8},{10,9... | collective-permute-start | bytes 786440 | tf_op jit(solution)/shard_map/ppermute | solution.py:49
  73.2 2.2 %copy-start.8 = (bf16[1,256,512]{2,1,0:T(8,128)(2,1)S(1)}, bf16[1,256,512]{2,1,0:T(8,128)(2,1)}, u32[]{:S(2)}) copy-start(bf16[1,256,512]{2,1,0:T(8,128)(2,1)} %param.6) | copy-start | bytes 786436
  73.3 6.8 %collective-permute-start.7 = (bf16[256,512]{1,0:T(8,128)(2,1)S(1)}, bf16[256,512]{1,0:T(8,128)(2,1)S(1)}, u32[]{:S(2)}, u32[]{:S(2)}) collective-permute-start(bf16[256,512]{1,0:T(8,128)(2,1)S(1)} %pad_maximum_fusion.4.gown_ref), channel_id=1, source_target_pairs={{0,4},{4,0},{1,5},{5,1},{2,6},{6,2},{3,7},{7,3},{8,12},{12,8},{9,1... | collective-permute-start | bytes 786440 | tf_op jit(solution)/shard_map/ppermute | solution.py:223
  87.4 5.3 %collective-permute-start.15 = (bf16[256,512]{1,0:T(8,128)(2,1)S(1)}, bf16[256,512]{1,0:T(8,128)(2,1)S(1)}, u32[]{:S(2)}, u32[]{:S(2)}) collective-permute-start(bf16[256,512]{1,0:T(8,128)(2,1)S(1)} %get-tuple-element.16), channel_id=1, source_target_pairs={{0,4},{4,0},{1,5},{5,1},{2,6},{6,2},{3,7},{7,3},{8,12},{12,8},{9,1... | collective-permute-start | bytes 786440 | tf_op jit(solution)/shard_map/ppermute | solution.py:227
  89.5 21.4 %collective-permute-start.8 = (bf16[256,1024]{1,0:T(8,128)(2,1)S(1)}, bf16[256,1024]{1,0:T(8,128)(2,1)S(1)}, u32[]{:S(2)}, u32[]{:S(2)}) collective-permute-start(bf16[256,1024]{1,0:T(8,128)(2,1)S(1)} %get-tuple-element.14), channel_id=1, source_target_pairs={{0,4},{4,0},{1,5},{5,1},{2,6},{6,2},{3,7},{7,3},{8,12},{12,8},{9,1... | collective-permute-start | bytes 1572872 | tf_op jit(solution)/shard_map/ppermute | solution.py:232
  94.2 48.6 %all-to-all-start.2 = ((bf16[128,8,256]{2,1,0:T(8,128)(2,1)}), bf16[128,8,256]{2,1,0:T(8,128)(2,1)}, u32[]{:S(2)}, u32[]{:S(2)}) async-start(bf16[128,8,256]{2,1,0:T(8,128)(2,1)} %fusion.2), calls=%async_computation.2 | async-start | bytes 1048576 | tf_op jit(solution)/shard_map/all_to_all | solution.py:44
  111.1 3.9 %copy-start = (bf16[128,256]{1,0:T(8,128)(2,1)S(1)}, bf16[128,256]{1,0:T(8,128)(2,1)}, u32[]{:S(2)}) copy-start(bf16[128,256]{1,0:T(8,128)(2,1)} %get-tuple-element.21) | copy-start | bytes 196612
  111.1 3.9 %copy-start.1 = (bf16[128,256]{1,0:T(8,128)(2,1)S(1)}, bf16[128,256]{1,0:T(8,128)(2,1)}, u32[]{:S(2)}) copy-start(bf16[128,256]{1,0:T(8,128)(2,1)} %get-tuple-element.22) | copy-start | bytes 196612
  111.1 10.5 %collective-permute-start.9 = (bf16[256,512]{1,0:T(8,128)(2,1)S(1)}, bf16[256,512]{1,0:T(8,128)(2,1)S(1)}, u32[]{:S(2)}, u32[]{:S(2)}) collective-permute-start(bf16[256,512]{1,0:T(8,128)(2,1)S(1)} %broadcast_select_fusion.2), channel_id=1, source_target_pairs={{0,1},{1,0},{2,3},{3,2},{4,5},{5,4},{6,7},{7,6},{8,9},{9,8},{10,11... | collective-permute-start | bytes 786440 | tf_op jit(solution)/shard_map/ppermute | solution.py:54
  115.2 12.7 %collective-permute-start.12 = (bf16[128,1024]{1,0:T(8,128)(2,1)S(1)}, bf16[128,1024]{1,0:T(8,128)(2,1)S(1)}, u32[]{:S(2)}, u32[]{:S(2)}) collective-permute-start(bf16[128,1024]{1,0:T(8,128)(2,1)S(1)} %bitcast.75), channel_id=1, source_target_pairs={{0,128},{128,0},{256,384},{384,256},{1,129},{129,1},{257,385},{385... | collective-permute-start | bytes 786440 | tf_op jit(solution)/shard_map/ppermute | solution.py:54
  121.7 8.9 %collective-permute-start.10 = (bf16[128,512]{1,0:T(8,128)(2,1)S(1)}, bf16[128,512]{1,0:T(8,128)(2,1)S(1)}, u32[]{:S(2)}, u32[]{:S(2)}) collective-permute-start(bf16[128,512]{1,0:T(8,128)(2,1)S(1)} %bitcast.76), channel_id=1, source_target_pairs={{0,128},{128,0},{256,384},{384,256},{1,129},{129,1},{257,385},{385... | collective-permute-start | bytes 393224 | tf_op jit(solution)/shard_map/ppermute | solution.py:54
  128.1 6.9 %collective-permute-start.13 = (bf16[128,512]{1,0:T(8,128)(2,1)S(1)}, bf16[128,512]{1,0:T(8,128)(2,1)S(1)}, u32[]{:S(2)}, u32[]{:S(2)}) collective-permute-start(bf16[128,512]{1,0:T(8,128)(2,1)S(1)} %broadcast_select_fusion.5), channel_id=1, source_target_pairs={{0,1},{1,0},{2,3},{3,2},{4,5},{5,4},{6,7},{7,6},{8,9},{9,8},{10,11... | collective-permute-start | bytes 393224 | tf_op jit(solution)/shard_map/ppermute | solution.py:54
  130.7 7.8 %collective-permute-start.11 = (bf16[64,512]{1,0:T(8,128)(2,1)S(1)}, bf16[64,512]{1,0:T(8,128)(2,1)S(1)}, u32[]{:S(2)}, u32[]{:S(2)}) collective-permute-start(bf16[64,512]{1,0:T(8,128)(2,1)S(1)} %select_bitcast_fusion.1), channel_id=1, source_target_pairs={{0,256},{128,384},{256,0},{384,128},{1,257},{129,385},{257,1},{385... | collective-permute-start | bytes 196616 | tf_op jit(solution)/shard_map/ppermute | solution.py:54
  135.0 7.7 %collective-permute-start.14 = (bf16[64,512]{1,0:T(8,128)(2,1)S(1)}, bf16[64,512]{1,0:T(8,128)(2,1)S(1)}, u32[]{:S(2)}, u32[]{:S(2)}) collective-permute-start(bf16[64,512]{1,0:T(8,128)(2,1)S(1)} %select_bitcast_fusion), channel_id=1, source_target_pairs={{0,256},{128,384},{256,0},{384,128},{1,257},{129,385},{257,1},{385... | collective-permute-start | bytes 196616 | tf_op jit(solution)/shard_map/ppermute | solution.py:54
  143.5 24.5 %all-to-all-start.3 = ((bf16[16,4,1024]{2,1,0:T(4,128)(2,1)}), bf16[16,4,1024]{2,1,0:T(4,128)(2,1)S(1)}, u32[]{:S(2)}, u32[]{:S(2)}) async-start(bf16[16,4,1024]{2,1,0:T(4,128)(2,1)} %reshape.526), calls=%async_computation.3 | async-start | bytes 262144 | tf_op jit(solution)/shard_map/all_to_all | solution.py:44
  168.7 3.4 %copy-start.6 = (s32[512]{0:T(512)S(1)}, s32[512]{0:T(512)}, u32[]{:S(2)}) copy-start(s32[512]{0:T(512)} %copy-done.5) | copy-start | bytes 6148
  168.7 9.0 %all-to-all-start.4 = ((f32[4,4,1024]{2,1,0:T(4,128)}), f32[4,4,1024]{2,1,0:T(4,128)S(1)}, u32[]{:S(2)}, u32[]{:S(2)}) async-start(f32[4,4,1024]{2,1,0:T(4,128)} %broadcast_in_dim.8), calls=%async_computation.4 | async-start | bytes 131072 | tf_op jit(solution)/shard_map/all_to_all | solution.py:44
  178.4 0.6 copy-start.7

commit v8 on v5

--- a/solution.py
+++ b/solution.py
@@ -233,31 +233,23 @@
     from_other = lax.ppermute(p_other, "core", pair)
     grad_hfeat = (p_own + from_other.astype(f32)).astype(bf)
     going = (mm(recv[0], grad_hfeat[:, :half], NN) + mm(recv[1], grad_hfeat[:, half:], NN)).astype(bf)
+    total = jnp.sum(swap(total, ("zh", "zl")).astype(f32), axis=0)
     total, going = lax.optimization_barrier((total, going))
     returned = swap(going.reshape(peers, chunk, half), ROWS)
-
-    for axis, here in (("zl", lax.axis_index("zl")), ("zh", lax.axis_index("zh"))):
-        size = lax.axis_size(axis)
-        bit = 1
-        while bit < size:
-            blocks = total.reshape(total.shape[0] // 2, 2, nc * share, own)
-            odd = here // bit % 2 == 1
-            stay = jnp.where(odd, blocks[:, 1], blocks[:, 0])
-            come = flip(jnp.where(odd, blocks[:, 0], blocks[:, 1]), axis, bit)
-            total = stay.astype(f32) + come.astype(f32)
-            total = total if total.shape[0] == 1 else total.astype(bf)
-            bit *= 2
-    total, returned = lax.optimization_barrier((total[0], returned))
     returned = returned.reshape(peers * chunk, half)
-    last = swap(jnp.broadcast_to(total[None], (nx * nr, nc * share, own)), ("x", "rep"))
-    last = last.reshape(nx, nr, nc, share, own)
-    here = lax.dynamic_index_in_dim(last, x_here, 0, keepdims=False)
-    partner = lax.dynamic_index_in_dim(last, (x_here + nx // 2) % nx, 0, keepdims=False)
-    cols = [here[p, c] for p in range(3) for c in range(nc)]
-    proj_cols = [lax.dynamic_index_in_dim(m[3], x_here // (nx // nc), 0, keepdims=False) for m in (here, partner)]
+
+    pieces = total.reshape(nc, share, own)
+    low = jnp.where(x_here // (nx // nc) == 0, pieces[0], pieces[1])
+    high = flip(jnp.where(x_here // (nx // nc) == 0, pieces[1], pieces[0]), "x", nx // 2)
+    ready = jnp.where(rep == 3, jnp.stack([low, high]), pieces).reshape(nc * share, own)
+    copies = jnp.stack([ready] + [shift(ready, "rep", k) for k in range(1, nr)])
+    cols = []
+    for p in range(4):
+        whole = lax.dynamic_index_in_dim(copies, (rep - p) % 4, 0, keepdims=False)
+        cols += [whole[:share], whole[share:]]
     grad_perm = jnp.concatenate([mm(send[h], returned, TN, bf) for h in range(2)], axis=1)
     grad_z = mm(grad_perm, perm, NT, bf)
-    return (grad_z[None], jnp.concatenate(cols, axis=1), jnp.concatenate(proj_cols, axis=1))
+    return (grad_z[None], jnp.concatenate(cols[:6], axis=1), jnp.concatenate(cols[6:], axis=1))
 
 
 def solution(mesh):

time: 199 us -> 183 us (0.920)
  starting transfers between devices: 105 us -> 89.5 us
  waiting for transfers between devices: 69.6 us -> 65.9 us
    ppermute x6 -> x3, waiting for transfers between devices: 38.4 us -> 14 us  [flip(): lax.ppermute(block, axis, [(here, here ^ bit) for here in range(count)])]
    ppermute x6 -> x3, starting transfers between devices: 30.9 us -> 8.29 us  [flip(): lax.ppermute(block, axis, [(here, here ^ bit) for here in range(count)])]
    all_to_all x5, waiting for transfers between devices: 25.8 us -> 43 us  [swap(): return lax.all_to_all(block, axis, split_axis=0, concat_axis=0, tiled=True)]
    ppermute x3 -> x6, starting transfers between devices: 11.5 us -> 21.5 us  [shift(): lax.ppermute(block, axis, [(here, (here + step) % count) for here in rang...]
    all_to_all x5, starting transfers between devices: 54.4 us -> 51.8 us  [swap(): return lax.all_to_all(block, axis, split_axis=0, concat_axis=0, tiled=True)]
    ppermute x3 -> x6, waiting for transfers between devices: 4.1 us -> 6.13 us  [shift(): lax.ppermute(block, axis, [(here, (here + step) % count) for here in rang...]
  transfers between devices with their start and end apart: 18 -> 18, of which waited for: 13 -> 13; matrix products, arithmetic and copies ran while one was open for 4% -> 5% of each run, Pallas kernels for 0% -> 0%
where the time goes in v8:
time: 183 us; the launch traced here: 180 us
  starting transfers between devices  89.5 us (49%)
  waiting for transfers between devices  65.9 us (36%)
  Pallas kernels  7.82 us (4%)
  matrix products  7.07 us (4%)
  other arithmetic  4.63 us (3%)
  local copies, waits for them, and re-layouts  4.17 us (2%)
    all_to_all x5, starting transfers between devices, swap(): return lax.all_to_all(block, axis, split_axis=0, concat_axis=0, tiled=True)  51.8 us
    all_to_all x5, waiting for transfers between devices, swap(): return lax.all_to_all(block, axis, split_axis=0, concat_axis=0, tiled=True)  43 us
    ppermute x6, starting transfers between devices, shift(): lax.ppermute(block, axis, [(here, (here + step) % count) for here in rang...  21.5 us
    ppermute x3, waiting for transfers between devices, flip(): lax.ppermute(block, axis, [(here, here ^ bit) for here in range(count)])  14 us
    ppermute x3, starting transfers between devices, flip(): lax.ppermute(block, axis, [(here, here ^ bit) for here in range(count)])  8.29 us
    pallas_call x1, Pallas kernels, patch_step(): pl.pallas_call(patch_body, out_shape=[jax.ShapeDtypeStruct((rows, channel...  7.82 us
    dot_general x12, matrix products, mm(): lax.dot_general(left, right, (dims, ((), ())), preferred_element_type=jnp...  7.07 us
    ppermute x6, waiting for transfers between devices, shift(): lax.ppermute(block, axis, [(here, (here + step) % count) for here in rang...  6.13 us
  transfers between devices with their start and end apart: 18, of which 13 were waited for; matrix products, arithmetic and copies ran while one was open for 5% of the time, Pallas kernels for 0%

profile of v8, /device:TPU:6, one launch (start us, length us, event | category | flops | bytes accessed | tf_op | source)
XLA Modules:
  0.0 180.3 jit_solution(15940897967073455259)
XLA Ops:
  0.7 0.7 copy-done.1
  1.4 0.6 broadcast_in_dim.4
  2.0 15.2 %all-to-all-start = ((bf16[16,8,256]{2,1,0:T(8,128)(2,1)}), bf16[16,8,256]{2,1,0:T(8,128)(2,1)S(1)}, u32[]{:S(2)}, u32[]{:S(2)}) async-start(bf16[16,8,256]{2,1,0:T(8,128)(2,1)} %broadcast_in_dim.4), calls=%async_computation | async-start | bytes 131072 | tf_op jit(solution)/shard_map/all_to_all | solution.py:44
  17.2 1.9 %collective-permute-start = (bf16[256,512]{1,0:T(8,128)(2,1)}, bf16[256,512]{1,0:T(8,128)(2,1)S(1)}, u32[]{:S(2)}, u32[]{:S(2)}) collective-permute-start(bf16[256,512]{1,0:T(8,128)(2,1)} %bitcast.86), channel_id=1, source_target_pairs={{0,4},{4,0},{1,5},{5,1},{2,6},{6,2},{3,7},{7,3},{8,12},{12,8},{9,1... | collective-permute-start | bytes 786440 | tf_op jit(solution)/shard_map/ppermute | solution.py:222
  19.2 0.7 and_select_fusion.5
  19.8 0.7 fusion.69
  21.3 0.6 copy-done.2
  22.1 1.1 fusion
  23.3 6.7 %all-to-all-done = bf16[16,8,256]{2,1,0:T(8,128)(2,1)S(1)} async-done(((bf16[16,8,256]{2,1,0:T(8,128)(2,1)}), bf16[16,8,256]{2,1,0:T(8,128)(2,1)S(1)}, u32[]{:S(2)}, u32[]{:S(2)}) %all-to-all-start) | async-done | bytes 65568 | tf_op jit(solution)/shard_map/all_to_all | solution.py:44
  30.0 10.1 %all-to-all-start.1 = ((bf16[128,8,256]{2,1,0:T(8,128)(2,1)}), bf16[128,8,256]{2,1,0:T(8,128)(2,1)S(1)}, u32[]{:S(2)}, u32[]{:S(2)}) async-start(bf16[128,8,256]{2,1,0:T(8,128)(2,1)} %bitcast.9), calls=%async_computation.1 | async-start | bytes 1048576 | tf_op jit(solution)/shard_map/all_to_all | solution.py:44
  40.5 2.9 %collective-permute-start.1 = (bf16[128,256]{1,0:T(8,128)(2,1)S(1)}, bf16[128,256]{1,0:T(8,128)(2,1)S(1)}, u32[]{:S(2)}, u32[]{:S(2)}) collective-permute-start(bf16[128,256]{1,0:T(8,128)(2,1)S(1)} %bitcast.73), channel_id=1, source_target_pairs={{0,256},{128,384},{256,0},{384,128},{1,257},{129,385},{257,1},{385... | collective-permute-start | bytes 196616 | tf_op jit(solution)/shard_map/ppermute | solution.py:54
  43.5 5.0 %collective-permute-done.1 = bf16[128,256]{1,0:T(8,128)(2,1)S(1)} collective-permute-done((bf16[128,256]{1,0:T(8,128)(2,1)S(1)}, bf16[128,256]{1,0:T(8,128)(2,1)S(1)}, u32[]{:S(2)}, u32[]{:S(2)}) %collective-permute-start.1) | collective-permute-done | bytes 65568 | tf_op jit(solution)/shard_map/ppermute | solution.py:54
  48.5 2.4 %collective-permute-start.2 = (bf16[256,256]{1,0:T(8,128)(2,1)S(1)}, bf16[256,256]{1,0:T(8,128)(2,1)S(1)}, u32[]{:S(2)}, u32[]{:S(2)}) collective-permute-start(bf16[256,256]{1,0:T(8,128)(2,1)S(1)} %pad_maximum_fusion.2), channel_id=1, source_target_pairs={{0,128},{128,0},{256,384},{384,256},{1,129},{129,1},{257,385},{385... | collective-permute-start | bytes 393224 | tf_op jit(solution)/shard_map/ppermute | solution.py:54
  51.0 5.0 %collective-permute-done.2 = bf16[256,256]{1,0:T(8,128)(2,1)S(1)} collective-permute-done((bf16[256,256]{1,0:T(8,128)(2,1)S(1)}, bf16[256,256]{1,0:T(8,128)(2,1)S(1)}, u32[]{:S(2)}, u32[]{:S(2)}) %collective-permute-start.2) | collective-permute-done | bytes 131104 | tf_op jit(solution)/shard_map/ppermute | solution.py:54
  56.5 1.9 %collective-permute-start.3 = (bf16[256,256]{1,0:T(8,128)(2,1)S(1)}, bf16[256,256]{1,0:T(8,128)(2,1)S(1)}, u32[]{:S(2)}, u32[]{:S(2)}) collective-permute-start(bf16[256,256]{1,0:T(8,128)(2,1)S(1)} %get-tuple-element.18), channel_id=1, source_target_pairs={{0,4},{4,0},{1,5},{5,1},{2,6},{6,2},{3,7},{7,3},{8,12},{12,8},{9,1... | collective-permute-start | bytes 393224 | tf_op jit(solution)/shard_map/ppermute | solution.py:210
  58.5 1.3 collective-permute-done.3
  59.8 3.5 %collective-permute-start.4 = (bf16[512,256]{1,0:T(8,128)(2,1)S(1)}, bf16[512,256]{1,0:T(8,128)(2,1)S(1)}, u32[]{:S(2)}, u32[]{:S(2)}) collective-permute-start(bf16[512,256]{1,0:T(8,128)(2,1)S(1)} %pad_maximum_fusion.w0_ref), channel_id=1, source_target_pairs={{0,1},{1,2},{2,3},{3,0},{4,5},{5,6},{6,7},{7,4},{8,9},{9,10},{10,1... | collective-permute-start | bytes 786440 | tf_op jit(solution)/shard_map/ppermute | solution.py:49
  63.3 5.5 %collective-permute-start.5 = (bf16[512,256]{1,0:T(8,128)(2,1)S(1)}, bf16[512,256]{1,0:T(8,128)(2,1)S(1)}, u32[]{:S(2)}, u32[]{:S(2)}) collective-permute-start(bf16[512,256]{1,0:T(8,128)(2,1)S(1)} %pad_maximum_fusion.w0_ref), channel_id=1, source_target_pairs={{0,2},{1,3},{2,0},{3,1},{4,6},{5,7},{6,4},{7,5},{8,10},{9,11},{10,... | collective-permute-start | bytes 786440 | tf_op jit(solution)/shard_map/ppermute | solution.py:49
  68.8 2.6 %collective-permute-start.6 = (bf16[512,256]{1,0:T(8,128)(2,1)S(1)}, bf16[512,256]{1,0:T(8,128)(2,1)S(1)}, u32[]{:S(2)}, u32[]{:S(2)}) collective-permute-start(bf16[512,256]{1,0:T(8,128)(2,1)S(1)} %pad_maximum_fusion.w0_ref), channel_id=1, source_target_pairs={{0,3},{1,0},{2,1},{3,2},{4,7},{5,4},{6,5},{7,6},{8,11},{9,8},{10,9... | collective-permute-start | bytes 786440 | tf_op jit(solution)/shard_map/ppermute | solution.py:49
  71.3 0.9 all-to-all-done.1
  72.2 0.5 convolution_convert_fusion.5
  72.7 0.5 convolution_convert_fusion.4
  73.3 2.1 %collective-permute-start.7 = (bf16[256,512]{1,0:T(8,128)(2,1)S(1)}, bf16[256,512]{1,0:T(8,128)(2,1)S(1)}, u32[]{:S(2)}, u32[]{:S(2)}) collective-permute-start(bf16[256,512]{1,0:T(8,128)(2,1)S(1)} %pad_maximum_fusion.1.gown_ref), channel_id=1, source_target_pairs={{0,4},{4,0},{1,5},{5,1},{2,6},{6,2},{3,7},{7,3},{8,12},{12,8},{9,1... | collective-permute-start | bytes 786440 | tf_op jit(solution)/shard_map/ppermute | solution.py:225
  75.4 0.6 convolution_convert_fusion.x_ref
  76.0 2.8 %collective-permute-done.5.w2_ref = bf16[512,256]{1,0:T(8,128)(2,1)S(1)} collective-permute-done((bf16[512,256]{1,0:T(8,128)(2,1)S(1)}, bf16[512,256]{1,0:T(8,128)(2,1)S(1)}, u32[]{:S(2)}, u32[]{:S(2)}) %collective-permute-start.5) | collective-permute-done | bytes 262176 | tf_op jit(solution)/shard_map/ppermute | solution.py:49
  78.8 1.3 collective-permute-done.6.w3_ref
  80.1 7.8 %shard_map.85 = (f32[256,512]{1,0:T(8,128)S(1)}, bf16[256,512]{1,0:T(8,128)(2,1)S(1)}, bf16[4,2,4,64,256]{4,3,2,1,0:T(8,128)(2,1)}) custom-call(s32[2]{0:T(128)S(1)} %pad_add_fusion.place_ref, bf16[512,512]{1,0:T(8,128)(2,1)S(1)} %convolution_convert_fusion.x_ref, bf16[512,256]{1,0:T(8,128)(2,1)S(1)} %pad_maximum_fusion.w0_ref, ...), custom_call_target="tpu_custom_call" | custom-call | tf_op jit(solution)/shard_map/pallas_call | solution.py:139
  87.9 6.8 %all-to-all-start.2 = ((bf16[32,64,256]{2,1,0:T(8,128)(2,1)}), bf16[32,64,256]{2,1,0:T(8,128)(2,1)S(1)}, u32[]{:S(2)}, u32[]{:S(2)}) async-start(bf16[32,64,256]{2,1,0:T(8,128)(2,1)} %bitcast.11), calls=%async_computation.2 | async-start | bytes 2097152 | tf_op jit(solution)/shard_map/all_to_all | solution.py:44
  94.8 2.1 %collective-permute-start.8 = (bf16[256,512]{1,0:T(8,128)(2,1)S(1)}, bf16[256,512]{1,0:T(8,128)(2,1)S(1)}, u32[]{:S(2)}, u32[]{:S(2)}) collective-permute-start(bf16[256,512]{1,0:T(8,128)(2,1)S(1)} %get-tuple-element.14), channel_id=1, source_target_pairs={{0,4},{4,0},{1,5},{5,1},{2,6},{6,2},{3,7},{7,3},{8,12},{12,8},{9,1... | collective-permute-start | bytes 786440 | tf_op jit(solution)/shard_map/ppermute | solution.py:233
  96.8 1.4 collective-permute-done.8
  98.6 11.2 %all-to-all-done.2 = bf16[32,64,256]{2,1,0:T(8,128)(2,1)S(1)} async-done(((bf16[32,64,256]{2,1,0:T(8,128)(2,1)}), bf16[32,64,256]{2,1,0:T(8,128)(2,1)S(1)}, u32[]{:S(2)}, u32[]{:S(2)}) %all-to-all-start.2) | async-done | bytes 1048608 | tf_op jit(solution)/shard_map/all_to_all | solution.py:44
  109.8 1.1 reshape.505
  110.9 1.7 reduce_sum.41
  112.7 0.7 copy.20
  113.3 11.9 %all-to-all-start.3 = ((bf16[16,8,256]{2,1,0:T(8,128)(2,1)}), bf16[16,8,256]{2,1,0:T(8,128)(2,1)S(1)}, u32[]{:S(2)}, u32[]{:S(2)}) async-start(bf16[16,8,256]{2,1,0:T(8,128)(2,1)} %copy.20), calls=%async_computation.3 | async-start | bytes 131072 | tf_op jit(solution)/shard_map/all_to_all | solution.py:44
  125.2 1.1 fusion.1
  126.3 11.9 %all-to-all-done.3 = bf16[16,8,256]{2,1,0:T(8,128)(2,1)S(1)} async-done(((bf16[16,8,256]{2,1,0:T(8,128)(2,1)}), bf16[16,8,256]{2,1,0:T(8,128)(2,1)S(1)}, u32[]{:S(2)}, u32[]{:S(2)}) %all-to-all-start.3) | async-done | bytes 65568 | tf_op jit(solution)/shard_map/all_to_all | solution.py:44
  138.2 7.8 %all-to-all-start.4 = ((bf16[128,8,256]{2,1,0:T(8,128)(2,1)}), bf16[128,8,256]{2,1,0:T(8,128)(2,1)S(1)}, u32[]{:S(2)}, u32[]{:S(2)}) async-start(bf16[128,8,256]{2,1,0:T(8,128)(2,1)} %bitcast.14), calls=%async_computation.4 | async-start | bytes 1048576 | tf_op jit(solution)/shard_map/all_to_all | solution.py:44
  146.1 2.9 %collective-permute-start.9 = (f32[4,256]{1,0:T(4,128)S(1)}, f32[4,256]{1,0:T(4,128)S(1)}, u32[]{:S(2)}, u32[]{:S(2)}) collective-permute-start(f32[4,256]{1,0:T(4,128)S(1)} %get-tuple-element.22), channel_id=1, source_target_pairs={{0,256},{128,384},{256,0},{384,128},{1,257},{129,385},{257,1},{385... | collective-permute-start | bytes 12296 | tf_op jit(solution)/shard_map/ppermute | solution.py:54
  149.0 4.1 %collective-permute-done.9 = f32[4,256]{1,0:T(4,128)S(1)} collective-permute-done((f32[4,256]{1,0:T(4,128)S(1)}, f32[4,256]{1,0:T(4,128)S(1)}, u32[]{:S(2)}, u32[]{:S(2)}) %collective-permute-start.9) | collective-permute-done | bytes 4128 | tf_op jit(solution)/shard_map/ppermute | solution.py:54
  153.1 2.2 %collective-permute-start.10 = (f32[8,256]{1,0:T(8,128)S(1)}, f32[8,256]{1,0:T(8,128)S(1)}, u32[]{:S(2)}, u32[]{:S(2)}) collective-permute-start(f32[8,256]{1,0:T(8,128)S(1)} %broadcast_select_fusion.2), channel_id=1, source_target_pairs={{0,1},{1,2},{2,3},{3,0},{4,5},{5,6},{6,7},{7,4},{8,9},{9,10},{10,1... | collective-permute-start | bytes 24584 | tf_op jit(solution)/shard_map/ppermute | solution.py:49
  155.4 4.3 %collective-permute-start.11 = (f32[8,256]{1,0:T(8,128)S(1)}, f32[8,256]{1,0:T(8,128)S(1)}, u32[]{:S(2)}, u32[]{:S(2)}) collective-permute-start(f32[8,256]{1,0:T(8,128)S(1)} %broadcast_select_fusion.2), channel_id=1, source_target_pairs={{0,2},{1,3},{2,0},{3,1},{4,6},{5,7},{6,4},{7,5},{8,10},{9,11},{10,... | collective-permute-start | bytes 24584 | tf_op jit(solution)/shard_map/ppermute | solution.py:49
  159.6 3.4 %collective-permute-start.12 = (f32[8,256]{1,0:T(8,128)S(1)}, f32[8,256]{1,0:T(8,128)S(1)}, u32[]{:S(2)}, u32[]{:S(2)}) collective-permute-start(f32[8,256]{1,0:T(8,128)S(1)} %broadcast_select_fusion.2), channel_id=1, source_target_pairs={{0,3},{1,0},{2,1},{3,2},{4,7},{5,4},{6,5},{7,6},{8,11},{9,8},{10,9... | collective-permute-start | bytes 24584 | tf_op jit(solution)/shard_map/ppermute | solution.py:49
  163.2 2.0 %collective-permute-done.12 = f32[8,256]{1,0:T(8,128)S(1)} collective-permute-done((f32[8,256]{1,0:T(8,128)S(1)}, f32[8,256]{1,0:T(8,128)S(1)}, u32[]{:S(2)}, u32[]{:S(2)}) %collective-permute-start.12) | collective-permute-done | bytes 8224 | tf_op jit(solution)/shard_map/ppermute | solution.py:49
  165.3 0.6 pad_maximum_fusion.5
  165.9 12.3 %all-to-all-done.4 = bf16[128,8,256]{2,1,0:T(8,128)(2,1)S(1)} async-done(((bf16[128,8,256]{2,1,0:T(8,128)(2,1)}), bf16[128,8,256]{2,1,0:T(8,128)(2,1)S(1)}, u32[]{:S(2)}, u32[]{:S(2)}) %all-to-all-start.4) | async-done | bytes 524320 | tf_op jit(solution)/shard_map/all_to_all | solution.py:44
  178.7 0.4 convolution_convert_fusion.2
  179.1 1.2 fusion.2
  (57 shorter events, 3.0 us)
Async XLA Ops:
  0.6 0.7 copy-start.1
  0.6 20.3 %copy-start = (bf16[1,256,512]{2,1,0:T(8,128)(2,1)S(1)}, bf16[1,256,512]{2,1,0:T(8,128)(2,1)}, u32[]{:S(2)}) copy-start(bf16[1,256,512]{2,1,0:T(8,128)(2,1)} %param.7) | copy-start | bytes 786436
  2.0 27.9 %all-to-all-start = ((bf16[16,8,256]{2,1,0:T(8,128)(2,1)}), bf16[16,8,256]{2,1,0:T(8,128)(2,1)S(1)}, u32[]{:S(2)}, u32[]{:S(2)}) async-start(bf16[16,8,256]{2,1,0:T(8,128)(2,1)} %broadcast_in_dim.4), calls=%async_computation | async-start | bytes 131072 | tf_op jit(solution)/shard_map/all_to_all | solution.py:44
  17.2 58.2 %collective-permute-start = (bf16[256,512]{1,0:T(8,128)(2,1)}, bf16[256,512]{1,0:T(8,128)(2,1)S(1)}, u32[]{:S(2)}, u32[]{:S(2)}) collective-permute-start(bf16[256,512]{1,0:T(8,128)(2,1)} %bitcast.86), channel_id=1, source_target_pairs={{0,4},{4,0},{1,5},{5,1},{2,6},{6,2},{3,7},{7,3},{8,12},{12,8},{9,1... | collective-permute-start | bytes 786440 | tf_op jit(solution)/shard_map/ppermute | solution.py:222
  21.3 0.7 copy-start.2
  30.0 42.3 %all-to-all-start.1 = ((bf16[128,8,256]{2,1,0:T(8,128)(2,1)}), bf16[128,8,256]{2,1,0:T(8,128)(2,1)S(1)}, u32[]{:S(2)}, u32[]{:S(2)}) async-start(bf16[128,8,256]{2,1,0:T(8,128)(2,1)} %bitcast.9), calls=%async_computation.1 | async-start | bytes 1048576 | tf_op jit(solution)/shard_map/all_to_all | solution.py:44
  40.5 8.0 %collective-permute-start.1 = (bf16[128,256]{1,0:T(8,128)(2,1)S(1)}, bf16[128,256]{1,0:T(8,128)(2,1)S(1)}, u32[]{:S(2)}, u32[]{:S(2)}) collective-permute-start(bf16[128,256]{1,0:T(8,128)(2,1)S(1)} %bitcast.73), channel_id=1, source_target_pairs={{0,256},{128,384},{256,0},{384,128},{1,257},{129,385},{257,1},{385... | collective-permute-start | bytes 196616 | tf_op jit(solution)/shard_map/ppermute | solution.py:54
  48.5 7.4 %collective-permute-start.2 = (bf16[256,256]{1,0:T(8,128)(2,1)S(1)}, bf16[256,256]{1,0:T(8,128)(2,1)S(1)}, u32[]{:S(2)}, u32[]{:S(2)}) collective-permute-start(bf16[256,256]{1,0:T(8,128)(2,1)S(1)} %pad_maximum_fusion.2), channel_id=1, source_target_pairs={{0,128},{128,0},{256,384},{384,256},{1,129},{129,1},{257,385},{385... | collective-permute-start | bytes 393224 | tf_op jit(solution)/shard_map/ppermute | solution.py:54
  56.5 3.2 %collective-permute-start.3 = (bf16[256,256]{1,0:T(8,128)(2,1)S(1)}, bf16[256,256]{1,0:T(8,128)(2,1)S(1)}, u32[]{:S(2)}, u32[]{:S(2)}) collective-permute-start(bf16[256,256]{1,0:T(8,128)(2,1)S(1)} %get-tuple-element.18), channel_id=1, source_target_pairs={{0,4},{4,0},{1,5},{5,1},{2,6},{6,2},{3,7},{7,3},{8,12},{12,8},{9,1... | collective-permute-start | bytes 393224 | tf_op jit(solution)/shard_map/ppermute | solution.py:210
  59.8 16.2 %collective-permute-start.4 = (bf16[512,256]{1,0:T(8,128)(2,1)S(1)}, bf16[512,256]{1,0:T(8,128)(2,1)S(1)}, u32[]{:S(2)}, u32[]{:S(2)}) collective-permute-start(bf16[512,256]{1,0:T(8,128)(2,1)S(1)} %pad_maximum_fusion.w0_ref), channel_id=1, source_target_pairs={{0,1},{1,2},{2,3},{3,0},{4,5},{5,6},{6,7},{7,4},{8,9},{9,10},{10,1... | collective-permute-start | bytes 786440 | tf_op jit(solution)/shard_map/ppermute | solution.py:49
  63.3 15.5 %collective-permute-start.5 = (bf16[512,256]{1,0:T(8,128)(2,1)S(1)}, bf16[512,256]{1,0:T(8,128)(2,1)S(1)}, u32[]{:S(2)}, u32[]{:S(2)}) collective-permute-start(bf16[512,256]{1,0:T(8,128)(2,1)S(1)} %pad_maximum_fusion.w0_ref), channel_id=1, source_target_pairs={{0,2},{1,3},{2,0},{3,1},{4,6},{5,7},{6,4},{7,5},{8,10},{9,11},{10,... | collective-permute-start | bytes 786440 | tf_op jit(solution)/shard_map/ppermute | solution.py:49
  68.8 11.4 %collective-permute-start.6 = (bf16[512,256]{1,0:T(8,128)(2,1)S(1)}, bf16[512,256]{1,0:T(8,128)(2,1)S(1)}, u32[]{:S(2)}, u32[]{:S(2)}) collective-permute-start(bf16[512,256]{1,0:T(8,128)(2,1)S(1)} %pad_maximum_fusion.w0_ref), channel_id=1, source_target_pairs={{0,3},{1,0},{2,1},{3,2},{4,7},{5,4},{6,5},{7,6},{8,11},{9,8},{10,9... | collective-permute-start | bytes 786440 | tf_op jit(solution)/shard_map/ppermute | solution.py:49
  73.3 2.2 %copy-start.4 = (bf16[1,256,512]{2,1,0:T(8,128)(2,1)S(1)}, bf16[1,256,512]{2,1,0:T(8,128)(2,1)}, u32[]{:S(2)}) copy-start(bf16[1,256,512]{2,1,0:T(8,128)(2,1)} %param.6) | copy-start | bytes 786436
  73.3 6.8 %collective-permute-start.7 = (bf16[256,512]{1,0:T(8,128)(2,1)S(1)}, bf16[256,512]{1,0:T(8,128)(2,1)S(1)}, u32[]{:S(2)}, u32[]{:S(2)}) collective-permute-start(bf16[256,512]{1,0:T(8,128)(2,1)S(1)} %pad_maximum_fusion.1.gown_ref), channel_id=1, source_target_pairs={{0,4},{4,0},{1,5},{5,1},{2,6},{6,2},{3,7},{7,3},{8,12},{12,8},{9,1... | collective-permute-start | bytes 786440 | tf_op jit(solution)/shard_map/ppermute | solution.py:225
  87.9 21.9 %all-to-all-start.2 = ((bf16[32,64,256]{2,1,0:T(8,128)(2,1)}), bf16[32,64,256]{2,1,0:T(8,128)(2,1)S(1)}, u32[]{:S(2)}, u32[]{:S(2)}) async-start(bf16[32,64,256]{2,1,0:T(8,128)(2,1)} %bitcast.11), calls=%async_computation.2 | async-start | bytes 2097152 | tf_op jit(solution)/shard_map/all_to_all | solution.py:44
  94.8 3.4 %collective-permute-start.8 = (bf16[256,512]{1,0:T(8,128)(2,1)S(1)}, bf16[256,512]{1,0:T(8,128)(2,1)S(1)}, u32[]{:S(2)}, u32[]{:S(2)}) collective-permute-start(bf16[256,512]{1,0:T(8,128)(2,1)S(1)} %get-tuple-element.14), channel_id=1, source_target_pairs={{0,4},{4,0},{1,5},{5,1},{2,6},{6,2},{3,7},{7,3},{8,12},{12,8},{9,1... | collective-permute-start | bytes 786440 | tf_op jit(solution)/shard_map/ppermute | solution.py:233
  113.3 24.9 %all-to-all-start.3 = ((bf16[16,8,256]{2,1,0:T(8,128)(2,1)}), bf16[16,8,256]{2,1,0:T(8,128)(2,1)S(1)}, u32[]{:S(2)}, u32[]{:S(2)}) async-start(bf16[16,8,256]{2,1,0:T(8,128)(2,1)} %copy.20), calls=%async_computation.3 | async-start | bytes 131072 | tf_op jit(solution)/shard_map/all_to_all | solution.py:44
  138.2 40.0 %all-to-all-start.4 = ((bf16[128,8,256]{2,1,0:T(8,128)(2,1)}), bf16[128,8,256]{2,1,0:T(8,128)(2,1)S(1)}, u32[]{:S(2)}, u32[]{:S(2)}) async-start(bf16[128,8,256]{2,1,0:T(8,128)(2,1)} %bitcast.14), calls=%async_computation.4 | async-start | bytes 1048576 | tf_op jit(solution)/shard_map/all_to_all | solution.py:44
  146.1 7.0 %collective-permute-start.9 = (f32[4,256]{1,0:T(4,128)S(1)}, f32[4,256]{1,0:T(4,128)S(1)}, u32[]{:S(2)}, u32[]{:S(2)}) collective-permute-start(f32[4,256]{1,0:T(4,128)S(1)} %get-tuple-element.22), channel_id=1, source_target_pairs={{0,256},{128,384},{256,0},{384,128},{1,257},{129,385},{257,1},{385... | collective-permute-start | bytes 12296 | tf_op jit(solution)/shard_map/ppermute | solution.py:54
  153.1 10.0 %collective-permute-start.10 = (f32[8,256]{1,0:T(8,128)S(1)}, f32[8,256]{1,0:T(8,128)S(1)}, u32[]{:S(2)}, u32[]{:S(2)}) collective-permute-start(f32[8,256]{1,0:T(8,128)S(1)} %broadcast_select_fusion.2), channel_id=1, source_target_pairs={{0,1},{1,2},{2,3},{3,0},{4,5},{5,6},{6,7},{7,4},{8,9},{9,10},{10,1... | collective-permute-start | bytes 24584 | tf_op jit(solution)/shard_map/ppermute | solution.py:49
  155.4 7.8 %collective-permute-start.11 = (f32[8,256]{1,0:T(8,128)S(1)}, f32[8,256]{1,0:T(8,128)S(1)}, u32[]{:S(2)}, u32[]{:S(2)}) collective-permute-start(f32[8,256]{1,0:T(8,128)S(1)} %broadcast_select_fusion.2), channel_id=1, source_target_pairs={{0,2},{1,3},{2,0},{3,1},{4,6},{5,7},{6,4},{7,5},{8,10},{9,11},{10,... | collective-permute-start | bytes 24584 | tf_op jit(solution)/shard_map/ppermute | solution.py:49
  159.6 5.5 %collective-permute-start.12 = (f32[8,256]{1,0:T(8,128)S(1)}, f32[8,256]{1,0:T(8,128)S(1)}, u32[]{:S(2)}, u32[]{:S(2)}) collective-permute-start(f32[8,256]{1,0:T(8,128)S(1)} %broadcast_select_fusion.2), channel_id=1, source_target_pairs={{0,3},{1,0},{2,1},{3,2},{4,7},{5,4},{6,5},{7,6},{8,11},{9,8},{10,9... | collective-permute-start | bytes 24584 | tf_op jit(solution)/shard_map/ppermute | solution.py:49
  165.3 13.4 %copy-start.3 = (f32[4,1536]{1,0:T(4,128)}, f32[4,1536]{1,0:T(4,128)S(1)}, u32[]{:S(2)}) copy-start(f32[4,1536]{1,0:T(4,128)S(1)} %constant_dynamic-update-slice_fusion.3) | copy-start | bytes 73732

commit v9 on v6

--- a/solution.py
+++ b/solution.py
@@ -13,6 +13,7 @@
 Z_LOW = 4
 CORES = 2
 ROWS = ("x", "zh", "zl", "core")
+CHIPS = ("x", "zh", "zl")
 INTERPRET = False
 NN = ((1,), (0,))
 NT = ((1,), (1,))
@@ -30,14 +31,12 @@
     return jnp.sum(jnp.logical_and(same_owner, earlier).astype(jnp.int32), axis=1)
 
 
-def slot_tables(owners, ranks, count):
-    base = owners * (2 * CAP * BLK) + ranks * BLK
+def slot_table(owners, ranks, count):
+    per_chip = CAP * CORES * CORES
+    base = (owners * per_chip + ranks) * BLK
     rows = (base[:, None] + jnp.arange(BLK, dtype=jnp.int32)[None, :]).reshape(-1)
-    slots = jnp.arange(count * 2 * CAP * BLK, dtype=jnp.int32)
-    return [
-        (slots[:, None] == (rows + half * CAP * BLK)[None, :]).astype(jnp.bfloat16)
-        for half in range(2)
-    ]
+    slots = jnp.arange(count * per_chip * BLK, dtype=jnp.int32)
+    return (slots[:, None] == rows[None, :]).astype(jnp.bfloat16)
 
 
 def swap(block, axis):
@@ -90,14 +89,13 @@
 
 
 def patch_body(
-    place_ref, x_ref, w0_ref, w1_ref, w2_ref, w3_ref, gown_ref, goth_ref, own_perm_ref,
+    place_ref, x_ref, w0_ref, w1_ref, w2_ref, w3_ref, gleft_ref, gright_ref, own_perm_ref,
     pown_ref, poth_ref, keep_ref, send_ref, w_ref, tq_ref, tp_ref,
 ):
     bf = jnp.bfloat16
     core, rep = place_ref[0], place_ref[1]
     channels = x_ref.shape[1]
     own = channels // CORES
-    rows = gown_ref.shape[0]
     part = own // CORES
     for k, ref in enumerate((w0_ref, w1_ref, w2_ref, w3_ref)):
         slot = lax.rem(rep + 4 - k, 4)
@@ -110,7 +108,7 @@
     own_perm = own_perm_ref[...]
     w_proj = mm(own_perm, jnp.concatenate(cols, axis=1), NN, bf)
     x = x_ref[...]
-    grad_pair = jnp.concatenate([gown_ref[...], goth_ref[...]], axis=0)
+    grad_pair = jnp.concatenate([gleft_ref[...], gright_ref[...]], axis=1)
     qkv = mm(x, w_qkv, NN, bf)
     grad_attn = mm(grad_pair, w_proj, NT, bf)
     attn_t, grad_qkv = attend(qkv, grad_attn, own, channels // HEADS)
@@ -122,20 +120,21 @@
         out_ref[:part, 3 * own :] = tp_ref[side, :, :own]
         out_ref[part:, 3 * own :] = tp_ref[side, :, own:]
     partial = mm(grad_qkv, w_qkv, NT)
-    pown_ref[...] = partial[:rows]
-    poth_ref[...] = partial[rows:].astype(bf)
-
-
-def patch_step(place, x, weights, gown, goth, own_perm):
-    bf = jnp.bfloat16
-    rows, channels = gown.shape
-    own = channels // CORES
+    left, right = partial[:, :own], partial[:, own:]
+    pown_ref[...] = jnp.where(core == 0, left, right)
+    poth_ref[...] = jnp.where(core == 0, right, left).astype(bf)
+
+
+def patch_step(place, x, weights, gleft, gright, own_perm):
+    bf = jnp.bfloat16
+    rows, own = gleft.shape
+    channels = own * CORES
     vmem = pl.BlockSpec(memory_space=pltpu.VMEM)
     return pl.pallas_call(
         patch_body,
         out_shape=[
-            jax.ShapeDtypeStruct((rows, channels), jnp.float32),
-            jax.ShapeDtypeStruct((rows, channels), bf),
+            jax.ShapeDtypeStruct((rows, own), jnp.float32),
+            jax.ShapeDtypeStruct((rows, own), bf),
             jax.ShapeDtypeStruct((own, 4 * own), bf),
             jax.ShapeDtypeStruct((own, 4 * own), bf),
         ],
@@ -148,7 +147,7 @@
         ],
         compiler_params=pltpu.CompilerParams(vmem_limit_bytes=48 << 20),
         interpret=INTERPRET,
-    )(place, x, *weights, gown, goth, own_perm)
+    )(place, x, *weights, gleft, gright, own_perm)
 
 
 def per_device(feats, grad_out, qkv_weight, proj_weight, to_hilbert, to_zorder):
@@ -156,7 +155,7 @@
     f32 = jnp.float32
     nx, zh, zl, nc, nr = (lax.axis_size(a) for a in ROWS + ("rep",))
     nz = zh * zl
-    peers = nx * nz * nc
+    chips = nx * nz
     x_here, core, rep = (lax.axis_index(a) for a in ("x", "core", "rep"))
     feature = feats[0]
     rows_dev, channels = feature.shape
@@ -165,7 +164,7 @@
     half = channels // 2
     share = qkv_weight.shape[0]
     blocks_dev = to_hilbert.shape[1]
-    chunk = 2 * CAP * BLK
+    chunk = CAP * nc * nc * BLK
     pair = [(0, 1), (1, 0)]
     bits = [1 << b for b in range(nx.bit_length() - 1)]
 
@@ -173,15 +172,25 @@
     mine = jnp.concatenate([mine[:, :own], mine[:, own:]], axis=0)
     plane = swap(jnp.broadcast_to(mine[None], (nz, 2 * share, own)), ("zh", "zl")).reshape(nz * 2 * share, own)
 
-    ids = jnp.arange(blocks_dev, dtype=jnp.int32)
-    target = to_hilbert[0] // blocks_dev
-    send = slot_tables(target, rank_within(ids, target), peers)
-    source = to_zorder[0] // blocks_dev
-    recv = slot_tables(source, rank_within(to_zorder[0], source), peers)
-    grad_z_in = grad_out[0]
-    outgoing = (mm(send[0], grad_z_in[:, :half], NN) + mm(send[1], grad_z_in[:, half:], NN)).astype(bf)
+    def both(block):
+        theirs = lax.ppermute(block, "core", pair)
+        return jnp.where(core == 0, block, theirs), jnp.where(core == 0, theirs, block)
+
+    lists = jnp.stack([to_hilbert[0], to_zorder[0]])
+    lists = jnp.concatenate(both(lists), axis=1)
+    forward_list, inverse_list = lists[0], lists[1]
+    ids = jnp.arange(nc * blocks_dev, dtype=jnp.int32)
+    target = forward_list // (nc * blocks_dev)
+    send = slot_table(target, rank_within(ids, target), chips)
+    source = inverse_list // (nc * blocks_dev)
+    recv = slot_table(source, rank_within(inverse_list, source), chips)
+    left, right = grad_out[0][:, :half], grad_out[0][:, half:]
+    stay = jnp.where(core == 0, left, right)
+    come = lax.ppermute(jnp.where(core == 0, right, left), "core", pair)
+    grad_z_in = jnp.concatenate([jnp.where(core == 0, stay, come), jnp.where(core == 0, come, stay)], axis=0)
+    outgoing = mm(send, grad_z_in, NN, bf)
     outgoing, plane = lax.optimization_barrier((outgoing, plane))
-    arrived = swap(outgoing.reshape(peers, chunk, half), ROWS).reshape(peers * chunk, half)
+    arrived = swap(outgoing.reshape(chips, chunk, half), CHIPS).reshape(chips * chunk, half)
 
     gathered = plane
     for bit in bits[::-1]:
@@ -208,6 +217,7 @@
     theirs = lax.ppermute(jnp.where(core == 0, picked[1], picked[0]), "core", pair)
     parts = jnp.concatenate([kept, theirs], axis=0)
     weights = [parts] + [shift(parts, "rep", k) for k in range(1, nr)]
+    weights[1], weights[2], weights[3], arrived = lax.optimization_barrier((*weights[1:], arrived))
 
     def order(count):
         nat = jnp.arange(count, dtype=jnp.int32)
@@ -217,17 +227,15 @@
 
     perm = order(channels)
     own_perm = order(own)
-    other_feat = lax.ppermute(feature, "core", pair)
-    x_pair = mm(jnp.concatenate([feature, other_feat], axis=0), perm, NN, bf)
-    grad_hil = jnp.concatenate([mm(recv[h], arrived, TN, bf) for h in range(2)], axis=1)
-    other_grad = lax.ppermute(grad_hil, "core", pair)
+    x_pair = mm(jnp.concatenate(both(feature), axis=0), perm, NN, bf)
+    grad_left, grad_right = both(mm(recv, arrived, TN, bf))
     place = jnp.stack([core, rep])
-    p_own, p_other, keep, away = patch_step(place, x_pair, weights, grad_hil, other_grad, own_perm)
+    p_own, p_other, keep, away = patch_step(place, x_pair, weights, grad_left, grad_right, own_perm)
 
     from_other = lax.ppermute(p_other, "core", pair)
     grad_hfeat = (p_own + from_other.astype(f32)).astype(bf)
-    going = (mm(recv[0], grad_hfeat[:, :half], NN) + mm(recv[1], grad_hfeat[:, half:], NN)).astype(bf)
-    returned = swap(going.reshape(peers, chunk, half), ROWS).reshape(peers * chunk, half)
+    going = mm(recv, grad_hfeat, NN, bf)
+    returned = swap(going.reshape(chips, chunk, half), CHIPS).reshape(chips * chunk, half)
 
     got = lax.ppermute(away, "core", pair)
     proj = [jnp.concatenate([m[:part, 3 * own :], m[part:, 3 * own :]], axis=1) for m in (keep, got)]
@@ -252,7 +260,10 @@
     summed = jnp.sum(far.astype(f32), axis=0)
     last = swap(jnp.broadcast_to(summed[None], (nr, share, wide)), "rep")
     last = jnp.concatenate([last[0] + last[2], last[1] + last[3]], axis=1)
-    grad_perm = jnp.concatenate([mm(send[h], returned, TN, bf) for h in range(2)], axis=1)
+    grad_half = mm(send, returned, TN, bf)
+    stay = jnp.where(core == 0, grad_half[:rows_dev], grad_half[rows_dev:])
+    come = lax.ppermute(jnp.where(core == 0, grad_half[rows_dev:], grad_half[:rows_dev]), "core", pair)
+    grad_perm = jnp.concatenate([jnp.where(core == 0, stay, come), jnp.where(core == 0, come, stay)], axis=1)
     grad_z = mm(grad_perm, perm, NT, bf)
     lower = jnp.where(core == 0, last[:, : 3 * own], last[:, 3 * own : 6 * own])
     upper = jnp.where(core == 0, last[:, 3 * own : 6 * own], last[:, : 3 * own])

time: 179 us -> 182 us (1.017)
  starting transfers between devices: 85.1 us -> 87.8 us
    ppermute x2 -> x5, starting transfers between devices: 3.97 us -> 10.1 us  [the longest x3 5.75 us: both(): theirs = lax.ppermute(block, 'core', pair)]
    all_to_all x5, starting transfers between devices: 48.7 us -> 44 us  [swap(): return lax.all_to_all(block, axis, split_axis=0, concat_axis=0, tiled=True)]
    ppermute x3, waiting for transfers between devices: 4.1 us -> 7.8 us  [shift(): lax.ppermute(block, axis, [(here, (here + step) % count) for here in rang...]
    ppermute x2 -> x5, waiting for transfers between devices: 0.01 us -> 2.18 us  [the longest x1 1.31 us: per_device(): lax.ppermute(jnp.where(core == 0, grad_half[rows_dev:], grad_half[:rows_d...]
    ppermute x5, waiting for transfers between devices: 25.7 us -> 23.8 us  [flip(): lax.ppermute(block, axis, [(here, here ^ bit) for here in range(count)])]
    dot_general x12 -> x8, matrix products: 7.07 us -> 6.43 us  [mm(): lax.dot_general(left, right, (dims, ((), ())), preferred_element_type=jnp...]
  transfers between devices with their start and end apart: 18 -> 21, of which waited for: 13 -> 13; matrix products, arithmetic and copies ran while one was open for 6% -> 6% of each run, Pallas kernels for 0% -> 0%
where the time goes in v9:
time: 182 us; the launch traced here: 180 us
  starting transfers between devices  87.8 us (48%)
  waiting for transfers between devices  69.7 us (38%)
  Pallas kernels  7.29 us (4%)
  matrix products  6.43 us (4%)
  other arithmetic  4.23 us (2%)
  local copies, waits for them, and re-layouts  3.67 us (2%)
    all_to_all x5, starting transfers between devices, swap(): return lax.all_to_all(block, axis, split_axis=0, concat_axis=0, tiled=True)  44 us
    all_to_all x5, waiting for transfers between devices, swap(): return lax.all_to_all(block, axis, split_axis=0, concat_axis=0, tiled=True)  34.9 us
    ppermute x5, waiting for transfers between devices, flip(): lax.ppermute(block, axis, [(here, here ^ bit) for here in range(count)])  23.8 us
    ppermute x5, starting transfers between devices, flip(): lax.ppermute(block, axis, [(here, here ^ bit) for here in range(count)])  16 us
    ppermute x3, starting transfers between devices, shift(): lax.ppermute(block, axis, [(here, (here + step) % count) for here in rang...  11.6 us
    ppermute x3, waiting for transfers between devices, shift(): lax.ppermute(block, axis, [(here, (here + step) % count) for here in rang...  7.8 us
    pallas_call x1, Pallas kernels, patch_step(): pl.pallas_call(patch_body, out_shape=[jax.ShapeDtypeStruct((rows, own), j...  7.29 us
    dot_general x8, matrix products, mm(): lax.dot_general(left, right, (dims, ((), ())), preferred_element_type=jnp...  6.43 us
  transfers between devices with their start and end apart: 21, of which 13 were waited for; matrix products, arithmetic and copies ran while one was open for 6% of the time, Pallas kernels for 0%

profile of v9, /device:TPU:6, one launch (start us, length us, event | category | flops | bytes accessed | tf_op | source)
XLA Modules:
  0.0 180.5 jit_solution(16444299810396850753)
XLA Ops:
  0.7 0.7 pad_add_fusion.1
  1.4 1.9 %collective-permute-start = (s32[2,128]{1,0:T(2,128)S(1)}, s32[2,128]{1,0:T(2,128)S(1)}, u32[]{:S(2)}, u32[]{:S(2)}) collective-permute-start(s32[2,128]{1,0:T(2,128)S(1)} %pad_add_fusion.1), channel_id=1, source_target_pairs={{0,4},{4,0},{1,5},{5,1},{2,6},{6,2},{3,7},{7,3},{8,12},{12,8},{9,1... | collective-permute-start | bytes 3080 | tf_op jit(solution)/shard_map/ppermute | solution.py:176
  3.3 1.0 broadcast_select_fusion.17
  4.4 2.4 %collective-permute-start.2 = (bf16[256,256]{1,0:T(8,128)(2,1)S(1)}, bf16[256,256]{1,0:T(8,128)(2,1)S(1)}, u32[]{:S(2)}, u32[]{:S(2)}) collective-permute-start(bf16[256,256]{1,0:T(8,128)(2,1)S(1)} %broadcast_select_fusion.17), channel_id=1, source_target_pairs={{0,4},{4,0},{1,5},{5,1},{2,6},{6,2},{3,7},{7,3},{8,12},{12,8},{9,1... | collective-permute-start | bytes 393224 | tf_op jit(solution)/shard_map/ppermute | solution.py:189
  6.8 0.7 fusion.36
  7.5 0.6 broadcast_in_dim.6
  8.1 15.2 %all-to-all-start = ((bf16[16,8,256]{2,1,0:T(8,128)(2,1)}), bf16[16,8,256]{2,1,0:T(8,128)(2,1)S(1)}, u32[]{:S(2)}, u32[]{:S(2)}) async-start(bf16[16,8,256]{2,1,0:T(8,128)(2,1)} %broadcast_in_dim.6), calls=%async_computation | async-start | bytes 131072 | tf_op jit(solution)/shard_map/all_to_all | solution.py:43
  23.4 1.9 %collective-permute-start.1 = (bf16[256,512]{1,0:T(8,128)(2,1)S(1)}, bf16[256,512]{1,0:T(8,128)(2,1)S(1)}, u32[]{:S(2)}, u32[]{:S(2)}) collective-permute-start(bf16[256,512]{1,0:T(8,128)(2,1)S(1)} %bitcast.46), channel_id=1, source_target_pairs={{0,4},{4,0},{1,5},{5,1},{2,6},{6,2},{3,7},{7,3},{8,12},{12,8},{9,1... | collective-permute-start | bytes 786440 | tf_op jit(solution)/shard_map/ppermute | solution.py:176
  26.0 1.3 fusion.4
  27.3 9.1 %all-to-all-done = bf16[16,8,256]{2,1,0:T(8,128)(2,1)S(1)} async-done(((bf16[16,8,256]{2,1,0:T(8,128)(2,1)}), bf16[16,8,256]{2,1,0:T(8,128)(2,1)S(1)}, u32[]{:S(2)}, u32[]{:S(2)}) %all-to-all-start) | async-done | bytes 65568 | tf_op jit(solution)/shard_map/all_to_all | solution.py:43
  36.4 6.5 %all-to-all-start.1 = ((bf16[64,16,256]{2,1,0:T(8,128)(2,1)}), bf16[64,16,256]{2,1,0:T(8,128)(2,1)S(1)}, u32[]{:S(2)}, u32[]{:S(2)}) async-start(bf16[64,16,256]{2,1,0:T(8,128)(2,1)} %bitcast.7), calls=%async_computation.1 | async-start | bytes 1048576 | tf_op jit(solution)/shard_map/all_to_all | solution.py:43
  43.0 3.2 %collective-permute-start.3 = (bf16[128,256]{1,0:T(8,128)(2,1)S(1)}, bf16[128,256]{1,0:T(8,128)(2,1)S(1)}, u32[]{:S(2)}, u32[]{:S(2)}) collective-permute-start(bf16[128,256]{1,0:T(8,128)(2,1)S(1)} %bitcast.41), channel_id=1, source_target_pairs={{0,256},{128,384},{256,0},{384,128},{1,257},{129,385},{257,1},{385... | collective-permute-start | bytes 196616 | tf_op jit(solution)/shard_map/ppermute | solution.py:53
  46.2 4.7 %collective-permute-done.3 = bf16[128,256]{1,0:T(8,128)(2,1)S(1)} collective-permute-done((bf16[128,256]{1,0:T(8,128)(2,1)S(1)}, bf16[128,256]{1,0:T(8,128)(2,1)S(1)}, u32[]{:S(2)}, u32[]{:S(2)}) %collective-permute-start.3) | collective-permute-done | bytes 65568 | tf_op jit(solution)/shard_map/ppermute | solution.py:53
  51.0 2.4 %collective-permute-start.4 = (bf16[256,256]{1,0:T(8,128)(2,1)S(1)}, bf16[256,256]{1,0:T(8,128)(2,1)S(1)}, u32[]{:S(2)}, u32[]{:S(2)}) collective-permute-start(bf16[256,256]{1,0:T(8,128)(2,1)S(1)} %pad_maximum_fusion.4), channel_id=1, source_target_pairs={{0,128},{128,0},{256,384},{384,256},{1,129},{129,1},{257,385},{385... | collective-permute-start | bytes 393224 | tf_op jit(solution)/shard_map/ppermute | solution.py:53
  53.4 5.2 %collective-permute-done.4 = bf16[256,256]{1,0:T(8,128)(2,1)S(1)} collective-permute-done((bf16[256,256]{1,0:T(8,128)(2,1)S(1)}, bf16[256,256]{1,0:T(8,128)(2,1)S(1)}, u32[]{:S(2)}, u32[]{:S(2)}) %collective-permute-start.4) | collective-permute-done | bytes 131104 | tf_op jit(solution)/shard_map/ppermute | solution.py:53
  59.1 1.9 %collective-permute-start.5 = (bf16[256,256]{1,0:T(8,128)(2,1)S(1)}, bf16[256,256]{1,0:T(8,128)(2,1)S(1)}, u32[]{:S(2)}, u32[]{:S(2)}) collective-permute-start(bf16[256,256]{1,0:T(8,128)(2,1)S(1)} %get-tuple-element.48), channel_id=1, source_target_pairs={{0,4},{4,0},{1,5},{5,1},{2,6},{6,2},{3,7},{7,3},{8,12},{12,8},{9,1... | collective-permute-start | bytes 393224 | tf_op jit(solution)/shard_map/ppermute | solution.py:217
  61.3 1.1 collective-permute-done.5
  62.4 3.5 %collective-permute-start.6 = (bf16[512,256]{1,0:T(8,128)(2,1)S(1)}, bf16[512,256]{1,0:T(8,128)(2,1)S(1)}, u32[]{:S(2)}, u32[]{:S(2)}) collective-permute-start(bf16[512,256]{1,0:T(8,128)(2,1)S(1)} %pad_maximum_fusion.3.w0_ref), channel_id=1, source_target_pairs={{0,1},{1,2},{2,3},{3,0},{4,5},{5,6},{6,7},{7,4},{8,9},{9,10},{10,1... | collective-permute-start | bytes 786440 | tf_op jit(solution)/shard_map/ppermute | solution.py:48
  65.9 4.8 %collective-permute-start.7 = (bf16[512,256]{1,0:T(8,128)(2,1)S(1)}, bf16[512,256]{1,0:T(8,128)(2,1)S(1)}, u32[]{:S(2)}, u32[]{:S(2)}) collective-permute-start(bf16[512,256]{1,0:T(8,128)(2,1)S(1)} %pad_maximum_fusion.3.w0_ref), channel_id=1, source_target_pairs={{0,2},{1,3},{2,0},{3,1},{4,6},{5,7},{6,4},{7,5},{8,10},{9,11},{10,... | collective-permute-start | bytes 786440 | tf_op jit(solution)/shard_map/ppermute | solution.py:48
  70.7 3.3 %collective-permute-start.8 = (bf16[512,256]{1,0:T(8,128)(2,1)S(1)}, bf16[512,256]{1,0:T(8,128)(2,1)S(1)}, u32[]{:S(2)}, u32[]{:S(2)}) collective-permute-start(bf16[512,256]{1,0:T(8,128)(2,1)S(1)} %pad_maximum_fusion.3.w0_ref), channel_id=1, source_target_pairs={{0,3},{1,0},{2,1},{3,2},{4,7},{5,4},{6,5},{7,6},{8,11},{9,8},{10,9... | collective-permute-start | bytes 786440 | tf_op jit(solution)/shard_map/ppermute | solution.py:48
  74.2 6.5 %collective-permute-done.7.w2_ref = bf16[512,256]{1,0:T(8,128)(2,1)S(1)} collective-permute-done((bf16[512,256]{1,0:T(8,128)(2,1)S(1)}, bf16[512,256]{1,0:T(8,128)(2,1)S(1)}, u32[]{:S(2)}, u32[]{:S(2)}) %collective-permute-start.7) | collective-permute-done | bytes 262176 | tf_op jit(solution)/shard_map/ppermute | solution.py:48
  80.7 1.3 collective-permute-done.8.w3_ref
  82.1 0.8 fusion.7
  82.8 1.9 %collective-permute-start.9 = (bf16[512,256]{1,0:T(8,128)(2,1)S(1)}, bf16[512,256]{1,0:T(8,128)(2,1)S(1)}, u32[]{:S(2)}, u32[]{:S(2)}) collective-permute-start(bf16[512,256]{1,0:T(8,128)(2,1)S(1)} %fusion.7), channel_id=1, source_target_pairs={{0,4},{4,0},{1,5},{5,1},{2,6},{6,2},{3,7},{7,3},{8,12},{12,8},{9,1... | collective-permute-start | bytes 786440 | tf_op jit(solution)/shard_map/ppermute | solution.py:176
  85.4 0.9 collective-permute-done.9
  86.3 7.3 %shard_map.85 = (f32[512,256]{1,0:T(8,128)S(1)}, bf16[512,256]{1,0:T(8,128)(2,1)S(1)}, bf16[256,1024]{1,0:T(8,128)(2,1)S(1)}, bf16[256,1024]{1,0:T(8,128)(2,1)S(1)}) custom-call(s32[2]{0:T(128)S(1)} %pad_add_fusion.2.place_ref, bf16[512,512]{1,0:T(8,128)(2,1)S(1)} %convolution_convert_fusion.x_ref, bf16[512,256]{1,0:T(8,128)(2,1)S(1)} %pad_maximum_fusion.3.w0_ref, ...), custom_call_target="tpu_custom_call" | custom-call | tf_op jit(solution)/shard_map/pallas_call | solution.py:133
  93.6 2.1 %collective-permute-start.10 = (bf16[256,1024]{1,0:T(8,128)(2,1)S(1)}, bf16[256,1024]{1,0:T(8,128)(2,1)S(1)}, u32[]{:S(2)}, u32[]{:S(2)}) collective-permute-start(bf16[256,1024]{1,0:T(8,128)(2,1)S(1)} %get-tuple-element.21), channel_id=1, source_target_pairs={{0,4},{4,0},{1,5},{5,1},{2,6},{6,2},{3,7},{7,3},{8,12},{12,8},{9,1... | collective-permute-start | bytes 1572872 | tf_op jit(solution)/shard_map/ppermute | solution.py:240
  95.7 2.3 %collective-permute-start.14 = (bf16[512,256]{1,0:T(8,128)(2,1)S(1)}, bf16[512,256]{1,0:T(8,128)(2,1)S(1)}, u32[]{:S(2)}, u32[]{:S(2)}) collective-permute-start(bf16[512,256]{1,0:T(8,128)(2,1)S(1)} %get-tuple-element.24), channel_id=1, source_target_pairs={{0,4},{4,0},{1,5},{5,1},{2,6},{6,2},{3,7},{7,3},{8,12},{12,8},{9,1... | collective-permute-start | bytes 786440 | tf_op jit(solution)/shard_map/ppermute | solution.py:235
  98.3 4.6 %collective-permute-start.11 = (bf16[256,1024]{1,0:T(8,128)(2,1)S(1)}, bf16[256,1024]{1,0:T(8,128)(2,1)S(1)}, u32[]{:S(2)}, u32[]{:S(2)}) collective-permute-start(bf16[256,1024]{1,0:T(8,128)(2,1)S(1)} %broadcast_select_fusion), channel_id=1, source_target_pairs={{0,1},{1,0},{2,3},{3,2},{4,5},{5,4},{6,7},{7,6},{8,9},{9,8},{10,11... | collective-permute-start | bytes 1572872 | tf_op jit(solution)/shard_map/ppermute | solution.py:53
  102.9 1.3 fusion.5
  104.2 15.4 %all-to-all-start.2 = ((bf16[64,16,256]{2,1,0:T(8,128)(2,1)}), bf16[64,16,256]{2,1,0:T(8,128)(2,1)S(1)}, u32[]{:S(2)}, u32[]{:S(2)}) async-start(bf16[64,16,256]{2,1,0:T(8,128)(2,1)} %bitcast.17), calls=%async_computation.2 | async-start | bytes 1048576 | tf_op jit(solution)/shard_map/all_to_all | solution.py:43
  120.0 2.7 %collective-permute-start.12 = (bf16[128,1024]{1,0:T(8,128)(2,1)S(1)}, bf16[128,1024]{1,0:T(8,128)(2,1)S(1)}, u32[]{:S(2)}, u32[]{:S(2)}) collective-permute-start(bf16[128,1024]{1,0:T(8,128)(2,1)S(1)} %bitcast.47), channel_id=1, source_target_pairs={{0,128},{128,0},{256,384},{384,256},{1,129},{129,1},{257,385},{385... | collective-permute-start | bytes 786440 | tf_op jit(solution)/shard_map/ppermute | solution.py:53
  122.7 8.0 %collective-permute-done.12 = bf16[128,1024]{1,0:T(8,128)(2,1)S(1)} collective-permute-done((bf16[128,1024]{1,0:T(8,128)(2,1)S(1)}, bf16[128,1024]{1,0:T(8,128)(2,1)S(1)}, u32[]{:S(2)}, u32[]{:S(2)}) %collective-permute-start.12) | collective-permute-done | bytes 262176 | tf_op jit(solution)/shard_map/ppermute | solution.py:53
  130.8 3.2 %collective-permute-start.13 = (bf16[64,1024]{1,0:T(8,128)(2,1)S(1)}, bf16[64,1024]{1,0:T(8,128)(2,1)S(1)}, u32[]{:S(2)}, u32[]{:S(2)}) collective-permute-start(bf16[64,1024]{1,0:T(8,128)(2,1)S(1)} %select_bitcast_fusion), channel_id=1, source_target_pairs={{0,256},{128,384},{256,0},{384,128},{1,257},{129,385},{257,1},{385... | collective-permute-start | bytes 393224 | tf_op jit(solution)/shard_map/ppermute | solution.py:53
  134.0 5.8 %collective-permute-done.13 = bf16[64,1024]{1,0:T(8,128)(2,1)S(1)} collective-permute-done((bf16[64,1024]{1,0:T(8,128)(2,1)S(1)}, bf16[64,1024]{1,0:T(8,128)(2,1)S(1)}, u32[]{:S(2)}, u32[]{:S(2)}) %collective-permute-start.13) | collective-permute-done | bytes 131104 | tf_op jit(solution)/shard_map/ppermute | solution.py:53
  139.9 11.5 %all-to-all-done.2 = bf16[64,16,256]{2,1,0:T(8,128)(2,1)S(1)} async-done(((bf16[64,16,256]{2,1,0:T(8,128)(2,1)}), bf16[64,16,256]{2,1,0:T(8,128)(2,1)S(1)}, u32[]{:S(2)}, u32[]{:S(2)}) %all-to-all-start.2) | async-done | bytes 524320 | tf_op jit(solution)/shard_map/all_to_all | solution.py:43
  151.4 0.7 reshape.484
  152.1 3.5 %all-to-all-start.3 = ((bf16[16,4,1024]{2,1,0:T(4,128)(2,1)}), bf16[16,4,1024]{2,1,0:T(4,128)(2,1)S(1)}, u32[]{:S(2)}, u32[]{:S(2)}) async-start(bf16[16,4,1024]{2,1,0:T(4,128)(2,1)} %reshape.484), calls=%async_computation.3 | async-start | bytes 262144 | tf_op jit(solution)/shard_map/all_to_all | solution.py:43
  155.6 0.8 fusion.6
  156.4 1.9 %collective-permute-start.15 = (bf16[256,256]{1,0:T(8,128)(2,1)S(1)}, bf16[256,256]{1,0:T(8,128)(2,1)S(1)}, u32[]{:S(2)}, u32[]{:S(2)}) collective-permute-start(bf16[256,256]{1,0:T(8,128)(2,1)S(1)} %broadcast_select_fusion.11), channel_id=1, source_target_pairs={{0,4},{4,0},{1,5},{5,1},{2,6},{6,2},{3,7},{7,3},{8,12},{12,8},{9,1... | collective-permute-start | bytes 393224 | tf_op jit(solution)/shard_map/ppermute | solution.py:265
  158.3 1.3 collective-permute-done.15
  159.7 9.9 %all-to-all-done.3 = bf16[16,4,1024]{2,1,0:T(4,128)(2,1)S(1)} async-done(((bf16[16,4,1024]{2,1,0:T(4,128)(2,1)}), bf16[16,4,1024]{2,1,0:T(4,128)(2,1)S(1)}, u32[]{:S(2)}, u32[]{:S(2)}) %all-to-all-start.3) | async-done | bytes 131104 | tf_op jit(solution)/shard_map/all_to_all | solution.py:43
  169.7 0.6 broadcast_in_dim.8
  170.3 3.3 %all-to-all-start.4 = ((f32[4,4,1024]{2,1,0:T(4,128)}), f32[4,4,1024]{2,1,0:T(4,128)S(1)}, u32[]{:S(2)}, u32[]{:S(2)}) async-start(f32[4,4,1024]{2,1,0:T(4,128)} %broadcast_in_dim.8), calls=%async_computation.4 | async-start | bytes 131072 | tf_op jit(solution)/shard_map/all_to_all | solution.py:43
  173.6 1.2 fusion.8
  174.8 4.4 %all-to-all-done.4 = f32[4,4,1024]{2,1,0:T(4,128)S(1)} async-done(((f32[4,4,1024]{2,1,0:T(4,128)}), f32[4,4,1024]{2,1,0:T(4,128)S(1)}, u32[]{:S(2)}, u32[]{:S(2)}) %all-to-all-start.4) | async-done | bytes 65568 | tf_op jit(solution)/shard_map/all_to_all | solution.py:43
  179.2 0.6 slice.164
  179.9 0.6 copy-done.4
  (69 shorter events, 3.4 us)
Async XLA Ops:
  0.6 24.8 %copy-start.3 = (s32[1,128]{1,0:T(1,128)S(1)}, s32[1,128]{1,0:T(1,128)}, u32[]{:S(2)}) copy-start(s32[1,128]{1,0:T(1,128)} %param.10) | copy-start | bytes 1540
  0.6 24.8 %copy-start.2 = (s32[1,128]{1,0:T(1,128)S(1)}, s32[1,128]{1,0:T(1,128)}, u32[]{:S(2)}) copy-start(s32[1,128]{1,0:T(1,128)} %param.11) | copy-start | bytes 1540
  0.7 22.7 %copy-start.1 = (bf16[1,256,512]{2,1,0:T(8,128)(2,1)S(1)}, bf16[1,256,512]{2,1,0:T(8,128)(2,1)}, u32[]{:S(2)}) copy-start(bf16[1,256,512]{2,1,0:T(8,128)(2,1)} %param.6) | copy-start | bytes 786436
  1.4 24.1 %collective-permute-start = (s32[2,128]{1,0:T(2,128)S(1)}, s32[2,128]{1,0:T(2,128)S(1)}, u32[]{:S(2)}, u32[]{:S(2)}) collective-permute-start(s32[2,128]{1,0:T(2,128)S(1)} %pad_add_fusion.1), channel_id=1, source_target_pairs={{0,4},{4,0},{1,5},{5,1},{2,6},{6,2},{3,7},{7,3},{8,12},{12,8},{9,1... | collective-permute-start | bytes 3080 | tf_op jit(solution)/shard_map/ppermute | solution.py:176
  3.3 22.7 %copy-start = (bf16[1,256,512]{2,1,0:T(8,128)(2,1)S(1)}, bf16[1,256,512]{2,1,0:T(8,128)(2,1)}, u32[]{:S(2)}) copy-start(bf16[1,256,512]{2,1,0:T(8,128)(2,1)} %param.7) | copy-start | bytes 786436
  4.4 21.6 %collective-permute-start.2 = (bf16[256,256]{1,0:T(8,128)(2,1)S(1)}, bf16[256,256]{1,0:T(8,128)(2,1)S(1)}, u32[]{:S(2)}, u32[]{:S(2)}) collective-permute-start(bf16[256,256]{1,0:T(8,128)(2,1)S(1)} %broadcast_select_fusion.17), channel_id=1, source_target_pairs={{0,4},{4,0},{1,5},{5,1},{2,6},{6,2},{3,7},{7,3},{8,12},{12,8},{9,1... | collective-permute-start | bytes 393224 | tf_op jit(solution)/shard_map/ppermute | solution.py:189
  8.1 28.2 %all-to-all-start = ((bf16[16,8,256]{2,1,0:T(8,128)(2,1)}), bf16[16,8,256]{2,1,0:T(8,128)(2,1)S(1)}, u32[]{:S(2)}, u32[]{:S(2)}) async-start(bf16[16,8,256]{2,1,0:T(8,128)(2,1)} %broadcast_in_dim.6), calls=%async_computation | async-start | bytes 131072 | tf_op jit(solution)/shard_map/all_to_all | solution.py:43
  23.4 61.4 %collective-permute-start.1 = (bf16[256,512]{1,0:T(8,128)(2,1)S(1)}, bf16[256,512]{1,0:T(8,128)(2,1)S(1)}, u32[]{:S(2)}, u32[]{:S(2)}) collective-permute-start(bf16[256,512]{1,0:T(8,128)(2,1)S(1)} %bitcast.46), channel_id=1, source_target_pairs={{0,4},{4,0},{1,5},{5,1},{2,6},{6,2},{3,7},{7,3},{8,12},{12,8},{9,1... | collective-permute-start | bytes 786440 | tf_op jit(solution)/shard_map/ppermute | solution.py:176
  36.4 45.7 %all-to-all-start.1 = ((bf16[64,16,256]{2,1,0:T(8,128)(2,1)}), bf16[64,16,256]{2,1,0:T(8,128)(2,1)S(1)}, u32[]{:S(2)}, u32[]{:S(2)}) async-start(bf16[64,16,256]{2,1,0:T(8,128)(2,1)} %bitcast.7), calls=%async_computation.1 | async-start | bytes 1048576 | tf_op jit(solution)/shard_map/all_to_all | solution.py:43
  43.0 8.0 %collective-permute-start.3 = (bf16[128,256]{1,0:T(8,128)(2,1)S(1)}, bf16[128,256]{1,0:T(8,128)(2,1)S(1)}, u32[]{:S(2)}, u32[]{:S(2)}) collective-permute-start(bf16[128,256]{1,0:T(8,128)(2,1)S(1)} %bitcast.41), channel_id=1, source_target_pairs={{0,256},{128,384},{256,0},{384,128},{1,257},{129,385},{257,1},{385... | collective-permute-start | bytes 196616 | tf_op jit(solution)/shard_map/ppermute | solution.py:53
  51.0 7.6 %collective-permute-start.4 = (bf16[256,256]{1,0:T(8,128)(2,1)S(1)}, bf16[256,256]{1,0:T(8,128)(2,1)S(1)}, u32[]{:S(2)}, u32[]{:S(2)}) collective-permute-start(bf16[256,256]{1,0:T(8,128)(2,1)S(1)} %pad_maximum_fusion.4), channel_id=1, source_target_pairs={{0,128},{128,0},{256,384},{384,256},{1,129},{129,1},{257,385},{385... | collective-permute-start | bytes 393224 | tf_op jit(solution)/shard_map/ppermute | solution.py:53
  59.1 3.2 %collective-permute-start.5 = (bf16[256,256]{1,0:T(8,128)(2,1)S(1)}, bf16[256,256]{1,0:T(8,128)(2,1)S(1)}, u32[]{:S(2)}, u32[]{:S(2)}) collective-permute-start(bf16[256,256]{1,0:T(8,128)(2,1)S(1)} %get-tuple-element.48), channel_id=1, source_target_pairs={{0,4},{4,0},{1,5},{5,1},{2,6},{6,2},{3,7},{7,3},{8,12},{12,8},{9,1... | collective-permute-start | bytes 393224 | tf_op jit(solution)/shard_map/ppermute | solution.py:217
  62.4 11.8 %collective-permute-start.6 = (bf16[512,256]{1,0:T(8,128)(2,1)S(1)}, bf16[512,256]{1,0:T(8,128)(2,1)S(1)}, u32[]{:S(2)}, u32[]{:S(2)}) collective-permute-start(bf16[512,256]{1,0:T(8,128)(2,1)S(1)} %pad_maximum_fusion.3.w0_ref), channel_id=1, source_target_pairs={{0,1},{1,2},{2,3},{3,0},{4,5},{5,6},{6,7},{7,4},{8,9},{9,10},{10,1... | collective-permute-start | bytes 786440 | tf_op jit(solution)/shard_map/ppermute | solution.py:48
  65.9 14.8 %collective-permute-start.7 = (bf16[512,256]{1,0:T(8,128)(2,1)S(1)}, bf16[512,256]{1,0:T(8,128)(2,1)S(1)}, u32[]{:S(2)}, u32[]{:S(2)}) collective-permute-start(bf16[512,256]{1,0:T(8,128)(2,1)S(1)} %pad_maximum_fusion.3.w0_ref), channel_id=1, source_target_pairs={{0,2},{1,3},{2,0},{3,1},{4,6},{5,7},{6,4},{7,5},{8,10},{9,11},{10,... | collective-permute-start | bytes 786440 | tf_op jit(solution)/shard_map/ppermute | solution.py:48
  70.7 11.3 %collective-permute-start.8 = (bf16[512,256]{1,0:T(8,128)(2,1)S(1)}, bf16[512,256]{1,0:T(8,128)(2,1)S(1)}, u32[]{:S(2)}, u32[]{:S(2)}) collective-permute-start(bf16[512,256]{1,0:T(8,128)(2,1)S(1)} %pad_maximum_fusion.3.w0_ref), channel_id=1, source_target_pairs={{0,3},{1,0},{2,1},{3,2},{4,7},{5,4},{6,5},{7,6},{8,11},{9,8},{10,9... | collective-permute-start | bytes 786440 | tf_op jit(solution)/shard_map/ppermute | solution.py:48
  82.8 3.4 %collective-permute-start.9 = (bf16[512,256]{1,0:T(8,128)(2,1)S(1)}, bf16[512,256]{1,0:T(8,128)(2,1)S(1)}, u32[]{:S(2)}, u32[]{:S(2)}) collective-permute-start(bf16[512,256]{1,0:T(8,128)(2,1)S(1)} %fusion.7), channel_id=1, source_target_pairs={{0,4},{4,0},{1,5},{5,1},{2,6},{6,2},{3,7},{7,3},{8,12},{12,8},{9,1... | collective-permute-start | bytes 786440 | tf_op jit(solution)/shard_map/ppermute | solution.py:176
  93.6 4.4 %collective-permute-start.10 = (bf16[256,1024]{1,0:T(8,128)(2,1)S(1)}, bf16[256,1024]{1,0:T(8,128)(2,1)S(1)}, u32[]{:S(2)}, u32[]{:S(2)}) collective-permute-start(bf16[256,1024]{1,0:T(8,128)(2,1)S(1)} %get-tuple-element.21), channel_id=1, source_target_pairs={{0,4},{4,0},{1,5},{5,1},{2,6},{6,2},{3,7},{7,3},{8,12},{12,8},{9,1... | collective-permute-start | bytes 1572872 | tf_op jit(solution)/shard_map/ppermute | solution.py:240
  95.7 7.3 %collective-permute-start.14 = (bf16[512,256]{1,0:T(8,128)(2,1)S(1)}, bf16[512,256]{1,0:T(8,128)(2,1)S(1)}, u32[]{:S(2)}, u32[]{:S(2)}) collective-permute-start(bf16[512,256]{1,0:T(8,128)(2,1)S(1)} %get-tuple-element.24), channel_id=1, source_target_pairs={{0,4},{4,0},{1,5},{5,1},{2,6},{6,2},{3,7},{7,3},{8,12},{12,8},{9,1... | collective-permute-start | bytes 786440 | tf_op jit(solution)/shard_map/ppermute | solution.py:235
  98.3 21.4 %collective-permute-start.11 = (bf16[256,1024]{1,0:T(8,128)(2,1)S(1)}, bf16[256,1024]{1,0:T(8,128)(2,1)S(1)}, u32[]{:S(2)}, u32[]{:S(2)}) collective-permute-start(bf16[256,1024]{1,0:T(8,128)(2,1)S(1)} %broadcast_select_fusion), channel_id=1, source_target_pairs={{0,1},{1,0},{2,3},{3,2},{4,5},{5,4},{6,7},{7,6},{8,9},{9,8},{10,11... | collective-permute-start | bytes 1572872 | tf_op jit(solution)/shard_map/ppermute | solution.py:53
  104.2 47.1 %all-to-all-start.2 = ((bf16[64,16,256]{2,1,0:T(8,128)(2,1)}), bf16[64,16,256]{2,1,0:T(8,128)(2,1)S(1)}, u32[]{:S(2)}, u32[]{:S(2)}) async-start(bf16[64,16,256]{2,1,0:T(8,128)(2,1)} %bitcast.17), calls=%async_computation.2 | async-start | bytes 1048576 | tf_op jit(solution)/shard_map/all_to_all | solution.py:43
  120.0 10.7 %collective-permute-start.12 = (bf16[128,1024]{1,0:T(8,128)(2,1)S(1)}, bf16[128,1024]{1,0:T(8,128)(2,1)S(1)}, u32[]{:S(2)}, u32[]{:S(2)}) collective-permute-start(bf16[128,1024]{1,0:T(8,128)(2,1)S(1)} %bitcast.47), channel_id=1, source_target_pairs={{0,128},{128,0},{256,384},{384,256},{1,129},{129,1},{257,385},{385... | collective-permute-start | bytes 786440 | tf_op jit(solution)/shard_map/ppermute | solution.py:53
  130.8 9.0 %collective-permute-start.13 = (bf16[64,1024]{1,0:T(8,128)(2,1)S(1)}, bf16[64,1024]{1,0:T(8,128)(2,1)S(1)}, u32[]{:S(2)}, u32[]{:S(2)}) collective-permute-start(bf16[64,1024]{1,0:T(8,128)(2,1)S(1)} %select_bitcast_fusion), channel_id=1, source_target_pairs={{0,256},{128,384},{256,0},{384,128},{1,257},{129,385},{257,1},{385... | collective-permute-start | bytes 393224 | tf_op jit(solution)/shard_map/ppermute | solution.py:53
  152.1 17.5 %all-to-all-start.3 = ((bf16[16,4,1024]{2,1,0:T(4,128)(2,1)}), bf16[16,4,1024]{2,1,0:T(4,128)(2,1)S(1)}, u32[]{:S(2)}, u32[]{:S(2)}) async-start(bf16[16,4,1024]{2,1,0:T(4,128)(2,1)} %reshape.484), calls=%async_computation.3 | async-start | bytes 262144 | tf_op jit(solution)/shard_map/all_to_all | solution.py:43
  156.4 3.2 %collective-permute-start.15 = (bf16[256,256]{1,0:T(8,128)(2,1)S(1)}, bf16[256,256]{1,0:T(8,128)(2,1)S(1)}, u32[]{:S(2)}, u32[]{:S(2)}) collective-permute-start(bf16[256,256]{1,0:T(8,128)(2,1)S(1)} %broadcast_select_fusion.11), channel_id=1, source_target_pairs={{0,4},{4,0},{1,5},{5,1},{2,6},{6,2},{3,7},{7,3},{8,12},{12,8},{9,1... | collective-permute-start | bytes 393224 | tf_op jit(solution)/shard_map/ppermute | solution.py:265
  170.3 8.9 %all-to-all-start.4 = ((f32[4,4,1024]{2,1,0:T(4,128)}), f32[4,4,1024]{2,1,0:T(4,128)S(1)}, u32[]{:S(2)}, u32[]{:S(2)}) async-start(f32[4,4,1024]{2,1,0:T(4,128)} %broadcast_in_dim.8), calls=%async_computation.4 | async-start | bytes 131072 | tf_op jit(solution)/shard_map/all_to_all | solution.py:43
  179.9 0.6 copy-start.4

commit v10 on v6

--- a/solution.py
+++ b/solution.py
@@ -13,6 +13,7 @@
 Z_LOW = 4
 CORES = 2
 ROWS = ("x", "zh", "zl", "core")
+CHIPS = ("x", "zh", "zl")
 INTERPRET = False
 NN = ((1,), (0,))
 NT = ((1,), (1,))
@@ -38,6 +39,14 @@
         (slots[:, None] == (rows + half * CAP * BLK)[None, :]).astype(jnp.bfloat16)
         for half in range(2)
     ]
+
+
+def slot_table(owners, ranks, count):
+    per_chip = CAP * CORES * CORES
+    base = (owners * per_chip + ranks) * BLK
+    rows = (base[:, None] + jnp.arange(BLK, dtype=jnp.int32)[None, :]).reshape(-1)
+    slots = jnp.arange(count * per_chip * BLK, dtype=jnp.int32)
+    return (slots[:, None] == rows[None, :]).astype(jnp.bfloat16)
 
 
 def swap(block, axis):
@@ -122,8 +131,11 @@
         out_ref[:part, 3 * own :] = tp_ref[side, :, :own]
         out_ref[part:, 3 * own :] = tp_ref[side, :, own:]
     partial = mm(grad_qkv, w_qkv, NT)
-    pown_ref[...] = partial[:rows]
-    poth_ref[...] = partial[rows:].astype(bf)
+    left, right = partial[:, :own], partial[:, own:]
+    pown_ref[...] = jnp.where(core == 0, left, right)
+    theirs = jnp.where(core == 0, right, left).astype(bf)
+    poth_ref[:rows] = theirs[rows:]
+    poth_ref[rows:] = theirs[:rows]
 
 
 def patch_step(place, x, weights, gown, goth, own_perm):
@@ -134,8 +146,8 @@
     return pl.pallas_call(
         patch_body,
         out_shape=[
-            jax.ShapeDtypeStruct((rows, channels), jnp.float32),
-            jax.ShapeDtypeStruct((rows, channels), bf),
+            jax.ShapeDtypeStruct((CORES * rows, own), jnp.float32),
+            jax.ShapeDtypeStruct((CORES * rows, own), bf),
             jax.ShapeDtypeStruct((own, 4 * own), bf),
             jax.ShapeDtypeStruct((own, 4 * own), bf),
         ],
@@ -224,10 +236,17 @@
     place = jnp.stack([core, rep])
     p_own, p_other, keep, away = patch_step(place, x_pair, weights, grad_hil, other_grad, own_perm)
 
+    lists = jnp.stack([to_hilbert[0], to_zorder[0]])
+    lists = jnp.concatenate([lists, lax.ppermute(lists, "core", pair)], axis=1)
+    keys = jnp.concatenate([ids + core * blocks_dev, ids + (1 - core) * blocks_dev])
+    target = lists[0] // (nc * blocks_dev)
+    send_chip = slot_table(target, rank_within(keys, target), nx * nz)
+    source = lists[1] // (nc * blocks_dev)
+    recv_chip = slot_table(source, rank_within(lists[1], source), nx * nz)
     from_other = lax.ppermute(p_other, "core", pair)
     grad_hfeat = (p_own + from_other.astype(f32)).astype(bf)
-    going = (mm(recv[0], grad_hfeat[:, :half], NN) + mm(recv[1], grad_hfeat[:, half:], NN)).astype(bf)
-    returned = swap(going.reshape(peers, chunk, half), ROWS).reshape(peers * chunk, half)
+    going = mm(recv_chip, grad_hfeat, NN, bf)
+    returned = swap(going.reshape(nx * nz, -1, half), CHIPS).reshape(-1, half)
 
     got = lax.ppermute(away, "core", pair)
     proj = [jnp.concatenate([m[:part, 3 * own :], m[part:, 3 * own :]], axis=1) for m in (keep, got)]
@@ -252,7 +271,10 @@
     summed = jnp.sum(far.astype(f32), axis=0)
     last = swap(jnp.broadcast_to(summed[None], (nr, share, wide)), "rep")
     last = jnp.concatenate([last[0] + last[2], last[1] + last[3]], axis=1)
-    grad_perm = jnp.concatenate([mm(send[h], returned, TN, bf) for h in range(2)], axis=1)
+    grad_half = mm(send_chip, returned, TN, bf)
+    stay = grad_half[:rows_dev]
+    come = lax.ppermute(grad_half[rows_dev:], "core", pair)
+    grad_perm = jnp.concatenate([jnp.where(core == 0, stay, come), jnp.where(core == 0, come, stay)], axis=1)
     grad_z = mm(grad_perm, perm, NT, bf)
     lower = jnp.where(core == 0, last[:, : 3 * own], last[:, 3 * own : 6 * own])
     upper = jnp.where(core == 0, last[:, 3 * own : 6 * own], last[:, : 3 * own])

time: 179 us -> 179 us (level)
  waiting for transfers between devices: 68 us -> 58.8 us
  starting transfers between devices: 85.1 us -> 92.8 us
  other arithmetic: 2.93 us -> 5 us
    all_to_all x5, waiting for transfers between devices: 35.8 us -> 29.6 us  [swap(): return lax.all_to_all(block, axis, split_axis=0, concat_axis=0, tiled=True)]
    ppermute x0 -> x2, starting transfers between devices: none -> 4.31 us  [the longest x1 2.39 us: per_device(): lists = jnp.concatenate([lists, lax.ppermute(lists, 'core', pair)], axis=1)]
    ppermute x5, waiting for transfers between devices: 25.7 us -> 23.2 us  [flip(): lax.ppermute(block, axis, [(here, here ^ bit) for here in range(count)])]
    all_to_all x5, starting transfers between devices: 48.7 us -> 50.8 us  [swap(): return lax.all_to_all(block, axis, split_axis=0, concat_axis=0, tiled=True)]
    dot_general x12 -> x10, matrix products: 7.07 us -> 7.79 us  [mm(): lax.dot_general(left, right, (dims, ((), ())), preferred_element_type=jnp...]
  transfers between devices with their start and end apart: 18 -> 20, of which waited for: 13 -> 13; matrix products, arithmetic and copies ran while one was open for 6% -> 7% of each run, Pallas kernels for 0% -> 0%
where the time goes in v10:
time: 179 us; the launch traced here: 177 us
  starting transfers between devices  92.8 us (52%)
  waiting for transfers between devices  58.8 us (33%)
  matrix products  7.79 us (4%)
  Pallas kernels  7.28 us (4%)
  other arithmetic  5 us (3%)
  local copies, waits for them, and re-layouts  3.95 us (2%)
    all_to_all x5, starting transfers between devices, swap(): return lax.all_to_all(block, axis, split_axis=0, concat_axis=0, tiled=True)  50.8 us
    all_to_all x5, waiting for transfers between devices, swap(): return lax.all_to_all(block, axis, split_axis=0, concat_axis=0, tiled=True)  29.6 us
    ppermute x5, waiting for transfers between devices, flip(): lax.ppermute(block, axis, [(here, here ^ bit) for here in range(count)])  23.2 us
    ppermute x5, starting transfers between devices, flip(): lax.ppermute(block, axis, [(here, here ^ bit) for here in range(count)])  15.7 us
    ppermute x3, starting transfers between devices, shift(): lax.ppermute(block, axis, [(here, (here + step) % count) for here in rang...  11.7 us
    dot_general x10, matrix products, mm(): lax.dot_general(left, right, (dims, ((), ())), preferred_element_type=jnp...  7.79 us
    pallas_call x1, Pallas kernels, patch_step(): pl.pallas_call(patch_body, out_shape=[jax.ShapeDtypeStruct((CORES * rows,...  7.28 us
  transfers between devices with their start and end apart: 20, of which 13 were waited for; matrix products, arithmetic and copies ran while one was open for 7% of the time, Pallas kernels for 0%

profile of v10, /device:TPU:6, one launch (start us, length us, event | category | flops | bytes accessed | tf_op | source)
XLA Modules:
  0.0 176.9 jit_solution(6530382850099891245)
XLA Ops:
  0.7 0.7 fusion.37
  1.4 0.6 broadcast_in_dim.6
  2.1 15.2 %all-to-all-start = ((bf16[16,8,256]{2,1,0:T(8,128)(2,1)}), bf16[16,8,256]{2,1,0:T(8,128)(2,1)S(1)}, u32[]{:S(2)}, u32[]{:S(2)}) async-start(bf16[16,8,256]{2,1,0:T(8,128)(2,1)} %broadcast_in_dim.6), calls=%async_computation | async-start | bytes 131072 | tf_op jit(solution)/shard_map/all_to_all | solution.py:53
  17.3 1.9 %collective-permute-start.1 = (bf16[256,512]{1,0:T(8,128)(2,1)}, bf16[256,512]{1,0:T(8,128)(2,1)S(1)}, u32[]{:S(2)}, u32[]{:S(2)}) collective-permute-start(bf16[256,512]{1,0:T(8,128)(2,1)} %bitcast.68), channel_id=1, source_target_pairs={{0,4},{4,0},{1,5},{5,1},{2,6},{6,2},{3,7},{7,3},{8,12},{12,8},{9,1... | collective-permute-start | bytes 786440 | tf_op jit(solution)/shard_map/ppermute | solution.py:232
  19.2 0.7 pad_add_fusion.1
  19.9 2.4 %collective-permute-start = (s32[2,128]{1,0:T(2,128)S(1)}, s32[2,128]{1,0:T(2,128)S(1)}, u32[]{:S(2)}, u32[]{:S(2)}) collective-permute-start(s32[2,128]{1,0:T(2,128)S(1)} %pad_add_fusion.1), channel_id=1, source_target_pairs={{0,4},{4,0},{1,5},{5,1},{2,6},{6,2},{3,7},{7,3},{8,12},{12,8},{9,1... | collective-permute-start | bytes 3080 | tf_op jit(solution)/shard_map/ppermute | solution.py:240
  22.3 0.7 and_select_fusion.8
  23.0 0.7 fusion.69
  24.1 1.2 fusion.8
  25.6 1.2 fusion.2
  26.8 3.2 %all-to-all-done = bf16[16,8,256]{2,1,0:T(8,128)(2,1)S(1)} async-done(((bf16[16,8,256]{2,1,0:T(8,128)(2,1)}), bf16[16,8,256]{2,1,0:T(8,128)(2,1)S(1)}, u32[]{:S(2)}, u32[]{:S(2)}) %all-to-all-start) | async-done | bytes 65568 | tf_op jit(solution)/shard_map/all_to_all | solution.py:53
  30.0 13.6 %all-to-all-start.1 = ((bf16[128,8,256]{2,1,0:T(8,128)(2,1)}), bf16[128,8,256]{2,1,0:T(8,128)(2,1)S(1)}, u32[]{:S(2)}, u32[]{:S(2)}) async-start(bf16[128,8,256]{2,1,0:T(8,128)(2,1)} %bitcast.11), calls=%async_computation.1 | async-start | bytes 1048576 | tf_op jit(solution)/shard_map/all_to_all | solution.py:53
  44.0 2.9 %collective-permute-start.2 = (bf16[128,256]{1,0:T(8,128)(2,1)S(1)}, bf16[128,256]{1,0:T(8,128)(2,1)S(1)}, u32[]{:S(2)}, u32[]{:S(2)}) collective-permute-start(bf16[128,256]{1,0:T(8,128)(2,1)S(1)} %bitcast.54), channel_id=1, source_target_pairs={{0,256},{128,384},{256,0},{384,128},{1,257},{129,385},{257,1},{385... | collective-permute-start | bytes 196616 | tf_op jit(solution)/shard_map/ppermute | solution.py:63
  47.0 5.1 %collective-permute-done.2 = bf16[128,256]{1,0:T(8,128)(2,1)S(1)} collective-permute-done((bf16[128,256]{1,0:T(8,128)(2,1)S(1)}, bf16[128,256]{1,0:T(8,128)(2,1)S(1)}, u32[]{:S(2)}, u32[]{:S(2)}) %collective-permute-start.2) | collective-permute-done | bytes 65568 | tf_op jit(solution)/shard_map/ppermute | solution.py:63
  52.1 2.5 %collective-permute-start.3 = (bf16[256,256]{1,0:T(8,128)(2,1)S(1)}, bf16[256,256]{1,0:T(8,128)(2,1)S(1)}, u32[]{:S(2)}, u32[]{:S(2)}) collective-permute-start(bf16[256,256]{1,0:T(8,128)(2,1)S(1)} %pad_maximum_fusion.5), channel_id=1, source_target_pairs={{0,128},{128,0},{256,384},{384,256},{1,129},{129,1},{257,385},{385... | collective-permute-start | bytes 393224 | tf_op jit(solution)/shard_map/ppermute | solution.py:63
  54.6 4.9 %collective-permute-done.3 = bf16[256,256]{1,0:T(8,128)(2,1)S(1)} collective-permute-done((bf16[256,256]{1,0:T(8,128)(2,1)S(1)}, bf16[256,256]{1,0:T(8,128)(2,1)S(1)}, u32[]{:S(2)}, u32[]{:S(2)}) %collective-permute-start.3) | collective-permute-done | bytes 131104 | tf_op jit(solution)/shard_map/ppermute | solution.py:63
  60.1 1.9 %collective-permute-start.4 = (bf16[256,256]{1,0:T(8,128)(2,1)S(1)}, bf16[256,256]{1,0:T(8,128)(2,1)S(1)}, u32[]{:S(2)}, u32[]{:S(2)}) collective-permute-start(bf16[256,256]{1,0:T(8,128)(2,1)S(1)} %get-tuple-element.30), channel_id=1, source_target_pairs={{0,4},{4,0},{1,5},{5,1},{2,6},{6,2},{3,7},{7,3},{8,12},{12,8},{9,1... | collective-permute-start | bytes 393224 | tf_op jit(solution)/shard_map/ppermute | solution.py:220
  62.0 1.3 collective-permute-done.4
  63.3 3.6 %collective-permute-start.5 = (bf16[512,256]{1,0:T(8,128)(2,1)S(1)}, bf16[512,256]{1,0:T(8,128)(2,1)S(1)}, u32[]{:S(2)}, u32[]{:S(2)}) collective-permute-start(bf16[512,256]{1,0:T(8,128)(2,1)S(1)} %pad_maximum_fusion.3.w0_ref), channel_id=1, source_target_pairs={{0,1},{1,2},{2,3},{3,0},{4,5},{5,6},{6,7},{7,4},{8,9},{9,10},{10,1... | collective-permute-start | bytes 786440 | tf_op jit(solution)/shard_map/ppermute | solution.py:58
  67.0 4.8 %collective-permute-start.6 = (bf16[512,256]{1,0:T(8,128)(2,1)S(1)}, bf16[512,256]{1,0:T(8,128)(2,1)S(1)}, u32[]{:S(2)}, u32[]{:S(2)}) collective-permute-start(bf16[512,256]{1,0:T(8,128)(2,1)S(1)} %pad_maximum_fusion.3.w0_ref), channel_id=1, source_target_pairs={{0,2},{1,3},{2,0},{3,1},{4,6},{5,7},{6,4},{7,5},{8,10},{9,11},{10,... | collective-permute-start | bytes 786440 | tf_op jit(solution)/shard_map/ppermute | solution.py:58
  71.8 3.3 %collective-permute-start.7 = (bf16[512,256]{1,0:T(8,128)(2,1)S(1)}, bf16[512,256]{1,0:T(8,128)(2,1)S(1)}, u32[]{:S(2)}, u32[]{:S(2)}) collective-permute-start(bf16[512,256]{1,0:T(8,128)(2,1)S(1)} %pad_maximum_fusion.3.w0_ref), channel_id=1, source_target_pairs={{0,3},{1,0},{2,1},{3,2},{4,7},{5,4},{6,5},{7,6},{8,11},{9,8},{10,9... | collective-permute-start | bytes 786440 | tf_op jit(solution)/shard_map/ppermute | solution.py:58
  75.0 0.7 all-to-all-done.1
  76.8 2.1 %collective-permute-start.8 = (bf16[256,512]{1,0:T(8,128)(2,1)S(1)}, bf16[256,512]{1,0:T(8,128)(2,1)S(1)}, u32[]{:S(2)}, u32[]{:S(2)}) collective-permute-start(bf16[256,512]{1,0:T(8,128)(2,1)S(1)} %pad_maximum_fusion.4.gown_ref), channel_id=1, source_target_pairs={{0,4},{4,0},{1,5},{5,1},{2,6},{6,2},{3,7},{7,3},{8,12},{12,8},{9,1... | collective-permute-start | bytes 786440 | tf_op jit(solution)/shard_map/ppermute | solution.py:235
  79.7 2.1 %collective-permute-done.6.w2_ref = bf16[512,256]{1,0:T(8,128)(2,1)S(1)} collective-permute-done((bf16[512,256]{1,0:T(8,128)(2,1)S(1)}, bf16[512,256]{1,0:T(8,128)(2,1)S(1)}, u32[]{:S(2)}, u32[]{:S(2)}) %collective-permute-start.6) | collective-permute-done | bytes 262176 | tf_op jit(solution)/shard_map/ppermute | solution.py:58
  81.8 1.3 collective-permute-done.7.w3_ref
  83.1 7.3 %shard_map.85 = (f32[512,256]{1,0:T(8,128)S(1)}, bf16[512,256]{1,0:T(8,128)(2,1)S(1)}, bf16[256,1024]{1,0:T(8,128)(2,1)S(1)}, bf16[256,1024]{1,0:T(8,128)(2,1)S(1)}) custom-call(s32[2]{0:T(128)S(1)} %pad_add_fusion.3.place_ref, bf16[512,512]{1,0:T(8,128)(2,1)S(1)} %convolution_convert_fusion.x_ref, bf16[512,256]{1,0:T(8,128)(2,1)S(1)} %pad_maximum_fusion.3.w0_ref, ...), custom_call_target="tpu_custom_call" | custom-call | tf_op jit(solution)/shard_map/pallas_call | solution.py:146
  90.4 1.9 %collective-permute-start.9 = (bf16[256,1024]{1,0:T(8,128)(2,1)S(1)}, bf16[256,1024]{1,0:T(8,128)(2,1)S(1)}, u32[]{:S(2)}, u32[]{:S(2)}) collective-permute-start(bf16[256,1024]{1,0:T(8,128)(2,1)S(1)} %get-tuple-element.13), channel_id=1, source_target_pairs={{0,4},{4,0},{1,5},{5,1},{2,6},{6,2},{3,7},{7,3},{8,12},{12,8},{9,1... | collective-permute-start | bytes 1572872 | tf_op jit(solution)/shard_map/ppermute | solution.py:251
  92.6 2.4 %collective-permute-start.13 = (bf16[512,256]{1,0:T(8,128)(2,1)S(1)}, bf16[512,256]{1,0:T(8,128)(2,1)S(1)}, u32[]{:S(2)}, u32[]{:S(2)}) collective-permute-start(bf16[512,256]{1,0:T(8,128)(2,1)S(1)} %get-tuple-element.16), channel_id=1, source_target_pairs={{0,4},{4,0},{1,5},{5,1},{2,6},{6,2},{3,7},{7,3},{8,12},{12,8},{9,1... | collective-permute-start | bytes 786440 | tf_op jit(solution)/shard_map/ppermute | solution.py:246
  95.4 4.4 %collective-permute-start.10 = (bf16[256,1024]{1,0:T(8,128)(2,1)S(1)}, bf16[256,1024]{1,0:T(8,128)(2,1)S(1)}, u32[]{:S(2)}, u32[]{:S(2)}) collective-permute-start(bf16[256,1024]{1,0:T(8,128)(2,1)S(1)} %broadcast_select_fusion), channel_id=1, source_target_pairs={{0,1},{1,0},{2,3},{3,2},{4,5},{5,4},{6,7},{7,6},{8,9},{9,8},{10,11... | collective-permute-start | bytes 1572872 | tf_op jit(solution)/shard_map/ppermute | solution.py:63
  99.8 1.3 fusion.3
  101.1 15.2 %all-to-all-start.2 = ((bf16[64,16,256]{2,1,0:T(8,128)(2,1)}), bf16[64,16,256]{2,1,0:T(8,128)(2,1)S(1)}, u32[]{:S(2)}, u32[]{:S(2)}) async-start(bf16[64,16,256]{2,1,0:T(8,128)(2,1)} %bitcast.21), calls=%async_computation.2 | async-start | bytes 1048576 | tf_op jit(solution)/shard_map/all_to_all | solution.py:53
  116.6 2.7 %collective-permute-start.11 = (bf16[128,1024]{1,0:T(8,128)(2,1)S(1)}, bf16[128,1024]{1,0:T(8,128)(2,1)S(1)}, u32[]{:S(2)}, u32[]{:S(2)}) collective-permute-start(bf16[128,1024]{1,0:T(8,128)(2,1)S(1)} %bitcast.60), channel_id=1, source_target_pairs={{0,128},{128,0},{256,384},{384,256},{1,129},{129,1},{257,385},{385... | collective-permute-start | bytes 786440 | tf_op jit(solution)/shard_map/ppermute | solution.py:63
  119.5 7.7 %collective-permute-done.11 = bf16[128,1024]{1,0:T(8,128)(2,1)S(1)} collective-permute-done((bf16[128,1024]{1,0:T(8,128)(2,1)S(1)}, bf16[128,1024]{1,0:T(8,128)(2,1)S(1)}, u32[]{:S(2)}, u32[]{:S(2)}) %collective-permute-start.11) | collective-permute-done | bytes 262176 | tf_op jit(solution)/shard_map/ppermute | solution.py:63
  127.4 3.2 %collective-permute-start.12 = (bf16[64,1024]{1,0:T(8,128)(2,1)S(1)}, bf16[64,1024]{1,0:T(8,128)(2,1)S(1)}, u32[]{:S(2)}, u32[]{:S(2)}) collective-permute-start(bf16[64,1024]{1,0:T(8,128)(2,1)S(1)} %select_bitcast_fusion), channel_id=1, source_target_pairs={{0,256},{128,384},{256,0},{384,128},{1,257},{129,385},{257,1},{385... | collective-permute-start | bytes 393224 | tf_op jit(solution)/shard_map/ppermute | solution.py:63
  130.8 5.5 %collective-permute-done.12 = bf16[64,1024]{1,0:T(8,128)(2,1)S(1)} collective-permute-done((bf16[64,1024]{1,0:T(8,128)(2,1)S(1)}, bf16[64,1024]{1,0:T(8,128)(2,1)S(1)}, u32[]{:S(2)}, u32[]{:S(2)}) %collective-permute-start.12) | collective-permute-done | bytes 131104 | tf_op jit(solution)/shard_map/ppermute | solution.py:63
  136.4 11.3 %all-to-all-done.2 = bf16[64,16,256]{2,1,0:T(8,128)(2,1)S(1)} async-done(((bf16[64,16,256]{2,1,0:T(8,128)(2,1)}), bf16[64,16,256]{2,1,0:T(8,128)(2,1)S(1)}, u32[]{:S(2)}, u32[]{:S(2)}) %all-to-all-start.2) | async-done | bytes 524320 | tf_op jit(solution)/shard_map/all_to_all | solution.py:53
  147.7 0.7 reshape.619
  148.4 3.5 %all-to-all-start.3 = ((bf16[16,4,1024]{2,1,0:T(4,128)(2,1)}), bf16[16,4,1024]{2,1,0:T(4,128)(2,1)S(1)}, u32[]{:S(2)}, u32[]{:S(2)}) async-start(bf16[16,4,1024]{2,1,0:T(4,128)(2,1)} %reshape.619), calls=%async_computation.3 | async-start | bytes 262144 | tf_op jit(solution)/shard_map/all_to_all | solution.py:53
  151.9 0.8 fusion.4
  152.7 1.9 %collective-permute-start.14 = (bf16[256,256]{1,0:T(8,128)(2,1)S(1)}, bf16[256,256]{1,0:T(8,128)(2,1)S(1)}, u32[]{:S(2)}, u32[]{:S(2)}) collective-permute-start(bf16[256,256]{1,0:T(8,128)(2,1)S(1)} %slice.151), channel_id=1, source_target_pairs={{0,4},{4,0},{1,5},{5,1},{2,6},{6,2},{3,7},{7,3},{8,12},{12,8},{9,1... | collective-permute-start | bytes 393224 | tf_op jit(solution)/shard_map/ppermute | solution.py:276
  154.6 1.3 collective-permute-done.14
  156.0 10.1 %all-to-all-done.3 = bf16[16,4,1024]{2,1,0:T(4,128)(2,1)S(1)} async-done(((bf16[16,4,1024]{2,1,0:T(4,128)(2,1)}), bf16[16,4,1024]{2,1,0:T(4,128)(2,1)S(1)}, u32[]{:S(2)}, u32[]{:S(2)}) %all-to-all-start.3) | async-done | bytes 131104 | tf_op jit(solution)/shard_map/all_to_all | solution.py:53
  166.1 0.6 broadcast_in_dim.8
  166.8 3.3 %all-to-all-start.4 = ((f32[4,4,1024]{2,1,0:T(4,128)}), f32[4,4,1024]{2,1,0:T(4,128)S(1)}, u32[]{:S(2)}, u32[]{:S(2)}) async-start(f32[4,4,1024]{2,1,0:T(4,128)} %broadcast_in_dim.8), calls=%async_computation.4 | async-start | bytes 131072 | tf_op jit(solution)/shard_map/all_to_all | solution.py:53
  170.0 1.2 fusion.5
  171.2 4.4 %all-to-all-done.4 = f32[4,4,1024]{2,1,0:T(4,128)S(1)} async-done(((f32[4,4,1024]{2,1,0:T(4,128)}), f32[4,4,1024]{2,1,0:T(4,128)S(1)}, u32[]{:S(2)}, u32[]{:S(2)}) %all-to-all-start.4) | async-done | bytes 65568 | tf_op jit(solution)/shard_map/all_to_all | solution.py:53
  175.7 0.6 slice.163
  176.3 0.6 copy-done.3
  (80 shorter events, 5.1 us)
Async XLA Ops:
  0.6 24.7 %copy-start.1 = (s32[1,128]{1,0:T(1,128)S(1)}, s32[1,128]{1,0:T(1,128)}, u32[]{:S(2)}) copy-start(s32[1,128]{1,0:T(1,128)} %param.11) | copy-start | bytes 1540
  0.6 24.9 %copy-start = (bf16[1,256,512]{2,1,0:T(8,128)(2,1)S(1)}, bf16[1,256,512]{2,1,0:T(8,128)(2,1)}, u32[]{:S(2)}) copy-start(bf16[1,256,512]{2,1,0:T(8,128)(2,1)} %param.7) | copy-start | bytes 786436
  2.1 27.9 %all-to-all-start = ((bf16[16,8,256]{2,1,0:T(8,128)(2,1)}), bf16[16,8,256]{2,1,0:T(8,128)(2,1)S(1)}, u32[]{:S(2)}, u32[]{:S(2)}) async-start(bf16[16,8,256]{2,1,0:T(8,128)(2,1)} %broadcast_in_dim.6), calls=%async_computation | async-start | bytes 131072 | tf_op jit(solution)/shard_map/all_to_all | solution.py:53
  17.3 61.8 %collective-permute-start.1 = (bf16[256,512]{1,0:T(8,128)(2,1)}, bf16[256,512]{1,0:T(8,128)(2,1)S(1)}, u32[]{:S(2)}, u32[]{:S(2)}) collective-permute-start(bf16[256,512]{1,0:T(8,128)(2,1)} %bitcast.68), channel_id=1, source_target_pairs={{0,4},{4,0},{1,5},{5,1},{2,6},{6,2},{3,7},{7,3},{8,12},{12,8},{9,1... | collective-permute-start | bytes 786440 | tf_op jit(solution)/shard_map/ppermute | solution.py:232
  19.9 24.1 %collective-permute-start = (s32[2,128]{1,0:T(2,128)S(1)}, s32[2,128]{1,0:T(2,128)S(1)}, u32[]{:S(2)}, u32[]{:S(2)}) collective-permute-start(s32[2,128]{1,0:T(2,128)S(1)} %pad_add_fusion.1), channel_id=1, source_target_pairs={{0,4},{4,0},{1,5},{5,1},{2,6},{6,2},{3,7},{7,3},{8,12},{12,8},{9,1... | collective-permute-start | bytes 3080 | tf_op jit(solution)/shard_map/ppermute | solution.py:240
  26.7 17.3 %copy-start.2 = (s32[1,128]{1,0:T(1,128)S(1)}, s32[1,128]{1,0:T(1,128)}, u32[]{:S(2)}) copy-start(s32[1,128]{1,0:T(1,128)} %param.10) | copy-start | bytes 1540
  30.0 45.7 %all-to-all-start.1 = ((bf16[128,8,256]{2,1,0:T(8,128)(2,1)}), bf16[128,8,256]{2,1,0:T(8,128)(2,1)S(1)}, u32[]{:S(2)}, u32[]{:S(2)}) async-start(bf16[128,8,256]{2,1,0:T(8,128)(2,1)} %bitcast.11), calls=%async_computation.1 | async-start | bytes 1048576 | tf_op jit(solution)/shard_map/all_to_all | solution.py:53
  44.0 8.0 %collective-permute-start.2 = (bf16[128,256]{1,0:T(8,128)(2,1)S(1)}, bf16[128,256]{1,0:T(8,128)(2,1)S(1)}, u32[]{:S(2)}, u32[]{:S(2)}) collective-permute-start(bf16[128,256]{1,0:T(8,128)(2,1)S(1)} %bitcast.54), channel_id=1, source_target_pairs={{0,256},{128,384},{256,0},{384,128},{1,257},{129,385},{257,1},{385... | collective-permute-start | bytes 196616 | tf_op jit(solution)/shard_map/ppermute | solution.py:63
  52.1 7.4 %collective-permute-start.3 = (bf16[256,256]{1,0:T(8,128)(2,1)S(1)}, bf16[256,256]{1,0:T(8,128)(2,1)S(1)}, u32[]{:S(2)}, u32[]{:S(2)}) collective-permute-start(bf16[256,256]{1,0:T(8,128)(2,1)S(1)} %pad_maximum_fusion.5), channel_id=1, source_target_pairs={{0,128},{128,0},{256,384},{384,256},{1,129},{129,1},{257,385},{385... | collective-permute-start | bytes 393224 | tf_op jit(solution)/shard_map/ppermute | solution.py:63
  60.1 3.2 %collective-permute-start.4 = (bf16[256,256]{1,0:T(8,128)(2,1)S(1)}, bf16[256,256]{1,0:T(8,128)(2,1)S(1)}, u32[]{:S(2)}, u32[]{:S(2)}) collective-permute-start(bf16[256,256]{1,0:T(8,128)(2,1)S(1)} %get-tuple-element.30), channel_id=1, source_target_pairs={{0,4},{4,0},{1,5},{5,1},{2,6},{6,2},{3,7},{7,3},{8,12},{12,8},{9,1... | collective-permute-start | bytes 393224 | tf_op jit(solution)/shard_map/ppermute | solution.py:220
  63.3 15.8 %copy-start.4 = (bf16[1,256,512]{2,1,0:T(8,128)(2,1)S(1)}, bf16[1,256,512]{2,1,0:T(8,128)(2,1)}, u32[]{:S(2)}) copy-start(bf16[1,256,512]{2,1,0:T(8,128)(2,1)} %param.6) | copy-start | bytes 786436
  63.3 16.3 %collective-permute-start.5 = (bf16[512,256]{1,0:T(8,128)(2,1)S(1)}, bf16[512,256]{1,0:T(8,128)(2,1)S(1)}, u32[]{:S(2)}, u32[]{:S(2)}) collective-permute-start(bf16[512,256]{1,0:T(8,128)(2,1)S(1)} %pad_maximum_fusion.3.w0_ref), channel_id=1, source_target_pairs={{0,1},{1,2},{2,3},{3,0},{4,5},{5,6},{6,7},{7,4},{8,9},{9,10},{10,1... | collective-permute-start | bytes 786440 | tf_op jit(solution)/shard_map/ppermute | solution.py:58
  67.0 14.8 %collective-permute-start.6 = (bf16[512,256]{1,0:T(8,128)(2,1)S(1)}, bf16[512,256]{1,0:T(8,128)(2,1)S(1)}, u32[]{:S(2)}, u32[]{:S(2)}) collective-permute-start(bf16[512,256]{1,0:T(8,128)(2,1)S(1)} %pad_maximum_fusion.3.w0_ref), channel_id=1, source_target_pairs={{0,2},{1,3},{2,0},{3,1},{4,6},{5,7},{6,4},{7,5},{8,10},{9,11},{10,... | collective-permute-start | bytes 786440 | tf_op jit(solution)/shard_map/ppermute | solution.py:58
  71.8 11.3 %collective-permute-start.7 = (bf16[512,256]{1,0:T(8,128)(2,1)S(1)}, bf16[512,256]{1,0:T(8,128)(2,1)S(1)}, u32[]{:S(2)}, u32[]{:S(2)}) collective-permute-start(bf16[512,256]{1,0:T(8,128)(2,1)S(1)} %pad_maximum_fusion.3.w0_ref), channel_id=1, source_target_pairs={{0,3},{1,0},{2,1},{3,2},{4,7},{5,4},{6,5},{7,6},{8,11},{9,8},{10,9... | collective-permute-start | bytes 786440 | tf_op jit(solution)/shard_map/ppermute | solution.py:58
  76.8 6.3 %collective-permute-start.8 = (bf16[256,512]{1,0:T(8,128)(2,1)S(1)}, bf16[256,512]{1,0:T(8,128)(2,1)S(1)}, u32[]{:S(2)}, u32[]{:S(2)}) collective-permute-start(bf16[256,512]{1,0:T(8,128)(2,1)S(1)} %pad_maximum_fusion.4.gown_ref), channel_id=1, source_target_pairs={{0,4},{4,0},{1,5},{5,1},{2,6},{6,2},{3,7},{7,3},{8,12},{12,8},{9,1... | collective-permute-start | bytes 786440 | tf_op jit(solution)/shard_map/ppermute | solution.py:235
  90.4 4.7 %collective-permute-start.9 = (bf16[256,1024]{1,0:T(8,128)(2,1)S(1)}, bf16[256,1024]{1,0:T(8,128)(2,1)S(1)}, u32[]{:S(2)}, u32[]{:S(2)}) collective-permute-start(bf16[256,1024]{1,0:T(8,128)(2,1)S(1)} %get-tuple-element.13), channel_id=1, source_target_pairs={{0,4},{4,0},{1,5},{5,1},{2,6},{6,2},{3,7},{7,3},{8,12},{12,8},{9,1... | collective-permute-start | bytes 1572872 | tf_op jit(solution)/shard_map/ppermute | solution.py:251
  92.6 7.2 %collective-permute-start.13 = (bf16[512,256]{1,0:T(8,128)(2,1)S(1)}, bf16[512,256]{1,0:T(8,128)(2,1)S(1)}, u32[]{:S(2)}, u32[]{:S(2)}) collective-permute-start(bf16[512,256]{1,0:T(8,128)(2,1)S(1)} %get-tuple-element.16), channel_id=1, source_target_pairs={{0,4},{4,0},{1,5},{5,1},{2,6},{6,2},{3,7},{7,3},{8,12},{12,8},{9,1... | collective-permute-start | bytes 786440 | tf_op jit(solution)/shard_map/ppermute | solution.py:246
  95.4 21.0 %collective-permute-start.10 = (bf16[256,1024]{1,0:T(8,128)(2,1)S(1)}, bf16[256,1024]{1,0:T(8,128)(2,1)S(1)}, u32[]{:S(2)}, u32[]{:S(2)}) collective-permute-start(bf16[256,1024]{1,0:T(8,128)(2,1)S(1)} %broadcast_select_fusion), channel_id=1, source_target_pairs={{0,1},{1,0},{2,3},{3,2},{4,5},{5,4},{6,7},{7,6},{8,9},{9,8},{10,11... | collective-permute-start | bytes 1572872 | tf_op jit(solution)/shard_map/ppermute | solution.py:63
  101.1 46.5 %all-to-all-start.2 = ((bf16[64,16,256]{2,1,0:T(8,128)(2,1)}), bf16[64,16,256]{2,1,0:T(8,128)(2,1)S(1)}, u32[]{:S(2)}, u32[]{:S(2)}) async-start(bf16[64,16,256]{2,1,0:T(8,128)(2,1)} %bitcast.21), calls=%async_computation.2 | async-start | bytes 1048576 | tf_op jit(solution)/shard_map/all_to_all | solution.py:53
  116.6 10.6 %collective-permute-start.11 = (bf16[128,1024]{1,0:T(8,128)(2,1)S(1)}, bf16[128,1024]{1,0:T(8,128)(2,1)S(1)}, u32[]{:S(2)}, u32[]{:S(2)}) collective-permute-start(bf16[128,1024]{1,0:T(8,128)(2,1)S(1)} %bitcast.60), channel_id=1, source_target_pairs={{0,128},{128,0},{256,384},{384,256},{1,129},{129,1},{257,385},{385... | collective-permute-start | bytes 786440 | tf_op jit(solution)/shard_map/ppermute | solution.py:63
  127.4 9.0 %collective-permute-start.12 = (bf16[64,1024]{1,0:T(8,128)(2,1)S(1)}, bf16[64,1024]{1,0:T(8,128)(2,1)S(1)}, u32[]{:S(2)}, u32[]{:S(2)}) collective-permute-start(bf16[64,1024]{1,0:T(8,128)(2,1)S(1)} %select_bitcast_fusion), channel_id=1, source_target_pairs={{0,256},{128,384},{256,0},{384,128},{1,257},{129,385},{257,1},{385... | collective-permute-start | bytes 393224 | tf_op jit(solution)/shard_map/ppermute | solution.py:63
  148.4 17.7 %all-to-all-start.3 = ((bf16[16,4,1024]{2,1,0:T(4,128)(2,1)}), bf16[16,4,1024]{2,1,0:T(4,128)(2,1)S(1)}, u32[]{:S(2)}, u32[]{:S(2)}) async-start(bf16[16,4,1024]{2,1,0:T(4,128)(2,1)} %reshape.619), calls=%async_computation.3 | async-start | bytes 262144 | tf_op jit(solution)/shard_map/all_to_all | solution.py:53
  152.7 3.2 %collective-permute-start.14 = (bf16[256,256]{1,0:T(8,128)(2,1)S(1)}, bf16[256,256]{1,0:T(8,128)(2,1)S(1)}, u32[]{:S(2)}, u32[]{:S(2)}) collective-permute-start(bf16[256,256]{1,0:T(8,128)(2,1)S(1)} %slice.151), channel_id=1, source_target_pairs={{0,4},{4,0},{1,5},{5,1},{2,6},{6,2},{3,7},{7,3},{8,12},{12,8},{9,1... | collective-permute-start | bytes 393224 | tf_op jit(solution)/shard_map/ppermute | solution.py:276
  166.8 8.9 %all-to-all-start.4 = ((f32[4,4,1024]{2,1,0:T(4,128)}), f32[4,4,1024]{2,1,0:T(4,128)S(1)}, u32[]{:S(2)}, u32[]{:S(2)}) async-start(f32[4,4,1024]{2,1,0:T(4,128)} %broadcast_in_dim.8), calls=%async_computation.4 | async-start | bytes 131072 | tf_op jit(solution)/shard_map/all_to_all | solution.py:53
  176.3 0.6 copy-start.3

commit v11 on v10

--- a/solution.py
+++ b/solution.py
@@ -219,7 +219,8 @@
     kept = jnp.where(core == 0, picked[0], picked[1])
     theirs = lax.ppermute(jnp.where(core == 0, picked[1], picked[0]), "core", pair)
     parts = jnp.concatenate([kept, theirs], axis=0)
-    weights = [parts] + [shift(parts, "rep", k) for k in range(1, nr)]
+    sent = {k: shift(parts, "rep", k) for k in (2, 1, 3)}
+    weights = [parts] + [sent[k] for k in range(1, nr)]
 
     def order(count):
         nat = jnp.arange(count, dtype=jnp.int32)

time: 179 us -> 179 us (level)
  no operation moved by 1% of the time
where the time goes in v11:
time: 179 us; the launch traced here: 177 us
  starting transfers between devices  92.8 us (52%)
  waiting for transfers between devices  58.8 us (33%)
  matrix products  7.79 us (4%)
  Pallas kernels  7.28 us (4%)
  other arithmetic  5 us (3%)
  local copies, waits for them, and re-layouts  3.95 us (2%)
    all_to_all x5, starting transfers between devices, swap(): return lax.all_to_all(block, axis, split_axis=0, concat_axis=0, tiled=True)  50.8 us
    all_to_all x5, waiting for transfers between devices, swap(): return lax.all_to_all(block, axis, split_axis=0, concat_axis=0, tiled=True)  29.6 us
    ppermute x5, waiting for transfers between devices, flip(): lax.ppermute(block, axis, [(here, here ^ bit) for here in range(count)])  23.2 us
    ppermute x5, starting transfers between devices, flip(): lax.ppermute(block, axis, [(here, here ^ bit) for here in range(count)])  15.7 us
    ppermute x3, starting transfers between devices, shift(): lax.ppermute(block, axis, [(here, (here + step) % count) for here in rang...  11.7 us
    dot_general x10, matrix products, mm(): lax.dot_general(left, right, (dims, ((), ())), preferred_element_type=jnp...  7.79 us
    pallas_call x1, Pallas kernels, patch_step(): pl.pallas_call(patch_body, out_shape=[jax.ShapeDtypeStruct((CORES * rows,...  7.28 us
  transfers between devices with their start and end apart: 20, of which 13 were waited for; matrix products, arithmetic and copies ran while one was open for 7% of the time, Pallas kernels for 0%

profile of v11, /device:TPU:6, one launch (start us, length us, event | category | flops | bytes accessed | tf_op | source)
XLA Modules:
  0.0 176.9 jit_solution(6530382850099891245)
XLA Ops:
  0.7 0.7 fusion.37
  1.4 0.6 broadcast_in_dim.6
  2.1 15.2 %all-to-all-start = ((bf16[16,8,256]{2,1,0:T(8,128)(2,1)}), bf16[16,8,256]{2,1,0:T(8,128)(2,1)S(1)}, u32[]{:S(2)}, u32[]{:S(2)}) async-start(bf16[16,8,256]{2,1,0:T(8,128)(2,1)} %broadcast_in_dim.6), calls=%async_computation | async-start | bytes 131072 | tf_op jit(solution)/shard_map/all_to_all | solution.py:53
  17.3 1.9 %collective-permute-start.1 = (bf16[256,512]{1,0:T(8,128)(2,1)}, bf16[256,512]{1,0:T(8,128)(2,1)S(1)}, u32[]{:S(2)}, u32[]{:S(2)}) collective-permute-start(bf16[256,512]{1,0:T(8,128)(2,1)} %bitcast.68), channel_id=1, source_target_pairs={{0,4},{4,0},{1,5},{5,1},{2,6},{6,2},{3,7},{7,3},{8,12},{12,8},{9,1... | collective-permute-start | bytes 786440 | tf_op jit(solution)/shard_map/ppermute | solution.py:233
  19.2 0.7 pad_add_fusion.1
  19.9 2.4 %collective-permute-start = (s32[2,128]{1,0:T(2,128)S(1)}, s32[2,128]{1,0:T(2,128)S(1)}, u32[]{:S(2)}, u32[]{:S(2)}) collective-permute-start(s32[2,128]{1,0:T(2,128)S(1)} %pad_add_fusion.1), channel_id=1, source_target_pairs={{0,4},{4,0},{1,5},{5,1},{2,6},{6,2},{3,7},{7,3},{8,12},{12,8},{9,1... | collective-permute-start | bytes 3080 | tf_op jit(solution)/shard_map/ppermute | solution.py:241
  22.3 0.7 and_select_fusion.8
  23.0 0.7 fusion.69
  24.1 1.2 fusion.8
  25.6 1.2 fusion.2
  26.8 3.2 %all-to-all-done = bf16[16,8,256]{2,1,0:T(8,128)(2,1)S(1)} async-done(((bf16[16,8,256]{2,1,0:T(8,128)(2,1)}), bf16[16,8,256]{2,1,0:T(8,128)(2,1)S(1)}, u32[]{:S(2)}, u32[]{:S(2)}) %all-to-all-start) | async-done | bytes 65568 | tf_op jit(solution)/shard_map/all_to_all | solution.py:53
  30.0 13.6 %all-to-all-start.1 = ((bf16[128,8,256]{2,1,0:T(8,128)(2,1)}), bf16[128,8,256]{2,1,0:T(8,128)(2,1)S(1)}, u32[]{:S(2)}, u32[]{:S(2)}) async-start(bf16[128,8,256]{2,1,0:T(8,128)(2,1)} %bitcast.11), calls=%async_computation.1 | async-start | bytes 1048576 | tf_op jit(solution)/shard_map/all_to_all | solution.py:53
  44.0 2.9 %collective-permute-start.2 = (bf16[128,256]{1,0:T(8,128)(2,1)S(1)}, bf16[128,256]{1,0:T(8,128)(2,1)S(1)}, u32[]{:S(2)}, u32[]{:S(2)}) collective-permute-start(bf16[128,256]{1,0:T(8,128)(2,1)S(1)} %bitcast.54), channel_id=1, source_target_pairs={{0,256},{128,384},{256,0},{384,128},{1,257},{129,385},{257,1},{385... | collective-permute-start | bytes 196616 | tf_op jit(solution)/shard_map/ppermute | solution.py:63
  47.0 5.1 %collective-permute-done.2 = bf16[128,256]{1,0:T(8,128)(2,1)S(1)} collective-permute-done((bf16[128,256]{1,0:T(8,128)(2,1)S(1)}, bf16[128,256]{1,0:T(8,128)(2,1)S(1)}, u32[]{:S(2)}, u32[]{:S(2)}) %collective-permute-start.2) | collective-permute-done | bytes 65568 | tf_op jit(solution)/shard_map/ppermute | solution.py:63
  52.1 2.5 %collective-permute-start.3 = (bf16[256,256]{1,0:T(8,128)(2,1)S(1)}, bf16[256,256]{1,0:T(8,128)(2,1)S(1)}, u32[]{:S(2)}, u32[]{:S(2)}) collective-permute-start(bf16[256,256]{1,0:T(8,128)(2,1)S(1)} %pad_maximum_fusion.5), channel_id=1, source_target_pairs={{0,128},{128,0},{256,384},{384,256},{1,129},{129,1},{257,385},{385... | collective-permute-start | bytes 393224 | tf_op jit(solution)/shard_map/ppermute | solution.py:63
  54.6 4.9 %collective-permute-done.3 = bf16[256,256]{1,0:T(8,128)(2,1)S(1)} collective-permute-done((bf16[256,256]{1,0:T(8,128)(2,1)S(1)}, bf16[256,256]{1,0:T(8,128)(2,1)S(1)}, u32[]{:S(2)}, u32[]{:S(2)}) %collective-permute-start.3) | collective-permute-done | bytes 131104 | tf_op jit(solution)/shard_map/ppermute | solution.py:63
  60.1 1.9 %collective-permute-start.4 = (bf16[256,256]{1,0:T(8,128)(2,1)S(1)}, bf16[256,256]{1,0:T(8,128)(2,1)S(1)}, u32[]{:S(2)}, u32[]{:S(2)}) collective-permute-start(bf16[256,256]{1,0:T(8,128)(2,1)S(1)} %get-tuple-element.30), channel_id=1, source_target_pairs={{0,4},{4,0},{1,5},{5,1},{2,6},{6,2},{3,7},{7,3},{8,12},{12,8},{9,1... | collective-permute-start | bytes 393224 | tf_op jit(solution)/shard_map/ppermute | solution.py:220
  62.0 1.3 collective-permute-done.4
  63.3 3.6 %collective-permute-start.5 = (bf16[512,256]{1,0:T(8,128)(2,1)S(1)}, bf16[512,256]{1,0:T(8,128)(2,1)S(1)}, u32[]{:S(2)}, u32[]{:S(2)}) collective-permute-start(bf16[512,256]{1,0:T(8,128)(2,1)S(1)} %pad_maximum_fusion.3.w0_ref), channel_id=1, source_target_pairs={{0,1},{1,2},{2,3},{3,0},{4,5},{5,6},{6,7},{7,4},{8,9},{9,10},{10,1... | collective-permute-start | bytes 786440 | tf_op jit(solution)/shard_map/ppermute | solution.py:58
  67.0 4.8 %collective-permute-start.6 = (bf16[512,256]{1,0:T(8,128)(2,1)S(1)}, bf16[512,256]{1,0:T(8,128)(2,1)S(1)}, u32[]{:S(2)}, u32[]{:S(2)}) collective-permute-start(bf16[512,256]{1,0:T(8,128)(2,1)S(1)} %pad_maximum_fusion.3.w0_ref), channel_id=1, source_target_pairs={{0,2},{1,3},{2,0},{3,1},{4,6},{5,7},{6,4},{7,5},{8,10},{9,11},{10,... | collective-permute-start | bytes 786440 | tf_op jit(solution)/shard_map/ppermute | solution.py:58
  71.8 3.3 %collective-permute-start.7 = (bf16[512,256]{1,0:T(8,128)(2,1)S(1)}, bf16[512,256]{1,0:T(8,128)(2,1)S(1)}, u32[]{:S(2)}, u32[]{:S(2)}) collective-permute-start(bf16[512,256]{1,0:T(8,128)(2,1)S(1)} %pad_maximum_fusion.3.w0_ref), channel_id=1, source_target_pairs={{0,3},{1,0},{2,1},{3,2},{4,7},{5,4},{6,5},{7,6},{8,11},{9,8},{10,9... | collective-permute-start | bytes 786440 | tf_op jit(solution)/shard_map/ppermute | solution.py:58
  75.0 0.7 all-to-all-done.1
  76.8 2.1 %collective-permute-start.8 = (bf16[256,512]{1,0:T(8,128)(2,1)S(1)}, bf16[256,512]{1,0:T(8,128)(2,1)S(1)}, u32[]{:S(2)}, u32[]{:S(2)}) collective-permute-start(bf16[256,512]{1,0:T(8,128)(2,1)S(1)} %pad_maximum_fusion.4.gown_ref), channel_id=1, source_target_pairs={{0,4},{4,0},{1,5},{5,1},{2,6},{6,2},{3,7},{7,3},{8,12},{12,8},{9,1... | collective-permute-start | bytes 786440 | tf_op jit(solution)/shard_map/ppermute | solution.py:236
  79.7 2.1 %collective-permute-done.6.w2_ref = bf16[512,256]{1,0:T(8,128)(2,1)S(1)} collective-permute-done((bf16[512,256]{1,0:T(8,128)(2,1)S(1)}, bf16[512,256]{1,0:T(8,128)(2,1)S(1)}, u32[]{:S(2)}, u32[]{:S(2)}) %collective-permute-start.6) | collective-permute-done | bytes 262176 | tf_op jit(solution)/shard_map/ppermute | solution.py:58
  81.8 1.3 collective-permute-done.7.w3_ref
  83.1 7.3 %shard_map.85 = (f32[512,256]{1,0:T(8,128)S(1)}, bf16[512,256]{1,0:T(8,128)(2,1)S(1)}, bf16[256,1024]{1,0:T(8,128)(2,1)S(1)}, bf16[256,1024]{1,0:T(8,128)(2,1)S(1)}) custom-call(s32[2]{0:T(128)S(1)} %pad_add_fusion.3.place_ref, bf16[512,512]{1,0:T(8,128)(2,1)S(1)} %convolution_convert_fusion.x_ref, bf16[512,256]{1,0:T(8,128)(2,1)S(1)} %pad_maximum_fusion.3.w0_ref, ...), custom_call_target="tpu_custom_call" | custom-call | tf_op jit(solution)/shard_map/pallas_call | solution.py:146
  90.4 1.9 %collective-permute-start.9 = (bf16[256,1024]{1,0:T(8,128)(2,1)S(1)}, bf16[256,1024]{1,0:T(8,128)(2,1)S(1)}, u32[]{:S(2)}, u32[]{:S(2)}) collective-permute-start(bf16[256,1024]{1,0:T(8,128)(2,1)S(1)} %get-tuple-element.13), channel_id=1, source_target_pairs={{0,4},{4,0},{1,5},{5,1},{2,6},{6,2},{3,7},{7,3},{8,12},{12,8},{9,1... | collective-permute-start | bytes 1572872 | tf_op jit(solution)/shard_map/ppermute | solution.py:252
  92.6 2.4 %collective-permute-start.13 = (bf16[512,256]{1,0:T(8,128)(2,1)S(1)}, bf16[512,256]{1,0:T(8,128)(2,1)S(1)}, u32[]{:S(2)}, u32[]{:S(2)}) collective-permute-start(bf16[512,256]{1,0:T(8,128)(2,1)S(1)} %get-tuple-element.16), channel_id=1, source_target_pairs={{0,4},{4,0},{1,5},{5,1},{2,6},{6,2},{3,7},{7,3},{8,12},{12,8},{9,1... | collective-permute-start | bytes 786440 | tf_op jit(solution)/shard_map/ppermute | solution.py:247
  95.4 4.4 %collective-permute-start.10 = (bf16[256,1024]{1,0:T(8,128)(2,1)S(1)}, bf16[256,1024]{1,0:T(8,128)(2,1)S(1)}, u32[]{:S(2)}, u32[]{:S(2)}) collective-permute-start(bf16[256,1024]{1,0:T(8,128)(2,1)S(1)} %broadcast_select_fusion), channel_id=1, source_target_pairs={{0,1},{1,0},{2,3},{3,2},{4,5},{5,4},{6,7},{7,6},{8,9},{9,8},{10,11... | collective-permute-start | bytes 1572872 | tf_op jit(solution)/shard_map/ppermute | solution.py:63
  99.8 1.3 fusion.3
  101.1 15.2 %all-to-all-start.2 = ((bf16[64,16,256]{2,1,0:T(8,128)(2,1)}), bf16[64,16,256]{2,1,0:T(8,128)(2,1)S(1)}, u32[]{:S(2)}, u32[]{:S(2)}) async-start(bf16[64,16,256]{2,1,0:T(8,128)(2,1)} %bitcast.21), calls=%async_computation.2 | async-start | bytes 1048576 | tf_op jit(solution)/shard_map/all_to_all | solution.py:53
  116.6 2.7 %collective-permute-start.11 = (bf16[128,1024]{1,0:T(8,128)(2,1)S(1)}, bf16[128,1024]{1,0:T(8,128)(2,1)S(1)}, u32[]{:S(2)}, u32[]{:S(2)}) collective-permute-start(bf16[128,1024]{1,0:T(8,128)(2,1)S(1)} %bitcast.60), channel_id=1, source_target_pairs={{0,128},{128,0},{256,384},{384,256},{1,129},{129,1},{257,385},{385... | collective-permute-start | bytes 786440 | tf_op jit(solution)/shard_map/ppermute | solution.py:63
  119.5 7.7 %collective-permute-done.11 = bf16[128,1024]{1,0:T(8,128)(2,1)S(1)} collective-permute-done((bf16[128,1024]{1,0:T(8,128)(2,1)S(1)}, bf16[128,1024]{1,0:T(8,128)(2,1)S(1)}, u32[]{:S(2)}, u32[]{:S(2)}) %collective-permute-start.11) | collective-permute-done | bytes 262176 | tf_op jit(solution)/shard_map/ppermute | solution.py:63
  127.4 3.2 %collective-permute-start.12 = (bf16[64,1024]{1,0:T(8,128)(2,1)S(1)}, bf16[64,1024]{1,0:T(8,128)(2,1)S(1)}, u32[]{:S(2)}, u32[]{:S(2)}) collective-permute-start(bf16[64,1024]{1,0:T(8,128)(2,1)S(1)} %select_bitcast_fusion), channel_id=1, source_target_pairs={{0,256},{128,384},{256,0},{384,128},{1,257},{129,385},{257,1},{385... | collective-permute-start | bytes 393224 | tf_op jit(solution)/shard_map/ppermute | solution.py:63
  130.8 5.5 %collective-permute-done.12 = bf16[64,1024]{1,0:T(8,128)(2,1)S(1)} collective-permute-done((bf16[64,1024]{1,0:T(8,128)(2,1)S(1)}, bf16[64,1024]{1,0:T(8,128)(2,1)S(1)}, u32[]{:S(2)}, u32[]{:S(2)}) %collective-permute-start.12) | collective-permute-done | bytes 131104 | tf_op jit(solution)/shard_map/ppermute | solution.py:63
  136.4 11.3 %all-to-all-done.2 = bf16[64,16,256]{2,1,0:T(8,128)(2,1)S(1)} async-done(((bf16[64,16,256]{2,1,0:T(8,128)(2,1)}), bf16[64,16,256]{2,1,0:T(8,128)(2,1)S(1)}, u32[]{:S(2)}, u32[]{:S(2)}) %all-to-all-start.2) | async-done | bytes 524320 | tf_op jit(solution)/shard_map/all_to_all | solution.py:53
  147.7 0.7 reshape.619
  148.4 3.5 %all-to-all-start.3 = ((bf16[16,4,1024]{2,1,0:T(4,128)(2,1)}), bf16[16,4,1024]{2,1,0:T(4,128)(2,1)S(1)}, u32[]{:S(2)}, u32[]{:S(2)}) async-start(bf16[16,4,1024]{2,1,0:T(4,128)(2,1)} %reshape.619), calls=%async_computation.3 | async-start | bytes 262144 | tf_op jit(solution)/shard_map/all_to_all | solution.py:53
  151.9 0.8 fusion.4
  152.7 1.9 %collective-permute-start.14 = (bf16[256,256]{1,0:T(8,128)(2,1)S(1)}, bf16[256,256]{1,0:T(8,128)(2,1)S(1)}, u32[]{:S(2)}, u32[]{:S(2)}) collective-permute-start(bf16[256,256]{1,0:T(8,128)(2,1)S(1)} %slice.151), channel_id=1, source_target_pairs={{0,4},{4,0},{1,5},{5,1},{2,6},{6,2},{3,7},{7,3},{8,12},{12,8},{9,1... | collective-permute-start | bytes 393224 | tf_op jit(solution)/shard_map/ppermute | solution.py:277
  154.6 1.3 collective-permute-done.14
  156.0 10.1 %all-to-all-done.3 = bf16[16,4,1024]{2,1,0:T(4,128)(2,1)S(1)} async-done(((bf16[16,4,1024]{2,1,0:T(4,128)(2,1)}), bf16[16,4,1024]{2,1,0:T(4,128)(2,1)S(1)}, u32[]{:S(2)}, u32[]{:S(2)}) %all-to-all-start.3) | async-done | bytes 131104 | tf_op jit(solution)/shard_map/all_to_all | solution.py:53
  166.1 0.6 broadcast_in_dim.8
  166.8 3.3 %all-to-all-start.4 = ((f32[4,4,1024]{2,1,0:T(4,128)}), f32[4,4,1024]{2,1,0:T(4,128)S(1)}, u32[]{:S(2)}, u32[]{:S(2)}) async-start(f32[4,4,1024]{2,1,0:T(4,128)} %broadcast_in_dim.8), calls=%async_computation.4 | async-start | bytes 131072 | tf_op jit(solution)/shard_map/all_to_all | solution.py:53
  170.0 1.2 fusion.5
  171.2 4.4 %all-to-all-done.4 = f32[4,4,1024]{2,1,0:T(4,128)S(1)} async-done(((f32[4,4,1024]{2,1,0:T(4,128)}), f32[4,4,1024]{2,1,0:T(4,128)S(1)}, u32[]{:S(2)}, u32[]{:S(2)}) %all-to-all-start.4) | async-done | bytes 65568 | tf_op jit(solution)/shard_map/all_to_all | solution.py:53
  175.7 0.6 slice.163
  176.3 0.6 copy-done.3
  (80 shorter events, 5.1 us)
Async XLA Ops:
  0.6 24.7 %copy-start.1 = (s32[1,128]{1,0:T(1,128)S(1)}, s32[1,128]{1,0:T(1,128)}, u32[]{:S(2)}) copy-start(s32[1,128]{1,0:T(1,128)} %param.11) | copy-start | bytes 1540
  0.6 24.9 %copy-start = (bf16[1,256,512]{2,1,0:T(8,128)(2,1)S(1)}, bf16[1,256,512]{2,1,0:T(8,128)(2,1)}, u32[]{:S(2)}) copy-start(bf16[1,256,512]{2,1,0:T(8,128)(2,1)} %param.7) | copy-start | bytes 786436
  2.1 27.9 %all-to-all-start = ((bf16[16,8,256]{2,1,0:T(8,128)(2,1)}), bf16[16,8,256]{2,1,0:T(8,128)(2,1)S(1)}, u32[]{:S(2)}, u32[]{:S(2)}) async-start(bf16[16,8,256]{2,1,0:T(8,128)(2,1)} %broadcast_in_dim.6), calls=%async_computation | async-start | bytes 131072 | tf_op jit(solution)/shard_map/all_to_all | solution.py:53
  17.3 61.8 %collective-permute-start.1 = (bf16[256,512]{1,0:T(8,128)(2,1)}, bf16[256,512]{1,0:T(8,128)(2,1)S(1)}, u32[]{:S(2)}, u32[]{:S(2)}) collective-permute-start(bf16[256,512]{1,0:T(8,128)(2,1)} %bitcast.68), channel_id=1, source_target_pairs={{0,4},{4,0},{1,5},{5,1},{2,6},{6,2},{3,7},{7,3},{8,12},{12,8},{9,1... | collective-permute-start | bytes 786440 | tf_op jit(solution)/shard_map/ppermute | solution.py:233
  19.9 24.1 %collective-permute-start = (s32[2,128]{1,0:T(2,128)S(1)}, s32[2,128]{1,0:T(2,128)S(1)}, u32[]{:S(2)}, u32[]{:S(2)}) collective-permute-start(s32[2,128]{1,0:T(2,128)S(1)} %pad_add_fusion.1), channel_id=1, source_target_pairs={{0,4},{4,0},{1,5},{5,1},{2,6},{6,2},{3,7},{7,3},{8,12},{12,8},{9,1... | collective-permute-start | bytes 3080 | tf_op jit(solution)/shard_map/ppermute | solution.py:241
  26.7 17.3 %copy-start.2 = (s32[1,128]{1,0:T(1,128)S(1)}, s32[1,128]{1,0:T(1,128)}, u32[]{:S(2)}) copy-start(s32[1,128]{1,0:T(1,128)} %param.10) | copy-start | bytes 1540
  30.0 45.7 %all-to-all-start.1 = ((bf16[128,8,256]{2,1,0:T(8,128)(2,1)}), bf16[128,8,256]{2,1,0:T(8,128)(2,1)S(1)}, u32[]{:S(2)}, u32[]{:S(2)}) async-start(bf16[128,8,256]{2,1,0:T(8,128)(2,1)} %bitcast.11), calls=%async_computation.1 | async-start | bytes 1048576 | tf_op jit(solution)/shard_map/all_to_all | solution.py:53
  44.0 8.0 %collective-permute-start.2 = (bf16[128,256]{1,0:T(8,128)(2,1)S(1)}, bf16[128,256]{1,0:T(8,128)(2,1)S(1)}, u32[]{:S(2)}, u32[]{:S(2)}) collective-permute-start(bf16[128,256]{1,0:T(8,128)(2,1)S(1)} %bitcast.54), channel_id=1, source_target_pairs={{0,256},{128,384},{256,0},{384,128},{1,257},{129,385},{257,1},{385... | collective-permute-start | bytes 196616 | tf_op jit(solution)/shard_map/ppermute | solution.py:63
  52.1 7.4 %collective-permute-start.3 = (bf16[256,256]{1,0:T(8,128)(2,1)S(1)}, bf16[256,256]{1,0:T(8,128)(2,1)S(1)}, u32[]{:S(2)}, u32[]{:S(2)}) collective-permute-start(bf16[256,256]{1,0:T(8,128)(2,1)S(1)} %pad_maximum_fusion.5), channel_id=1, source_target_pairs={{0,128},{128,0},{256,384},{384,256},{1,129},{129,1},{257,385},{385... | collective-permute-start | bytes 393224 | tf_op jit(solution)/shard_map/ppermute | solution.py:63
  60.1 3.2 %collective-permute-start.4 = (bf16[256,256]{1,0:T(8,128)(2,1)S(1)}, bf16[256,256]{1,0:T(8,128)(2,1)S(1)}, u32[]{:S(2)}, u32[]{:S(2)}) collective-permute-start(bf16[256,256]{1,0:T(8,128)(2,1)S(1)} %get-tuple-element.30), channel_id=1, source_target_pairs={{0,4},{4,0},{1,5},{5,1},{2,6},{6,2},{3,7},{7,3},{8,12},{12,8},{9,1... | collective-permute-start | bytes 393224 | tf_op jit(solution)/shard_map/ppermute | solution.py:220
  63.3 15.8 %copy-start.4 = (bf16[1,256,512]{2,1,0:T(8,128)(2,1)S(1)}, bf16[1,256,512]{2,1,0:T(8,128)(2,1)}, u32[]{:S(2)}) copy-start(bf16[1,256,512]{2,1,0:T(8,128)(2,1)} %param.6) | copy-start | bytes 786436
  63.3 16.3 %collective-permute-start.5 = (bf16[512,256]{1,0:T(8,128)(2,1)S(1)}, bf16[512,256]{1,0:T(8,128)(2,1)S(1)}, u32[]{:S(2)}, u32[]{:S(2)}) collective-permute-start(bf16[512,256]{1,0:T(8,128)(2,1)S(1)} %pad_maximum_fusion.3.w0_ref), channel_id=1, source_target_pairs={{0,1},{1,2},{2,3},{3,0},{4,5},{5,6},{6,7},{7,4},{8,9},{9,10},{10,1... | collective-permute-start | bytes 786440 | tf_op jit(solution)/shard_map/ppermute | solution.py:58
  67.0 14.8 %collective-permute-start.6 = (bf16[512,256]{1,0:T(8,128)(2,1)S(1)}, bf16[512,256]{1,0:T(8,128)(2,1)S(1)}, u32[]{:S(2)}, u32[]{:S(2)}) collective-permute-start(bf16[512,256]{1,0:T(8,128)(2,1)S(1)} %pad_maximum_fusion.3.w0_ref), channel_id=1, source_target_pairs={{0,2},{1,3},{2,0},{3,1},{4,6},{5,7},{6,4},{7,5},{8,10},{9,11},{10,... | collective-permute-start | bytes 786440 | tf_op jit(solution)/shard_map/ppermute | solution.py:58
  71.8 11.3 %collective-permute-start.7 = (bf16[512,256]{1,0:T(8,128)(2,1)S(1)}, bf16[512,256]{1,0:T(8,128)(2,1)S(1)}, u32[]{:S(2)}, u32[]{:S(2)}) collective-permute-start(bf16[512,256]{1,0:T(8,128)(2,1)S(1)} %pad_maximum_fusion.3.w0_ref), channel_id=1, source_target_pairs={{0,3},{1,0},{2,1},{3,2},{4,7},{5,4},{6,5},{7,6},{8,11},{9,8},{10,9... | collective-permute-start | bytes 786440 | tf_op jit(solution)/shard_map/ppermute | solution.py:58
  76.8 6.3 %collective-permute-start.8 = (bf16[256,512]{1,0:T(8,128)(2,1)S(1)}, bf16[256,512]{1,0:T(8,128)(2,1)S(1)}, u32[]{:S(2)}, u32[]{:S(2)}) collective-permute-start(bf16[256,512]{1,0:T(8,128)(2,1)S(1)} %pad_maximum_fusion.4.gown_ref), channel_id=1, source_target_pairs={{0,4},{4,0},{1,5},{5,1},{2,6},{6,2},{3,7},{7,3},{8,12},{12,8},{9,1... | collective-permute-start | bytes 786440 | tf_op jit(solution)/shard_map/ppermute | solution.py:236
  90.4 4.7 %collective-permute-start.9 = (bf16[256,1024]{1,0:T(8,128)(2,1)S(1)}, bf16[256,1024]{1,0:T(8,128)(2,1)S(1)}, u32[]{:S(2)}, u32[]{:S(2)}) collective-permute-start(bf16[256,1024]{1,0:T(8,128)(2,1)S(1)} %get-tuple-element.13), channel_id=1, source_target_pairs={{0,4},{4,0},{1,5},{5,1},{2,6},{6,2},{3,7},{7,3},{8,12},{12,8},{9,1... | collective-permute-start | bytes 1572872 | tf_op jit(solution)/shard_map/ppermute | solution.py:252
  92.6 7.2 %collective-permute-start.13 = (bf16[512,256]{1,0:T(8,128)(2,1)S(1)}, bf16[512,256]{1,0:T(8,128)(2,1)S(1)}, u32[]{:S(2)}, u32[]{:S(2)}) collective-permute-start(bf16[512,256]{1,0:T(8,128)(2,1)S(1)} %get-tuple-element.16), channel_id=1, source_target_pairs={{0,4},{4,0},{1,5},{5,1},{2,6},{6,2},{3,7},{7,3},{8,12},{12,8},{9,1... | collective-permute-start | bytes 786440 | tf_op jit(solution)/shard_map/ppermute | solution.py:247
  95.4 21.0 %collective-permute-start.10 = (bf16[256,1024]{1,0:T(8,128)(2,1)S(1)}, bf16[256,1024]{1,0:T(8,128)(2,1)S(1)}, u32[]{:S(2)}, u32[]{:S(2)}) collective-permute-start(bf16[256,1024]{1,0:T(8,128)(2,1)S(1)} %broadcast_select_fusion), channel_id=1, source_target_pairs={{0,1},{1,0},{2,3},{3,2},{4,5},{5,4},{6,7},{7,6},{8,9},{9,8},{10,11... | collective-permute-start | bytes 1572872 | tf_op jit(solution)/shard_map/ppermute | solution.py:63
  101.1 46.5 %all-to-all-start.2 = ((bf16[64,16,256]{2,1,0:T(8,128)(2,1)}), bf16[64,16,256]{2,1,0:T(8,128)(2,1)S(1)}, u32[]{:S(2)}, u32[]{:S(2)}) async-start(bf16[64,16,256]{2,1,0:T(8,128)(2,1)} %bitcast.21), calls=%async_computation.2 | async-start | bytes 1048576 | tf_op jit(solution)/shard_map/all_to_all | solution.py:53
  116.6 10.6 %collective-permute-start.11 = (bf16[128,1024]{1,0:T(8,128)(2,1)S(1)}, bf16[128,1024]{1,0:T(8,128)(2,1)S(1)}, u32[]{:S(2)}, u32[]{:S(2)}) collective-permute-start(bf16[128,1024]{1,0:T(8,128)(2,1)S(1)} %bitcast.60), channel_id=1, source_target_pairs={{0,128},{128,0},{256,384},{384,256},{1,129},{129,1},{257,385},{385... | collective-permute-start | bytes 786440 | tf_op jit(solution)/shard_map/ppermute | solution.py:63
  127.4 9.0 %collective-permute-start.12 = (bf16[64,1024]{1,0:T(8,128)(2,1)S(1)}, bf16[64,1024]{1,0:T(8,128)(2,1)S(1)}, u32[]{:S(2)}, u32[]{:S(2)}) collective-permute-start(bf16[64,1024]{1,0:T(8,128)(2,1)S(1)} %select_bitcast_fusion), channel_id=1, source_target_pairs={{0,256},{128,384},{256,0},{384,128},{1,257},{129,385},{257,1},{385... | collective-permute-start | bytes 393224 | tf_op jit(solution)/shard_map/ppermute | solution.py:63
  148.4 17.7 %all-to-all-start.3 = ((bf16[16,4,1024]{2,1,0:T(4,128)(2,1)}), bf16[16,4,1024]{2,1,0:T(4,128)(2,1)S(1)}, u32[]{:S(2)}, u32[]{:S(2)}) async-start(bf16[16,4,1024]{2,1,0:T(4,128)(2,1)} %reshape.619), calls=%async_computation.3 | async-start | bytes 262144 | tf_op jit(solution)/shard_map/all_to_all | solution.py:53
  152.7 3.2 %collective-permute-start.14 = (bf16[256,256]{1,0:T(8,128)(2,1)S(1)}, bf16[256,256]{1,0:T(8,128)(2,1)S(1)}, u32[]{:S(2)}, u32[]{:S(2)}) collective-permute-start(bf16[256,256]{1,0:T(8,128)(2,1)S(1)} %slice.151), channel_id=1, source_target_pairs={{0,4},{4,0},{1,5},{5,1},{2,6},{6,2},{3,7},{7,3},{8,12},{12,8},{9,1... | collective-permute-start | bytes 393224 | tf_op jit(solution)/shard_map/ppermute | solution.py:277
  166.8 8.9 %all-to-all-start.4 = ((f32[4,4,1024]{2,1,0:T(4,128)}), f32[4,4,1024]{2,1,0:T(4,128)S(1)}, u32[]{:S(2)}, u32[]{:S(2)}) async-start(f32[4,4,1024]{2,1,0:T(4,128)} %broadcast_in_dim.8), calls=%async_computation.4 | async-start | bytes 131072 | tf_op jit(solution)/shard_map/all_to_all | solution.py:53
  176.3 0.6 copy-start.3
